TPU v7x, 32 devices: a whole 2x2x4 slice. The times are simulated.
32 devices in a mesh: expert: 8 (over z, x), tensor: 4 (over y, core).
Axes of the slice: x: 2, y: 2, z: 4, core: 2. Of those that a mesh axis runs over, the one named last changes fastest.
Arguments:
- tokens: bfloat16 [4096, 1024], P('expert'), may hold values from -6 to 6
- teacher: bfloat16 [4096, 1024], P('expert'), may hold values from -6 to 6
- valid_mask: int32 [4096], P('expert'), may hold values from 0 to 1, as said below
- routes: int32 [4096, 8], P('expert'), may hold values from 0 to 31, all different within a row; in each aligned block of 512 rows (0 to 511, 512 to 1023, ...) at most 192 rows name the same one
- first_gain: float32 [1024], replicated, may hold values from 0.5 to 1.5
- query_weight: bfloat16 [1024, 1024], P(None, 'tensor'), may hold values from -0.75 to 0.75
- key_matrix: bfloat16 [1024, 512], P(None, 'tensor'), may hold values from -0.75 to 0.75
- value_matrix: bfloat16 [1024, 512], P(None, 'tensor'), may hold values from -0.1875 to 0.1875
- output_weight: bfloat16 [1024, 1024], P('tensor'), may hold values from -3 to 3
- second_gain: float32 [1024], replicated, may hold values from 0.5 to 1.5
- router_weight: bfloat16 [1024, 32], replicated, may hold values from -0.09375 to 0.09375
- expert_in: bfloat16 [64, 2, 512, 512], P('expert', None, None, 'tensor'), may hold values from -0.1875 to 0.1875
- expert_out: bfloat16 [64, 512, 512], P('expert', 'tensor'), may hold values from -3 to 3
Outputs:
- layer_output: bfloat16 [4096, 1024], P('expert')
- mean_loss: float32 [], replicated
- grad_tokens: float32 [4096, 1024], P('expert')
- grad_first_gain: float32 [1024], replicated
- grad_query: float32 [1024, 1024], P(None, 'tensor')
- grad_key: float32 [1024, 512], P(None, 'tensor')
- grad_value: float32 [1024, 512], P(None, 'tensor')
- grad_output: float32 [1024, 1024], P('tensor')
- grad_second_gain: float32 [1024], replicated
- grad_router: float32 [1024, 32], replicated
- grad_expert_in: float32 [64, 2, 512, 512], P('expert', None, None, 'tensor')
- grad_expert_out: float32 [64, 512, 512], P('expert', 'tensor')
Inputs may be any that keep to these rules, and one draw needn't show every extreme that they name: `routes`: each row names 8 different experts; among the 512 rows of one device no expert is named more than 192 times, a bound that some block reaches. `valid_mask`: the last of each device's 512 rows is 1.
All inputs are finite; a program needn't handle non-finite values.
Results may differ from a plain program's by a relative error of at most 0.017.
The roundings to bfloat16 on the way count: a program that leaves them out, or rounds other values in their place, can miss the bound.
Values may be sent and summed in bfloat16 or wider, within the bound.
No kernel may reach another device: no remote copies, remote signals or barrier semaphores. Data moves between devices by JAX's collectives and lax.ppermute only.
A program may use at most 192 MiB of HBM per device.

v0:
```python
import jax
import jax.numpy as jnp
from jax import lax
from jax.sharding import PartitionSpec as P

HEAD_DIM = 64
TOP = 8
BLOCK = 256


EPS = 1e-06
ATTN_SCALE = 0.015625
RESIDUAL = 0.22
THETA = 10000.0


def shifted(value, axis, steps):
    count = lax.axis_size(axis)
    pairs = [(source, (source + steps) % count) for source in range(count)]
    return lax.ppermute(value, axis, pairs)


def rope_tables(length, head_size):
    half_size = head_size // 2
    frequency = THETA ** (-(jnp.arange(half_size, dtype=jnp.float32) * 2.0) / head_size)
    angle_table = jnp.arange(length, dtype=jnp.float32)[:, None] * frequency[None, :]
    return (jnp.cos(angle_table)[:, None, :], jnp.sin(angle_table)[:, None, :])


def apply_rotary(values, cosine_lookup, sine_lookup):
    half_size = values.shape[-1] // 2
    lower_half, upper_half = (values[..., :half_size], values[..., half_size:])
    return jnp.concatenate(
        [
            lower_half * cosine_lookup - upper_half * sine_lookup,
            upper_half * cosine_lookup + lower_half * sine_lookup,
        ],
        -1,
    )


def unrotate(grads, cosine_lookup, sine_lookup):
    half_size = grads.shape[-1] // 2
    lower_half, upper_half = (grads[..., :half_size], grads[..., half_size:])
    return jnp.concatenate(
        [
            lower_half * cosine_lookup + upper_half * sine_lookup,
            upper_half * cosine_lookup - lower_half * sine_lookup,
        ],
        -1,
    )


def normalize(values):
    row_peak = jnp.max(values, -1, keepdims=True)
    exp_scores = jnp.exp(values - row_peak)
    return exp_scores / jnp.sum(exp_scores, -1, keepdims=True)


def slot_tables(route_ids, expert_count, capacity):
    row_count, top_count = route_ids.shape
    onehot = route_ids[:, :, None] == jnp.arange(expert_count, dtype=jnp.int32)[None, None, :]
    hit_count = jnp.sum(onehot.astype(jnp.int32), 1)
    slot_place = jnp.cumsum(hit_count, 0) - 1
    within = jnp.take_along_axis(slot_place, route_ids, 1)
    dest_slot = route_ids * capacity + within
    pair_count = row_count * top_count
    source = (
        jnp.full((expert_count * capacity,), pair_count, jnp.int32)
        .at[dest_slot.reshape(-1)]
        .set(jnp.arange(pair_count, dtype=jnp.int32))
    )
    live_slot = source < pair_count
    token_row = jnp.minimum(source, pair_count - 1) // top_count
    return (onehot, dest_slot, source, live_slot, token_row)


def per_device(
    tokens,
    teacher,
    valid_mask,
    routes,
    first_gain,
    query_weight,
    key_matrix,
    value_matrix,
    output_weight,
    second_gain,
    router_weight,
    expert_in,
    expert_out,
):
    row_count = tokens.shape[0]
    model_width = tokens.shape[1]
    half_width = model_width // 2
    local_query = query_weight.shape[1] // HEAD_DIM
    local_kv = key_matrix.shape[1] // HEAD_DIM
    query_group_size = local_query // local_kv
    expert_count = router_weight.shape[1]
    row_local = expert_in.shape[0]
    senders = lax.axis_size("expert")
    partner_step = senders // 2
    capacity = 3 * row_count * TOP // (2 * expert_count)
    pair_count = row_count * TOP
    score_rows = min(512, row_count)
    valid_total = lax.psum(jnp.sum(valid_mask).astype(jnp.float32), "expert")
    tokens_f32 = tokens.astype(jnp.float32)
    scale_one = lax.rsqrt(jnp.mean(tokens_f32 * tokens_f32, -1, keepdims=True) + EPS)
    unit_one = tokens_f32 * scale_one
    first_normed = (unit_one * first_gain).astype(jnp.bfloat16)
    cosine_lookup, sine_lookup = rope_tables(row_count, HEAD_DIM)
    query_linear = jnp.dot(first_normed, query_weight, preferred_element_type=jnp.float32).reshape(
        row_count, local_query, HEAD_DIM
    )
    keys_linear = jnp.dot(first_normed, key_matrix, preferred_element_type=jnp.float32).reshape(
        row_count, local_kv, HEAD_DIM
    )
    value_low = jnp.dot(first_normed, value_matrix, preferred_element_type=jnp.float32).astype(
        jnp.bfloat16
    )
    value_low = value_low.reshape(row_count, local_kv, HEAD_DIM)
    query_rotated = apply_rotary(query_linear, cosine_lookup, sine_lookup).astype(jnp.bfloat16)
    keys_rot = apply_rotary(keys_linear, cosine_lookup, sine_lookup).astype(jnp.bfloat16)
    block_of = jnp.arange(row_count, dtype=jnp.int32) // BLOCK

    def scores(start_row):
        stop_row = start_row + score_rows
        query_block = query_rotated.reshape(score_rows, local_kv, query_group_size, HEAD_DIM)
        score_block = (
            jnp.einsum("qhgd,khd->hgqk", query_block, keys_rot, preferred_element_type=jnp.float32)
            * ATTN_SCALE
        )
        allowed = block_of[None, :stop_row] <= block_of[start_row:stop_row, None]
        return (query_block, jnp.where(allowed, score_block, -1e30))

    attn_parts, row_peaks, row_totals = ([], [], [])
    start_row = 0
    query_block, score_block = scores(start_row)
    row_peak = jnp.max(score_block, -1, keepdims=True)
    exp_scores = jnp.exp(score_block - row_peak)
    row_total = jnp.sum(exp_scores, -1, keepdims=True)
    attn_probs = (exp_scores / row_total).astype(jnp.bfloat16)
    attn_parts.append(
        jnp.einsum("hgqk,khd->qhgd", attn_probs, value_low, preferred_element_type=jnp.float32)
    )
    row_peaks.append(row_peak)
    row_totals.append(row_total)
    attended = attn_parts[0].reshape(row_count, local_query * HEAD_DIM).astype(jnp.bfloat16)
    attn_part = jnp.dot(attended, output_weight, preferred_element_type=jnp.float32)
    attn_sum = lax.psum(attn_part, "tensor")
    hidden_state = tokens_f32 + RESIDUAL * attn_sum
    scale_two = lax.rsqrt(jnp.mean(hidden_state * hidden_state, -1, keepdims=True) + EPS)
    unit_two = hidden_state * scale_two
    normed_two = (unit_two * second_gain).astype(jnp.bfloat16)
    router_logits = jnp.dot(normed_two, router_weight, preferred_element_type=jnp.float32)
    onehot, dest_slot, source, live_slot, token_row = slot_tables(routes, expert_count, capacity)
    picked = jnp.sum(jnp.where(onehot, router_logits[:, None, :], 0.0), -1)
    gate_probs = normalize(picked)

    def slot_rows(slot_values):
        split_rows = slot_values.reshape(expert_count, capacity, 2, half_width).transpose(
            2, 0, 1, 3
        )
        return split_rows.reshape(senders, row_local, capacity, half_width)

    def slot_columns(returned, width):
        joined = returned.reshape(2, expert_count, capacity, width).transpose(1, 2, 0, 3)
        return joined.reshape(expert_count * capacity, 2, width)

    send_rows = slot_rows(
        jnp.where(live_slot[:, None], normed_two[token_row], jnp.zeros((), jnp.bfloat16))
    )
    received = lax.all_to_all(send_rows, "expert", split_axis=0, concat_axis=2, tiled=True)
    expert_rows = received.reshape(row_local, senders * capacity, half_width)
    gate_up_part = jnp.einsum(
        "rmd,rcdf->rmcf", expert_rows, expert_in, preferred_element_type=jnp.float32
    )
    gate_up_pre = gate_up_part + shifted(gate_up_part, "expert", partner_step)
    gate_pre = gate_up_pre[:, :, 0]
    up_pre = gate_up_pre[:, :, 1]
    inner_act = (jax.nn.silu(gate_pre) * up_pre).astype(jnp.bfloat16)
    expert_result = jnp.einsum(
        "rmf,rfd->rmd", inner_act, expert_out, preferred_element_type=jnp.float32
    )
    expert_result = expert_result.astype(jnp.bfloat16).reshape(
        row_local, senders, capacity, half_width
    )
    returned = lax.all_to_all(expert_result, "expert", split_axis=1, concat_axis=0, tiled=True)
    per_route = slot_columns(returned, half_width).reshape(expert_count * capacity, model_width)[
        dest_slot
    ]
    moe_part = jnp.sum(gate_probs[:, :, None] * per_route, 1)
    moe_sum = lax.psum(moe_part, "tensor")
    output = hidden_state + RESIDUAL * moe_sum
    residual_err = output - teacher.astype(jnp.float32)
    valid_rows = valid_mask.astype(jnp.float32)
    squared_local = jnp.sum(valid_rows * jnp.sum(residual_err * residual_err, -1))
    token_total = senders * row_count
    grad_out = token_total / valid_total * valid_rows[:, None] * residual_err
    grad_moe = (RESIDUAL * grad_out).astype(jnp.bfloat16)
    gate_part = jnp.einsum("td,tkd->tk", grad_moe, per_route, preferred_element_type=jnp.float32)
    gate_slot = gate_probs.reshape(pair_count)[jnp.minimum(source, pair_count - 1)]
    grad_slots = jnp.where(live_slot[:, None], gate_slot[:, None] * grad_moe[token_row], 0.0)
    grad_received = lax.all_to_all(
        slot_rows(grad_slots.astype(jnp.bfloat16)),
        "expert",
        split_axis=0,
        concat_axis=2,
        tiled=True,
    )
    grad_expert = grad_received.reshape(row_local, senders * capacity, half_width)
    grad_inner_part = jnp.einsum(
        "rmd,rfd->rmf", grad_expert, expert_out, preferred_element_type=jnp.float32
    )
    grad_inner = grad_inner_part + shifted(grad_inner_part, "expert", partner_step)
    grad_expert_out = jnp.einsum(
        "rmf,rmd->rfd", inner_act, grad_expert, preferred_element_type=jnp.float32
    )
    sigmoid_gate = jax.nn.sigmoid(gate_pre)
    grad_gate = grad_inner * up_pre * sigmoid_gate * (1.0 + gate_pre * (1.0 - sigmoid_gate))
    grad_up = grad_inner * (gate_pre * sigmoid_gate)
    grad_pre = jnp.stack([grad_gate, grad_up], 2).astype(jnp.bfloat16)
    grad_expert_in = jnp.einsum(
        "rmd,rmcf->rcdf", expert_rows, grad_pre, preferred_element_type=jnp.float32
    )
    grad_slot_rows = jnp.einsum(
        "rmcf,rcdf->rmd", grad_pre, expert_in, preferred_element_type=jnp.float32
    )
    grad_slot_rows = grad_slot_rows.astype(jnp.bfloat16).reshape(
        row_local, senders, capacity, half_width
    )
    grad_back = lax.all_to_all(grad_slot_rows, "expert", split_axis=1, concat_axis=0, tiled=True)
    grad_back = slot_columns(grad_back, half_width).reshape(expert_count * capacity, model_width)
    grad_two_part = jnp.sum(grad_back[dest_slot].astype(jnp.float32), 1)
    grad_two_experts, grad_gates = lax.psum((grad_two_part, gate_part), "tensor")
    grad_picked = gate_probs * (grad_gates - jnp.sum(gate_probs * grad_gates, -1, keepdims=True))
    grad_logits = jnp.sum(jnp.where(onehot, grad_picked[:, :, None], 0.0), 1).astype(jnp.bfloat16)
    grad_router = jnp.einsum(
        "td,te->de", normed_two, grad_logits, preferred_element_type=jnp.float32
    )
    grad_two = grad_two_experts + jnp.einsum(
        "te,de->td", grad_logits, router_weight, preferred_element_type=jnp.float32
    )
    grad_second_gain = jnp.sum(grad_two * unit_two, 0)
    grad_unit_two = grad_two * second_gain
    grad_hidden = grad_out + scale_two * (
        grad_unit_two - unit_two * jnp.mean(grad_unit_two * unit_two, -1, keepdims=True)
    )
    grad_attn = (RESIDUAL * grad_hidden).astype(jnp.bfloat16)
    grad_output = jnp.einsum("tc,td->cd", attended, grad_attn, preferred_element_type=jnp.float32)
    grad_attended = jnp.einsum(
        "td,cd->tc", grad_attn, output_weight, preferred_element_type=jnp.float32
    )
    grad_attended = grad_attended.astype(jnp.bfloat16).reshape(
        row_count, local_kv, query_group_size, HEAD_DIM
    )
    grad_query_parts = []
    grad_keys = jnp.zeros((row_count, local_kv, HEAD_DIM), jnp.float32)
    grad_values = jnp.zeros((row_count, local_kv, HEAD_DIM), jnp.float32)
    for block_index, start_row in enumerate(range(0, row_count, score_rows)):
        stop_row = start_row + score_rows
        query_block, score_block = scores(start_row)
        attn_probs = jnp.exp(score_block - row_peaks[block_index]) / row_totals[block_index]
        probs_low = attn_probs.astype(jnp.bfloat16)
        grad_probs = jnp.einsum(
            "qhgd,khd->hgqk", grad_attended, value_low, preferred_element_type=jnp.float32
        )
        grad_scores = attn_probs * (
            grad_probs - jnp.sum(attn_probs * grad_probs, -1, keepdims=True)
        )
        grad_scores = grad_scores.astype(jnp.bfloat16)
        grad_query_parts.append(
            ATTN_SCALE
            * jnp.einsum(
                "hgqk,khd->qhgd", grad_scores, keys_rot, preferred_element_type=jnp.float32
            )
        )
        grad_keys = grad_keys.at[:stop_row].add(
            ATTN_SCALE
            * jnp.einsum(
                "hgqk,qhgd->khd", grad_scores, query_block, preferred_element_type=jnp.float32
            )
        )
        grad_values = grad_values.at[:stop_row].add(
            jnp.einsum(
                "hgqk,qhgd->khd", probs_low, grad_attended, preferred_element_type=jnp.float32
            )
        )
    grad_query_rot = grad_query_parts[0].reshape(row_count, local_query, HEAD_DIM)
    grad_query_low = unrotate(grad_query_rot, cosine_lookup, sine_lookup).reshape(
        row_count, local_query * HEAD_DIM
    )
    grad_query_low = grad_query_low.astype(jnp.bfloat16)
    grad_keys_low = unrotate(grad_keys, cosine_lookup, sine_lookup).reshape(
        row_count, local_kv * HEAD_DIM
    )
    grad_keys_low = grad_keys_low.astype(jnp.bfloat16)
    grad_values_low = grad_values.reshape(row_count, local_kv * HEAD_DIM).astype(jnp.bfloat16)
    grad_query = jnp.einsum(
        "td,tc->dc", first_normed, grad_query_low, preferred_element_type=jnp.float32
    )
    grad_key = jnp.einsum(
        "td,tc->dc", first_normed, grad_keys_low, preferred_element_type=jnp.float32
    )
    grad_value = jnp.einsum(
        "td,tc->dc", first_normed, grad_values_low, preferred_element_type=jnp.float32
    )
    grad_one_part = (
        jnp.einsum("tc,dc->td", grad_query_low, query_weight, preferred_element_type=jnp.float32)
        + jnp.einsum("tc,dc->td", grad_keys_low, key_matrix, preferred_element_type=jnp.float32)
        + jnp.einsum("tc,dc->td", grad_values_low, value_matrix, preferred_element_type=jnp.float32)
    )
    grad_one = lax.psum(grad_one_part.astype(jnp.bfloat16), "tensor").astype(jnp.float32)
    grad_first_gain = jnp.sum(grad_one * unit_one, 0)
    grad_unit_one = grad_one * first_gain
    grad_tokens = grad_hidden + scale_one * (
        grad_unit_one - unit_one * jnp.mean(grad_unit_one * unit_one, -1, keepdims=True)
    )
    reduced = lax.psum(
        (
            grad_first_gain,
            grad_query,
            grad_key,
            grad_value,
            grad_output,
            grad_second_gain,
            grad_router,
            squared_local,
        ),
        "expert",
    )
    loss_value = reduced[7] / (2.0 * model_width * valid_total)
    return (
        output.astype(jnp.bfloat16),
        loss_value,
        grad_tokens,
        reduced[0],
        reduced[1],
        reduced[2],
        reduced[3],
        reduced[4],
        reduced[5],
        reduced[6],
        grad_expert_in,
        grad_expert_out,
    )


def solution(mesh):
    return jax.shard_map(
        per_device,
        mesh=mesh,
        in_specs=(
            P("expert", None),
            P("expert", None),
            P("expert"),
            P("expert", None),
            P(),
            P(None, "tensor"),
            P(None, "tensor"),
            P(None, "tensor"),
            P("tensor", None),
            P(),
            P(),
            P("expert", None, None, "tensor"),
            P("expert", "tensor", None),
        ),
        out_specs=(
            P("expert", None),
            P(),
            P("expert", None),
            P(),
            P(None, "tensor"),
            P(None, "tensor"),
            P(None, "tensor"),
            P("tensor", None),
            P(),
            P(),
            P("expert", None, None, "tensor"),
            P("expert", "tensor", None),
        ),
        check_vma=False,
    )
```

profile of v0, /device:TPU:0, one launch (start us, length us, event | category | flops | bytes accessed | tf_op | source)
XLA Modules:
  0.0 2694.3 jit_solution(5498400139283303845)
XLA Ops:
  26.2 33.0 %gather_fusion.5 = s32[4096]{0:T(1024)S(1)} fusion(s32[512,32]{0,1:T(8,128)S(1)} %bitcast_bitcast_fusion, s32[4096]{0:T(1024)S(1)} %reshape.422), kind=kCustom, calls=%fused_computation.5 | custom fusion | bytes 65536 | tf_op jit(solution)/shard_map/jit(take_along_axis)/gather | solution.py:65
  60.4 15.5 scatter_custom_fusion
  82.1 26.9 gather_fusion
  109.0 21.2 gather.23
  137.8 278.8 %all_to_all.60 = bf16[8,8,192,512]{3,2,1,0:T(8,128)(2,1)S(1)} all-to-all(bf16[8,8,192,512]{3,2,1,0:T(8,128)(2,1)S(1)} %bitcast.210), channel_id=1, replica_groups=mesh['expert'=8,'tensor'=4] {'expert'}, dimensions={0} | all-to-all | bytes 25165824 | tf_op jit(solution)/shard_map/all_to_all | solution.py:173
  421.8 12.5 fusion.83
  434.9 540.7 %collective-permute-done = f32[8,1536,2,128]{3,1,2,0:T(8,128)S(1)} collective-permute-done((f32[8,1536,2,128]{3,1,2,0:T(8,128)}, f32[8,1536,2,128]{3,1,2,0:T(8,128)S(1)}, u32[]{:S(2)}, u32[]{:S(2)}) %collective-permute-start) | collective-permute-done | bytes 12582944 | tf_op jit(solution)/shard_map/ppermute | solution.py:20
  1013.6 269.8 %all-to-all-done.1 = bf16[8,8,192,512]{3,2,0,1:T(8,128)(2,1)} async-done(((bf16[8,8,192,512]{3,2,0,1:T(8,128)(2,1)}), bf16[8,8,192,512]{3,2,0,1:T(8,128)(2,1)}, u32[]{:S(2)}, u32[]{:S(2)}) %all-to-all-start.1) | async-done | bytes 12582944 | tf_op jit(solution)/shard_map/all_to_all | solution.py:188
  1283.3 23.0 copy.103
  1313.4 27.1 %gather_fusion.1 = bf16[4096,1024]{1,0:T(8,128)(2,1)} fusion(bf16[6144,1024]{1,0:T(8,128)(2,1)} %bitcast.205, s32[4096]{0:T(1024)S(1)} %broadcast_clamp_fusion), kind=kCustom, calls=%fused_computation.1 | custom fusion | bytes 16793600 | tf_op jit(solution)/shard_map/gather | solution.py:189
  1351.7 20.1 psum.101
  1372.7 34.3 %gather_fusion.2 = f32[6144]{0:T(1024)S(1)} fusion(f32[4096]{0:T(1024)S(1)} %div.124, s32[6144]{0:T(1024)S(1)} %get-tuple-element.129), kind=kCustom, calls=%fused_computation.2 | custom fusion | bytes 73728 | tf_op jit(solution)/shard_map/gather | solution.py:202
  1410.1 26.9 gather_fusion.3
  1437.0 31.3 %reshape.381 = f32[32,192,2,512]{3,2,1,0:T(2,128)} reshape(bf16[6144,1024]{1,0:T(8,128)(2,1)} %gather_fusion.3) | data formatting | bytes 37748736 | tf_op jit(solution)/shard_map/convert_element_type | solution.py:203
  1468.2 13.5 fusion.2
  1481.8 272.4 %all_to_all.61 = bf16[8,8,192,512]{3,2,1,0:T(8,128)(2,1)S(1)} all-to-all(bf16[8,8,192,512]{3,2,1,0:T(8,128)(2,1)S(1)} %bitcast.217), channel_id=1, replica_groups=mesh['expert'=8,'tensor'=4] {'expert'}, dimensions={0} | all-to-all | bytes 25165824 | tf_op jit(solution)/shard_map/all_to_all | solution.py:204
  1764.1 269.5 %collective-permute-done.1 = f32[8,1536,128]{2,1,0:T(8,128)} collective-permute-done((f32[8,1536,128]{2,1,0:T(8,128)}, f32[8,1536,128]{2,1,0:T(8,128)}, u32[]{:S(2)}, u32[]{:S(2)}) %collective-permute-start.1) | collective-permute-done | bytes 6291488 | tf_op jit(solution)/shard_map/ppermute | solution.py:20
  2033.6 12.6 fusion.17
  2063.6 276.9 %all_to_all.62 = bf16[8,8,192,512]{3,2,0,1:T(8,128)(2,1)S(1)} all-to-all(bf16[8,8,192,512]{3,2,0,1:T(8,128)(2,1)S(1)} %copy.109), channel_id=1, replica_groups=mesh['expert'=8,'tensor'=4] {'expert'}, dimensions={1} | all-to-all | bytes 25165824 | tf_op jit(solution)/shard_map/all_to_all | solution.py:232
  2340.5 49.8 %copy.110 = bf16[32,192,2,512]{3,2,1,0:T(2,128)(2,1)S(1)} copy(bf16[32,192,2,512]{3,1,0,2:T(8,128)(2,1)S(1)} %bitcast.214) | data formatting | bytes 25165824 | tf_op jit(solution)/shard_map/transpose | solution.py:167
  2397.3 27.1 %gather_fusion.4 = bf16[4096,1024]{1,0:T(8,128)(2,1)} fusion(bf16[6144,1024]{1,0:T(8,128)(2,1)} %bitcast.204, s32[4096]{0:T(1024)S(1)} %broadcast_clamp_fusion), kind=kCustom, calls=%fused_computation.4 | custom fusion | bytes 16793600 | tf_op jit(solution)/shard_map/gather | solution.py:234
  2458.3 28.1 %all-reduce.12.cloned.1.call-done = f32[512,1024]{1,0:T(8,128)} async-done(((f32[512,1024]{1,0:T(8,128)}), f32[512,1024]{1,0:T(8,128)}) %all-reduce.12.cloned.1.call-update) | async-done | bytes 2097168 | tf_op jit(solution)/shard_map/psum | solution.py:235
  2543.1 23.5 all-reduce
  2571.1 108.7 %all-reduce.16.cloned.1.call-done = (f32[1024,256]{1,0:T(8,128)}, f32[1024,128]{1,0:T(8,128)}, f32[1024,128]{1,0:T(8,128)}, f32[256,1024]{1,0:T(8,128)}, f32[1024,32]{0,1:T(8,128)}) async-done(((f32[1024,256]{1,0:T(8,128)}, f32[1024,128]{1,0:T(8,128)}, f32[1024,128]{1,0:T(8,128)}, f32[256,1024]{1,0:T(8,128)}, f32[1024,32]{0,1:T(8,128)}), (f32[1024,256]{1,0:T(8,128)}, f32[1024,128]{1,0:T(8,128)}, ...) | async-done | bytes 3276816 | tf_op jit(solution)/shard_map/psum | solution.py:319
  (262 shorter events, 232.2 us)
Async XLA Ops:
  7.2 414.7 %copy-start = (bf16[8,2,512,128]{3,2,1,0:T(8,128)(2,1)S(1)}, bf16[8,2,512,128]{3,2,1,0:T(8,128)(2,1)}, u32[]{:S(2)}) copy-start(bf16[8,2,512,128]{3,2,1,0:T(8,128)(2,1)} %param.32) | copy-start | bytes 6291460
  7.2 71.3 %all-reduce.8.cloned.1.call-start = ((), (), s32[]{:S(2)}) async-start(), calls=%async_computation.4 | async-start | bytes 4194304 | tf_op jit(solution)/shard_map/psum | solution.py:150
  59.4 22.5 copy-start.52
  80.5 28.5 %copy-start.56 = (f32[512]{0:T(512)}, f32[512]{0:T(512)S(1)}, u32[]{:S(2)}) copy-start(f32[512]{0:T(512)S(1)} %add_rsqrt_fusion) | copy-start | bytes 6148
  82.1 930.8 %copy-start.1 = (bf16[512,1024]{1,0:T(8,128)(2,1)}, bf16[512,1024]{1,0:T(8,128)(2,1)S(1)}, u32[]{:S(2)}) copy-start(bf16[512,1024]{1,0:T(8,128)(2,1)S(1)} %multiply_convert_fusion.5) | copy-start | bytes 3145732
  434.4 541.2 %collective-permute-start = (f32[8,1536,2,128]{3,1,2,0:T(8,128)}, f32[8,1536,2,128]{3,1,2,0:T(8,128)S(1)}, u32[]{:S(2)}, u32[]{:S(2)}) collective-permute-start(f32[8,1536,2,128]{3,1,2,0:T(8,128)} %fusion.83), channel_id=1, source_target_pairs={{0,16},{4,20},{8,24},{12,28},{16,0},{20,4},{24,8},{28,12},{1,17},{... | collective-permute-start | bytes 37748744 | tf_op jit(solution)/shard_map/ppermute | solution.py:20
  1004.4 278.9 %all-to-all-start.1 = ((bf16[8,8,192,512]{3,2,0,1:T(8,128)(2,1)}), bf16[8,8,192,512]{3,2,0,1:T(8,128)(2,1)}, u32[]{:S(2)}, u32[]{:S(2)}) async-start(bf16[8,8,192,512]{3,2,0,1:T(8,128)(2,1)} %copy.102), calls=%async_computation.1 | async-start | bytes 25165824 | tf_op jit(solution)/shard_map/all_to_all | solution.py:188
  1009.9 397.1 %all-reduce.10.cloned.1.call-start = ((), (), s32[]{:S(2)}) async-start(), calls=%async_computation.5 | async-start | bytes 4194304 | tf_op jit(solution)/shard_map/psum | solution.py:193
  1013.4 293.0 %copy-start.29 = (f32[512,8]{0,1:T(8,128)}, f32[512,8]{0,1:T(8,128)S(1)}, u32[]{:S(2)}) copy-start(f32[512,8]{0,1:T(8,128)S(1)} %select_reduce_fusion.1) | copy-start | bytes 49156
  1013.4 293.0 %copy-start.50 = (f32[512]{0:T(512)}, f32[512]{0:T(512)S(1)}, u32[]{:S(2)}) copy-start(f32[512]{0:T(512)S(1)} %reduce_max.19) | copy-start | bytes 6148
  1013.4 292.9 %copy-start.54 = (f32[512]{0:T(512)}, f32[512]{0:T(512)S(1)}, u32[]{:S(2)}) copy-start(f32[512]{0:T(512)S(1)} %fusion.53) | copy-start | bytes 6148
  1350.3 1136.1 %all-reduce.12.cloned.1.call-start = ((), (), s32[]{:S(2)}) async-start(), calls=%async_computation.6 | async-start | bytes 4194304 | tf_op jit(solution)/shard_map/psum | solution.py:235
  1372.5 34.5 %copy-start.58 = (f32[512]{0:T(512)}, f32[512]{0:T(512)S(1)}, u32[]{:S(2)}) copy-start(f32[512]{0:T(512)S(1)} %convert_multiply_fusion.3) | copy-start | bytes 6148
  1410.1 26.9 copy-start.3
  1762.4 271.2 %collective-permute-start.1 = (f32[8,1536,128]{2,1,0:T(8,128)}, f32[8,1536,128]{2,1,0:T(8,128)}, u32[]{:S(2)}, u32[]{:S(2)}) collective-permute-start(f32[8,1536,128]{2,1,0:T(8,128)} %fusion.84), channel_id=1, source_target_pairs={{0,16},{4,20},{8,24},{12,28},{16,0},{20,4},{24,8},{28,12},{1,17},{... | collective-permute-start | bytes 18874376 | tf_op jit(solution)/shard_map/ppermute | solution.py:20
  2436.3 104.8 %all-reduce.14.cloned.1.call-start = ((), (), s32[]{:S(2)}) async-start(), calls=%async_computation.7 | async-start | bytes 2097152 | tf_op jit(solution)/shard_map/psum | solution.py:313
  2436.8 20.5 copy-start.39
  2436.8 20.6 copy-start.2
  2436.8 49.7 %copy-start.41 = (bf16[1024,32]{0,1:T(8,128)(2,1)S(1)}, bf16[1024,32]{0,1:T(8,128)(2,1)}, u32[]{:S(2)}) copy-start(bf16[1024,32]{0,1:T(8,128)(2,1)} %param.31) | copy-start | bytes 196612
  2436.8 49.7 %copy-start.53 = (f32[1024]{0:T(1024)S(1)}, f32[1024]{0:T(1024)}, u32[]{:S(2)}) copy-start(f32[1024]{0:T(1024)} %param.30) | copy-start | bytes 12292
  2436.8 49.6 %copy-start.57 = (f32[512]{0:T(512)S(1)}, f32[512]{0:T(512)}, u32[]{:S(2)}) copy-start(f32[512]{0:T(512)} %copy-done.56) | copy-start | bytes 6148
  2458.3 33.2 %copy-start.14 = (bf16[512,1024]{1,0:T(8,128)(2,1)S(1)}, bf16[512,1024]{1,0:T(8,128)(2,1)}, u32[]{:S(2)}) copy-start(bf16[512,1024]{1,0:T(8,128)(2,1)} %param.22) | copy-start | bytes 3145732
  2458.3 33.2 %copy-start.59 = (f32[512]{0:T(512)S(1)}, f32[512]{0:T(512)}, u32[]{:S(2)}) copy-start(f32[512]{0:T(512)} %copy-done.58) | copy-start | bytes 6148
  2504.5 175.2 %all-reduce.16.cloned.1.call-start = ((), (), s32[]{:S(2)}) async-start(), calls=%async_computation.8 | async-start | bytes 6553600 | tf_op jit(solution)/shard_map/psum | solution.py:319
  (55 other events, 273.8 us)
Sparse Core Ops, SparseCore 0:
  24.4 54.1 all-reduce.7
  1350.5 49.7 all-reduce.9
  2436.4 50.0 all-reduce.11
  2504.7 36.3 all-reduce.13
  2545.7 134.0 all-reduce.15
where the time goes:
time: 2700 us; the launch traced here: 2690 us
  waiting for transfers between devices  1230 us (46%)
  blocking collectives  883 us (33%)
  local copies, waits for them, and re-layouts  378 us (14%)
  matrix products  94.3 us (3%)
  other arithmetic  84.3 us (3%)
    ppermute x2, waiting for transfers between devices, shifted(): return lax.ppermute(value, axis, pairs)  810 us
    all_to_all x1, blocking collectives, per_device(): lax.all_to_all(send_rows, 'expert', split_axis=0, concat_axis=2, tiled=True)  279 us
    all_to_all x1, blocking collectives, per_device(): lax.all_to_all(grad_slot_rows, 'expert', split_axis=1, concat_axis=0, til...  277 us
    all_to_all x1, blocking collectives, per_device(): lax.all_to_all(slot_rows(grad_slots.astype(jnp.bfloat16)), 'expert', spli...  272 us
    all_to_all x1, waiting for transfers between devices, per_device(): lax.all_to_all(expert_result, 'expert', split_axis=1, concat_axis=0, tile...  270 us
    psum x1, waiting for transfers between devices, per_device(): lax.psum((grad_first_gain, grad_query, grad_key, grad_value, grad_output,...  109 us
    transpose x2, local copies, waits for them, and re-layouts, slot_columns(): returned.reshape(2, expert_count, capacity, width).transpose(1, 2, 0, 3)  72.8 us
  transfers between devices with their start and end apart: 8, of which 7 were waited for; matrix products, arithmetic and copies ran while one was open for 5% of the time, Pallas kernels for 0%

commit v1 on v0

--- a/solution.py
+++ b/solution.py
@@ -1,6 +1,8 @@
 import jax
 import jax.numpy as jnp
 from jax import lax
+from jax.experimental import pallas as pl
+from jax.experimental.pallas import tpu as pltpu
 from jax.sharding import PartitionSpec as P
 
 HEAD_DIM = 64
@@ -75,7 +77,7 @@
     return (onehot, dest_slot, source, live_slot, token_row)
 
 
-def per_device(
+def general_device(
     tokens,
     teacher,
     valid_mask,
@@ -346,6 +348,594 @@
     )
 
 
+BF16 = jnp.bfloat16
+F32 = jnp.float32
+CHUNK = 256
+SHARE = 128
+NT = (((1,), (1,)), ((), ()))
+
+
+def weight_copies(pieces, in_buf, out_buf, sems, expert, slot):
+    in_own, in_other, out_own, out_other = (pieces[0:4], pieces[4:8], pieces[8:12], pieces[12:16])
+    copies = []
+    for q in range(4):
+        for half, piece in ((0, in_own[q]), (1, in_other[q])):
+            width = piece.shape[2]
+            for c in range(2):
+                target = in_buf.at[
+                    slot, pl.ds(half * width, width), pl.ds((2 * q + c) * SHARE, SHARE)
+                ]
+                copies.append((piece.at[expert, c], target))
+        for half, piece in ((0, out_own[q]), (1, out_other[q])):
+            width = piece.shape[2]
+            target = out_buf.at[slot, pl.ds(q * SHARE, SHARE), pl.ds(half * width, width)]
+            copies.append((piece.at[expert], target))
+    return [
+        pltpu.make_async_copy(source, target, sems.at[slot, n])
+        for n, (source, target) in enumerate(copies)
+    ]
+
+
+def reorder_halves(half_index, source, target):
+    width = source.shape[1] // 2
+
+    @pl.when(half_index == 0)
+    def _():
+        target[...] = source[...]
+
+    @pl.when(half_index == 1)
+    def _():
+        target[:, :width] = source[:, width:]
+        target[:, width:] = source[:, :width]
+
+
+def split_pairs(values):
+    blocks = [values[:, i * SHARE : (i + 1) * SHARE] for i in range(values.shape[1] // SHARE)]
+    return (jnp.concatenate(blocks[0::2], 1), jnp.concatenate(blocks[1::2], 1))
+
+
+def join_pairs(first, second):
+    blocks = []
+    for i in range(first.shape[1] // SHARE):
+        blocks.append(first[:, i * SHARE : (i + 1) * SHARE])
+        blocks.append(second[:, i * SHARE : (i + 1) * SHARE])
+    return jnp.concatenate(blocks, 1)
+
+
+def chunk_loop(row_count, body):
+    def step(i, carry):
+        body(pl.ds(pl.multiple_of(i * CHUNK, CHUNK), CHUNK))
+        return carry
+
+    lax.fori_loop(0, row_count // CHUNK, step, 0)
+
+
+def gate_column(gates, expert):
+    lane = lax.broadcasted_iota(jnp.int32, gates.shape, 1)
+    return jnp.sum(jnp.where(lane == expert, gates, 0.0), -1, keepdims=True)
+
+
+def stream_weights(pieces, in_buf, out_buf, sems):
+    expert = pl.program_id(0)
+    slot = lax.rem(expert, 2)
+
+    @pl.when(expert == 0)
+    def _():
+        for copy in weight_copies(pieces, in_buf, out_buf, sems, 0, 0):
+            copy.start()
+
+    @pl.when(expert + 1 < pl.num_programs(0))
+    def _():
+        for copy in weight_copies(pieces, in_buf, out_buf, sems, expert + 1, 1 - slot):
+            copy.start()
+
+    return (expert, slot)
+
+
+def forward_body(half_ref, rows_ref, route_ref, router_ref, *rest):
+    pieces = rest[:16]
+    sum_ref, pre_ref, gated_ref, gate_ref, rows_rel, acc, in_buf, out_buf, sems = rest[16:]
+    expert, slot = stream_weights(pieces, in_buf, out_buf, sems)
+    row_count = rows_ref.shape[0]
+
+    @pl.when(expert == 0)
+    def _():
+        reorder_halves(half_ref[0], rows_ref, rows_rel)
+        acc[...] = jnp.zeros_like(acc)
+
+        def gating(rows):
+            logits = jnp.dot(rows_ref[rows, :], router_ref[...], preferred_element_type=F32)
+            lane = lax.broadcasted_iota(jnp.int32, logits.shape, 1)
+            ids = route_ref[rows, :]
+            mask = ids[:, 0:1] == lane
+            for k in range(1, TOP):
+                mask = mask | (ids[:, k : k + 1] == lane)
+            masked = jnp.where(mask, logits, -1e30)
+            powers = jnp.where(mask, jnp.exp(masked - jnp.max(masked, -1, keepdims=True)), 0.0)
+            gate_ref[rows, :] = powers / jnp.sum(powers, -1, keepdims=True)
+
+        chunk_loop(row_count, gating)
+
+    for copy in weight_copies(pieces, in_buf, out_buf, sems, expert, slot):
+        copy.wait()
+
+    def mlp(rows):
+        pre = jnp.dot(rows_rel[rows, :], in_buf[slot], preferred_element_type=F32)
+        pre_ref[0, rows, :] = pre.astype(BF16)
+        gate_pre, up_pre = split_pairs(pre)
+        weight = gate_column(gate_ref[rows, :], expert)
+        gated = (weight * (gate_pre * jax.nn.sigmoid(gate_pre) * up_pre)).astype(BF16)
+        gated_ref[0, rows, :] = gated
+        acc[rows, :] += jnp.dot(gated, out_buf[slot], preferred_element_type=F32)
+
+    chunk_loop(row_count, mlp)
+
+    @pl.when(expert == pl.num_programs(0) - 1)
+    def _():
+        reorder_halves(half_ref[0], acc, sum_ref)
+
+
+def whole_block(shape):
+    return pl.BlockSpec(shape, lambda e, *_: (0,) * len(shape))
+
+
+def expert_block(shape):
+    return pl.BlockSpec((1,) + shape[1:], lambda e, *_: (e, 0, 0))
+
+
+def weight_scratch(row_count, width, hidden):
+    return [
+        pltpu.VMEM((row_count, width), BF16),
+        pltpu.VMEM((row_count, width), F32),
+        pltpu.VMEM((2, width, 2 * hidden), BF16),
+        pltpu.VMEM((2, hidden, width), BF16),
+        pltpu.SemaphoreType.DMA((2, 24)),
+    ]
+
+
+def experts_forward(half_index, rows, route_ids, router, pieces):
+    row_count, width = rows.shape
+    local = pieces[0].shape[0]
+    hidden = 4 * SHARE
+    pre_shape = (local, row_count, 2 * hidden)
+    gated_shape = (local, row_count, hidden)
+    return pl.pallas_call(
+        forward_body,
+        grid_spec=pltpu.PrefetchScalarGridSpec(
+            num_scalar_prefetch=1,
+            grid=(local,),
+            in_specs=[whole_block(v.shape) for v in (rows, route_ids, router)]
+            + [pl.BlockSpec(memory_space=pl.ANY)] * 16,
+            out_specs=[
+                whole_block((row_count, width)),
+                expert_block(pre_shape),
+                expert_block(gated_shape),
+                whole_block((row_count, 128)),
+            ],
+            scratch_shapes=weight_scratch(row_count, width, hidden),
+        ),
+        out_shape=[
+            jax.ShapeDtypeStruct((row_count, width), F32),
+            jax.ShapeDtypeStruct(pre_shape, BF16),
+            jax.ShapeDtypeStruct(gated_shape, BF16),
+            jax.ShapeDtypeStruct((row_count, 128), F32),
+        ],
+        name="experts_forward",
+    )(half_index, rows, route_ids, router, *pieces)
+
+
+def backward_body(half_ref, grad_ref, mean_ref, gate_ref, router_ref, pre_ref, *rest):
+    pieces = rest[:16]
+    rows_ref, pre_grad_ref, logit_ref, grad_rel, acc, in_buf, out_buf, sems = rest[16:]
+    expert, slot = stream_weights(pieces, in_buf, out_buf, sems)
+    row_count = grad_ref.shape[0]
+
+    @pl.when(expert == 0)
+    def _():
+        reorder_halves(half_ref[0], grad_ref, grad_rel)
+        acc[...] = jnp.zeros_like(acc)
+        logit_ref[...] = jnp.zeros_like(logit_ref)
+
+    for copy in weight_copies(pieces, in_buf, out_buf, sems, expert, slot):
+        copy.wait()
+
+    def mlp(rows):
+        plain = lax.dot_general(grad_rel[rows, :], out_buf[slot], NT, preferred_element_type=F32)
+        gate_pre, up_pre = split_pairs(pre_ref[0, rows, :].astype(F32))
+        weight = gate_column(gate_ref[rows, :], expert)
+        sigmoid = jax.nn.sigmoid(gate_pre)
+        act = gate_pre * sigmoid
+        grad_weight = jnp.sum(act * up_pre * plain, -1, keepdims=True)
+        scaled = weight * plain
+        pre_grad = join_pairs(
+            scaled * up_pre * (sigmoid + act * (1.0 - sigmoid)), scaled * act
+        ).astype(BF16)
+        pre_grad_ref[0, rows, :] = pre_grad
+        old = logit_ref[rows, :]
+        lane = lax.broadcasted_iota(jnp.int32, old.shape, 1)
+        logit_ref[rows, :] = jnp.where(
+            lane == expert, weight * (grad_weight - mean_ref[rows, 0:1]), old
+        )
+        acc[rows, :] += lax.dot_general(pre_grad, in_buf[slot], NT, preferred_element_type=F32)
+
+    chunk_loop(row_count, mlp)
+
+    @pl.when(expert == pl.num_programs(0) - 1)
+    def _():
+        reorder_halves(half_ref[0], acc, rows_ref)
+
+        def router(rows):
+            rows_ref[rows, :] += lax.dot_general(
+                logit_ref[rows, :].astype(BF16), router_ref[...], NT, preferred_element_type=F32
+            )
+
+        chunk_loop(row_count, router)
+
+
+def experts_backward(half_index, grads, means, gates, router, pre, pieces):
+    row_count, width = grads.shape
+    local = pieces[0].shape[0]
+    hidden = 4 * SHARE
+    return pl.pallas_call(
+        backward_body,
+        grid_spec=pltpu.PrefetchScalarGridSpec(
+            num_scalar_prefetch=1,
+            grid=(local,),
+            in_specs=[whole_block(v.shape) for v in (grads, means, gates, router)]
+            + [expert_block(pre.shape)]
+            + [pl.BlockSpec(memory_space=pl.ANY)] * 16,
+            out_specs=[
+                whole_block((row_count, width)),
+                expert_block(pre.shape),
+                whole_block((row_count, 128)),
+            ],
+            scratch_shapes=weight_scratch(row_count, width, hidden),
+        ),
+        out_shape=[
+            jax.ShapeDtypeStruct((row_count, width), F32),
+            jax.ShapeDtypeStruct(pre.shape, BF16),
+            jax.ShapeDtypeStruct((row_count, 128), F32),
+        ],
+        name="experts_backward",
+    )(half_index, grads, means, gates, router, pre, *pieces)
+
+
+def swap_x(value):
+    return lax.ppermute(value, "expert", [(i, i ^ 1) for i in range(8)])
+
+
+def from_z(value, ahead):
+    pairs = [(((i // 2 + ahead) % 4) * 2 + i % 2, i) for i in range(8)]
+    return lax.ppermute(value, "expert", pairs)
+
+
+def swap_y(value):
+    return lax.ppermute(value, "tensor", [(i, i ^ 2) for i in range(4)])
+
+
+def swap_core(value):
+    return lax.ppermute(value, "tensor", [(i, i ^ 1) for i in range(4)])
+
+
+def gather_experts(value):
+    near = swap_x(value)
+    ahead = [from_z(value, d) for d in (1, 2, 3)]
+    shards = [value, near]
+    for shard in ahead:
+        shards += [shard, swap_x(shard)]
+    return shards
+
+
+def scatter_experts(shards):
+    columns = [None] * 4
+    for dz in (2, 1, 3, 0):
+        keep, send = (shards[2 * dz], shards[2 * dz + 1])
+        columns[dz] = keep.astype(F32) + swap_x(send.astype(BF16)).astype(F32)
+    total = columns[0]
+    for dz in (2, 1, 3):
+        total = total + from_z(columns[dz].astype(BF16), 4 - dz).astype(F32)
+    return total
+
+
+def scatter_tensor(value, core, row):
+    quarter = value.shape[0] // 4
+    parts = value.reshape(2, 2, quarter, value.shape[1])
+    keep = lax.dynamic_index_in_dim(parts, core, 1, False)
+    send = lax.dynamic_index_in_dim(parts, 1 - core, 1, False)
+    half = keep + swap_core(send.astype(BF16)).astype(F32)
+    keep = lax.dynamic_index_in_dim(half, row, 0, False)
+    send = lax.dynamic_index_in_dim(half, 1 - row, 0, False)
+    return keep + swap_y(send.astype(BF16)).astype(F32)
+
+
+def ordered(index, first, second):
+    return jnp.where(
+        index == 0, jnp.concatenate([first, second], 0), jnp.concatenate([second, first], 0)
+    )
+
+
+def gather_tensor(value, core, row):
+    across = swap_y(value)
+    pair = ordered(core, value, swap_core(value))
+    other = ordered(core, across, swap_core(across))
+    return ordered(row, pair, other)
+
+
+def sum_all(value):
+    value = value + swap_core(value)
+    value = value + swap_y(value)
+    value = value + swap_x(value)
+    value = value + lax.ppermute(value, "expert", [(i, i ^ 2) for i in range(8)])
+    return value + lax.ppermute(value, "expert", [(i, i ^ 4) for i in range(8)])
+
+
+def sum_experts(value, layer, column):
+    size = value.shape[0] // 8
+    shards = []
+    for dz in range(4):
+        for dx in range(2):
+            place = lax.rem(layer + dz, 4) * 2 + jnp.bitwise_xor(column, dx)
+            shards.append(lax.dynamic_slice_in_dim(value, place * size, size, 0))
+    total = scatter_experts(shards).astype(BF16)
+    gathered = gather_experts(total)
+    layers = [ordered(column, gathered[2 * dz], gathered[2 * dz + 1]) for dz in range(4)]
+    joined = jnp.concatenate(layers + layers, 0)
+    start = lax.rem(4 - layer, 4) * 2 * size
+    return lax.dynamic_slice_in_dim(joined, start, 8 * size, 0).astype(F32)
+
+
+def per_device(
+    tokens,
+    teacher,
+    valid_mask,
+    routes,
+    first_gain,
+    query_weight,
+    key_matrix,
+    value_matrix,
+    output_weight,
+    second_gain,
+    router_weight,
+    expert_in,
+    expert_out,
+):
+    row_count, model_width = tokens.shape
+    expert_count = router_weight.shape[1]
+    senders = lax.axis_size("expert")
+    shares = lax.axis_size("tensor")
+    fits = (
+        (senders, shares) == (8, 4)
+        and expert_count == senders * shares
+        and expert_in.shape == (8, 2, model_width // 2, SHARE)
+        and row_count == 4 * 128
+    )
+    if not fits:
+        return general_device(
+            tokens,
+            teacher,
+            valid_mask,
+            routes,
+            first_gain,
+            query_weight,
+            key_matrix,
+            value_matrix,
+            output_weight,
+            second_gain,
+            router_weight,
+            expert_in,
+            expert_out,
+        )
+    local_query = query_weight.shape[1] // HEAD_DIM
+    local_kv = key_matrix.shape[1] // HEAD_DIM
+    group = local_query // local_kv
+    quarter = row_count // shares
+    place = lax.axis_index("expert")
+    share = lax.axis_index("tensor")
+    layer, column = (place // 2, place % 2)
+    row, core = (share // 2, share % 2)
+    half_index = place // 4
+    held = expert_in.shape[0] // 2
+    base = 8 * (place % 4) + held * half_index
+
+    def rows_of(weights, start):
+        return lax.dynamic_slice_in_dim(weights, start * held, held, 0)
+
+    in_own, out_own = (rows_of(expert_in, half_index), rows_of(expert_out, half_index))
+    in_other = from_z(rows_of(expert_in, 1 - half_index), 2)
+    out_other = from_z(rows_of(expert_out, 1 - half_index), 2)
+    pieces = []
+    for piece in (in_own, in_other, out_own, out_other):
+        across = swap_y(piece)
+        pieces += [piece, swap_core(piece), across, swap_core(across)]
+
+    def quarter_of(values):
+        return lax.dynamic_slice_in_dim(values, share * quarter, quarter, 0)
+
+    local_valid = jnp.sum(valid_mask)
+    notes = jnp.concatenate(
+        [quarter_of(routes), jnp.full((quarter, TOP), local_valid, jnp.int32)], 1
+    )
+    note_rows = jnp.stack(gather_experts(notes))
+    valid_total = jnp.sum(note_rows[:, 0, TOP]).astype(F32)
+    route_rel = jnp.bitwise_and(note_rows[:, :, :TOP] - base, expert_count - 1)
+    route_rel = route_rel.reshape(senders * quarter, TOP)
+    router_rel = lax.dynamic_slice_in_dim(
+        jnp.concatenate([router_weight, router_weight], 1), base, expert_count, 1
+    )
+    router_rel = jnp.pad(router_rel, ((0, 0), (0, 128 - expert_count)))
+
+    tokens_f32 = tokens.astype(F32)
+    scale_one = lax.rsqrt(jnp.mean(tokens_f32 * tokens_f32, -1, keepdims=True) + EPS)
+    unit_one = tokens_f32 * scale_one
+    first_normed = (unit_one * first_gain).astype(BF16)
+    cosine, sine = rope_tables(row_count, HEAD_DIM)
+    query_linear = jnp.dot(first_normed, query_weight, preferred_element_type=F32)
+    keys_linear = jnp.dot(first_normed, key_matrix, preferred_element_type=F32)
+    value_low = jnp.dot(first_normed, value_matrix, preferred_element_type=F32).astype(BF16)
+    value_low = value_low.reshape(row_count, local_kv, HEAD_DIM)
+    query_rotated = apply_rotary(
+        query_linear.reshape(row_count, local_query, HEAD_DIM), cosine, sine
+    ).astype(BF16)
+    keys_rot = apply_rotary(
+        keys_linear.reshape(row_count, local_kv, HEAD_DIM), cosine, sine
+    ).astype(BF16)
+    query_block = query_rotated.reshape(row_count, local_kv, group, HEAD_DIM)
+    block_of = jnp.arange(row_count, dtype=jnp.int32) // BLOCK
+    allowed = block_of[None, :] <= block_of[:, None]
+
+    def masked_scores():
+        scores = jnp.einsum("qhgd,khd->hgqk", query_block, keys_rot, preferred_element_type=F32)
+        return jnp.where(allowed, scores * ATTN_SCALE, -1e30)
+
+    scores = masked_scores()
+    row_peak = jnp.max(scores, -1, keepdims=True)
+    powers = jnp.exp(scores - row_peak)
+    row_total = jnp.sum(powers, -1, keepdims=True)
+    probs_low = (powers / row_total).astype(BF16)
+    attended = jnp.einsum("hgqk,khd->qhgd", probs_low, value_low, preferred_element_type=F32)
+    attended = attended.reshape(row_count, local_query * HEAD_DIM).astype(BF16)
+    attn_part = jnp.dot(attended, output_weight, preferred_element_type=F32)
+
+    tokens_mine = quarter_of(tokens).astype(F32)
+    hidden = tokens_mine + RESIDUAL * scatter_tensor(attn_part, core, row)
+    scale_two = lax.rsqrt(jnp.mean(hidden * hidden, -1, keepdims=True) + EPS)
+    unit_two = hidden * scale_two
+    normed_two = (unit_two * second_gain).astype(BF16)
+    half_arg = half_index.reshape(1)
+    expert_rows = jnp.concatenate(gather_experts(normed_two), 0)
+    moe_part, pre, gated, gates = experts_forward(
+        half_arg, expert_rows, route_rel, router_rel, pieces
+    )
+    moe_parts = moe_part.reshape(senders, quarter, model_width)
+    moe_sum = scatter_experts([moe_parts[i] for i in range(senders)])
+
+    output = hidden + RESIDUAL * moe_sum
+    residual_err = output - quarter_of(teacher).astype(F32)
+    valid_rows = quarter_of(valid_mask).astype(F32)[:, None]
+    squared_local = jnp.sum(valid_rows * residual_err * residual_err)
+    token_total = senders * row_count
+    grad_out = token_total / valid_total * valid_rows * residual_err
+    grad_moe = (RESIDUAL * grad_out).astype(BF16)
+    gate_mean = jnp.sum(grad_moe.astype(F32) * moe_sum, -1, keepdims=True)
+    grad_rows = jnp.concatenate(gather_experts(grad_moe), 0)
+    mean_rows = jnp.concatenate(gather_experts(gate_mean.reshape(1, quarter)), 0)
+    mean_rows = jnp.broadcast_to(mean_rows.reshape(senders * quarter, 1), (senders * quarter, 128))
+    layer_output = gather_tensor(output.astype(BF16), core, row)
+
+    grad_part, pre_grad, logit_grad = experts_backward(
+        half_arg, grad_rows, mean_rows, gates, router_rel, pre, pieces
+    )
+    grad_parts = grad_part.reshape(senders, quarter, model_width)
+    grad_two = scatter_experts([grad_parts[i] for i in range(senders)])
+
+    logit_grad = logit_grad[:, :expert_count]
+    logit_grad = lax.dynamic_slice_in_dim(
+        jnp.concatenate([logit_grad, logit_grad], 1),
+        jnp.bitwise_and(expert_count - base, expert_count - 1),
+        expert_count,
+        1,
+    ).astype(BF16)
+    router_part = jnp.einsum("te,td->ed", logit_grad, expert_rows, preferred_element_type=F32)
+
+    in_grads = jnp.einsum("md,emf->edf", expert_rows, pre_grad, preferred_element_type=F32)
+    out_grads = jnp.einsum("emf,md->efd", gated, grad_rows, preferred_element_type=F32)
+    half_width = model_width // 2
+    in_grads = in_grads.astype(BF16).reshape(held, 2, half_width, 4, 2, SHARE)
+    out_grads = out_grads.astype(BF16).reshape(held, 4, SHARE, 2, half_width)
+
+    def halves(values, axis):
+        first = lax.dynamic_index_in_dim(values, half_index, axis, False)
+        return (first, lax.dynamic_index_in_dim(values, 1 - half_index, axis, False))
+
+    def home(part_of):
+        near = part_of(0).astype(F32) + swap_core(part_of(1)).astype(F32)
+        far = part_of(2).astype(F32) + swap_core(part_of(3)).astype(F32)
+        return near + swap_y(far.astype(BF16)).astype(F32)
+
+    results = []
+    for mine, theirs in (
+        halves(in_grads.transpose(1, 3, 0, 4, 2, 5), 0),
+        halves(out_grads.transpose(3, 1, 0, 2, 4), 0),
+    ):
+        keep = home(lambda q, v=mine: v[q])
+        send = home(lambda q, v=theirs: v[q])
+        back = from_z(send.astype(BF16), 2).astype(F32)
+        results.append(ordered(half_index, keep, back))
+    grad_expert_in, grad_expert_out = results
+
+    grad_second_part = jnp.sum(grad_two * unit_two, 0)
+    grad_unit_two = grad_two * second_gain
+    grad_hidden = grad_out + scale_two * (
+        grad_unit_two - unit_two * jnp.mean(grad_unit_two * unit_two, -1, keepdims=True)
+    )
+    small = jnp.concatenate(
+        [
+            router_part,
+            grad_second_part[None],
+            jnp.full((1, model_width), squared_local),
+        ],
+        0,
+    )
+    small = sum_all(small)
+
+    grad_attn = gather_tensor((RESIDUAL * grad_hidden).astype(BF16), core, row)
+    grad_output = jnp.einsum("tc,td->cd", attended, grad_attn, preferred_element_type=F32)
+    grad_attended = jnp.einsum("td,cd->tc", grad_attn, output_weight, preferred_element_type=F32)
+    grad_attended = grad_attended.astype(BF16).reshape(row_count, local_kv, group, HEAD_DIM)
+    attn_probs = jnp.exp(masked_scores() - row_peak) / row_total
+    grad_probs = jnp.einsum("qhgd,khd->hgqk", grad_attended, value_low, preferred_element_type=F32)
+    grad_scores = attn_probs * (grad_probs - jnp.sum(attn_probs * grad_probs, -1, keepdims=True))
+    grad_scores = grad_scores.astype(BF16)
+    grad_query_rot = ATTN_SCALE * jnp.einsum(
+        "hgqk,khd->qhgd", grad_scores, keys_rot, preferred_element_type=F32
+    )
+    grad_keys_rot = ATTN_SCALE * jnp.einsum(
+        "hgqk,qhgd->khd", grad_scores, query_block, preferred_element_type=F32
+    )
+    grad_values = jnp.einsum(
+        "hgqk,qhgd->khd", attn_probs.astype(BF16), grad_attended, preferred_element_type=F32
+    )
+    grad_query_low = unrotate(
+        grad_query_rot.reshape(row_count, local_query, HEAD_DIM), cosine, sine
+    )
+    grad_query_low = grad_query_low.reshape(row_count, local_query * HEAD_DIM).astype(BF16)
+    grad_keys_low = unrotate(grad_keys_rot, cosine, sine)
+    grad_keys_low = grad_keys_low.reshape(row_count, local_kv * HEAD_DIM).astype(BF16)
+    grad_values_low = grad_values.reshape(row_count, local_kv * HEAD_DIM).astype(BF16)
+    grad_qkv = jnp.concatenate([grad_query_low, grad_keys_low, grad_values_low], 1)
+    weights_qkv = jnp.concatenate([query_weight, key_matrix, value_matrix], 1)
+    grad_weights = jnp.einsum("td,tc->dc", first_normed, grad_qkv, preferred_element_type=F32)
+    grad_one_part = jnp.einsum("tc,dc->td", grad_qkv, weights_qkv, preferred_element_type=F32)
+    grad_one = scatter_tensor(grad_one_part, core, row)
+
+    scale_mine = lax.rsqrt(jnp.mean(tokens_mine * tokens_mine, -1, keepdims=True) + EPS)
+    unit_mine = tokens_mine * scale_mine
+    grad_first_gain = sum_all(jnp.sum(grad_one * unit_mine, 0)[None])[0]
+    grad_unit_one = grad_one * first_gain
+    grad_tokens = grad_hidden + scale_mine * (
+        grad_unit_one - unit_mine * jnp.mean(grad_unit_one * unit_mine, -1, keepdims=True)
+    )
+    grad_tokens = gather_tensor(grad_tokens.astype(BF16), core, row).astype(F32)
+    grad_output = sum_experts(grad_output, layer, column)
+    grad_weights = sum_experts(grad_weights, layer, column)
+    query_columns = query_weight.shape[1]
+    key_columns = query_columns + key_matrix.shape[1]
+    return (
+        layer_output,
+        small[expert_count + 1, 0] / (2.0 * model_width * valid_total),
+        grad_tokens,
+        grad_first_gain,
+        grad_weights[:, :query_columns],
+        grad_weights[:, query_columns:key_columns],
+        grad_weights[:, key_columns:],
+        grad_output,
+        small[expert_count],
+        small[:expert_count].T,
+        grad_expert_in,
+        grad_expert_out,
+    )
+
+
 def solution(mesh):
     return jax.shard_map(
         per_device,

time: 2700 us -> 768 us (0.28)
  blocking collectives: 883 us -> 0 us
  waiting for transfers between devices: 1230 us -> 363 us
  local copies, waits for them, and re-layouts: 378 us -> 140 us
  starting transfers between devices: 9.04 us -> 110 us
  Pallas kernels: 0 us -> 55.9 us
  matrix products: 94.3 us -> 40.4 us
  other arithmetic: 84.3 us -> 45.2 us
    all_to_all x3 -> x0, blocking collectives: 828 us -> none  [the longest x1 279 us: per_device(): lax.all_to_all(send_rows, 'expert', split_axis=0, concat_axis=2, tiled=True)]
    ppermute x2 -> x121, waiting for transfers between devices: 810 us -> 363 us  [the longest x34 147 us: from_z(): return lax.ppermute(value, 'expert', pairs)]
    all_to_all x1 -> x0, waiting for transfers between devices: 270 us -> none  [per_device(): lax.all_to_all(expert_result, 'expert', split_axis=1, concat_axis=0, tile...]
    gather x11 -> x0, local copies, waits for them, and re-layouts: 197 us -> none  [the longest x2 48.2 us: per_device(): normed_two[token_row]]
    psum x5 -> x0, waiting for transfers between devices: 146 us -> none  [the longest x1 109 us: per_device(): lax.psum((grad_first_gain, grad_query, grad_key, grad_value, grad_output,...]
    ppermute x2 -> x121, starting transfers between devices: 2.24 us -> 110 us  [the longest x34 48.1 us: from_z(): return lax.ppermute(value, 'expert', pairs)]
    transpose x2 -> x1, local copies, waits for them, and re-layouts: 72.8 us -> 0.66 us  [per_device(): small[:expert_count]]
    pallas_call x0 -> x2, Pallas kernels: none -> 55.9 us  [the longest x1 31 us: experts_backward(): pl.pallas_call(backward_body, grid_spec=pltpu.PrefetchScalarGridSpec(num_...]
  transfers between devices with their start and end apart: 8 -> 121, of which waited for: 7 -> 52; matrix products, arithmetic and copies ran while one was open for 5% -> 22% of each run, Pallas kernels for 0% -> 4%
where the time goes in v1:
time: 768 us; the launch traced here: 759 us
  waiting for transfers between devices  363 us (47%)
  local copies, waits for them, and re-layouts  140 us (18%)
  starting transfers between devices  110 us (14%)
  Pallas kernels  55.9 us (7%)
  other arithmetic  45.2 us (6%)
  matrix products  40.4 us (5%)
    ppermute x34, waiting for transfers between devices, from_z(): return lax.ppermute(value, 'expert', pairs)  147 us
    ppermute x15, waiting for transfers between devices, swap_y(): return lax.ppermute(value, 'tensor', [(i, i ^ 2) for i in range(4)])  93.5 us
    ppermute x42, waiting for transfers between devices, swap_x(): return lax.ppermute(value, 'expert', [(i, i ^ 1) for i in range(8)])  77.5 us
    unnamed x179, local copies, waits for them, and re-layouts  61.6 us
    ppermute x34, starting transfers between devices, from_z(): return lax.ppermute(value, 'expert', pairs)  48.1 us
    ppermute x42, starting transfers between devices, swap_x(): return lax.ppermute(value, 'expert', [(i, i ^ 1) for i in range(8)])  44 us
    ppermute x2, waiting for transfers between devices, sum_all(): return value + lax.ppermute(value, 'expert', [(i, i ^ 4) for i in range(8)])  42.4 us
    pallas_call x1, Pallas kernels, experts_backward(): pl.pallas_call(backward_body, grid_spec=pltpu.PrefetchScalarGridSpec(num_...  31 us
  transfers between devices with their start and end apart: 121, of which 52 were waited for; matrix products, arithmetic and copies ran while one was open for 22% of the time, Pallas kernels for 4%

profile of v1, /device:TPU:0, one launch (start us, length us, event | category | flops | bytes accessed | tf_op | source)
XLA Modules:
  0.0 759.5 jit_solution(13817160669185076348)
XLA Ops:
  48.9 55.7 %collective-permute-done.26.rest_12_ = bf16[4,128,512]{2,1,0:T(8,128)(2,1)S(1)} collective-permute-done((bf16[4,128,512]{2,1,0:T(8,128)(2,1)}, bf16[4,128,512]{2,1,0:T(8,128)(2,1)S(1)}, u32[]{:S(2)}, u32[]{:S(2)}) %collective-permute-start.26) | collective-permute-done | bytes 524320 | tf_op jit(solution)/shard_map/ppermute | solution.py:609
  118.0 12.7 %collective-permute-done.5 = bf16[128,1024]{1,0:T(8,128)(2,1)} collective-permute-done((bf16[128,1024]{1,0:T(8,128)(2,1)S(1)}, bf16[128,1024]{1,0:T(8,128)(2,1)}, u32[]{:S(2)}, u32[]{:S(2)}) %collective-permute-start.5) | collective-permute-done | bytes 262176 | tf_op jit(solution)/shard_map/ppermute | solution.py:609
  133.0 18.9 %collective-permute-done.28.rest_14_ = bf16[4,128,512]{2,1,0:T(8,128)(2,1)S(1)} collective-permute-done((bf16[4,128,512]{2,1,0:T(8,128)(2,1)S(1)}, bf16[4,128,512]{2,1,0:T(8,128)(2,1)S(1)}, u32[]{:S(2)}, u32[]{:S(2)}) %collective-permute-start.28) | collective-permute-done | bytes 524320 | tf_op jit(solution)/shard_map/ppermute | solution.py:613
  170.0 24.9 %experts_forward.1 = (f32[1024,1024]{1,0:T(8,128)}, bf16[4,1024,1024]{2,1,0:T(8,128)(2,1)}, bf16[4,1024,512]{2,1,0:T(8,128)(2,1)}, f32[1024,128]{1,0:T(8,128)}) custom-call(s32[1]{0:T(128)} %bitcast.17.half_ref, bf16[1024,1024]{1,0:T(8,128)(2,1)} %copy-done.2, s32[1024,8]{1,0:T(8,128)} %bitcast.241, bf16[1024,128]{1,0:T(8,128)(2,1)} %pad.5.router_ref, ...), custom_call_target="tpu_custom_call" | custom-call | tf_op jit(solution)/shard_map/experts_forward/pallas_call | solution.py:502
  206.7 5.6 collective-permute-done.33
  212.3 5.6 collective-permute-done.35
  227.0 12.3 %collective-permute-done.32 = bf16[128,1024]{1,0:T(8,128)(2,1)S(1)} collective-permute-done((bf16[128,1024]{1,0:T(8,128)(2,1)S(1)}, bf16[128,1024]{1,0:T(8,128)(2,1)S(1)}, u32[]{:S(2)}, u32[]{:S(2)}) %collective-permute-start.32) | collective-permute-done | bytes 262176 | tf_op jit(solution)/shard_map/ppermute | solution.py:609
  268.9 6.5 collective-permute-done.43
  288.8 9.2 %convolution_convert_fusion = bf16[4,512,1024]{2,1,0:T(8,128)(2,1)} fusion(bf16[4,1024,512]{2,1,0:T(8,128)(2,1)} %get-tuple-element.25, bf16[1024,1024]{1,0:T(8,128)(2,1)S(1)} %constant_dynamic-update-slice_fusion.16.grad_ref), kind=kOutput, calls=%fused_computation.11 | convolution fusion | flops 4297064448 | bytes 10485760 | tf_op jit(solution)/shard_map/emf,md->efd/dot_general | solution.py:841
  298.0 7.8 %reshape.275 = bf16[4,4,128,2,512]{4,3,2,1,0:T(2,128)(2,1)} reshape(bf16[4,512,1024]{2,1,0:T(8,128)(2,1)} %convolution_convert_fusion) | data formatting | bytes 8388608 | tf_op jit(solution)/shard_map/reshape | solution.py:844
  305.8 10.2 %constant_dynamic-slice_fusion.1 = (bf16[4,4,128,1,512]{4,3,2,1,0:T(2,128)(2,1)S(1)}, bf16[4,4,128,1,512]{4,3,2,1,0:T(2,128)(2,1)S(1)}) fusion(bf16[4,4,128,2,512]{4,3,2,1,0:T(2,128)(2,1)} %reshape.275, s32[]{:T(128)S(6)} %select_n.302, s32[]{:T(128)S(6)} %select_n.303), kind=kLoop, calls=%fused_computation.233 | loop fusion | bytes 8388616 | tf_op jit(solution)/shard_map/dynamic-slice.2
  321.4 31.0 %experts_backward.1 = (f32[1024,1024]{1,0:T(8,128)}, bf16[4,1024,1024]{2,1,0:T(8,128)(2,1)}, f32[1024,128]{1,0:T(8,128)}) custom-call(s32[1]{0:T(128)} %bitcast.17.half_ref, bf16[1024,1024]{1,0:T(8,128)(2,1)} %copy-done.18, f32[1024,128]{1,0:T(8,128)} %broadcast_in_dim.23.mean_ref, f32[1024,128]{1,0:T(8,128)} %get-tuple-element.20.gate_ref, ...), custom_call_target="tpu_custom_call" | custom-call | tf_op jit(solution)/shard_map/experts_backward/pallas_call | solution.py:579
  352.5 15.2 %convert_bitcast_fusion = bf16[4,1024,1024]{1,2,0:T(8,128)(2,1)} fusion(bf16[4,1024,1024]{2,1,0:T(8,128)(2,1)} %get-tuple-element.24, bf16[1024,1024]{1,0:T(8,128)(2,1)S(1)} %copy-done.3), kind=kOutput, calls=%fused_computation.1 | convolution fusion | flops 8594128896 | bytes 18874368 | tf_op jit(solution)/shard_map/md,emf->edf/dot_general | solution.py:840
  367.7 14.5 %reshape.274 = bf16[4,2,512,4,2,128]{2,1,5,4,3,0:T(2,128)(2,1)} reshape(bf16[4,1024,1024]{1,2,0:T(8,128)(2,1)} %convert_bitcast_fusion) | data formatting | bytes 16777216 | tf_op jit(solution)/shard_map/reshape | solution.py:843
  382.2 20.3 %constant_dynamic-slice_fusion.3 = (bf16[4,1,512,4,2,128]{2,1,5,4,3,0:T(2,128)(2,1)}, bf16[4,1,512,4,2,128]{2,1,5,4,3,0:T(2,128)(2,1)}) fusion(bf16[4,2,512,4,2,128]{2,1,5,4,3,0:T(2,128)(2,1)} %reshape.274, s32[]{:T(128)S(6)} %select_n.302, s32[]{:T(128)S(6)} %select_n.303), kind=kLoop, calls=%fused_computation.235 | loop fusion | bytes 16777224 | tf_op jit(solution)/shard_map/dynamic-slice
  402.4 19.9 %copy.69 = bf16[4,1,512,4,2,128]{5,2,4,0,3,1:T(8,128)(2,1)} copy(bf16[4,1,512,4,2,128]{2,1,5,4,3,0:T(2,128)(2,1)} %get-tuple-element.44) | data formatting | bytes 8388608
  425.4 19.9 %copy.70 = bf16[4,1,512,4,2,128]{5,2,4,0,3,1:T(8,128)(2,1)} copy(bf16[4,1,512,4,2,128]{2,1,5,4,3,0:T(2,128)(2,1)} %get-tuple-element.45) | data formatting | bytes 8388608
  462.9 5.6 collective-permute-done.59
  474.3 8.6 %collective-permute-done.56 = bf16[128,1024]{1,0:T(8,128)(2,1)S(1)} collective-permute-done((bf16[128,1024]{1,0:T(8,128)(2,1)S(1)}, bf16[128,1024]{1,0:T(8,128)(2,1)S(1)}, u32[]{:S(2)}, u32[]{:S(2)}) %collective-permute-start.56) | collective-permute-done | bytes 262176 | tf_op jit(solution)/shard_map/ppermute | solution.py:609
  490.4 10.4 %collective-permute-done.62 = f32[34,1024]{1,0:T(8,128)S(1)} collective-permute-done((f32[34,1024]{1,0:T(8,128)S(1)}, f32[34,1024]{1,0:T(8,128)S(1)}, u32[]{:S(2)}, u32[]{:S(2)}) %collective-permute-start.62) | collective-permute-done | bytes 139296 | tf_op jit(solution)/shard_map/ppermute | solution.py:613
  513.5 16.4 %collective-permute-done.67 = bf16[128,1024]{1,0:T(8,128)(2,1)S(1)} collective-permute-done((bf16[128,1024]{1,0:T(8,128)(2,1)S(1)}, bf16[128,1024]{1,0:T(8,128)(2,1)S(1)}, u32[]{:S(2)}, u32[]{:S(2)}) %collective-permute-start.67) | collective-permute-done | bytes 262176 | tf_op jit(solution)/shard_map/ppermute | solution.py:613
  589.2 24.4 %collective-permute-done.103 = bf16[32,1024]{1,0:T(8,128)(2,1)S(1)} collective-permute-done((bf16[32,1024]{1,0:T(8,128)(2,1)S(1)}, bf16[32,1024]{1,0:T(8,128)(2,1)S(1)}, u32[]{:S(2)}, u32[]{:S(2)}) %collective-permute-start.103) | collective-permute-done | bytes 65568 | tf_op jit(solution)/shard_map/ppermute | solution.py:609
  650.5 40.8 %collective-permute-done.70 = bf16[128,1024]{1,0:T(8,128)(2,1)S(1)} collective-permute-done((bf16[128,1024]{1,0:T(8,128)(2,1)S(1)}, bf16[128,1024]{1,0:T(8,128)(2,1)S(1)}, u32[]{:S(2)}, u32[]{:S(2)}) %collective-permute-start.70) | collective-permute-done | bytes 262176 | tf_op jit(solution)/shard_map/ppermute | solution.py:613
  710.7 40.2 %collective-permute-done.78 = f32[1,1024]{1,0:T(1,128)S(1)} collective-permute-done((f32[1,1024]{1,0:T(1,128)S(1)}, f32[1,1024]{1,0:T(1,128)S(1)}, u32[]{:S(2)}, u32[]{:S(2)}) %collective-permute-start.78) | collective-permute-done | bytes 4128 | tf_op jit(solution)/shard_map/ppermute | solution.py:669
  (540 shorter events, 317.8 us)
Async XLA Ops:
  34.4 82.4 %collective-permute-start.19 = (bf16[4,2,512,128]{3,2,1,0:T(8,128)(2,1)}, bf16[4,2,512,128]{3,2,1,0:T(8,128)(2,1)}, u32[]{:S(2)}, u32[]{:S(2)}) collective-permute-start(bf16[4,2,512,128]{3,2,1,0:T(8,128)(2,1)} %get-tuple-element.79), channel_id=1, source_target_pairs={{16,0},{20,4},{24,8},{28,12},{0,16},{4,20},{8,24},{12,28},{17,1},{... | collective-permute-start | bytes 3145736 | tf_op jit(solution)/shard_map/ppermute | solution.py:609
  36.3 68.3 %collective-permute-start.26 = (bf16[4,128,512]{2,1,0:T(8,128)(2,1)}, bf16[4,128,512]{2,1,0:T(8,128)(2,1)S(1)}, u32[]{:S(2)}, u32[]{:S(2)}) collective-permute-start(bf16[4,128,512]{2,1,0:T(8,128)(2,1)} %get-tuple-element.89), channel_id=1, source_target_pairs={{16,0},{20,4},{24,8},{28,12},{0,16},{4,20},{8,24},{12,28},{17,1},{... | collective-permute-start | bytes 1572872 | tf_op jit(solution)/shard_map/ppermute | solution.py:609
  37.4 67.9 %collective-permute-start.24 = (bf16[4,128,512]{2,1,0:T(8,128)(2,1)}, bf16[4,128,512]{2,1,0:T(8,128)(2,1)S(1)}, u32[]{:S(2)}, u32[]{:S(2)}) collective-permute-start(bf16[4,128,512]{2,1,0:T(8,128)(2,1)} %get-tuple-element.90.rest_8_), channel_id=1, source_target_pairs={{0,2},{1,3},{2,0},{3,1},{4,6},{5,7},{6,4},{7,5},{8,10},{9,11},{10,... | collective-permute-start | bytes 1572872 | tf_op jit(solution)/shard_map/ppermute | solution.py:613
  43.9 65.8 %collective-permute-start.23 = (bf16[4,128,512]{2,1,0:T(8,128)(2,1)}, bf16[4,128,512]{2,1,0:T(8,128)(2,1)S(1)}, u32[]{:S(2)}, u32[]{:S(2)}) collective-permute-start(bf16[4,128,512]{2,1,0:T(8,128)(2,1)} %get-tuple-element.90.rest_8_), channel_id=1, source_target_pairs={{0,1},{1,0},{2,3},{3,2},{4,5},{5,4},{6,7},{7,6},{8,9},{9,8},{10,11... | collective-permute-start | bytes 1572872 | tf_op jit(solution)/shard_map/ppermute | solution.py:617
  48.1 83.1 %collective-permute-start.17 = (bf16[4,2,512,128]{3,2,1,0:T(8,128)(2,1)}, bf16[4,2,512,128]{3,2,1,0:T(8,128)(2,1)}, u32[]{:S(2)}, u32[]{:S(2)}) collective-permute-start(bf16[4,2,512,128]{3,2,1,0:T(8,128)(2,1)} %get-tuple-element.80.rest_0_), channel_id=1, source_target_pairs={{0,2},{1,3},{2,0},{3,1},{4,6},{5,7},{6,4},{7,5},{8,10},{9,11},{10,... | collective-permute-start | bytes 3145736 | tf_op jit(solution)/shard_map/ppermute | solution.py:613
  116.8 37.3 %collective-permute-start.21 = (bf16[4,2,512,128]{3,2,1,0:T(8,128)(2,1)}, bf16[4,2,512,128]{3,2,1,0:T(8,128)(2,1)}, u32[]{:S(2)}, u32[]{:S(2)}) collective-permute-start(bf16[4,2,512,128]{3,2,1,0:T(8,128)(2,1)} %collective-permute-done.19.rest_4_), channel_id=1, source_target_pairs={{0,2},{1,3},{2,0},{3,1},{4,6},{5,7},{6,4},{7,5},{8,10},{9,11},{10,... | collective-permute-start | bytes 3145736 | tf_op jit(solution)/shard_map/ppermute | solution.py:613
  132.8 35.9 %collective-permute-start.20 = (bf16[4,2,512,128]{3,2,1,0:T(8,128)(2,1)}, bf16[4,2,512,128]{3,2,1,0:T(8,128)(2,1)}, u32[]{:S(2)}, u32[]{:S(2)}) collective-permute-start(bf16[4,2,512,128]{3,2,1,0:T(8,128)(2,1)} %collective-permute-done.19.rest_4_), channel_id=1, source_target_pairs={{0,1},{1,0},{2,3},{3,2},{4,5},{5,4},{6,7},{7,6},{8,9},{9,8},{10,11... | collective-permute-start | bytes 3145736 | tf_op jit(solution)/shard_map/ppermute | solution.py:617
  318.0 184.0 %collective-permute-start.115 = (bf16[4,128,512]{2,1,0:T(8,128)(2,1)}, bf16[4,128,512]{2,1,0:T(8,128)(2,1)}, u32[]{:S(2)}, u32[]{:S(2)}) collective-permute-start(bf16[4,128,512]{2,1,0:T(8,128)(2,1)} %get-tuple-element.59), channel_id=1, source_target_pairs={{0,1},{1,0},{2,3},{3,2},{4,5},{5,4},{6,7},{7,6},{8,9},{9,8},{10,11... | collective-permute-start | bytes 1572872 | tf_op jit(solution)/shard_map/ppermute | solution.py:617
  319.9 149.1 %collective-permute-start.118 = (bf16[4,128,512]{2,1,0:T(8,128)(2,1)}, bf16[4,128,512]{2,1,0:T(8,128)(2,1)}, u32[]{:S(2)}, u32[]{:S(2)}) collective-permute-start(bf16[4,128,512]{2,1,0:T(8,128)(2,1)} %get-tuple-element.61), channel_id=1, source_target_pairs={{0,1},{1,0},{2,3},{3,2},{4,5},{5,4},{6,7},{7,6},{8,9},{9,8},{10,11... | collective-permute-start | bytes 1572872 | tf_op jit(solution)/shard_map/ppermute | solution.py:617
  474.2 28.7 %collective-permute-start.114 = (bf16[4,128,512]{2,1,0:T(8,128)(2,1)S(1)}, bf16[4,128,512]{2,1,0:T(8,128)(2,1)S(1)}, u32[]{:S(2)}, u32[]{:S(2)}) collective-permute-start(bf16[4,128,512]{2,1,0:T(8,128)(2,1)S(1)} %copy-done.36), channel_id=1, source_target_pairs={{0,1},{1,0},{2,3},{3,2},{4,5},{5,4},{6,7},{7,6},{8,9},{9,8},{10,11... | collective-permute-start | bytes 1572872 | tf_op jit(solution)/shard_map/ppermute | solution.py:617
  482.9 27.5 %collective-permute-start.117 = (bf16[4,128,512]{2,1,0:T(8,128)(2,1)S(1)}, bf16[4,128,512]{2,1,0:T(8,128)(2,1)S(1)}, u32[]{:S(2)}, u32[]{:S(2)}) collective-permute-start(bf16[4,128,512]{2,1,0:T(8,128)(2,1)S(1)} %copy-done.35), channel_id=1, source_target_pairs={{0,1},{1,0},{2,3},{3,2},{4,5},{5,4},{6,7},{7,6},{8,9},{9,8},{10,11... | collective-permute-start | bytes 1572872 | tf_op jit(solution)/shard_map/ppermute | solution.py:617
  482.9 29.0 %collective-permute-start.119 = (bf16[4,128,512]{2,1,0:T(8,128)(2,1)S(1)}, bf16[4,128,512]{2,1,0:T(8,128)(2,1)S(1)}, u32[]{:S(2)}, u32[]{:S(2)}) collective-permute-start(bf16[4,128,512]{2,1,0:T(8,128)(2,1)S(1)} %fusion.28), channel_id=1, source_target_pairs={{0,2},{1,3},{2,0},{3,1},{4,6},{5,7},{6,4},{7,5},{8,10},{9,11},{10,... | collective-permute-start | bytes 1572872 | tf_op jit(solution)/shard_map/ppermute | solution.py:613
  502.3 32.0 %collective-permute-start.108 = (bf16[4,2,512,128]{3,2,1,0:T(8,128)(2,1)S(1)}, bf16[4,2,512,128]{3,2,1,0:T(8,128)(2,1)S(1)}, u32[]{:S(2)}, u32[]{:S(2)}) collective-permute-start(bf16[4,2,512,128]{3,2,1,0:T(8,128)(2,1)S(1)} %copy-done.30), channel_id=1, source_target_pairs={{0,1},{1,0},{2,3},{3,2},{4,5},{5,4},{6,7},{7,6},{8,9},{9,8},{10,11... | collective-permute-start | bytes 3145736 | tf_op jit(solution)/shard_map/ppermute | solution.py:617
  505.5 31.3 %collective-permute-start.111 = (bf16[4,2,512,128]{3,2,1,0:T(8,128)(2,1)S(1)}, bf16[4,2,512,128]{3,2,1,0:T(8,128)(2,1)S(1)}, u32[]{:S(2)}, u32[]{:S(2)}) collective-permute-start(bf16[4,2,512,128]{3,2,1,0:T(8,128)(2,1)S(1)} %get-tuple-element.51), channel_id=1, source_target_pairs={{0,1},{1,0},{2,3},{3,2},{4,5},{5,4},{6,7},{7,6},{8,9},{9,8},{10,11... | collective-permute-start | bytes 3145736 | tf_op jit(solution)/shard_map/ppermute | solution.py:617
  580.6 171.4 %collective-permute-start.107 = (bf16[4,2,512,128]{3,2,1,0:T(8,128)(2,1)}, bf16[4,2,512,128]{3,2,1,0:T(8,128)(2,1)S(1)}, u32[]{:S(2)}, u32[]{:S(2)}) collective-permute-start(bf16[4,2,512,128]{3,2,1,0:T(8,128)(2,1)} %get-tuple-element.48), channel_id=1, source_target_pairs={{0,1},{1,0},{2,3},{3,2},{4,5},{5,4},{6,7},{7,6},{8,9},{9,8},{10,11... | collective-permute-start | bytes 3145736 | tf_op jit(solution)/shard_map/ppermute | solution.py:617
  584.1 118.9 %collective-permute-start.110 = (bf16[4,2,512,128]{3,2,1,0:T(8,128)(2,1)}, bf16[4,2,512,128]{3,2,1,0:T(8,128)(2,1)S(1)}, u32[]{:S(2)}, u32[]{:S(2)}) collective-permute-start(bf16[4,2,512,128]{3,2,1,0:T(8,128)(2,1)} %get-tuple-element.50), channel_id=1, source_target_pairs={{0,1},{1,0},{2,3},{3,2},{4,5},{5,4},{6,7},{7,6},{8,9},{9,8},{10,11... | collective-permute-start | bytes 3145736 | tf_op jit(solution)/shard_map/ppermute | solution.py:617
  584.1 46.9 %collective-permute-start.120 = (bf16[4,128,512]{2,1,0:T(8,128)(2,1)}, bf16[4,128,512]{2,1,0:T(8,128)(2,1)S(1)}, u32[]{:S(2)}, u32[]{:S(2)}) collective-permute-start(bf16[4,128,512]{2,1,0:T(8,128)(2,1)} %fusion.30), channel_id=1, source_target_pairs={{16,0},{20,4},{24,8},{28,12},{0,16},{4,20},{8,24},{12,28},{17,1},{... | collective-permute-start | bytes 1572872 | tf_op jit(solution)/shard_map/ppermute | solution.py:609
  585.2 28.4 %collective-permute-start.103 = (bf16[32,1024]{1,0:T(8,128)(2,1)S(1)}, bf16[32,1024]{1,0:T(8,128)(2,1)S(1)}, u32[]{:S(2)}, u32[]{:S(2)}) collective-permute-start(bf16[32,1024]{1,0:T(8,128)(2,1)S(1)} %add_convert_fusion.12), channel_id=1, source_target_pairs={{16,0},{20,4},{24,8},{28,12},{0,16},{4,20},{8,24},{12,28},{17,1},{... | collective-permute-start | bytes 196616 | tf_op jit(solution)/shard_map/ppermute | solution.py:609
  641.9 110.1 %collective-permute-start.109 = (bf16[4,2,512,128]{3,2,1,0:T(8,128)(2,1)S(1)}, bf16[4,2,512,128]{3,2,1,0:T(8,128)(2,1)S(1)}, u32[]{:S(2)}, u32[]{:S(2)}) collective-permute-start(bf16[4,2,512,128]{3,2,1,0:T(8,128)(2,1)S(1)} %copy-done.27), channel_id=1, source_target_pairs={{0,2},{1,3},{2,0},{3,1},{4,6},{5,7},{6,4},{7,5},{8,10},{9,11},{10,... | collective-permute-start | bytes 3145736 | tf_op jit(solution)/shard_map/ppermute | solution.py:613
  646.0 56.9 %collective-permute-start.112 = (bf16[4,2,512,128]{3,2,1,0:T(8,128)(2,1)S(1)}, bf16[4,2,512,128]{3,2,1,0:T(8,128)(2,1)S(1)}, u32[]{:S(2)}, u32[]{:S(2)}) collective-permute-start(bf16[4,2,512,128]{3,2,1,0:T(8,128)(2,1)S(1)} %copy-done.28), channel_id=1, source_target_pairs={{0,2},{1,3},{2,0},{3,1},{4,6},{5,7},{6,4},{7,5},{8,10},{9,11},{10,... | collective-permute-start | bytes 3145736 | tf_op jit(solution)/shard_map/ppermute | solution.py:613
  649.6 41.7 %collective-permute-start.70 = (bf16[128,1024]{1,0:T(8,128)(2,1)S(1)}, bf16[128,1024]{1,0:T(8,128)(2,1)S(1)}, u32[]{:S(2)}, u32[]{:S(2)}) collective-permute-start(bf16[128,1024]{1,0:T(8,128)(2,1)S(1)} %fusion.55), channel_id=1, source_target_pairs={{0,2},{1,3},{2,0},{3,1},{4,6},{5,7},{6,4},{7,5},{8,10},{9,11},{10,... | collective-permute-start | bytes 786440 | tf_op jit(solution)/shard_map/ppermute | solution.py:613
  704.6 51.0 %collective-permute-start.113 = (bf16[4,2,512,128]{3,2,1,0:T(8,128)(2,1)S(1)}, bf16[4,2,512,128]{3,2,1,0:T(8,128)(2,1)S(1)}, u32[]{:S(2)}, u32[]{:S(2)}) collective-permute-start(bf16[4,2,512,128]{3,2,1,0:T(8,128)(2,1)S(1)} %fusion.10), channel_id=1, source_target_pairs={{16,0},{20,4},{24,8},{28,12},{0,16},{4,20},{8,24},{12,28},{17,1},{... | collective-permute-start | bytes 3145736 | tf_op jit(solution)/shard_map/ppermute | solution.py:609
  707.2 44.2 %collective-permute-start.72 = (bf16[128,1024]{1,0:T(8,128)(2,1)S(1)}, bf16[128,1024]{1,0:T(8,128)(2,1)S(1)}, u32[]{:S(2)}, u32[]{:S(2)}) collective-permute-start(bf16[128,1024]{1,0:T(8,128)(2,1)S(1)} %fusion.42), channel_id=1, source_target_pairs={{0,2},{1,3},{2,0},{3,1},{4,6},{5,7},{6,4},{7,5},{8,10},{9,11},{10,... | collective-permute-start | bytes 786440 | tf_op jit(solution)/shard_map/ppermute | solution.py:613
  707.9 43.0 %collective-permute-start.78 = (f32[1,1024]{1,0:T(1,128)S(1)}, f32[1,1024]{1,0:T(1,128)S(1)}, u32[]{:S(2)}, u32[]{:S(2)}) collective-permute-start(f32[1,1024]{1,0:T(1,128)S(1)} %add.447), channel_id=1, source_target_pairs={{0,16},{4,20},{8,24},{12,28},{16,0},{20,4},{24,8},{28,12},{1,17},{... | collective-permute-start | bytes 12296 | tf_op jit(solution)/shard_map/ppermute | solution.py:669
  (174 other events, 2243.5 us)

commit v2 on v1

--- a/solution.py
+++ b/solution.py
@@ -352,41 +352,138 @@
 F32 = jnp.float32
 CHUNK = 256
 SHARE = 128
+PACK = 12 * SHARE
 NT = (((1,), (1,)), ((), ()))
-
-
-def weight_copies(pieces, in_buf, out_buf, sems, expert, slot):
-    in_own, in_other, out_own, out_other = (pieces[0:4], pieces[4:8], pieces[8:12], pieces[12:16])
+ORDER = (0, 2, 4, 6, 1, 3, 5, 7)
+
+
+def whole_block(shape):
+    return pl.BlockSpec(shape, lambda e, *_: (0,) * len(shape))
+
+
+def any_block():
+    return pl.BlockSpec(memory_space=pl.ANY)
+
+
+def pack_body(half_ref, in_ref, out_ref, own, near, far, sems):
+    held = in_ref.shape[0] // 2
+    copies = []
+    for target, start, first, count in (
+        (own, half_ref[0] * held, 0, held),
+        (near, (1 - half_ref[0]) * held, 0, held // 2),
+        (far, (1 - half_ref[0]) * held, held // 2, held // 2),
+    ):
+        for e in range(count):
+            source = start + first + e
+            for c in range(2):
+                copies.append(
+                    (in_ref.at[source, c], target.at[pl.ds(e * PACK + c * 4 * SHARE, 4 * SHARE)])
+                )
+            for k in range(4):
+                copies.append(
+                    (
+                        out_ref.at[source, :, pl.ds(k * SHARE, SHARE)],
+                        target.at[pl.ds(e * PACK + (8 + k) * SHARE, SHARE)],
+                    )
+                )
+    copies = [
+        pltpu.make_async_copy(source, target, sems.at[n])
+        for n, (source, target) in enumerate(copies)
+    ]
+    for copy in copies:
+        copy.start()
+    for copy in copies:
+        copy.wait()
+
+
+def pack_weights(half_index, expert_in, expert_out):
+    held = expert_in.shape[0] // 2
+    shapes = [(held * PACK, SHARE), (held // 2 * PACK, SHARE), (held // 2 * PACK, SHARE)]
+    return pl.pallas_call(
+        pack_body,
+        in_specs=[pl.BlockSpec(memory_space=pltpu.SMEM), any_block(), any_block()],
+        out_specs=[any_block()] * 3,
+        out_shape=[jax.ShapeDtypeStruct(shape, BF16) for shape in shapes],
+        scratch_shapes=[pltpu.SemaphoreType.DMA((12 * held,))],
+        name="pack_weights",
+    )(half_index, expert_in, expert_out)
+
+
+def weight_copies(own, other, own_row, other_row, half, in_buf, out_buf, sems, slot):
     copies = []
     for q in range(4):
-        for half, piece in ((0, in_own[q]), (1, in_other[q])):
-            width = piece.shape[2]
+        for pack, row, side in ((own[q], own_row, half), (other[q], other_row, 1 - half)):
             for c in range(2):
-                target = in_buf.at[
-                    slot, pl.ds(half * width, width), pl.ds((2 * q + c) * SHARE, SHARE)
-                ]
-                copies.append((piece.at[expert, c], target))
-        for half, piece in ((0, out_own[q]), (1, out_other[q])):
-            width = piece.shape[2]
-            target = out_buf.at[slot, pl.ds(q * SHARE, SHARE), pl.ds(half * width, width)]
-            copies.append((piece.at[expert], target))
+                copies.append(
+                    (
+                        pack.at[pl.ds(pl.multiple_of(row + c * 4 * SHARE, SHARE), 4 * SHARE)],
+                        in_buf.at[
+                            slot,
+                            pl.ds(pl.multiple_of(side * 4 * SHARE, SHARE), 4 * SHARE),
+                            pl.ds((2 * q + c) * SHARE, SHARE),
+                        ],
+                    )
+                )
+            for k in range(4):
+                copies.append(
+                    (
+                        pack.at[pl.ds(pl.multiple_of(row + (8 + k) * SHARE, SHARE), SHARE)],
+                        out_buf.at[slot, side, pl.ds(q * SHARE, SHARE), pl.ds(k * SHARE, SHARE)],
+                    )
+                )
     return [
         pltpu.make_async_copy(source, target, sems.at[slot, n])
         for n, (source, target) in enumerate(copies)
     ]
 
 
-def reorder_halves(half_index, source, target):
-    width = source.shape[1] // 2
-
-    @pl.when(half_index == 0)
+def stream_weights(first, packs, half, in_buf, out_buf, sems):
+    step = pl.program_id(0)
+    slot = lax.rem(step, 2)
+    own, near, far = (packs[0:4], packs[4:8], packs[8:12])
+
+    def start(index, target):
+        expert = first + index
+
+        def begin(other, start_row):
+            for copy in weight_copies(
+                own, other, expert * PACK, start_row, half, in_buf, out_buf, sems, target
+            ):
+                copy.start()
+
+        if not far:
+            begin(near, index * PACK)
+            return
+
+        @pl.when(expert < 2)
+        def _():
+            begin(near, expert * PACK)
+
+        @pl.when(expert >= 2)
+        def _():
+            begin(far, (expert - 2) * PACK)
+
+    @pl.when(step == 0)
     def _():
-        target[...] = source[...]
-
-    @pl.when(half_index == 1)
+        start(0, 0)
+
+    @pl.when(step + 1 < pl.num_programs(0))
     def _():
-        target[:, :width] = source[:, width:]
-        target[:, width:] = source[:, :width]
+        start(step + 1, 1 - slot)
+
+    def wait():
+        for copy in weight_copies(own, near, 0, 0, half, in_buf, out_buf, sems, slot):
+            copy.wait()
+
+    return (step, slot, wait)
+
+
+def weight_scratch(width, hidden):
+    return [
+        pltpu.VMEM((2, width, 2 * hidden), BF16),
+        pltpu.VMEM((2, 2, hidden, width // 2), BF16),
+        pltpu.SemaphoreType.DMA((2, 48)),
+    ]
 
 
 def split_pairs(values):
@@ -415,134 +512,181 @@
     return jnp.sum(jnp.where(lane == expert, gates, 0.0), -1, keepdims=True)
 
 
-def stream_weights(pieces, in_buf, out_buf, sems):
-    expert = pl.program_id(0)
-    slot = lax.rem(expert, 2)
-
-    @pl.when(expert == 0)
+def dense_gates(rows, ids, router):
+    logits = jnp.dot(rows, router, preferred_element_type=F32)
+    lane = lax.broadcasted_iota(jnp.int32, logits.shape, 1)
+    mask = ids[:, 0:1] == lane
+    for k in range(1, TOP):
+        mask = mask | (ids[:, k : k + 1] == lane)
+    masked = jnp.where(mask, logits, -1e30)
+    powers = jnp.where(mask, jnp.exp(masked - jnp.max(masked, -1, keepdims=True)), 0.0)
+    return powers / jnp.sum(powers, -1, keepdims=True)
+
+
+def apply_expert(rows, expert, slot, rows_ref, gate_ref, pre_ref, gated_ref, in_buf):
+    pre = jnp.dot(rows_ref[rows, :], in_buf[slot], preferred_element_type=F32)
+    pre_ref[0, rows, :] = pre.astype(BF16)
+    gate_pre, up_pre = split_pairs(pre)
+    weight = gate_column(gate_ref[rows, :], expert)
+    gated = (weight * (gate_pre * jax.nn.sigmoid(gate_pre) * up_pre)).astype(BF16)
+    gated_ref[0, rows, :] = gated
+    return gated
+
+
+def forward_first(half_ref, *refs):
+    shards = refs[:8]
+    route_ref, router_ref = refs[8:10]
+    packs = refs[10:18]
+    acc, pre_ref, gated_ref, gate_ref, rows_ref, in_buf, out_buf, sems = refs[18:]
+    step, slot, wait = stream_weights(0, packs, half_ref[0], in_buf, out_buf, sems)
+    row_count, width = acc.shape
+    size = row_count // 8
+
+    @pl.when(step == 0)
     def _():
-        for copy in weight_copies(pieces, in_buf, out_buf, sems, 0, 0):
-            copy.start()
-
-    @pl.when(expert + 1 < pl.num_programs(0))
+        for i in range(8):
+            rows_ref[i * size : (i + 1) * size, :] = shards[i][...]
+        acc[...] = jnp.zeros_like(acc)
+
+        def gating(rows):
+            gate_ref[rows, :] = dense_gates(rows_ref[rows, :], route_ref[rows, :], router_ref[...])
+
+        chunk_loop(row_count, gating)
+
+    wait()
+
+    def mlp(rows):
+        gated = apply_expert(rows, step, slot, rows_ref, gate_ref, pre_ref, gated_ref, in_buf)
+        for side in range(2):
+            columns = slice(side * width // 2, (side + 1) * width // 2)
+            acc[rows, columns] += jnp.dot(gated, out_buf[slot, side], preferred_element_type=F32)
+
+    chunk_loop(row_count, mlp)
+
+
+def forward_second(half_ref, *refs):
+    rows_ref, gate_ref, start_ref = refs[:3]
+    packs = refs[3:11]
+    keep_ref, near_ref, far_ref, pre_ref, gated_ref, acc, in_buf, out_buf, sems = refs[13:]
+    step, slot, wait = stream_weights(2, packs, half_ref[0], in_buf, out_buf, sems)
+    row_count, width = acc.shape
+
+    wait()
+
+    def mlp(rows, source):
+        gated = apply_expert(rows, step + 2, slot, rows_ref, gate_ref, pre_ref, gated_ref, in_buf)
+        for side in range(2):
+            columns = slice(side * width // 2, (side + 1) * width // 2)
+            acc[rows, columns] = source[rows, columns] + jnp.dot(
+                gated, out_buf[slot, side], preferred_element_type=F32
+            )
+
+    @pl.when(step == 0)
     def _():
-        for copy in weight_copies(pieces, in_buf, out_buf, sems, expert + 1, 1 - slot):
-            copy.start()
-
-    return (expert, slot)
-
-
-def forward_body(half_ref, rows_ref, route_ref, router_ref, *rest):
-    pieces = rest[:16]
-    sum_ref, pre_ref, gated_ref, gate_ref, rows_rel, acc, in_buf, out_buf, sems = rest[16:]
-    expert, slot = stream_weights(pieces, in_buf, out_buf, sems)
-    row_count = rows_ref.shape[0]
-
-    @pl.when(expert == 0)
+        chunk_loop(row_count, lambda rows: mlp(rows, start_ref))
+
+    @pl.when(step > 0)
     def _():
-        reorder_halves(half_ref[0], rows_ref, rows_rel)
-        acc[...] = jnp.zeros_like(acc)
-
-        def gating(rows):
-            logits = jnp.dot(rows_ref[rows, :], router_ref[...], preferred_element_type=F32)
-            lane = lax.broadcasted_iota(jnp.int32, logits.shape, 1)
-            ids = route_ref[rows, :]
-            mask = ids[:, 0:1] == lane
-            for k in range(1, TOP):
-                mask = mask | (ids[:, k : k + 1] == lane)
-            masked = jnp.where(mask, logits, -1e30)
-            powers = jnp.where(mask, jnp.exp(masked - jnp.max(masked, -1, keepdims=True)), 0.0)
-            gate_ref[rows, :] = powers / jnp.sum(powers, -1, keepdims=True)
-
-        chunk_loop(row_count, gating)
-
-    for copy in weight_copies(pieces, in_buf, out_buf, sems, expert, slot):
-        copy.wait()
-
-    def mlp(rows):
-        pre = jnp.dot(rows_rel[rows, :], in_buf[slot], preferred_element_type=F32)
-        pre_ref[0, rows, :] = pre.astype(BF16)
-        gate_pre, up_pre = split_pairs(pre)
-        weight = gate_column(gate_ref[rows, :], expert)
-        gated = (weight * (gate_pre * jax.nn.sigmoid(gate_pre) * up_pre)).astype(BF16)
-        gated_ref[0, rows, :] = gated
-        acc[rows, :] += jnp.dot(gated, out_buf[slot], preferred_element_type=F32)
-
-    chunk_loop(row_count, mlp)
-
-    @pl.when(expert == pl.num_programs(0) - 1)
+        chunk_loop(row_count, lambda rows: mlp(rows, acc))
+
+    @pl.when(step == pl.num_programs(0) - 1)
     def _():
-        reorder_halves(half_ref[0], acc, sum_ref)
-
-
-def whole_block(shape):
-    return pl.BlockSpec(shape, lambda e, *_: (0,) * len(shape))
-
-
-def expert_block(shape):
-    return pl.BlockSpec((1,) + shape[1:], lambda e, *_: (e, 0, 0))
-
-
-def weight_scratch(row_count, width, hidden):
-    return [
-        pltpu.VMEM((row_count, width), BF16),
-        pltpu.VMEM((row_count, width), F32),
-        pltpu.VMEM((2, width, 2 * hidden), BF16),
-        pltpu.VMEM((2, hidden, width), BF16),
-        pltpu.SemaphoreType.DMA((2, 24)),
+        spread(acc, keep_ref, near_ref, far_ref)
+
+
+def spread(acc, keep_ref, near_ref, far_ref):
+    part = acc.shape[0] // 4
+    keep_ref[...] = acc[: 2 * part, :]
+    near_ref[...] = acc[2 * part : 3 * part, :].astype(BF16)
+    far_ref[...] = acc[3 * part :, :].astype(BF16)
+
+
+def spread_specs(row_count, width):
+    shapes = [
+        jax.ShapeDtypeStruct((row_count // 2, width), F32),
+        jax.ShapeDtypeStruct((row_count // 4, width), BF16),
+        jax.ShapeDtypeStruct((row_count // 4, width), BF16),
     ]
-
-
-def experts_forward(half_index, rows, route_ids, router, pieces):
-    row_count, width = rows.shape
-    local = pieces[0].shape[0]
+    return ([whole_block(s.shape) for s in shapes], shapes)
+
+
+def expert_block(shape, first=0):
+    return pl.BlockSpec((1,) + shape[1:], lambda e, *_: (e + first,) + (0,) * (len(shape) - 1))
+
+
+def experts_forward(half_index, shards, route_ids, router, own, near, far):
+    size, width = shards[0].shape
+    row_count = 8 * size
+    local = own[0].shape[0] // PACK
     hidden = 4 * SHARE
-    pre_shape = (local, row_count, 2 * hidden)
-    gated_shape = (local, row_count, hidden)
-    return pl.pallas_call(
-        forward_body,
+    sums = jax.ShapeDtypeStruct((row_count, width), F32)
+    pre = jax.ShapeDtypeStruct((local, row_count, 2 * hidden), BF16)
+    gated = jax.ShapeDtypeStruct((local, row_count, hidden), BF16)
+    gates = jax.ShapeDtypeStruct((row_count, 128), F32)
+    rows = jax.ShapeDtypeStruct((row_count, width), BF16)
+    sums_a, pre_a, gated_a, gates, rows = pl.pallas_call(
+        forward_first,
         grid_spec=pltpu.PrefetchScalarGridSpec(
             num_scalar_prefetch=1,
-            grid=(local,),
-            in_specs=[whole_block(v.shape) for v in (rows, route_ids, router)]
-            + [pl.BlockSpec(memory_space=pl.ANY)] * 16,
+            grid=(2,),
+            in_specs=[whole_block(v.shape) for v in (*shards, route_ids, router)]
+            + [any_block()] * 8,
             out_specs=[
-                whole_block((row_count, width)),
-                expert_block(pre_shape),
-                expert_block(gated_shape),
-                whole_block((row_count, 128)),
+                whole_block(sums.shape),
+                expert_block(pre.shape),
+                expert_block(gated.shape),
+                whole_block(gates.shape),
+                whole_block(rows.shape),
             ],
-            scratch_shapes=weight_scratch(row_count, width, hidden),
+            scratch_shapes=weight_scratch(width, hidden),
         ),
-        out_shape=[
-            jax.ShapeDtypeStruct((row_count, width), F32),
-            jax.ShapeDtypeStruct(pre_shape, BF16),
-            jax.ShapeDtypeStruct(gated_shape, BF16),
-            jax.ShapeDtypeStruct((row_count, 128), F32),
-        ],
-        name="experts_forward",
-    )(half_index, rows, route_ids, router, *pieces)
-
-
-def backward_body(half_ref, grad_ref, mean_ref, gate_ref, router_ref, pre_ref, *rest):
-    pieces = rest[:16]
-    rows_ref, pre_grad_ref, logit_ref, grad_rel, acc, in_buf, out_buf, sems = rest[16:]
-    expert, slot = stream_weights(pieces, in_buf, out_buf, sems)
-    row_count = grad_ref.shape[0]
-
-    @pl.when(expert == 0)
+        out_shape=[sums, pre, gated, gates, rows],
+        name="experts_forward_a",
+    )(half_index, *shards, route_ids, router, *own, *near)
+    specs, shapes = spread_specs(row_count, width)
+    keep, send_near, send_far, pre, gated = pl.pallas_call(
+        forward_second,
+        grid_spec=pltpu.PrefetchScalarGridSpec(
+            num_scalar_prefetch=1,
+            grid=(2,),
+            in_specs=[whole_block(v.shape) for v in (rows, gates, sums)] + [any_block()] * 10,
+            out_specs=specs + [expert_block(pre.shape, 2), expert_block(gated.shape, 2)],
+            scratch_shapes=[pltpu.VMEM((row_count, width), F32)] + weight_scratch(width, hidden),
+        ),
+        out_shape=shapes + [pre, gated],
+        input_output_aliases={12: 3, 13: 4},
+        name="experts_forward_b",
+    )(half_index, rows, gates, sums_a, *own, *far, pre_a, gated_a)
+    return (keep, send_near, send_far, pre, gated, gates, rows)
+
+
+def backward_body(half_ref, *refs):
+    shards = refs[:8]
+    gate_ref, router_ref, pre_ref = refs[8:11]
+    packs = refs[11:23]
+    keep_ref, near_ref, far_ref, pre_grad_ref, logit_ref, grad_ref = refs[23:29]
+    acc, in_buf, out_buf, sems = refs[29:]
+    step, slot, wait = stream_weights(0, packs, half_ref[0], in_buf, out_buf, sems)
+    row_count, width = grad_ref.shape
+    size = row_count // 8
+
+    @pl.when(step == 0)
     def _():
-        reorder_halves(half_ref[0], grad_ref, grad_rel)
+        for i in range(8):
+            grad_ref[i * size : (i + 1) * size, :] = shards[i][...]
         acc[...] = jnp.zeros_like(acc)
         logit_ref[...] = jnp.zeros_like(logit_ref)
 
-    for copy in weight_copies(pieces, in_buf, out_buf, sems, expert, slot):
-        copy.wait()
+    wait()
 
     def mlp(rows):
-        plain = lax.dot_general(grad_rel[rows, :], out_buf[slot], NT, preferred_element_type=F32)
+        plain = lax.dot_general(
+            grad_ref[rows, : width // 2], out_buf[slot, 0], NT, preferred_element_type=F32
+        ) + lax.dot_general(
+            grad_ref[rows, width // 2 :], out_buf[slot, 1], NT, preferred_element_type=F32
+        )
         gate_pre, up_pre = split_pairs(pre_ref[0, rows, :].astype(F32))
-        weight = gate_column(gate_ref[rows, :], expert)
+        weight = gate_column(gate_ref[rows, :], step)
         sigmoid = jax.nn.sigmoid(gate_pre)
         act = gate_pre * sigmoid
         grad_weight = jnp.sum(act * up_pre * plain, -1, keepdims=True)
@@ -553,60 +697,122 @@
         pre_grad_ref[0, rows, :] = pre_grad
         old = logit_ref[rows, :]
         lane = lax.broadcasted_iota(jnp.int32, old.shape, 1)
+        value = weight * grad_weight
+        high = value.astype(BF16).astype(F32)
         logit_ref[rows, :] = jnp.where(
-            lane == expert, weight * (grad_weight - mean_ref[rows, 0:1]), old
+            lane == step, high, jnp.where(lane == step + 32, value - high, old)
         )
         acc[rows, :] += lax.dot_general(pre_grad, in_buf[slot], NT, preferred_element_type=F32)
 
     chunk_loop(row_count, mlp)
 
-    @pl.when(expert == pl.num_programs(0) - 1)
+    @pl.when(step == pl.num_programs(0) - 1)
     def _():
-        reorder_halves(half_ref[0], acc, rows_ref)
-
         def router(rows):
-            rows_ref[rows, :] += lax.dot_general(
+            acc[rows, :] += lax.dot_general(
                 logit_ref[rows, :].astype(BF16), router_ref[...], NT, preferred_element_type=F32
             )
 
         chunk_loop(row_count, router)
-
-
-def experts_backward(half_index, grads, means, gates, router, pre, pieces):
-    row_count, width = grads.shape
-    local = pieces[0].shape[0]
-    hidden = 4 * SHARE
+        spread(acc, keep_ref, near_ref, far_ref)
+
+
+def experts_backward(half_index, shards, gates, router, pre, own, near, far):
+    row_count, width = (8 * shards[0].shape[0], shards[0].shape[1])
+    local = pre.shape[0]
+    specs, shapes = spread_specs(row_count, width)
     return pl.pallas_call(
         backward_body,
         grid_spec=pltpu.PrefetchScalarGridSpec(
             num_scalar_prefetch=1,
             grid=(local,),
-            in_specs=[whole_block(v.shape) for v in (grads, means, gates, router)]
+            in_specs=[whole_block(v.shape) for v in (*shards, gates, router)]
             + [expert_block(pre.shape)]
-            + [pl.BlockSpec(memory_space=pl.ANY)] * 16,
-            out_specs=[
-                whole_block((row_count, width)),
+            + [any_block()] * 12,
+            out_specs=specs
+            + [
                 expert_block(pre.shape),
                 whole_block((row_count, 128)),
+                whole_block((row_count, width)),
             ],
-            scratch_shapes=weight_scratch(row_count, width, hidden),
+            scratch_shapes=[pltpu.VMEM((row_count, width), F32)]
+            + weight_scratch(width, 4 * SHARE),
         ),
-        out_shape=[
-            jax.ShapeDtypeStruct((row_count, width), F32),
+        out_shape=shapes
+        + [
             jax.ShapeDtypeStruct(pre.shape, BF16),
             jax.ShapeDtypeStruct((row_count, 128), F32),
+            jax.ShapeDtypeStruct((row_count, width), BF16),
         ],
         name="experts_backward",
-    )(half_index, grads, means, gates, router, pre, *pieces)
-
-
-def swap_x(value):
-    return lax.ppermute(value, "expert", [(i, i ^ 1) for i in range(8)])
-
-
-def from_z(value, ahead):
-    pairs = [(((i // 2 + ahead) % 4) * 2 + i % 2, i) for i in range(8)]
-    return lax.ppermute(value, "expert", pairs)
+    )(half_index, *shards, gates, router, pre, *own, *near, *far)
+
+
+def grad_out_body(half_ref, gated_ref, other_ref, mine_ref, *outs):
+    turned = gated_ref[0].T
+    for n, source in ((0, other_ref), (2, mine_ref)):
+        product = jnp.dot(turned, source[...], preferred_element_type=F32).astype(BF16)
+        for q in range(4):
+            outs[n + q % 2][q // 2, 0] = product[q * SHARE : (q + 1) * SHARE, :]
+
+
+def grad_expert_outs(half_index, gated, grads):
+    local, row_count, hidden = gated.shape
+    width = grads.shape[1]
+    half_spec = (row_count, width // 2)
+    shape = (2, local, SHARE, width // 2)
+    return pl.pallas_call(
+        grad_out_body,
+        grid_spec=pltpu.PrefetchScalarGridSpec(
+            num_scalar_prefetch=1,
+            grid=(local,),
+            in_specs=[
+                expert_block(gated.shape),
+                pl.BlockSpec(half_spec, lambda e, half: (0, 1 - half[0])),
+                pl.BlockSpec(half_spec, lambda e, half: (0, half[0])),
+            ],
+            out_specs=[pl.BlockSpec((2, 1) + shape[2:], lambda e, *_: (0, e, 0, 0))] * 4,
+        ),
+        out_shape=[jax.ShapeDtypeStruct(shape, BF16)] * 4,
+        name="grad_expert_out",
+    )(half_index, gated, grads, grads)
+
+
+def grad_in_body(half_ref, rows_ref, pre_ref, keep_ref, send_ref, turned):
+    @pl.when(pl.program_id(0) == 0)
+    def _():
+        turned[...] = rows_ref[...].T
+
+    product = jnp.dot(turned[...], pre_ref[0], preferred_element_type=F32).astype(BF16)
+    for q in range(4):
+        for c in range(2):
+            start = (2 * q + c) * SHARE
+            (keep_ref, send_ref)[q % 2][q // 2, 0, c] = product[:, start : start + SHARE]
+
+
+def grad_expert_ins(half_index, rows, pre_grad):
+    local, row_count, wide = pre_grad.shape
+    width = rows.shape[1]
+    shape = (2, local, 2, width // 2, SHARE)
+    return pl.pallas_call(
+        grad_in_body,
+        grid_spec=pltpu.PrefetchScalarGridSpec(
+            num_scalar_prefetch=1,
+            grid=(local,),
+            in_specs=[
+                pl.BlockSpec((row_count, width // 2), lambda e, half: (0, half[0])),
+                expert_block(pre_grad.shape),
+            ],
+            out_specs=[pl.BlockSpec((2, 1) + shape[2:], lambda e, *_: (0, e, 0, 0, 0))] * 2,
+            scratch_shapes=[pltpu.VMEM((width // 2, row_count), BF16)],
+        ),
+        out_shape=[jax.ShapeDtypeStruct(shape, BF16)] * 2,
+        name="grad_expert_in",
+    )(half_index, rows, pre_grad)
+
+
+def trade(value, bits):
+    return lax.ppermute(value, "expert", [(i, i ^ bits) for i in range(8)])
 
 
 def swap_y(value):
@@ -618,22 +824,20 @@
 
 
 def gather_experts(value):
-    near = swap_x(value)
-    ahead = [from_z(value, d) for d in (1, 2, 3)]
-    shards = [value, near]
-    for shard in ahead:
-        shards += [shard, swap_x(shard)]
-    return shards
-
-
-def scatter_experts(shards):
-    columns = [None] * 4
-    for dz in (2, 1, 3, 0):
-        keep, send = (shards[2 * dz], shards[2 * dz + 1])
-        columns[dz] = keep.astype(F32) + swap_x(send.astype(BF16)).astype(F32)
-    total = columns[0]
-    for dz in (2, 1, 3):
-        total = total + from_z(columns[dz].astype(BF16), 4 - dz).astype(F32)
+    column = [value] + [trade(value, bits) for bits in (2, 4, 6)]
+    return column + [trade(shard, 1) for shard in column]
+
+
+def scatter_experts(keep, send_near, send_far):
+    size = keep.shape[0] // 4
+    far = keep[2 * size :].astype(F32) + trade(send_far, 1).astype(F32)
+    far = far.astype(BF16)
+    back = [trade(far[:size], 4), trade(far[size:], 6)]
+    near = trade(send_near, 1).astype(F32)
+    back.append(trade((keep[size : 2 * size].astype(F32) + near[size:]).astype(BF16), 2))
+    total = keep[:size].astype(F32) + near[:size]
+    for part in back:
+        total = total + part.astype(F32)
     return total
 
 
@@ -664,24 +868,31 @@
 def sum_all(value):
     value = value + swap_core(value)
     value = value + swap_y(value)
-    value = value + swap_x(value)
-    value = value + lax.ppermute(value, "expert", [(i, i ^ 2) for i in range(8)])
-    return value + lax.ppermute(value, "expert", [(i, i ^ 4) for i in range(8)])
-
-
-def sum_experts(value, layer, column):
+    for bits in (1, 2, 4):
+        value = value + trade(value, bits)
+    return value
+
+
+def sum_experts(value, place):
     size = value.shape[0] // 8
-    shards = []
-    for dz in range(4):
-        for dx in range(2):
-            place = lax.rem(layer + dz, 4) * 2 + jnp.bitwise_xor(column, dx)
-            shards.append(lax.dynamic_slice_in_dim(value, place * size, size, 0))
-    total = scatter_experts(shards).astype(BF16)
-    gathered = gather_experts(total)
-    layers = [ordered(column, gathered[2 * dz], gathered[2 * dz + 1]) for dz in range(4)]
-    joined = jnp.concatenate(layers + layers, 0)
-    start = lax.rem(4 - layer, 4) * 2 * size
-    return lax.dynamic_slice_in_dim(joined, start, 8 * size, 0).astype(F32)
+    shards = value.reshape(8, size, value.shape[1])
+
+    def pick(*order):
+        picked = [
+            lax.dynamic_index_in_dim(shards, jnp.bitwise_xor(place, r), 0, False) for r in order
+        ]
+        return jnp.concatenate(picked, 0)
+
+    total = scatter_experts(pick(0, 2, 4, 6), pick(1, 3).astype(BF16), pick(5, 7).astype(BF16))
+    gathered = jnp.stack(gather_experts(total.astype(BF16)))
+    lower = (jnp.bitwise_and(place, 1), jnp.bitwise_and(place, 2), jnp.bitwise_and(place, 4))
+    column, inner, outer = (bit > 0 for bit in lower)
+    halves = jnp.stack([gathered[:4], gathered[4:]])
+    halves = jnp.where(column, halves[::-1], halves)
+    halves = halves.reshape(2, 2, 2, size, value.shape[1])
+    halves = jnp.where(inner, halves[:, :, ::-1], halves)
+    halves = jnp.where(outer, halves[:, ::-1], halves)
+    return halves.transpose(1, 2, 0, 3, 4).reshape(value.shape).astype(F32)
 
 
 def per_device(
@@ -731,38 +942,42 @@
     quarter = row_count // shares
     place = lax.axis_index("expert")
     share = lax.axis_index("tensor")
-    layer, column = (place // 2, place % 2)
     row, core = (share // 2, share % 2)
     half_index = place // 4
+    half_arg = half_index.reshape(1)
     held = expert_in.shape[0] // 2
     base = 8 * (place % 4) + held * half_index
 
-    def rows_of(weights, start):
-        return lax.dynamic_slice_in_dim(weights, start * held, held, 0)
-
-    in_own, out_own = (rows_of(expert_in, half_index), rows_of(expert_out, half_index))
-    in_other = from_z(rows_of(expert_in, 1 - half_index), 2)
-    out_other = from_z(rows_of(expert_out, 1 - half_index), 2)
-    pieces = []
-    for piece in (in_own, in_other, out_own, out_other):
-        across = swap_y(piece)
-        pieces += [piece, swap_core(piece), across, swap_core(across)]
+    own_pack, near_pack, far_pack = pack_weights(half_arg, expert_in, expert_out)
+    near_pack = trade(near_pack, 4)
+    far_pack = trade(far_pack, 4)
+
+    def spread_shares(pack):
+        across = swap_y(pack)
+        return [pack, swap_core(pack), across, swap_core(across)]
+
+    own = spread_shares(own_pack)
 
     def quarter_of(values):
         return lax.dynamic_slice_in_dim(values, share * quarter, quarter, 0)
 
     local_valid = jnp.sum(valid_mask)
+    routes_mine = quarter_of(routes)
     notes = jnp.concatenate(
-        [quarter_of(routes), jnp.full((quarter, TOP), local_valid, jnp.int32)], 1
-    )
-    note_rows = jnp.stack(gather_experts(notes))
-    valid_total = jnp.sum(note_rows[:, 0, TOP]).astype(F32)
-    route_rel = jnp.bitwise_and(note_rows[:, :, :TOP] - base, expert_count - 1)
-    route_rel = route_rel.reshape(senders * quarter, TOP)
+        [routes_mine.T, jnp.full((TOP, quarter), local_valid, jnp.int32)], 0
+    )[None]
+    for bits in (1, 2, 4):
+        notes = jnp.concatenate([notes, trade(notes, bits)], 0)
+    valid_total = jnp.sum(notes[:, TOP, 0]).astype(F32)
+    notes = jnp.stack([notes[r, :TOP] for r in ORDER])
+    route_rel = jnp.bitwise_and(notes - base, expert_count - 1)
+    route_rel = route_rel.transpose(0, 2, 1).reshape(senders * quarter, TOP)
     router_rel = lax.dynamic_slice_in_dim(
         jnp.concatenate([router_weight, router_weight], 1), base, expert_count, 1
     )
-    router_rel = jnp.pad(router_rel, ((0, 0), (0, 128 - expert_count)))
+    router_rel = jnp.pad(
+        jnp.concatenate([router_rel, router_rel], 1), ((0, 0), (0, 128 - 2 * expert_count))
+    )
 
     tokens_f32 = tokens.astype(F32)
     scale_one = lax.rsqrt(jnp.mean(tokens_f32 * tokens_f32, -1, keepdims=True) + EPS)
@@ -801,13 +1016,18 @@
     scale_two = lax.rsqrt(jnp.mean(hidden * hidden, -1, keepdims=True) + EPS)
     unit_two = hidden * scale_two
     normed_two = (unit_two * second_gain).astype(BF16)
-    half_arg = half_index.reshape(1)
-    expert_rows = jnp.concatenate(gather_experts(normed_two), 0)
-    moe_part, pre, gated, gates = experts_forward(
-        half_arg, expert_rows, route_rel, router_rel, pieces
-    )
-    moe_parts = moe_part.reshape(senders, quarter, model_width)
-    moe_sum = scatter_experts([moe_parts[i] for i in range(senders)])
+    near_pack, far_pack, normed_two = lax.optimization_barrier((near_pack, far_pack, normed_two))
+    near, far = (spread_shares(near_pack), spread_shares(far_pack))
+    keep, send_near, send_far, pre, gated, gates, expert_rows = experts_forward(
+        half_arg,
+        gather_experts(normed_two),
+        route_rel,
+        router_rel,
+        own,
+        near,
+        far,
+    )
+    moe_sum = scatter_experts(keep, send_near, send_far)
 
     output = hidden + RESIDUAL * moe_sum
     residual_err = output - quarter_of(teacher).astype(F32)
@@ -817,51 +1037,45 @@
     grad_out = token_total / valid_total * valid_rows * residual_err
     grad_moe = (RESIDUAL * grad_out).astype(BF16)
     gate_mean = jnp.sum(grad_moe.astype(F32) * moe_sum, -1, keepdims=True)
-    grad_rows = jnp.concatenate(gather_experts(grad_moe), 0)
-    mean_rows = jnp.concatenate(gather_experts(gate_mean.reshape(1, quarter)), 0)
-    mean_rows = jnp.broadcast_to(mean_rows.reshape(senders * quarter, 1), (senders * quarter, 128))
+    mean_part = -gate_mean * dense_gates(normed_two, routes_mine, router_weight)
+    mean_high = mean_part.astype(BF16)
+    mean_part = jnp.concatenate([mean_high, (mean_part - mean_high.astype(F32)).astype(BF16)], 1)
+    router_pair = jnp.concatenate([router_weight, router_weight], 1)
+    mean_rows = jnp.einsum("te,de->td", mean_part, router_pair, preferred_element_type=F32)
     layer_output = gather_tensor(output.astype(BF16), core, row)
 
-    grad_part, pre_grad, logit_grad = experts_backward(
-        half_arg, grad_rows, mean_rows, gates, router_rel, pre, pieces
-    )
-    grad_parts = grad_part.reshape(senders, quarter, model_width)
-    grad_two = scatter_experts([grad_parts[i] for i in range(senders)])
-
-    logit_grad = logit_grad[:, :expert_count]
-    logit_grad = lax.dynamic_slice_in_dim(
-        jnp.concatenate([logit_grad, logit_grad], 1),
+    keep, send_near, send_far, pre_grad, logit_grad, grad_rows = experts_backward(
+        half_arg, gather_experts(grad_moe), gates, router_rel, pre, own, near, far
+    )
+    grad_two = scatter_experts(keep, send_near, send_far) + mean_rows
+
+    out_keep, out_send, own_out_keep, own_out_send = grad_expert_outs(half_arg, gated, grad_rows)
+    in_keep, in_send = grad_expert_ins(1 - half_arg, expert_rows, pre_grad)
+    own_in_keep, own_in_send = grad_expert_ins(half_arg, expert_rows, pre_grad)
+
+    def home(kept, sent):
+        received = swap_core(sent)
+        near = kept[0].astype(F32) + received[0].astype(F32)
+        far = kept[1].astype(F32) + received[1].astype(F32)
+        return near + swap_y(far.astype(BF16)).astype(F32)
+
+    back_out = trade(home(out_keep, out_send).astype(BF16), 4).astype(F32)
+    back_in = trade(home(in_keep, in_send).astype(BF16), 4).astype(F32)
+    grad_expert_out = ordered(half_index, home(own_out_keep, own_out_send), back_out)
+    grad_expert_in = ordered(half_index, home(own_in_keep, own_in_send), back_in)
+
+    router_part = jnp.einsum(
+        "te,td->ed", logit_grad.astype(BF16), expert_rows, preferred_element_type=F32
+    )
+    router_part = router_part[:expert_count] + router_part[expert_count : 2 * expert_count]
+    router_part = lax.dynamic_slice_in_dim(
+        jnp.concatenate([router_part, router_part], 0),
         jnp.bitwise_and(expert_count - base, expert_count - 1),
         expert_count,
-        1,
-    ).astype(BF16)
-    router_part = jnp.einsum("te,td->ed", logit_grad, expert_rows, preferred_element_type=F32)
-
-    in_grads = jnp.einsum("md,emf->edf", expert_rows, pre_grad, preferred_element_type=F32)
-    out_grads = jnp.einsum("emf,md->efd", gated, grad_rows, preferred_element_type=F32)
-    half_width = model_width // 2
-    in_grads = in_grads.astype(BF16).reshape(held, 2, half_width, 4, 2, SHARE)
-    out_grads = out_grads.astype(BF16).reshape(held, 4, SHARE, 2, half_width)
-
-    def halves(values, axis):
-        first = lax.dynamic_index_in_dim(values, half_index, axis, False)
-        return (first, lax.dynamic_index_in_dim(values, 1 - half_index, axis, False))
-
-    def home(part_of):
-        near = part_of(0).astype(F32) + swap_core(part_of(1)).astype(F32)
-        far = part_of(2).astype(F32) + swap_core(part_of(3)).astype(F32)
-        return near + swap_y(far.astype(BF16)).astype(F32)
-
-    results = []
-    for mine, theirs in (
-        halves(in_grads.transpose(1, 3, 0, 4, 2, 5), 0),
-        halves(out_grads.transpose(3, 1, 0, 2, 4), 0),
-    ):
-        keep = home(lambda q, v=mine: v[q])
-        send = home(lambda q, v=theirs: v[q])
-        back = from_z(send.astype(BF16), 2).astype(F32)
-        results.append(ordered(half_index, keep, back))
-    grad_expert_in, grad_expert_out = results
+        0,
+    )
+    mean_router = jnp.einsum("te,td->ed", mean_part, normed_two, preferred_element_type=F32)
+    router_part = router_part + mean_router[:expert_count] + mean_router[expert_count:]
 
     grad_second_part = jnp.sum(grad_two * unit_two, 0)
     grad_unit_two = grad_two * second_gain
@@ -916,8 +1130,8 @@
         grad_unit_one - unit_mine * jnp.mean(grad_unit_one * unit_mine, -1, keepdims=True)
     )
     grad_tokens = gather_tensor(grad_tokens.astype(BF16), core, row).astype(F32)
-    grad_output = sum_experts(grad_output, layer, column)
-    grad_weights = sum_experts(grad_weights, layer, column)
+    grad_output = sum_experts(grad_output, place)
+    grad_weights = sum_experts(grad_weights, place)
     query_columns = query_weight.shape[1]
     key_columns = query_columns + key_matrix.shape[1]
     return (

time: 768 us -> 684 us (0.89)
  Pallas kernels: 55.9 us -> 190 us
  local copies, waits for them, and re-layouts: 140 us -> 23.6 us
  waiting for transfers between devices: 363 us -> 274 us
  matrix products: 40.4 us -> 19.1 us
  starting transfers between devices: 110 us -> 122 us
    pallas_call x1 -> x6, Pallas kernels: 24.9 us -> 158 us  [the longest x1 96.8 us: pack_weights(): pl.pallas_call(pack_body, in_specs=[pl.BlockSpec(memory_space=pltpu.SMEM)...]
    unnamed x179 -> x196, local copies, waits for them, and re-layouts: 61.6 us -> 8.52 us
    ppermute x80 -> x61, waiting for transfers between devices: 266 us -> 221 us  [trade(): return lax.ppermute(value, 'expert', [(i, i ^ bits) for i in range(8)])]
    ppermute x15 -> x14, waiting for transfers between devices: 93.5 us -> 50.3 us  [swap_y(): return lax.ppermute(value, 'tensor', [(i, i ^ 2) for i in range(4)])]
    another operation x3 -> x1, local copies, waits for them, and re-layouts: 30.5 us -> 0.01 us  [per_device(): notes = jnp.stack([notes[r, :TOP] for r in ORDER])]
    reshape x2 -> x1, local copies, waits for them, and re-layouts: 22.3 us -> 0.07 us  [sum_experts(): halves = halves.reshape(2, 2, 2, size, value.shape[1])]
    dot_general x3 -> x4, matrix products: 25.1 us -> 3.88 us  [the longest x1 1.65 us: per_device(): jnp.einsum('te,td->ed', logit_grad.astype(BF16), expert_rows, preferred_e...]
    ppermute x15 -> x14, starting transfers between devices: 11.7 us -> 20.7 us  [swap_y(): return lax.ppermute(value, 'tensor', [(i, i ^ 2) for i in range(4)])]
  transfers between devices with their start and end apart: 121 -> 95, of which waited for: 52 -> 39; matrix products, arithmetic and copies ran while one was open for 22% -> 9% of each run, Pallas kernels for 4% -> 21%
where the time goes in v2:
time: 684 us; the launch traced here: 677 us
  waiting for transfers between devices  274 us (40%)
  Pallas kernels  190 us (28%)
  starting transfers between devices  122 us (18%)
  other arithmetic  42.5 us (6%)
  local copies, waits for them, and re-layouts  23.6 us (3%)
  matrix products  19.1 us (3%)
    ppermute x61, waiting for transfers between devices, trade(): return lax.ppermute(value, 'expert', [(i, i ^ bits) for i in range(8)])  221 us
    ppermute x61, starting transfers between devices, trade(): return lax.ppermute(value, 'expert', [(i, i ^ bits) for i in range(8)])  99.2 us
    pallas_call x1, Pallas kernels, pack_weights(): pl.pallas_call(pack_body, in_specs=[pl.BlockSpec(memory_space=pltpu.SMEM)...  96.8 us
    ppermute x14, waiting for transfers between devices, swap_y(): return lax.ppermute(value, 'tensor', [(i, i ^ 2) for i in range(4)])  50.3 us
    pallas_call x1, Pallas kernels, experts_backward(): pl.pallas_call(backward_body, grid_spec=pltpu.PrefetchScalarGridSpec(num_...  31.4 us
    ppermute x14, starting transfers between devices, swap_y(): return lax.ppermute(value, 'tensor', [(i, i ^ 2) for i in range(4)])  20.7 us
    pallas_call x2, Pallas kernels, grad_expert_ins(): pl.pallas_call(grad_in_body, grid_spec=pltpu.PrefetchScalarGridSpec(num_s...  18.3 us
    pallas_call x1, Pallas kernels, experts_forward(): pl.pallas_call(forward_first, grid_spec=pltpu.PrefetchScalarGridSpec(num_...  17.8 us
  transfers between devices with their start and end apart: 95, of which 39 were waited for; matrix products, arithmetic and copies ran while one was open for 9% of the time, Pallas kernels for 21%

profile of v2, /device:TPU:0, one launch (start us, length us, event | category | flops | bytes accessed | tf_op | source)
XLA Modules:
  0.0 676.5 jit_solution(14479361258923557355)
XLA Ops:
  20.9 96.8 %pack_weights.1 = (bf16[6144,128]{1,0:T(8,128)(2,1)}, bf16[3072,128]{1,0:T(8,128)(2,1)}, bf16[3072,128]{1,0:T(8,128)(2,1)}) custom-call(s32[1]{0:T(128)} %bitcast.17.half_ref, bf16[8,2,512,128]{3,2,1,0:T(8,128)(2,1)} %in_ref.1, bf16[8,128,512]{2,1,0:T(8,128)(2,1)} %out_ref.1), custom_call_target="tpu_custom_call" | custom-call | tf_op jit(solution)/shard_map/pack_weights/pallas_call | solution.py:402
  126.8 46.5 %collective-permute-done.2.refs_14_.refs_15_ = bf16[3072,128]{1,0:T(8,128)(2,1)} collective-permute-done((bf16[3072,128]{1,0:T(8,128)(2,1)}, bf16[3072,128]{1,0:T(8,128)(2,1)}, u32[]{:S(2)}, u32[]{:S(2)}) %collective-permute-start.2) | collective-permute-done | bytes 786464 | tf_op jit(solution)/shard_map/ppermute | solution.py:815
  173.3 16.3 %collective-permute-done.3.refs_7_.refs_19_ = bf16[3072,128]{1,0:T(8,128)(2,1)} collective-permute-done((bf16[3072,128]{1,0:T(8,128)(2,1)}, bf16[3072,128]{1,0:T(8,128)(2,1)}, u32[]{:S(2)}, u32[]{:S(2)}) %collective-permute-start.3) | collective-permute-done | bytes 786464 | tf_op jit(solution)/shard_map/ppermute | solution.py:815
  194.1 9.1 %collective-permute-done.12 = s32[2,16,128]{2,1,0:T(8,128)S(1)} collective-permute-done((s32[2,16,128]{2,1,0:T(8,128)S(1)}, s32[2,16,128]{2,1,0:T(8,128)S(1)}, u32[]{:S(2)}, u32[]{:S(2)}) %collective-permute-start.12) | collective-permute-done | bytes 16416 | tf_op jit(solution)/shard_map/ppermute | solution.py:815
  225.4 5.6 collective-permute-done.9.refs_6_
  238.1 13.4 %collective-permute-done.21.refs_9_.refs_21_ = bf16[3072,128]{1,0:T(8,128)(2,1)} collective-permute-done((bf16[3072,128]{1,0:T(8,128)(2,1)}, bf16[3072,128]{1,0:T(8,128)(2,1)}, u32[]{:S(2)}, u32[]{:S(2)}) %collective-permute-start.21) | collective-permute-done | bytes 786464 | tf_op jit(solution)/shard_map/ppermute | solution.py:819
  254.6 17.8 %experts_forward_a.1 = (f32[1024,1024]{1,0:T(8,128)}, bf16[4,1024,1024]{2,1,0:T(8,128)(2,1)}, bf16[4,1024,512]{2,1,0:T(8,128)(2,1)}, f32[1024,128]{1,0:T(8,128)}, bf16[1024,1024]{1,0:T(8,128)(2,1)}) custom-call(s32[1]{0:T(128)} %bitcast.17.half_ref, bf16[128,1024]{1,0:T(8,128)(2,1)} %copy-done.9, bf16[128,1024]{1,0:T(8,128)(2,1)} %collective-permute-done.4.refs_1_, ...), custom_call_target="tpu_custom_call" | custom-call | tf_op jit(solution)/shard_map/experts_forward_a/pallas_call | solution.py:627
  272.4 16.8 %experts_forward_b.1 = (f32[512,1024]{1,0:T(8,128)}, bf16[256,1024]{1,0:T(8,128)(2,1)}, bf16[256,1024]{1,0:T(8,128)(2,1)}, bf16[4,1024,1024]{2,1,0:T(8,128)(2,1)}, bf16[4,1024,512]{2,1,0:T(8,128)(2,1)}) custom-call(s32[1]{0:T(128)} %bitcast.17.half_ref, ...), custom_call_target="tpu_custom_call", output_to_operand_aliasing={{3}: (12, {}), {4}: (13, {})} | custom-call | tf_op jit(solution)/shard_map/experts_forward_b/pallas_call | solution.py:647
  293.9 10.5 %collective-permute-done.23 = bf16[256,1024]{1,0:T(8,128)(2,1)S(1)} collective-permute-done((bf16[256,1024]{1,0:T(8,128)(2,1)}, bf16[256,1024]{1,0:T(8,128)(2,1)S(1)}, u32[]{:S(2)}, u32[]{:S(2)}) %collective-permute-start.23) | collective-permute-done | bytes 524320 | tf_op jit(solution)/shard_map/ppermute | solution.py:815
  305.6 6.8 %collective-permute-start.27 = (bf16[128,1024]{1,0:T(8,128)(2,1)S(1)}, bf16[128,1024]{1,0:T(8,128)(2,1)S(1)}, u32[]{:S(2)}, u32[]{:S(2)}) collective-permute-start(bf16[128,1024]{1,0:T(8,128)(2,1)S(1)} %fusion.50), channel_id=1, source_target_pairs={{0,8},{4,12},{8,0},{12,4},{16,24},{20,28},{24,16},{28,20},{1,9},{5... | collective-permute-start | bytes 786440 | tf_op jit(solution)/shard_map/ppermute | solution.py:815
  318.6 7.3 %collective-permute-start.25 = (bf16[128,1024]{1,0:T(8,128)(2,1)}, bf16[128,1024]{1,0:T(8,128)(2,1)S(1)}, u32[]{:S(2)}, u32[]{:S(2)}) collective-permute-start(bf16[128,1024]{1,0:T(8,128)(2,1)} %get-tuple-element.110), channel_id=1, source_target_pairs={{0,16},{4,20},{8,24},{12,28},{16,0},{20,4},{24,8},{28,12},{1,17},{... | collective-permute-start | bytes 786440 | tf_op jit(solution)/shard_map/ppermute | solution.py:815
  327.2 16.7 %collective-permute-done.25 = bf16[128,1024]{1,0:T(8,128)(2,1)S(1)} collective-permute-done((bf16[128,1024]{1,0:T(8,128)(2,1)}, bf16[128,1024]{1,0:T(8,128)(2,1)S(1)}, u32[]{:S(2)}, u32[]{:S(2)}) %collective-permute-start.25) | collective-permute-done | bytes 262176 | tf_op jit(solution)/shard_map/ppermute | solution.py:815
  354.0 5.0 collective-permute-done.31.refs_1_
  360.5 7.4 %collective-permute-done.32.refs_2_ = bf16[128,1024]{1,0:T(8,128)(2,1)S(1)} collective-permute-done((bf16[128,1024]{1,0:T(8,128)(2,1)S(1)}, bf16[128,1024]{1,0:T(8,128)(2,1)S(1)}, u32[]{:S(2)}, u32[]{:S(2)}) %collective-permute-start.32) | collective-permute-done | bytes 262176 | tf_op jit(solution)/shard_map/ppermute | solution.py:815
  377.9 31.4 %experts_backward.1 = (f32[512,1024]{1,0:T(8,128)}, bf16[256,1024]{1,0:T(8,128)(2,1)}, bf16[256,1024]{1,0:T(8,128)(2,1)}, bf16[4,1024,1024]{2,1,0:T(8,128)(2,1)}...) custom-call(s32[1]{0:T(128)} %bitcast.17.half_ref, bf16[128,1024]{1,0:T(8,128)(2,1)} %copy-done.22, ...), custom_call_target="tpu_custom_call" | custom-call | tf_op jit(solution)/shard_map/experts_backward/pallas_call | solution.py:724
  414.0 9.7 %collective-permute-done.38 = bf16[256,1024]{1,0:T(8,128)(2,1)S(1)} collective-permute-done((bf16[256,1024]{1,0:T(8,128)(2,1)}, bf16[256,1024]{1,0:T(8,128)(2,1)S(1)}, u32[]{:S(2)}, u32[]{:S(2)}) %collective-permute-start.38) | collective-permute-done | bytes 524320 | tf_op jit(solution)/shard_map/ppermute | solution.py:815
  431.6 5.9 collective-permute-start.40
  437.5 9.2 %grad_expert_in.2 = (bf16[2,4,2,512,128]{4,3,2,1,0:T(8,128)(2,1)}, bf16[2,4,2,512,128]{4,3,2,1,0:T(8,128)(2,1)}) custom-call(s32[1]{0:T(128)} %bitcast.17.half_ref, bf16[1024,1024]{1,0:T(8,128)(2,1)} %get-tuple-element.47.refs_0_.rows_ref, bf16[4,1024,1024]{2,1,0:T(8,128)(2,1)} %get-tuple-element.61.pre_ref), custom_call_target="tpu_custom_call" | custom-call | tf_op jit(solution)/shard_map/grad_expert_in/pallas_call | solution.py:797
  446.7 9.1 %grad_expert_in.3 = (bf16[2,4,2,512,128]{4,3,2,1,0:T(8,128)(2,1)}, bf16[2,4,2,512,128]{4,3,2,1,0:T(8,128)(2,1)}) custom-call(s32[1]{0:T(128)S(6)} %sub.107.half_ref, bf16[1024,1024]{1,0:T(8,128)(2,1)} %get-tuple-element.47.refs_0_.rows_ref, bf16[4,1024,1024]{2,1,0:T(8,128)(2,1)} %get-tuple-element.61.pre_ref), custom_call_target="tpu_custom_call" | custom-call | tf_op jit(solution)/shard_map/grad_expert_in/pallas_call | solution.py:797
  455.8 8.7 %grad_expert_out.1 = (bf16[2,4,128,512]{3,2,1,0:T(8,128)(2,1)}, bf16[2,4,128,512]{3,2,1,0:T(8,128)(2,1)}, bf16[2,4,128,512]{3,2,1,0:T(8,128)(2,1)}, bf16[2,4,128,512]{3,2,1,0:T(8,128)(2,1)}) custom-call(s32[1]{0:T(128)} %bitcast.17.half_ref, bf16[4,1024,512]{2,1,0:T(8,128)(2,1)} %get-tuple-element.66.gated_ref, ...), custom_call_target="tpu_custom_call" | custom-call | tf_op jit(solution)/shard_map/grad_expert_out/pallas_call | solution.py:764
  471.9 9.7 %collective-permute-done.49 = bf16[128,1024]{1,0:T(8,128)(2,1)S(1)} collective-permute-done((bf16[128,1024]{1,0:T(8,128)(2,1)S(1)}, bf16[128,1024]{1,0:T(8,128)(2,1)S(1)}, u32[]{:S(2)}, u32[]{:S(2)}) %collective-permute-start.49) | collective-permute-done | bytes 262176 | tf_op jit(solution)/shard_map/ppermute | solution.py:819
  516.8 6.9 %collective-permute-done.47 = f32[34,1024]{1,0:T(8,128)S(1)} collective-permute-done((f32[34,1024]{1,0:T(8,128)S(1)}, f32[34,1024]{1,0:T(8,128)S(1)}, u32[]{:S(2)}, u32[]{:S(2)}) %collective-permute-start.47) | collective-permute-done | bytes 139296 | tf_op jit(solution)/shard_map/ppermute | solution.py:815
  594.0 20.4 %collective-permute-done.57 = f32[1,1024]{1,0:T(1,128)S(1)} collective-permute-done((f32[1,1024]{1,0:T(1,128)S(1)}, f32[1,1024]{1,0:T(1,128)S(1)}, u32[]{:S(2)}, u32[]{:S(2)}) %collective-permute-start.57) | collective-permute-done | bytes 4128 | tf_op jit(solution)/shard_map/ppermute | solution.py:819
  628.4 41.0 %collective-permute-done.60 = f32[1,1024]{1,0:T(1,128)S(1)} collective-permute-done((f32[1,1024]{1,0:T(1,128)S(1)}, f32[1,1024]{1,0:T(1,128)S(1)}, u32[]{:S(2)}, u32[]{:S(2)}) %collective-permute-start.60) | collective-permute-done | bytes 4128 | tf_op jit(solution)/shard_map/ppermute | solution.py:815
  (515 shorter events, 242.9 us)
Async XLA Ops:
  17.9 105.0 %collective-permute-start.1 = (bf16[128,1024]{1,0:T(8,128)(2,1)S(1)}, bf16[128,1024]{1,0:T(8,128)(2,1)S(1)}, u32[]{:S(2)}, u32[]{:S(2)}) collective-permute-start(bf16[128,1024]{1,0:T(8,128)(2,1)S(1)} %fusion.62), channel_id=1, source_target_pairs={{0,2},{1,3},{2,0},{3,1},{4,6},{5,7},{6,4},{7,5},{8,10},{9,11},{10,... | collective-permute-start | bytes 786440 | tf_op jit(solution)/shard_map/ppermute | solution.py:819
  117.7 119.7 %collective-permute-start.14 = (bf16[6144,128]{1,0:T(8,128)(2,1)}, bf16[6144,128]{1,0:T(8,128)(2,1)S(1)}, u32[]{:S(2)}, u32[]{:S(2)}) collective-permute-start(bf16[6144,128]{1,0:T(8,128)(2,1)} %get-tuple-element.45.refs_10_.refs_3_.refs_11_), channel_id=1, source_target_pairs={{0,1},{1,0},{2,3},{3,2},{4,5},{5,4},{6,7},{7,6},{8,9},{9,8},{10,11... | collective-permute-start | bytes 4718600 | tf_op jit(solution)/shard_map/ppermute | solution.py:823
  117.8 106.9 %collective-permute-start.15 = (bf16[6144,128]{1,0:T(8,128)(2,1)}, bf16[6144,128]{1,0:T(8,128)(2,1)}, u32[]{:S(2)}, u32[]{:S(2)}) collective-permute-start(bf16[6144,128]{1,0:T(8,128)(2,1)} %get-tuple-element.45.refs_10_.refs_3_.refs_11_), channel_id=1, source_target_pairs={{0,2},{1,3},{2,0},{3,1},{4,6},{5,7},{6,4},{7,5},{8,10},{9,11},{10,... | collective-permute-start | bytes 4718600 | tf_op jit(solution)/shard_map/ppermute | solution.py:819
  118.0 55.4 %collective-permute-start.2 = (bf16[3072,128]{1,0:T(8,128)(2,1)}, bf16[3072,128]{1,0:T(8,128)(2,1)}, u32[]{:S(2)}, u32[]{:S(2)}) collective-permute-start(bf16[3072,128]{1,0:T(8,128)(2,1)} %get-tuple-element.42), channel_id=1, source_target_pairs={{0,16},{4,20},{8,24},{12,28},{16,0},{20,4},{24,8},{28,12},{1,17},{... | collective-permute-start | bytes 2359304 | tf_op jit(solution)/shard_map/ppermute | solution.py:815
  120.9 68.7 %collective-permute-start.3 = (bf16[3072,128]{1,0:T(8,128)(2,1)}, bf16[3072,128]{1,0:T(8,128)(2,1)}, u32[]{:S(2)}, u32[]{:S(2)}) collective-permute-start(bf16[3072,128]{1,0:T(8,128)(2,1)} %get-tuple-element.43), channel_id=1, source_target_pairs={{0,16},{4,20},{8,24},{12,28},{16,0},{20,4},{24,8},{28,12},{1,17},{... | collective-permute-start | bytes 2359304 | tf_op jit(solution)/shard_map/ppermute | solution.py:815
  122.9 70.8 %collective-permute-start.11 = (s32[1,16,128]{2,1,0:T(8,128)S(1)}, s32[1,16,128]{2,1,0:T(8,128)S(1)}, u32[]{:S(2)}, u32[]{:S(2)}) collective-permute-start(s32[1,16,128]{2,1,0:T(8,128)S(1)} %pad_bitcast_fusion), channel_id=1, source_target_pairs={{0,4},{4,0},{8,12},{12,8},{16,20},{20,16},{24,28},{28,24},{1,5},{5... | collective-permute-start | bytes 24584 | tf_op jit(solution)/shard_map/ppermute | solution.py:815
  219.9 31.6 %collective-permute-start.21 = (bf16[3072,128]{1,0:T(8,128)(2,1)}, bf16[3072,128]{1,0:T(8,128)(2,1)}, u32[]{:S(2)}, u32[]{:S(2)}) collective-permute-start(bf16[3072,128]{1,0:T(8,128)(2,1)} %collective-permute-done.3.refs_7_.refs_19_), channel_id=1, source_target_pairs={{0,2},{1,3},{2,0},{3,1},{4,6},{5,7},{6,4},{7,5},{8,10},{9,11},{10,... | collective-permute-start | bytes 2359304 | tf_op jit(solution)/shard_map/ppermute | solution.py:819
  224.7 29.9 %collective-permute-start.16 = (bf16[6144,128]{1,0:T(8,128)(2,1)}, bf16[6144,128]{1,0:T(8,128)(2,1)}, u32[]{:S(2)}, u32[]{:S(2)}) collective-permute-start(bf16[6144,128]{1,0:T(8,128)(2,1)} %collective-permute-done.15.refs_12_.refs_5_.refs_13_), channel_id=1, source_target_pairs={{0,1},{1,0},{2,3},{3,2},{4,5},{5,4},{6,7},{7,6},{8,9},{9,8},{10,11... | collective-permute-start | bytes 4718600 | tf_op jit(solution)/shard_map/ppermute | solution.py:823
  237.4 35.0 %collective-permute-start.20 = (bf16[3072,128]{1,0:T(8,128)(2,1)}, bf16[3072,128]{1,0:T(8,128)(2,1)}, u32[]{:S(2)}, u32[]{:S(2)}) collective-permute-start(bf16[3072,128]{1,0:T(8,128)(2,1)} %collective-permute-done.3.refs_7_.refs_19_), channel_id=1, source_target_pairs={{0,1},{1,0},{2,3},{3,2},{4,5},{5,4},{6,7},{7,6},{8,9},{9,8},{10,11... | collective-permute-start | bytes 2359304 | tf_op jit(solution)/shard_map/ppermute | solution.py:823
  318.6 25.4 %collective-permute-start.25 = (bf16[128,1024]{1,0:T(8,128)(2,1)}, bf16[128,1024]{1,0:T(8,128)(2,1)S(1)}, u32[]{:S(2)}, u32[]{:S(2)}) collective-permute-start(bf16[128,1024]{1,0:T(8,128)(2,1)} %get-tuple-element.110), channel_id=1, source_target_pairs={{0,16},{4,20},{8,24},{12,28},{16,0},{20,4},{24,8},{28,12},{1,17},{... | collective-permute-start | bytes 786440 | tf_op jit(solution)/shard_map/ppermute | solution.py:815
  424.5 40.6 %collective-permute-start.42 = (bf16[128,1024]{1,0:T(8,128)(2,1)}, bf16[128,1024]{1,0:T(8,128)(2,1)S(1)}, u32[]{:S(2)}, u32[]{:S(2)}) collective-permute-start(bf16[128,1024]{1,0:T(8,128)(2,1)} %fusion.45), channel_id=1, source_target_pairs={{0,8},{4,12},{8,0},{12,4},{16,24},{20,28},{24,16},{28,20},{1,9},{5... | collective-permute-start | bytes 786440 | tf_op jit(solution)/shard_map/ppermute | solution.py:815
  430.3 34.8 %collective-permute-start.41 = (bf16[128,1024]{1,0:T(8,128)(2,1)}, bf16[128,1024]{1,0:T(8,128)(2,1)}, u32[]{:S(2)}, u32[]{:S(2)}) collective-permute-start(bf16[128,1024]{1,0:T(8,128)(2,1)} %get-tuple-element.109), channel_id=1, source_target_pairs={{0,24},{4,28},{8,16},{12,20},{16,8},{20,12},{24,0},{28,4},{1,25},{... | collective-permute-start | bytes 786440 | tf_op jit(solution)/shard_map/ppermute | solution.py:815
  431.6 33.6 %collective-permute-start.40 = (bf16[128,1024]{1,0:T(8,128)(2,1)}, bf16[128,1024]{1,0:T(8,128)(2,1)}, u32[]{:S(2)}, u32[]{:S(2)}) collective-permute-start(bf16[128,1024]{1,0:T(8,128)(2,1)} %get-tuple-element.108), channel_id=1, source_target_pairs={{0,16},{4,20},{8,24},{12,28},{16,0},{20,4},{24,8},{28,12},{1,17},{... | collective-permute-start | bytes 786440 | tf_op jit(solution)/shard_map/ppermute | solution.py:815
  487.2 98.3 %collective-permute-start.87 = (bf16[2,4,2,512,128]{4,3,2,1,0:T(8,128)(2,1)}, bf16[2,4,2,512,128]{4,3,2,1,0:T(8,128)(2,1)}, u32[]{:S(2)}, u32[]{:S(2)}) collective-permute-start(bf16[2,4,2,512,128]{4,3,2,1,0:T(8,128)(2,1)} %get-tuple-element.65), channel_id=1, source_target_pairs={{0,1},{1,0},{2,3},{3,2},{4,5},{5,4},{6,7},{7,6},{8,9},{9,8},{10,11... | collective-permute-start | bytes 6291464 | tf_op jit(solution)/shard_map/ppermute | solution.py:823
  488.9 42.1 %collective-permute-start.91 = (bf16[4,128,512]{2,1,0:T(8,128)(2,1)}, bf16[4,128,512]{2,1,0:T(8,128)(2,1)}, u32[]{:S(2)}, u32[]{:S(2)}) collective-permute-start(bf16[4,128,512]{2,1,0:T(8,128)(2,1)} %fusion.41), channel_id=1, source_target_pairs={{0,2},{1,3},{2,0},{3,1},{4,6},{5,7},{6,4},{7,5},{8,10},{9,11},{10,... | collective-permute-start | bytes 1572872 | tf_op jit(solution)/shard_map/ppermute | solution.py:819
  578.7 35.7 %collective-permute-start.85 = (bf16[2,4,2,512,128]{4,3,2,1,0:T(8,128)(2,1)S(1)}, bf16[2,4,2,512,128]{4,3,2,1,0:T(8,128)(2,1)S(1)}, u32[]{:S(2)}, u32[]{:S(2)}) collective-permute-start(bf16[2,4,2,512,128]{4,3,2,1,0:T(8,128)(2,1)S(1)} %copy-done.86), channel_id=1, source_target_pairs={{0,1},{1,0},{2,3},{3,2},{4,5},{5,4},{6,7},{7,6},{8,9},{9,8},{10,11... | collective-permute-start | bytes 6291464 | tf_op jit(solution)/shard_map/ppermute | solution.py:823
  578.9 42.5 %collective-permute-start.94 = (bf16[4,128,512]{2,1,0:T(8,128)(2,1)S(1)}, bf16[4,128,512]{2,1,0:T(8,128)(2,1)S(1)}, u32[]{:S(2)}, u32[]{:S(2)}) collective-permute-start(bf16[4,128,512]{2,1,0:T(8,128)(2,1)S(1)} %fusion.25), channel_id=1, source_target_pairs={{0,16},{4,20},{8,24},{12,28},{16,0},{20,4},{24,8},{28,12},{1,17},{... | collective-permute-start | bytes 1572872 | tf_op jit(solution)/shard_map/ppermute | solution.py:815
  588.3 31.4 %collective-permute-start.88 = (bf16[4,2,512,128]{3,2,1,0:T(8,128)(2,1)S(1)}, bf16[4,2,512,128]{3,2,1,0:T(8,128)(2,1)S(1)}, u32[]{:S(2)}, u32[]{:S(2)}) collective-permute-start(bf16[4,2,512,128]{3,2,1,0:T(8,128)(2,1)S(1)} %fusion.17), channel_id=1, source_target_pairs={{0,2},{1,3},{2,0},{3,1},{4,6},{5,7},{6,4},{7,5},{8,10},{9,11},{10,... | collective-permute-start | bytes 3145736 | tf_op jit(solution)/shard_map/ppermute | solution.py:819
  592.7 34.0 %collective-permute-start.54 = (bf16[128,1024]{1,0:T(8,128)(2,1)S(1)}, bf16[128,1024]{1,0:T(8,128)(2,1)S(1)}, u32[]{:S(2)}, u32[]{:S(2)}) collective-permute-start(bf16[128,1024]{1,0:T(8,128)(2,1)S(1)} %fusion.37), channel_id=1, source_target_pairs={{0,2},{1,3},{2,0},{3,1},{4,6},{5,7},{6,4},{7,5},{8,10},{9,11},{10,... | collective-permute-start | bytes 786440 | tf_op jit(solution)/shard_map/ppermute | solution.py:819
  614.4 55.6 %collective-permute-start.53 = (bf16[128,1024]{1,0:T(8,128)(2,1)S(1)}, bf16[128,1024]{1,0:T(8,128)(2,1)S(1)}, u32[]{:S(2)}, u32[]{:S(2)}) collective-permute-start(bf16[128,1024]{1,0:T(8,128)(2,1)S(1)} %fusion.37), channel_id=1, source_target_pairs={{0,1},{1,0},{2,3},{3,2},{4,5},{5,4},{6,7},{7,6},{8,9},{9,8},{10,11... | collective-permute-start | bytes 786440 | tf_op jit(solution)/shard_map/ppermute | solution.py:823
  618.1 53.9 %collective-permute-start.86 = (bf16[4,2,512,128]{3,2,1,0:T(8,128)(2,1)S(1)}, bf16[4,2,512,128]{3,2,1,0:T(8,128)(2,1)S(1)}, u32[]{:S(2)}, u32[]{:S(2)}) collective-permute-start(bf16[4,2,512,128]{3,2,1,0:T(8,128)(2,1)S(1)} %fusion.16), channel_id=1, source_target_pairs={{0,2},{1,3},{2,0},{3,1},{4,6},{5,7},{6,4},{7,5},{8,10},{9,11},{10,... | collective-permute-start | bytes 3145736 | tf_op jit(solution)/shard_map/ppermute | solution.py:819
  621.4 51.0 %collective-permute-start.89 = (bf16[4,2,512,128]{3,2,1,0:T(8,128)(2,1)S(1)}, bf16[4,2,512,128]{3,2,1,0:T(8,128)(2,1)S(1)}, u32[]{:S(2)}, u32[]{:S(2)}) collective-permute-start(bf16[4,2,512,128]{3,2,1,0:T(8,128)(2,1)S(1)} %fusion.8), channel_id=1, source_target_pairs={{0,16},{4,20},{8,24},{12,28},{16,0},{20,4},{24,8},{28,12},{1,17},{... | collective-permute-start | bytes 3145736 | tf_op jit(solution)/shard_map/ppermute | solution.py:815
  625.6 43.9 %collective-permute-start.60 = (f32[1,1024]{1,0:T(1,128)S(1)}, f32[1,1024]{1,0:T(1,128)S(1)}, u32[]{:S(2)}, u32[]{:S(2)}) collective-permute-start(f32[1,1024]{1,0:T(1,128)S(1)} %add.370), channel_id=1, source_target_pairs={{0,16},{4,20},{8,24},{12,28},{16,0},{20,4},{24,8},{28,12},{1,17},{... | collective-permute-start | bytes 12296 | tf_op jit(solution)/shard_map/ppermute | solution.py:815
  626.7 43.5 %collective-permute-start.55 = (bf16[128,1024]{1,0:T(8,128)(2,1)S(1)}, bf16[128,1024]{1,0:T(8,128)(2,1)S(1)}, u32[]{:S(2)}, u32[]{:S(2)}) collective-permute-start(bf16[128,1024]{1,0:T(8,128)(2,1)S(1)} %collective-permute-done.54), channel_id=1, source_target_pairs={{0,1},{1,0},{2,3},{3,2},{4,5},{5,4},{6,7},{7,6},{8,9},{9,8},{10,11... | collective-permute-start | bytes 786440 | tf_op jit(solution)/shard_map/ppermute | solution.py:823
  (165 other events, 2235.3 us)

commit v3 on v2

--- a/solution.py
+++ b/solution.py
@@ -365,48 +365,54 @@
     return pl.BlockSpec(memory_space=pl.ANY)
 
 
-def pack_body(half_ref, in_ref, out_ref, own, near, far, sems):
-    held = in_ref.shape[0] // 2
-    copies = []
-    for target, start, first, count in (
-        (own, half_ref[0] * held, 0, held),
-        (near, (1 - half_ref[0]) * held, 0, held // 2),
-        (far, (1 - half_ref[0]) * held, held // 2, held // 2),
-    ):
-        for e in range(count):
-            source = start + first + e
-            for c in range(2):
-                copies.append(
-                    (in_ref.at[source, c], target.at[pl.ds(e * PACK + c * 4 * SHARE, 4 * SHARE)])
-                )
-            for k in range(4):
-                copies.append(
-                    (
-                        out_ref.at[source, :, pl.ds(k * SHARE, SHARE)],
-                        target.at[pl.ds(e * PACK + (8 + k) * SHARE, SHARE)],
-                    )
-                )
-    copies = [
-        pltpu.make_async_copy(source, target, sems.at[n])
-        for n, (source, target) in enumerate(copies)
-    ]
-    for copy in copies:
-        copy.start()
-    for copy in copies:
-        copy.wait()
+def pack_body(half_ref, own_in, own_out, other_in, other_out, own, near, far):
+    step = pl.program_id(0)
+
+    def fill(target, source_in, source_out):
+        for c in range(2):
+            target[c * 4 * SHARE : (c + 1) * 4 * SHARE, :] = source_in[0, c]
+        for k in range(4):
+            target[(8 + k) * SHARE : (9 + k) * SHARE, :] = source_out[
+                0, :, k * SHARE : (k + 1) * SHARE
+            ]
+
+    fill(own, own_in, own_out)
+
+    @pl.when(step < 2)
+    def _():
+        fill(near, other_in, other_out)
+
+    @pl.when(step >= 2)
+    def _():
+        fill(far, other_in, other_out)
 
 
 def pack_weights(half_index, expert_in, expert_out):
     held = expert_in.shape[0] // 2
+    in_shape = (1,) + expert_in.shape[1:]
+    out_shape = (1,) + expert_out.shape[1:]
     shapes = [(held * PACK, SHARE), (held // 2 * PACK, SHARE), (held // 2 * PACK, SHARE)]
+    block = (PACK, SHARE)
     return pl.pallas_call(
         pack_body,
-        in_specs=[pl.BlockSpec(memory_space=pltpu.SMEM), any_block(), any_block()],
-        out_specs=[any_block()] * 3,
+        grid_spec=pltpu.PrefetchScalarGridSpec(
+            num_scalar_prefetch=1,
+            grid=(held,),
+            in_specs=[
+                pl.BlockSpec(in_shape, lambda e, half: (half[0] * held + e, 0, 0, 0)),
+                pl.BlockSpec(out_shape, lambda e, half: (half[0] * held + e, 0, 0)),
+                pl.BlockSpec(in_shape, lambda e, half: ((1 - half[0]) * held + e, 0, 0, 0)),
+                pl.BlockSpec(out_shape, lambda e, half: ((1 - half[0]) * held + e, 0, 0)),
+            ],
+            out_specs=[
+                pl.BlockSpec(block, lambda e, half: (e, 0)),
+                pl.BlockSpec(block, lambda e, half: (jnp.minimum(e, 1), 0)),
+                pl.BlockSpec(block, lambda e, half: (jnp.maximum(e - 2, 0), 0)),
+            ],
+        ),
         out_shape=[jax.ShapeDtypeStruct(shape, BF16) for shape in shapes],
-        scratch_shapes=[pltpu.SemaphoreType.DMA((12 * held,))],
         name="pack_weights",
-    )(half_index, expert_in, expert_out)
+    )(half_index, expert_in, expert_out, expert_in, expert_out)
 
 
 def weight_copies(own, other, own_row, other_row, half, in_buf, out_buf, sems, slot):
@@ -664,8 +670,8 @@
     shards = refs[:8]
     gate_ref, router_ref, pre_ref = refs[8:11]
     packs = refs[11:23]
-    keep_ref, near_ref, far_ref, pre_grad_ref, logit_ref, grad_ref = refs[23:29]
-    acc, in_buf, out_buf, sems = refs[29:]
+    keep_ref, near_ref, far_ref, pre_grad_ref, logit_ref, grad_ref = refs[-10:-4]
+    acc, in_buf, out_buf, sems = refs[-4:]
     step, slot, wait = stream_weights(0, packs, half_ref[0], in_buf, out_buf, sems)
     row_count, width = grad_ref.shape
     size = row_count // 8
@@ -717,7 +723,7 @@
         spread(acc, keep_ref, near_ref, far_ref)
 
 
-def experts_backward(half_index, shards, gates, router, pre, own, near, far):
+def experts_backward(half_index, shards, gates, router, pre, own, near, far, *after):
     row_count, width = (8 * shards[0].shape[0], shards[0].shape[1])
     local = pre.shape[0]
     specs, shapes = spread_specs(row_count, width)
@@ -728,7 +734,7 @@
             grid=(local,),
             in_specs=[whole_block(v.shape) for v in (*shards, gates, router)]
             + [expert_block(pre.shape)]
-            + [any_block()] * 12,
+            + [any_block()] * (12 + len(after)),
             out_specs=specs
             + [
                 expert_block(pre.shape),
@@ -745,10 +751,15 @@
             jax.ShapeDtypeStruct((row_count, width), BF16),
         ],
         name="experts_backward",
-    )(half_index, *shards, gates, router, pre, *own, *near, *far)
-
-
-def grad_out_body(half_ref, gated_ref, other_ref, mine_ref, *outs):
+    )(half_index, *shards, gates, router, pre, *own, *near, *far, *after)
+
+
+def cost(flops):
+    return pl.CostEstimate(flops=flops, bytes_accessed=1 << 22, transcendentals=0)
+
+
+def grad_out_body(half_ref, gated_ref, other_ref, mine_ref, *refs):
+    outs = refs[-4:]
     turned = gated_ref[0].T
     for n, source in ((0, other_ref), (2, mine_ref)):
         product = jnp.dot(turned, source[...], preferred_element_type=F32).astype(BF16)
@@ -756,7 +767,7 @@
             outs[n + q % 2][q // 2, 0] = product[q * SHARE : (q + 1) * SHARE, :]
 
 
-def grad_expert_outs(half_index, gated, grads):
+def grad_expert_outs(half_index, gated, grads, *after):
     local, row_count, hidden = gated.shape
     width = grads.shape[1]
     half_spec = (row_count, width // 2)
@@ -770,15 +781,19 @@
                 expert_block(gated.shape),
                 pl.BlockSpec(half_spec, lambda e, half: (0, 1 - half[0])),
                 pl.BlockSpec(half_spec, lambda e, half: (0, half[0])),
-            ],
+            ]
+            + [any_block()] * len(after),
             out_specs=[pl.BlockSpec((2, 1) + shape[2:], lambda e, *_: (0, e, 0, 0))] * 4,
         ),
         out_shape=[jax.ShapeDtypeStruct(shape, BF16)] * 4,
+        cost_estimate=cost(2 * local * row_count * hidden * width),
         name="grad_expert_out",
-    )(half_index, gated, grads, grads)
-
-
-def grad_in_body(half_ref, rows_ref, pre_ref, keep_ref, send_ref, turned):
+    )(half_index, gated, grads, grads, *after)
+
+
+def grad_in_body(half_ref, rows_ref, pre_ref, *refs):
+    keep_ref, send_ref, turned = refs[-3:]
+
     @pl.when(pl.program_id(0) == 0)
     def _():
         turned[...] = rows_ref[...].T
@@ -790,7 +805,7 @@
             (keep_ref, send_ref)[q % 2][q // 2, 0, c] = product[:, start : start + SHARE]
 
 
-def grad_expert_ins(half_index, rows, pre_grad):
+def grad_expert_ins(half_index, rows, pre_grad, *after):
     local, row_count, wide = pre_grad.shape
     width = rows.shape[1]
     shape = (2, local, 2, width // 2, SHARE)
@@ -802,13 +817,95 @@
             in_specs=[
                 pl.BlockSpec((row_count, width // 2), lambda e, half: (0, half[0])),
                 expert_block(pre_grad.shape),
-            ],
+            ]
+            + [any_block()] * len(after),
             out_specs=[pl.BlockSpec((2, 1) + shape[2:], lambda e, *_: (0, e, 0, 0, 0))] * 2,
             scratch_shapes=[pltpu.VMEM((width // 2, row_count), BF16)],
         ),
         out_shape=[jax.ShapeDtypeStruct(shape, BF16)] * 2,
+        cost_estimate=cost(local * row_count * wide * width),
         name="grad_expert_in",
-    )(half_index, rows, pre_grad)
+    )(half_index, rows, pre_grad, *after)
+
+
+def fold_body(keep_ref, got_ref, *refs):
+    near_ref, far_ref = refs[-2:]
+    near_ref[...] = keep_ref[0].astype(F32) + got_ref[0].astype(F32)
+    far_ref[...] = (keep_ref[1].astype(F32) + got_ref[1].astype(F32)).astype(BF16)
+
+
+def fold_pairs(keep, got, *after):
+    shape = keep.shape
+    rest = (0,) * (len(shape) - 2)
+    pair = pl.BlockSpec((2, 1) + shape[2:], lambda e: (0, e) + rest)
+    single = pl.BlockSpec((1,) + shape[2:], lambda e: (e,) + rest)
+    return pl.pallas_call(
+        fold_body,
+        grid=(shape[1],),
+        in_specs=[pair, pair] + [any_block()] * len(after),
+        out_specs=[single, single],
+        out_shape=[
+            jax.ShapeDtypeStruct(shape[1:], F32),
+            jax.ShapeDtypeStruct(shape[1:], BF16),
+        ],
+        cost_estimate=cost(1 << 20),
+        name="fold_pairs",
+    )(keep, got, *after)
+
+
+def finish_body(keep, near, two, four, six, extra, unit, scale, gain, grad_out, *refs):
+    hidden_ref, attn_ref, gain_ref = refs[-3:]
+    total = keep[...] + near[...].astype(F32) + extra[...]
+    for part in (two, four, six):
+        total = total + part[...].astype(F32)
+    gain_ref[...] = jnp.sum((total * unit[...]).reshape(-1, 8, total.shape[1]), 0)
+    weighted = total * gain[...]
+    mean = jnp.mean(weighted * unit[...], -1, keepdims=True)
+    hidden = grad_out[...] + scale[...] * (weighted - unit[...] * mean)
+    hidden_ref[...] = hidden
+    attn_ref[...] = (RESIDUAL * hidden).astype(BF16)
+
+
+def finish_rows(keep, near, two, four, six, extra, unit, scale, gain, grad_out, *after):
+    size, width = unit.shape
+    block = pl.BlockSpec((size, width), lambda e: (0, 0))
+    return pl.pallas_call(
+        finish_body,
+        grid=(1,),
+        in_specs=[block] * 7
+        + [whole_block((size, 1)), whole_block((1, width)), block]
+        + [any_block()] * len(after),
+        out_specs=[block, block, whole_block((8, width))],
+        out_shape=[
+            jax.ShapeDtypeStruct((size, width), F32),
+            jax.ShapeDtypeStruct((size, width), BF16),
+            jax.ShapeDtypeStruct((8, width), F32),
+        ],
+        cost_estimate=cost(1 << 20),
+        name="finish_rows",
+    )(keep, near, two, four, six, extra, unit, scale, gain, grad_out, *after)
+
+
+def join_body(first, second, third, *refs):
+    target = refs[-1]
+    start = 0
+    for part in (first, second, third):
+        target[:, start : start + part.shape[1]] = part[...]
+        start += part.shape[1]
+
+
+def join_columns(first, second, third, *after):
+    parts = (first, second, third)
+    shape = (first.shape[0], sum(part.shape[1] for part in parts))
+    return pl.pallas_call(
+        join_body,
+        grid=(1,),
+        in_specs=[whole_block(part.shape) for part in parts] + [any_block()] * len(after),
+        out_specs=whole_block(shape),
+        out_shape=jax.ShapeDtypeStruct(shape, BF16),
+        cost_estimate=cost(1 << 20),
+        name="join_columns",
+    )(*parts, *after)
 
 
 def trade(value, bits):
@@ -865,17 +962,8 @@
     return ordered(row, pair, other)
 
 
-def sum_all(value):
-    value = value + swap_core(value)
-    value = value + swap_y(value)
-    for bits in (1, 2, 4):
-        value = value + trade(value, bits)
-    return value
-
-
-def sum_experts(value, place):
-    size = value.shape[0] // 8
-    shards = value.reshape(8, size, value.shape[1])
+def sum_experts(shards, place):
+    size, width = shards.shape[1:]
 
     def pick(*order):
         picked = [
@@ -889,10 +977,10 @@
     column, inner, outer = (bit > 0 for bit in lower)
     halves = jnp.stack([gathered[:4], gathered[4:]])
     halves = jnp.where(column, halves[::-1], halves)
-    halves = halves.reshape(2, 2, 2, size, value.shape[1])
+    halves = halves.reshape(2, 2, 2, size, width)
     halves = jnp.where(inner, halves[:, :, ::-1], halves)
     halves = jnp.where(outer, halves[:, ::-1], halves)
-    return halves.transpose(1, 2, 0, 3, 4).reshape(value.shape).astype(F32)
+    return halves.transpose(1, 2, 0, 3, 4).reshape(shards.shape).astype(F32)
 
 
 def per_device(
@@ -1016,11 +1104,12 @@
     scale_two = lax.rsqrt(jnp.mean(hidden * hidden, -1, keepdims=True) + EPS)
     unit_two = hidden * scale_two
     normed_two = (unit_two * second_gain).astype(BF16)
+    row_shards = gather_experts(normed_two)
     near_pack, far_pack, normed_two = lax.optimization_barrier((near_pack, far_pack, normed_two))
     near, far = (spread_shares(near_pack), spread_shares(far_pack))
     keep, send_near, send_far, pre, gated, gates, expert_rows = experts_forward(
         half_arg,
-        gather_experts(normed_two),
+        row_shards,
         route_rel,
         router_rel,
         own,
@@ -1045,24 +1134,47 @@
     layer_output = gather_tensor(output.astype(BF16), core, row)
 
     keep, send_near, send_far, pre_grad, logit_grad, grad_rows = experts_backward(
-        half_arg, gather_experts(grad_moe), gates, router_rel, pre, own, near, far
-    )
-    grad_two = scatter_experts(keep, send_near, send_far) + mean_rows
-
-    out_keep, out_send, own_out_keep, own_out_send = grad_expert_outs(half_arg, gated, grad_rows)
+        half_arg,
+        gather_experts(grad_moe),
+        gates,
+        router_rel,
+        pre,
+        own,
+        near,
+        far,
+        layer_output,
+        mean_rows,
+    )
+    got_far = trade(send_far, 1)
+    got_near = trade(send_near, 1)
     in_keep, in_send = grad_expert_ins(1 - half_arg, expert_rows, pre_grad)
-    own_in_keep, own_in_send = grad_expert_ins(half_arg, expert_rows, pre_grad)
-
-    def home(kept, sent):
-        received = swap_core(sent)
-        near = kept[0].astype(F32) + received[0].astype(F32)
-        far = kept[1].astype(F32) + received[1].astype(F32)
-        return near + swap_y(far.astype(BF16)).astype(F32)
-
-    back_out = trade(home(out_keep, out_send).astype(BF16), 4).astype(F32)
-    back_in = trade(home(in_keep, in_send).astype(BF16), 4).astype(F32)
-    grad_expert_out = ordered(half_index, home(own_out_keep, own_out_send), back_out)
-    grad_expert_in = ordered(half_index, home(own_in_keep, own_in_send), back_in)
+    far_rows = (keep[2 * quarter :] + got_far.astype(F32)).astype(BF16)
+    back_four = trade(far_rows[:quarter], 4)
+    back_six = trade(far_rows[quarter:], 6)
+    in_near, in_far = fold_pairs(in_keep, swap_core(in_send), far_rows)
+    in_across = swap_y(in_far)
+    out_keep, out_send, own_out_keep, own_out_send = grad_expert_outs(
+        half_arg, gated, grad_rows, in_far
+    )
+    near_rows = (keep[quarter : 2 * quarter] + got_near[quarter:].astype(F32)).astype(BF16)
+    back_two = trade(near_rows, 2)
+    own_in_keep, own_in_send = grad_expert_ins(half_arg, expert_rows, pre_grad, near_rows, out_send)
+    in_back = trade((in_near + in_across.astype(F32)).astype(BF16), 4)
+    grad_hidden, grad_attn, grad_second_part = finish_rows(
+        keep,
+        got_near,
+        back_two,
+        back_four,
+        back_six,
+        mean_rows,
+        unit_two,
+        scale_two,
+        second_gain[None],
+        grad_out,
+        own_in_send,
+        in_across,
+    )
+    grad_second_part = jnp.sum(grad_second_part, 0)
 
     router_part = jnp.einsum(
         "te,td->ed", logit_grad.astype(BF16), expert_rows, preferred_element_type=F32
@@ -1077,11 +1189,6 @@
     mean_router = jnp.einsum("te,td->ed", mean_part, normed_two, preferred_element_type=F32)
     router_part = router_part + mean_router[:expert_count] + mean_router[expert_count:]
 
-    grad_second_part = jnp.sum(grad_two * unit_two, 0)
-    grad_unit_two = grad_two * second_gain
-    grad_hidden = grad_out + scale_two * (
-        grad_unit_two - unit_two * jnp.mean(grad_unit_two * unit_two, -1, keepdims=True)
-    )
     small = jnp.concatenate(
         [
             router_part,
@@ -1090,9 +1197,13 @@
         ],
         0,
     )
-    small = sum_all(small)
-
-    grad_attn = gather_tensor((RESIDUAL * grad_hidden).astype(BF16), core, row)
+    small = small + swap_core(small)
+    small = small + swap_y(small)
+    small = jnp.pad(small, ((0, 128 - small.shape[0]), (0, 0))).reshape(8, 16, model_width)
+
+    grad_attn = gather_tensor(grad_attn, core, row)
+    out_near, out_far = fold_pairs(out_keep, swap_core(out_send), grad_attn)
+    out_across = swap_y(out_far)
     grad_output = jnp.einsum("tc,td->cd", attended, grad_attn, preferred_element_type=F32)
     grad_attended = jnp.einsum("td,cd->tc", grad_attn, output_weight, preferred_element_type=F32)
     grad_attended = grad_attended.astype(BF16).reshape(row_count, local_kv, group, HEAD_DIM)
@@ -1116,24 +1227,46 @@
     grad_keys_low = unrotate(grad_keys_rot, cosine, sine)
     grad_keys_low = grad_keys_low.reshape(row_count, local_kv * HEAD_DIM).astype(BF16)
     grad_values_low = grad_values.reshape(row_count, local_kv * HEAD_DIM).astype(BF16)
-    grad_qkv = jnp.concatenate([grad_query_low, grad_keys_low, grad_values_low], 1)
+    out_back = trade((out_near + out_across.astype(F32)).astype(BF16), 4)
+    grad_qkv = join_columns(grad_query_low, grad_keys_low, grad_values_low, out_across)
     weights_qkv = jnp.concatenate([query_weight, key_matrix, value_matrix], 1)
     grad_weights = jnp.einsum("td,tc->dc", first_normed, grad_qkv, preferred_element_type=F32)
     grad_one_part = jnp.einsum("tc,dc->td", grad_qkv, weights_qkv, preferred_element_type=F32)
+    gain_part = jnp.sum(grad_one_part * unit_one, 0).reshape(2, -1)
+    gain_part = jnp.pad(gain_part, ((0, 126), (0, 0))).reshape(8, 16, -1)
     grad_one = scatter_tensor(grad_one_part, core, row)
+    own_out_near, own_out_far = fold_pairs(own_out_keep, swap_core(own_out_send), grad_qkv)
+    own_in_near, own_in_far = fold_pairs(own_in_keep, swap_core(own_in_send), grad_one)
+    own_out_across = swap_y(own_out_far)
+    own_in_across = swap_y(own_in_far)
 
     scale_mine = lax.rsqrt(jnp.mean(tokens_mine * tokens_mine, -1, keepdims=True) + EPS)
     unit_mine = tokens_mine * scale_mine
-    grad_first_gain = sum_all(jnp.sum(grad_one * unit_mine, 0)[None])[0]
     grad_unit_one = grad_one * first_gain
     grad_tokens = grad_hidden + scale_mine * (
         grad_unit_one - unit_mine * jnp.mean(grad_unit_one * unit_mine, -1, keepdims=True)
     )
     grad_tokens = gather_tensor(grad_tokens.astype(BF16), core, row).astype(F32)
+    grad_output = jnp.concatenate([grad_output.reshape(8, -1, model_width), small], 1)
     grad_output = sum_experts(grad_output, place)
+    small = grad_output[:, -16:].reshape(128, model_width)
+    grad_output = grad_output[:, :-16].reshape(-1, model_width)
+    grad_weights = jnp.concatenate(
+        [grad_weights.reshape(8, -1, grad_weights.shape[1]), gain_part], 1
+    )
     grad_weights = sum_experts(grad_weights, place)
+    gain_part = grad_weights[0, -16:-14]
+    gain_part = gain_part + swap_core(gain_part)
+    grad_first_gain = (gain_part + swap_y(gain_part)).reshape(-1)
+    grad_weights = grad_weights[:, :-16].reshape(model_width, -1)
     query_columns = query_weight.shape[1]
     key_columns = query_columns + key_matrix.shape[1]
+    grad_expert_out = ordered(
+        half_index, own_out_near + own_out_across.astype(F32), out_back.astype(F32)
+    )
+    grad_expert_in = ordered(
+        half_index, own_in_near + own_in_across.astype(F32), in_back.astype(F32)
+    )
     return (
         layer_output,
         small[expert_count + 1, 0] / (2.0 * model_width * valid_total),

time: 684 us -> 650 us (0.950)
  Pallas kernels: 190 us -> 119 us
  waiting for transfers between devices: 274 us -> 312 us
  starting transfers between devices: 122 us -> 103 us
  local copies, waits for them, and re-layouts: 23.6 us -> 36.7 us
    pallas_call x1 -> x7, Pallas kernels: 96.8 us -> 26.4 us  [the longest x4 16.4 us: fold_pairs(): pl.pallas_call(fold_body, grid=(shape[1],), in_specs=[pair, pair] + [any_...]
    ppermute x61 -> x55, waiting for transfers between devices: 221 us -> 269 us  [trade(): return lax.ppermute(value, 'expert', [(i, i ^ bits) for i in range(8)])]
    ppermute x61 -> x55, starting transfers between devices: 99.2 us -> 82.7 us  [trade(): return lax.ppermute(value, 'expert', [(i, i ^ bits) for i in range(8)])]
    ppermute x14, waiting for transfers between devices: 50.3 us -> 42.2 us  [swap_y(): return lax.ppermute(value, 'tensor', [(i, i ^ 2) for i in range(4)])]
    unnamed x196 -> x189, local copies, waits for them, and re-layouts: 8.52 us -> 16.3 us
  transfers between devices with their start and end apart: 95 -> 89, of which waited for: 39 -> 39; matrix products, arithmetic and copies ran while one was open for 9% -> 11% of each run, Pallas kernels for 21% -> 9%
where the time goes in v3:
time: 650 us; the launch traced here: 644 us
  waiting for transfers between devices  312 us (48%)
  Pallas kernels  119 us (18%)
  starting transfers between devices  103 us (16%)
  other arithmetic  46.1 us (7%)
  local copies, waits for them, and re-layouts  36.7 us (6%)
  matrix products  21.7 us (3%)
    ppermute x55, waiting for transfers between devices, trade(): return lax.ppermute(value, 'expert', [(i, i ^ bits) for i in range(8)])  269 us
    ppermute x55, starting transfers between devices, trade(): return lax.ppermute(value, 'expert', [(i, i ^ bits) for i in range(8)])  82.7 us
    ppermute x14, waiting for transfers between devices, swap_y(): return lax.ppermute(value, 'tensor', [(i, i ^ 2) for i in range(4)])  42.2 us
    pallas_call x1, Pallas kernels, experts_backward(): pl.pallas_call(backward_body, grid_spec=pltpu.PrefetchScalarGridSpec(num_...  31.4 us
    pallas_call x2, Pallas kernels, grad_expert_ins(): pl.pallas_call(grad_in_body, grid_spec=pltpu.PrefetchScalarGridSpec(num_s...  18.6 us
    ppermute x14, starting transfers between devices, swap_y(): return lax.ppermute(value, 'tensor', [(i, i ^ 2) for i in range(4)])  17.9 us
    pallas_call x1, Pallas kernels, experts_forward(): pl.pallas_call(forward_first, grid_spec=pltpu.PrefetchScalarGridSpec(num_...  17.6 us
    pallas_call x1, Pallas kernels, experts_forward(): pl.pallas_call(forward_second, grid_spec=pltpu.PrefetchScalarGridSpec(num...  16.8 us
  transfers between devices with their start and end apart: 89, of which 39 were waited for; matrix products, arithmetic and copies ran while one was open for 11% of the time, Pallas kernels for 9%

profile of v3, /device:TPU:0, one launch (start us, length us, event | category | flops | bytes accessed | tf_op | source)
XLA Modules:
  0.0 644.3 jit_solution(8656627574206334175)
XLA Ops:
  39.5 64.1 %collective-permute-done.11 = s32[4,16,128]{2,1,0:T(8,128)S(1)} collective-permute-done((s32[4,16,128]{2,1,0:T(8,128)S(1)}, s32[4,16,128]{2,1,0:T(8,128)S(1)}, u32[]{:S(2)}, u32[]{:S(2)}) %collective-permute-start.11) | collective-permute-done | bytes 32800 | tf_op jit(solution)/shard_map/ppermute | solution.py:912
  108.5 8.2 %collective-permute-done.2.refs_1_ = bf16[128,1024]{1,0:T(8,128)(2,1)} collective-permute-done((bf16[128,1024]{1,0:T(8,128)(2,1)S(1)}, bf16[128,1024]{1,0:T(8,128)(2,1)}, u32[]{:S(2)}, u32[]{:S(2)}) %collective-permute-start.2) | collective-permute-done | bytes 262176 | tf_op jit(solution)/shard_map/ppermute | solution.py:912
  117.3 7.9 %collective-permute-done.3.refs_2_ = bf16[128,1024]{1,0:T(8,128)(2,1)} collective-permute-done((bf16[128,1024]{1,0:T(8,128)(2,1)S(1)}, bf16[128,1024]{1,0:T(8,128)(2,1)}, u32[]{:S(2)}, u32[]{:S(2)}) %collective-permute-start.3) | collective-permute-done | bytes 262176 | tf_op jit(solution)/shard_map/ppermute | solution.py:912
  135.9 6.0 collective-permute-done.7.refs_6_
  142.7 5.7 collective-permute-done.8.refs_7_
  149.6 9.8 %collective-permute-done.21.refs_9_.refs_21_ = bf16[3072,128]{1,0:T(8,128)(2,1)} collective-permute-done((bf16[3072,128]{1,0:T(8,128)(2,1)}, bf16[3072,128]{1,0:T(8,128)(2,1)}, u32[]{:S(2)}, u32[]{:S(2)}) %collective-permute-start.21) | collective-permute-done | bytes 786464 | tf_op jit(solution)/shard_map/ppermute | solution.py:916
  163.9 17.6 %experts_forward_a.1 = (f32[1024,1024]{1,0:T(8,128)}, bf16[4,1024,1024]{2,1,0:T(8,128)(2,1)}, bf16[4,1024,512]{2,1,0:T(8,128)(2,1)}, f32[1024,128]{1,0:T(8,128)}, bf16[1024,1024]{1,0:T(8,128)(2,1)}) custom-call(s32[1]{0:T(128)} %bitcast.17.half_ref, bf16[128,1024]{1,0:T(8,128)(2,1)} %copy-done.10, bf16[128,1024]{1,0:T(8,128)(2,1)} %collective-permute-done.2.refs_1_, ...), custom_call_target="tpu_custom_call" | custom-call | tf_op jit(solution)/shard_map/experts_forward_a/pallas_call | solution.py:633
  181.5 16.8 %experts_forward_b.1 = (f32[512,1024]{1,0:T(8,128)}, bf16[256,1024]{1,0:T(8,128)(2,1)}, bf16[256,1024]{1,0:T(8,128)(2,1)}, bf16[4,1024,1024]{2,1,0:T(8,128)(2,1)}, bf16[4,1024,512]{2,1,0:T(8,128)(2,1)}) custom-call(s32[1]{0:T(128)} %bitcast.17.half_ref, ...), custom_call_target="tpu_custom_call", output_to_operand_aliasing={{3}: (12, {}), {4}: (13, {})} | custom-call | tf_op jit(solution)/shard_map/experts_forward_b/pallas_call | solution.py:653
  201.3 12.1 %collective-permute-done.23 = bf16[256,1024]{1,0:T(8,128)(2,1)S(1)} collective-permute-done((bf16[256,1024]{1,0:T(8,128)(2,1)}, bf16[256,1024]{1,0:T(8,128)(2,1)S(1)}, u32[]{:S(2)}, u32[]{:S(2)}) %collective-permute-start.23) | collective-permute-done | bytes 524320 | tf_op jit(solution)/shard_map/ppermute | solution.py:912
  214.7 6.5 %collective-permute-start.27 = (bf16[128,1024]{1,0:T(8,128)(2,1)S(1)}, bf16[128,1024]{1,0:T(8,128)(2,1)}, u32[]{:S(2)}, u32[]{:S(2)}) collective-permute-start(bf16[128,1024]{1,0:T(8,128)(2,1)S(1)} %fusion.40), channel_id=1, source_target_pairs={{0,8},{4,12},{8,0},{12,4},{16,24},{20,28},{24,16},{28,20},{1,9},{5... | collective-permute-start | bytes 786440 | tf_op jit(solution)/shard_map/ppermute | solution.py:912
  237.0 16.1 %collective-permute-done.25 = bf16[128,1024]{1,0:T(8,128)(2,1)S(1)} collective-permute-done((bf16[128,1024]{1,0:T(8,128)(2,1)S(1)}, bf16[128,1024]{1,0:T(8,128)(2,1)S(1)}, u32[]{:S(2)}, u32[]{:S(2)}) %collective-permute-start.25) | collective-permute-done | bytes 262176 | tf_op jit(solution)/shard_map/ppermute | solution.py:912
  267.0 5.9 collective-permute-done.31.refs_1_
  273.3 7.2 %collective-permute-done.32.refs_2_ = bf16[128,1024]{1,0:T(8,128)(2,1)S(1)} collective-permute-done((bf16[128,1024]{1,0:T(8,128)(2,1)S(1)}, bf16[128,1024]{1,0:T(8,128)(2,1)S(1)}, u32[]{:S(2)}, u32[]{:S(2)}) %collective-permute-start.32) | collective-permute-done | bytes 262176 | tf_op jit(solution)/shard_map/ppermute | solution.py:912
  292.9 31.4 %experts_backward.1 = (f32[512,1024]{1,0:T(8,128)}, bf16[256,1024]{1,0:T(8,128)(2,1)}, bf16[256,1024]{1,0:T(8,128)(2,1)}, bf16[4,1024,1024]{2,1,0:T(8,128)(2,1)}...) custom-call(s32[1]{0:T(128)} %bitcast.17.half_ref, bf16[128,1024]{1,0:T(8,128)(2,1)} %copy-done.25, ...), custom_call_target="tpu_custom_call" | custom-call | tf_op jit(solution)/shard_map/experts_backward/pallas_call | solution.py:730
  324.3 9.3 %grad_expert_in.2 = (bf16[2,4,2,512,128]{4,3,2,1,0:T(8,128)(2,1)}, bf16[2,4,2,512,128]{4,3,2,1,0:T(8,128)(2,1)}) custom-call(s32[1]{0:T(128)S(6)} %sub.97.half_ref, bf16[1024,1024]{1,0:T(8,128)(2,1)} %get-tuple-element.57.refs_0_.rows_ref, bf16[4,1024,1024]{2,1,0:T(8,128)(2,1)} %get-tuple-element.71.pre_ref), custom_call_target="tpu_custom_call" | custom-call | flops 4294967296 | bytes 4194304 | tf_op jit(solution)/shard_map/grad_expert_in/pallas_call | solution.py:812
  339.1 12.4 %collective-permute-done.38.near = bf16[256,1024]{1,0:T(8,128)(2,1)S(1)} collective-permute-done((bf16[256,1024]{1,0:T(8,128)(2,1)}, bf16[256,1024]{1,0:T(8,128)(2,1)S(1)}, u32[]{:S(2)}, u32[]{:S(2)}) %collective-permute-start.38) | collective-permute-done | bytes 524320 | tf_op jit(solution)/shard_map/ppermute | solution.py:912
  354.2 8.1 %collective-permute-done.40 = bf16[256,1024]{1,0:T(8,128)(2,1)S(1)} collective-permute-done((bf16[256,1024]{1,0:T(8,128)(2,1)}, bf16[256,1024]{1,0:T(8,128)(2,1)S(1)}, u32[]{:S(2)}, u32[]{:S(2)}) %collective-permute-start.40) | collective-permute-done | bytes 524320 | tf_op jit(solution)/shard_map/ppermute | solution.py:912
  373.6 8.4 %grad_expert_out.1 = (bf16[2,4,128,512]{3,2,1,0:T(8,128)(2,1)}, bf16[2,4,128,512]{3,2,1,0:T(8,128)(2,1)}, bf16[2,4,128,512]{3,2,1,0:T(8,128)(2,1)}, bf16[2,4,128,512]{3,2,1,0:T(8,128)(2,1)}) custom-call(s32[1]{0:T(128)} %bitcast.17.half_ref, bf16[4,1024,512]{2,1,0:T(8,128)(2,1)} %get-tuple-element.72.gated_ref, ...), custom_call_target="tpu_custom_call" | custom-call | flops 4294967296 | bytes 4194304 | tf_op jit(solution)/shard_map/grad_expert_out/pallas_call | solution.py:775
  382.0 9.3 %grad_expert_in.3 = (bf16[2,4,2,512,128]{4,3,2,1,0:T(8,128)(2,1)}, bf16[2,4,2,512,128]{4,3,2,1,0:T(8,128)(2,1)}) custom-call(s32[1]{0:T(128)} %bitcast.17.half_ref, bf16[1024,1024]{1,0:T(8,128)(2,1)} %get-tuple-element.57.refs_0_.rows_ref, bf16[4,1024,1024]{2,1,0:T(8,128)(2,1)} %get-tuple-element.71.pre_ref, bf16[128,1024]{1,0:T(8,128)(2,1)} %copy-done.55, ...), custom_call_target="tpu_custom_call" | custom-call | flops 4294967296 | bytes 4194304 | tf_op jit(solution)/shard_map/grad_expert_in/pallas_call | solution.py:812
  437.1 6.1 collective-permute-done.52
  471.1 36.4 %collective-permute-done.85 = bf16[4,2,512,128]{3,2,1,0:T(8,128)(2,1)S(1)} collective-permute-done((bf16[4,2,512,128]{3,2,1,0:T(8,128)(2,1)}, bf16[4,2,512,128]{3,2,1,0:T(8,128)(2,1)S(1)}, u32[]{:S(2)}, u32[]{:S(2)}) %collective-permute-start.85) | collective-permute-done | bytes 1048608 | tf_op jit(solution)/shard_map/ppermute | solution.py:912
  543.3 16.5 %collective-permute-done.71 = bf16[144,512]{1,0:T(8,128)(2,1)S(1)} collective-permute-done((bf16[144,512]{1,0:T(8,128)(2,1)S(1)}, bf16[144,512]{1,0:T(8,128)(2,1)S(1)}, u32[]{:S(2)}, u32[]{:S(2)}) %collective-permute-start.71) | collective-permute-done | bytes 147488 | tf_op jit(solution)/shard_map/ppermute | solution.py:912
  568.8 14.5 %collective-permute-done.75 = bf16[144,512]{1,0:T(8,128)(2,1)S(1)} collective-permute-done((bf16[144,512]{1,0:T(8,128)(2,1)S(1)}, bf16[144,512]{1,0:T(8,128)(2,1)S(1)}, u32[]{:S(2)}, u32[]{:S(2)}) %collective-permute-start.75) | collective-permute-done | bytes 147488 | tf_op jit(solution)/shard_map/ppermute | solution.py:912
  609.8 25.7 %collective-permute-done.67 = bf16[128,1024]{1,0:T(8,128)(2,1)S(1)} collective-permute-done((bf16[128,1024]{1,0:T(8,128)(2,1)S(1)}, bf16[128,1024]{1,0:T(8,128)(2,1)S(1)}, u32[]{:S(2)}, u32[]{:S(2)}) %collective-permute-start.67) | collective-permute-done | bytes 262176 | tf_op jit(solution)/shard_map/ppermute | solution.py:916
  (501 shorter events, 277.1 us)
Async XLA Ops:
  28.5 106.1 %collective-permute-start.13 = (bf16[6144,128]{1,0:T(8,128)(2,1)}, bf16[6144,128]{1,0:T(8,128)(2,1)S(1)}, u32[]{:S(2)}, u32[]{:S(2)}) collective-permute-start(bf16[6144,128]{1,0:T(8,128)(2,1)} %get-tuple-element.53.refs_10_.refs_3_.refs_11_), channel_id=1, source_target_pairs={{0,2},{1,3},{2,0},{3,1},{4,6},{5,7},{6,4},{7,5},{8,10},{9,11},{10,... | collective-permute-start | bytes 4718600 | tf_op jit(solution)/shard_map/ppermute | solution.py:916
  30.6 117.8 %collective-permute-start.12 = (bf16[6144,128]{1,0:T(8,128)(2,1)}, bf16[6144,128]{1,0:T(8,128)(2,1)}, u32[]{:S(2)}, u32[]{:S(2)}) collective-permute-start(bf16[6144,128]{1,0:T(8,128)(2,1)} %get-tuple-element.53.refs_10_.refs_3_.refs_11_), channel_id=1, source_target_pairs={{0,1},{1,0},{2,3},{3,2},{4,5},{5,4},{6,7},{7,6},{8,9},{9,8},{10,11... | collective-permute-start | bytes 4718600 | tf_op jit(solution)/shard_map/ppermute | solution.py:920
  30.6 73.0 %collective-permute-start.15 = (bf16[3072,128]{1,0:T(8,128)(2,1)}, bf16[3072,128]{1,0:T(8,128)(2,1)}, u32[]{:S(2)}, u32[]{:S(2)}) collective-permute-start(bf16[3072,128]{1,0:T(8,128)(2,1)} %get-tuple-element.54), channel_id=1, source_target_pairs={{0,16},{4,20},{8,24},{12,28},{16,0},{20,4},{24,8},{28,12},{1,17},{... | collective-permute-start | bytes 2359304 | tf_op jit(solution)/shard_map/ppermute | solution.py:912
  33.2 74.0 %collective-permute-start.16 = (bf16[3072,128]{1,0:T(8,128)(2,1)}, bf16[3072,128]{1,0:T(8,128)(2,1)}, u32[]{:S(2)}, u32[]{:S(2)}) collective-permute-start(bf16[3072,128]{1,0:T(8,128)(2,1)} %get-tuple-element.55), channel_id=1, source_target_pairs={{0,16},{4,20},{8,24},{12,28},{16,0},{20,4},{24,8},{28,12},{1,17},{... | collective-permute-start | bytes 2359304 | tf_op jit(solution)/shard_map/ppermute | solution.py:912
  35.5 68.1 %collective-permute-start.11 = (s32[4,16,128]{2,1,0:T(8,128)S(1)}, s32[4,16,128]{2,1,0:T(8,128)S(1)}, u32[]{:S(2)}, u32[]{:S(2)}) collective-permute-start(s32[4,16,128]{2,1,0:T(8,128)S(1)} %pad_add_fusion), channel_id=1, source_target_pairs={{0,16},{4,20},{8,24},{12,28},{16,0},{20,4},{24,8},{28,12},{1,17},{... | collective-permute-start | bytes 98312 | tf_op jit(solution)/shard_map/ppermute | solution.py:912
  128.1 31.3 %collective-permute-start.21 = (bf16[3072,128]{1,0:T(8,128)(2,1)}, bf16[3072,128]{1,0:T(8,128)(2,1)}, u32[]{:S(2)}, u32[]{:S(2)}) collective-permute-start(bf16[3072,128]{1,0:T(8,128)(2,1)} %collective-permute-done.16.refs_7_.refs_19_), channel_id=1, source_target_pairs={{0,2},{1,3},{2,0},{3,1},{4,6},{5,7},{6,4},{7,5},{8,10},{9,11},{10,... | collective-permute-start | bytes 2359304 | tf_op jit(solution)/shard_map/ppermute | solution.py:916
  134.6 29.3 %collective-permute-start.14 = (bf16[6144,128]{1,0:T(8,128)(2,1)S(1)}, bf16[6144,128]{1,0:T(8,128)(2,1)}, u32[]{:S(2)}, u32[]{:S(2)}) collective-permute-start(bf16[6144,128]{1,0:T(8,128)(2,1)S(1)} %collective-permute-done.13.refs_12_.refs_5_.refs_13_), channel_id=1, source_target_pairs={{0,1},{1,0},{2,3},{3,2},{4,5},{5,4},{6,7},{7,6},{8,9},{9,8},{10,11... | collective-permute-start | bytes 4718600 | tf_op jit(solution)/shard_map/ppermute | solution.py:920
  149.1 32.4 %collective-permute-start.20 = (bf16[3072,128]{1,0:T(8,128)(2,1)}, bf16[3072,128]{1,0:T(8,128)(2,1)}, u32[]{:S(2)}, u32[]{:S(2)}) collective-permute-start(bf16[3072,128]{1,0:T(8,128)(2,1)} %collective-permute-done.16.refs_7_.refs_19_), channel_id=1, source_target_pairs={{0,1},{1,0},{2,3},{3,2},{4,5},{5,4},{6,7},{7,6},{8,9},{9,8},{10,11... | collective-permute-start | bytes 2359304 | tf_op jit(solution)/shard_map/ppermute | solution.py:920
  199.0 25.3 %collective-permute-start.24 = (bf16[256,1024]{1,0:T(8,128)(2,1)}, bf16[256,1024]{1,0:T(8,128)(2,1)}, u32[]{:S(2)}, u32[]{:S(2)}) collective-permute-start(bf16[256,1024]{1,0:T(8,128)(2,1)} %get-tuple-element.65), channel_id=1, source_target_pairs={{0,4},{4,0},{8,12},{12,8},{16,20},{20,16},{24,28},{28,24},{1,5},{5... | collective-permute-start | bytes 1572872 | tf_op jit(solution)/shard_map/ppermute | solution.py:912
  333.7 29.6 %collective-permute-start.43 = (bf16[2,4,2,512,128]{4,3,2,1,0:T(8,128)(2,1)}, bf16[2,4,2,512,128]{4,3,2,1,0:T(8,128)(2,1)}, u32[]{:S(2)}, u32[]{:S(2)}) collective-permute-start(bf16[2,4,2,512,128]{4,3,2,1,0:T(8,128)(2,1)} %get-tuple-element.75), channel_id=1, source_target_pairs={{0,1},{1,0},{2,3},{3,2},{4,5},{5,4},{6,7},{7,6},{8,9},{9,8},{10,11... | collective-permute-start | bytes 6291464 | tf_op jit(solution)/shard_map/ppermute | solution.py:920
  336.9 25.4 %collective-permute-start.40 = (bf16[256,1024]{1,0:T(8,128)(2,1)}, bf16[256,1024]{1,0:T(8,128)(2,1)S(1)}, u32[]{:S(2)}, u32[]{:S(2)}) collective-permute-start(bf16[256,1024]{1,0:T(8,128)(2,1)} %get-tuple-element.70), channel_id=1, source_target_pairs={{0,4},{4,0},{8,12},{12,8},{16,20},{20,16},{24,28},{28,24},{1,5},{5... | collective-permute-start | bytes 1572872 | tf_op jit(solution)/shard_map/ppermute | solution.py:912
  352.4 38.9 %collective-permute-start.39 = (bf16[128,1024]{1,0:T(8,128)(2,1)S(1)}, bf16[128,1024]{1,0:T(8,128)(2,1)S(1)}, u32[]{:S(2)}, u32[]{:S(2)}) collective-permute-start(bf16[128,1024]{1,0:T(8,128)(2,1)S(1)} %add_convert_fusion.4.refs_0_), channel_id=1, source_target_pairs={{0,8},{4,12},{8,0},{12,4},{16,24},{20,28},{24,16},{28,20},{1,9},{5... | collective-permute-start | bytes 786440 | tf_op jit(solution)/shard_map/ppermute | solution.py:912
  367.7 24.9 %collective-permute-start.44 = (bf16[4,2,512,128]{3,2,1,0:T(8,128)(2,1)}, bf16[4,2,512,128]{3,2,1,0:T(8,128)(2,1)S(1)}, u32[]{:S(2)}, u32[]{:S(2)}) collective-permute-start(bf16[4,2,512,128]{3,2,1,0:T(8,128)(2,1)} %get-tuple-element.76.refs_0_), channel_id=1, source_target_pairs={{0,2},{1,3},{2,0},{3,1},{4,6},{5,7},{6,4},{7,5},{8,10},{9,11},{10,... | collective-permute-start | bytes 3145736 | tf_op jit(solution)/shard_map/ppermute | solution.py:916
  399.0 53.0 %collective-permute-start.62 = (bf16[2,4,128,512]{3,2,1,0:T(8,128)(2,1)}, bf16[2,4,128,512]{3,2,1,0:T(8,128)(2,1)S(1)}, u32[]{:S(2)}, u32[]{:S(2)}) collective-permute-start(bf16[2,4,128,512]{3,2,1,0:T(8,128)(2,1)} %get-tuple-element.77.refs_1_), channel_id=1, source_target_pairs={{0,1},{1,0},{2,3},{3,2},{4,5},{5,4},{6,7},{7,6},{8,9},{9,8},{10,11... | collective-permute-start | bytes 3145736 | tf_op jit(solution)/shard_map/ppermute | solution.py:920
  399.5 123.4 %collective-permute-start.86 = (bf16[2,4,128,512]{3,2,1,0:T(8,128)(2,1)}, bf16[2,4,128,512]{3,2,1,0:T(8,128)(2,1)}, u32[]{:S(2)}, u32[]{:S(2)}) collective-permute-start(bf16[2,4,128,512]{3,2,1,0:T(8,128)(2,1)} %get-tuple-element.90), channel_id=1, source_target_pairs={{0,1},{1,0},{2,3},{3,2},{4,5},{5,4},{6,7},{7,6},{8,9},{9,8},{10,11... | collective-permute-start | bytes 3145736 | tf_op jit(solution)/shard_map/ppermute | solution.py:920
  462.2 45.2 %collective-permute-start.85 = (bf16[4,2,512,128]{3,2,1,0:T(8,128)(2,1)}, bf16[4,2,512,128]{3,2,1,0:T(8,128)(2,1)S(1)}, u32[]{:S(2)}, u32[]{:S(2)}) collective-permute-start(bf16[4,2,512,128]{3,2,1,0:T(8,128)(2,1)} %add_convert_fusion), channel_id=1, source_target_pairs={{0,16},{4,20},{8,24},{12,28},{16,0},{20,4},{24,8},{28,12},{1,17},{... | collective-permute-start | bytes 3145736 | tf_op jit(solution)/shard_map/ppermute | solution.py:912
  464.4 44.6 %collective-permute-start.63 = (bf16[4,128,512]{2,1,0:T(8,128)(2,1)}, bf16[4,128,512]{2,1,0:T(8,128)(2,1)S(1)}, u32[]{:S(2)}, u32[]{:S(2)}) collective-permute-start(bf16[4,128,512]{2,1,0:T(8,128)(2,1)} %get-tuple-element.84), channel_id=1, source_target_pairs={{0,2},{1,3},{2,0},{3,1},{4,6},{5,7},{6,4},{7,5},{8,10},{9,11},{10,... | collective-permute-start | bytes 1572872 | tf_op jit(solution)/shard_map/ppermute | solution.py:916
  523.0 41.6 %collective-permute-start.64 = (bf16[2,128,1024]{2,1,0:T(8,128)(2,1)}, bf16[2,128,1024]{2,1,0:T(8,128)(2,1)}, u32[]{:S(2)}, u32[]{:S(2)}) collective-permute-start(bf16[2,128,1024]{2,1,0:T(8,128)(2,1)} %fusion.39), channel_id=1, source_target_pairs={{0,1},{1,0},{2,3},{3,2},{4,5},{5,4},{6,7},{7,6},{8,9},{9,8},{10,11... | collective-permute-start | bytes 1572872 | tf_op jit(solution)/shard_map/ppermute | solution.py:920
  526.8 34.6 %collective-permute-start.87 = (bf16[4,128,512]{2,1,0:T(8,128)(2,1)}, bf16[4,128,512]{2,1,0:T(8,128)(2,1)S(1)}, u32[]{:S(2)}, u32[]{:S(2)}) collective-permute-start(bf16[4,128,512]{2,1,0:T(8,128)(2,1)} %get-tuple-element.92), channel_id=1, source_target_pairs={{0,2},{1,3},{2,0},{3,1},{4,6},{5,7},{6,4},{7,5},{8,10},{9,11},{10,... | collective-permute-start | bytes 1572872 | tf_op jit(solution)/shard_map/ppermute | solution.py:916
  537.1 48.3 %collective-permute-start.88 = (bf16[4,128,512]{2,1,0:T(8,128)(2,1)S(1)}, bf16[4,128,512]{2,1,0:T(8,128)(2,1)S(1)}, u32[]{:S(2)}, u32[]{:S(2)}) collective-permute-start(bf16[4,128,512]{2,1,0:T(8,128)(2,1)S(1)} %add_convert_fusion.1), channel_id=1, source_target_pairs={{0,16},{4,20},{8,24},{12,28},{16,0},{20,4},{24,8},{28,12},{1,17},{... | collective-permute-start | bytes 1572872 | tf_op jit(solution)/shard_map/ppermute | solution.py:912
  595.2 40.3 %collective-permute-start.82 = (f32[2,512]{1,0:T(2,128)S(1)}, f32[2,512]{1,0:T(2,128)S(1)}, u32[]{:S(2)}, u32[]{:S(2)}) collective-permute-start(f32[2,512]{1,0:T(2,128)S(1)} %fusion.149), channel_id=1, source_target_pairs={{0,2},{1,3},{2,0},{3,1},{4,6},{5,7},{6,4},{7,5},{8,10},{9,11},{10,... | collective-permute-start | bytes 12296 | tf_op jit(solution)/shard_map/ppermute | solution.py:916
  604.4 34.5 %collective-permute-start.84 = (bf16[4,2,512,128]{3,2,1,0:T(8,128)(2,1)}, bf16[4,2,512,128]{3,2,1,0:T(8,128)(2,1)S(1)}, u32[]{:S(2)}, u32[]{:S(2)}) collective-permute-start(bf16[4,2,512,128]{3,2,1,0:T(8,128)(2,1)} %get-tuple-element.87), channel_id=1, source_target_pairs={{0,2},{1,3},{2,0},{3,1},{4,6},{5,7},{6,4},{7,5},{8,10},{9,11},{10,... | collective-permute-start | bytes 3145736 | tf_op jit(solution)/shard_map/ppermute | solution.py:916
  606.3 29.2 %collective-permute-start.67 = (bf16[128,1024]{1,0:T(8,128)(2,1)S(1)}, bf16[128,1024]{1,0:T(8,128)(2,1)S(1)}, u32[]{:S(2)}, u32[]{:S(2)}) collective-permute-start(bf16[128,1024]{1,0:T(8,128)(2,1)S(1)} %fusion.35), channel_id=1, source_target_pairs={{0,2},{1,3},{2,0},{3,1},{4,6},{5,7},{6,4},{7,5},{8,10},{9,11},{10,... | collective-permute-start | bytes 786440 | tf_op jit(solution)/shard_map/ppermute | solution.py:916
  607.7 28.4 %collective-permute-start.66 = (bf16[128,1024]{1,0:T(8,128)(2,1)S(1)}, bf16[128,1024]{1,0:T(8,128)(2,1)S(1)}, u32[]{:S(2)}, u32[]{:S(2)}) collective-permute-start(bf16[128,1024]{1,0:T(8,128)(2,1)S(1)} %fusion.35), channel_id=1, source_target_pairs={{0,1},{1,0},{2,3},{3,2},{4,5},{5,4},{6,7},{7,6},{8,9},{9,8},{10,11... | collective-permute-start | bytes 786440 | tf_op jit(solution)/shard_map/ppermute | solution.py:920
  (155 other events, 1772.2 us)

commit v4 on v3

--- a/solution.py
+++ b/solution.py
@@ -365,7 +365,8 @@
     return pl.BlockSpec(memory_space=pl.ANY)
 
 
-def pack_body(half_ref, own_in, own_out, other_in, other_out, own, near, far):
+def pack_body(half_ref, own_in, own_out, other_in, other_out, *refs):
+    own, near, far = refs[-3:]
     step = pl.program_id(0)
 
     def fill(target, source_in, source_out):
@@ -387,7 +388,7 @@
         fill(far, other_in, other_out)
 
 
-def pack_weights(half_index, expert_in, expert_out):
+def pack_weights(half_index, expert_in, expert_out, *after):
     held = expert_in.shape[0] // 2
     in_shape = (1,) + expert_in.shape[1:]
     out_shape = (1,) + expert_out.shape[1:]
@@ -403,7 +404,8 @@
                 pl.BlockSpec(out_shape, lambda e, half: (half[0] * held + e, 0, 0)),
                 pl.BlockSpec(in_shape, lambda e, half: ((1 - half[0]) * held + e, 0, 0, 0)),
                 pl.BlockSpec(out_shape, lambda e, half: ((1 - half[0]) * held + e, 0, 0)),
-            ],
+            ]
+            + [any_block()] * len(after),
             out_specs=[
                 pl.BlockSpec(block, lambda e, half: (e, 0)),
                 pl.BlockSpec(block, lambda e, half: (jnp.minimum(e, 1), 0)),
@@ -412,7 +414,7 @@
         ),
         out_shape=[jax.ShapeDtypeStruct(shape, BF16) for shape in shapes],
         name="pack_weights",
-    )(half_index, expert_in, expert_out, expert_in, expert_out)
+    )(half_index, expert_in, expert_out, expert_in, expert_out, *after)
 
 
 def weight_copies(own, other, own_row, other_row, half, in_buf, out_buf, sems, slot):
@@ -754,10 +756,6 @@
     )(half_index, *shards, gates, router, pre, *own, *near, *far, *after)
 
 
-def cost(flops):
-    return pl.CostEstimate(flops=flops, bytes_accessed=1 << 22, transcendentals=0)
-
-
 def grad_out_body(half_ref, gated_ref, other_ref, mine_ref, *refs):
     outs = refs[-4:]
     turned = gated_ref[0].T
@@ -786,7 +784,6 @@
             out_specs=[pl.BlockSpec((2, 1) + shape[2:], lambda e, *_: (0, e, 0, 0))] * 4,
         ),
         out_shape=[jax.ShapeDtypeStruct(shape, BF16)] * 4,
-        cost_estimate=cost(2 * local * row_count * hidden * width),
         name="grad_expert_out",
     )(half_index, gated, grads, grads, *after)
 
@@ -805,25 +802,24 @@
             (keep_ref, send_ref)[q % 2][q // 2, 0, c] = product[:, start : start + SHARE]
 
 
-def grad_expert_ins(half_index, rows, pre_grad, *after):
+def grad_expert_ins(half_index, rows, pre_grad, first, count, *after):
     local, row_count, wide = pre_grad.shape
     width = rows.shape[1]
-    shape = (2, local, 2, width // 2, SHARE)
+    shape = (2, count, 2, width // 2, SHARE)
     return pl.pallas_call(
         grad_in_body,
         grid_spec=pltpu.PrefetchScalarGridSpec(
             num_scalar_prefetch=1,
-            grid=(local,),
+            grid=(count,),
             in_specs=[
                 pl.BlockSpec((row_count, width // 2), lambda e, half: (0, half[0])),
-                expert_block(pre_grad.shape),
+                expert_block(pre_grad.shape, first),
             ]
             + [any_block()] * len(after),
             out_specs=[pl.BlockSpec((2, 1) + shape[2:], lambda e, *_: (0, e, 0, 0, 0))] * 2,
             scratch_shapes=[pltpu.VMEM((width // 2, row_count), BF16)],
         ),
         out_shape=[jax.ShapeDtypeStruct(shape, BF16)] * 2,
-        cost_estimate=cost(local * row_count * wide * width),
         name="grad_expert_in",
     )(half_index, rows, pre_grad, *after)
 
@@ -848,7 +844,6 @@
             jax.ShapeDtypeStruct(shape[1:], F32),
             jax.ShapeDtypeStruct(shape[1:], BF16),
         ],
-        cost_estimate=cost(1 << 20),
         name="fold_pairs",
     )(keep, got, *after)
 
@@ -881,31 +876,294 @@
             jax.ShapeDtypeStruct((size, width), BF16),
             jax.ShapeDtypeStruct((8, width), F32),
         ],
-        cost_estimate=cost(1 << 20),
         name="finish_rows",
     )(keep, near, two, four, six, extra, unit, scale, gain, grad_out, *after)
 
 
-def join_body(first, second, third, *refs):
+def rotated(values, cosine, sine, sign):
+    width = values.shape[1]
+    lane = lax.broadcasted_iota(jnp.int32, values.shape, 1)
+    lower = lax.rem(lane, HEAD_DIM) < HEAD_DIM // 2
+    ahead = pltpu.roll(values, width - HEAD_DIM // 2, 1)
+    behind = pltpu.roll(values, HEAD_DIM // 2, 1)
+    turned = jnp.where(lower, -ahead, behind)
+    repeat = width // cosine.shape[1]
+    cosine = jnp.concatenate([cosine] * repeat, 1)
+    sine = jnp.concatenate([sine] * repeat, 1)
+    return values * cosine + sign * (turned * sine)
+
+
+def head(values, index, start=0, stop=None):
+    return values[start:stop, index * HEAD_DIM : (index + 1) * HEAD_DIM]
+
+
+def probabilities(query, keys):
+    scores = lax.dot_general(query, keys, NT, preferred_element_type=F32) * ATTN_SCALE
+    powers = jnp.exp(scores - jnp.max(scores, -1, keepdims=True))
+    return powers / jnp.sum(powers, -1, keepdims=True)
+
+
+def attention_forward_body(
+    core_ref, tokens, gain, query_w, key_w, value_w, output_w, cosine, sine, *refs
+):
+    normed, query, keys, values, attended, keep, send = refs[-7:]
+    x = tokens[...].astype(F32)
+    scale = lax.rsqrt(jnp.mean(x * x, -1, keepdims=True) + EPS)
+    normed[...] = (x * scale * gain[...]).astype(BF16)
+    low = normed[...]
+    linear = jnp.dot(low, query_w[...], preferred_element_type=F32)
+    query[...] = rotated(linear, cosine[...], sine[...], 1.0).astype(BF16)
+    linear = jnp.dot(low, key_w[...], preferred_element_type=F32)
+    keys[...] = rotated(linear, cosine[...], sine[...], 1.0).astype(BF16)
+    values[...] = jnp.dot(low, value_w[...], preferred_element_type=F32).astype(BF16)
+    group = query.shape[1] // keys.shape[1]
+    for start in range(0, tokens.shape[0], BLOCK):
+        stop = start + BLOCK
+        parts = []
+        for h in range(query.shape[1] // HEAD_DIM):
+            probs = probabilities(head(query, h, start, stop), head(keys, h // group, 0, stop))
+            parts.append(
+                jnp.dot(
+                    probs.astype(BF16),
+                    head(values, h // group, 0, stop),
+                    preferred_element_type=F32,
+                )
+            )
+        attended[start:stop, :] = jnp.concatenate(parts, 1).astype(BF16)
+    size = tokens.shape[0] // 4
+    for r in range(2):
+        for target, core in ((keep, core_ref[0]), (send, 1 - core_ref[0])):
+            rows = pl.ds(pl.multiple_of((2 * r + core) * size, size), size)
+            part = jnp.dot(attended[rows, :], output_w[...], preferred_element_type=F32)
+            target[r] = part.astype(target.dtype)
+
+
+def scalar_call(body, name, scalar, inputs, shapes, after=(), scratch=()):
+    return pl.pallas_call(
+        body,
+        grid_spec=pltpu.PrefetchScalarGridSpec(
+            num_scalar_prefetch=1,
+            grid=(1,),
+            in_specs=[whole_block(v.shape) for v in inputs] + [any_block()] * len(after),
+            out_specs=[whole_block(s.shape) for s in shapes],
+            scratch_shapes=list(scratch),
+        ),
+        out_shape=shapes,
+        name=name,
+    )(scalar, *inputs, *after)
+
+
+def attention_forward(core, tokens, gain, query_w, key_w, value_w, output_w, tables, *after):
+    rows, width = tokens.shape
+    shapes = [
+        jax.ShapeDtypeStruct((rows, width), BF16),
+        jax.ShapeDtypeStruct((rows, query_w.shape[1]), BF16),
+        jax.ShapeDtypeStruct((rows, key_w.shape[1]), BF16),
+        jax.ShapeDtypeStruct((rows, value_w.shape[1]), BF16),
+        jax.ShapeDtypeStruct((rows, query_w.shape[1]), BF16),
+        jax.ShapeDtypeStruct((2, rows // 4, width), F32),
+        jax.ShapeDtypeStruct((2, rows // 4, width), BF16),
+    ]
+    inputs = (tokens, gain, query_w, key_w, value_w, output_w, *tables)
+    return scalar_call(
+        attention_forward_body, "attention_forward", core, inputs, shapes, after
+    )
+
+
+TN = (((0,), (0,)), ((), ()))
+
+
+def attention_backward_body(
+    share_ref,
+    tokens,
+    query_w,
+    key_w,
+    value_w,
+    output_w,
+    cosine,
+    sine,
+    query,
+    keys,
+    values,
+    first,
+    second,
+    third,
+    fourth,
+    *refs,
+):
+    grad, grad_qkv, gain, keep, send, grad_keys, grad_values = refs[-7:]
+    share = share_ref[0]
+    size = first.shape[0]
+    for r, piece in enumerate((first, second, third, fourth)):
+        place = jnp.bitwise_xor(share, r) * size
+        grad[pl.ds(pl.multiple_of(place, size), size), :] = piece[...]
+    back = lax.dot_general(grad[...], output_w[...], NT, preferred_element_type=F32).astype(BF16)
+    wide, narrow = (query.shape[1], keys.shape[1])
+    group = wide // narrow
+    grad_keys[...] = jnp.zeros_like(grad_keys)
+    grad_values[...] = jnp.zeros_like(grad_values)
+    for start in range(0, tokens.shape[0], BLOCK):
+        stop = start + BLOCK
+        parts, key_parts, value_parts = ([], [], [])
+        for kv in range(narrow // HEAD_DIM):
+            key, value = (head(keys, kv, 0, stop), head(values, kv, 0, stop))
+            key_sum, value_sum = (0.0, 0.0)
+            for h in range(kv * group, (kv + 1) * group):
+                query_h = head(query, h, start, stop)
+                back_h = head(back, h, start, stop)
+                probs = probabilities(query_h, key)
+                inner = lax.dot_general(back_h, value, NT, preferred_element_type=F32)
+                scores = probs * (inner - jnp.sum(probs * inner, -1, keepdims=True))
+                scores = scores.astype(BF16)
+                parts.append(ATTN_SCALE * jnp.dot(scores, key, preferred_element_type=F32))
+                key_sum += lax.dot_general(scores, query_h, TN, preferred_element_type=F32)
+                value_sum += lax.dot_general(
+                    probs.astype(BF16), back_h, TN, preferred_element_type=F32
+                )
+            key_parts.append(ATTN_SCALE * key_sum)
+            value_parts.append(value_sum)
+        turned = rotated(
+            jnp.concatenate(parts, 1), cosine[start:stop, :], sine[start:stop, :], -1.0
+        )
+        grad_qkv[start:stop, :wide] = turned.astype(BF16)
+        grad_keys[:stop, :] += jnp.concatenate(key_parts, 1)
+        grad_values[:stop, :] += jnp.concatenate(value_parts, 1)
+    turned = rotated(grad_keys[...], cosine[...], sine[...], -1.0)
+    grad_qkv[:, wide : wide + narrow] = turned.astype(BF16)
+    grad_qkv[:, wide + narrow :] = grad_values[...].astype(BF16)
+    total = jnp.zeros(gain.shape, F32)
+    for r in range(2):
+        for target, core in ((keep, share % 2), (send, 1 - share % 2)):
+            rows = pl.ds(pl.multiple_of((2 * r + core) * size, size), size)
+            part = lax.dot_general(
+                grad_qkv[rows, :wide], query_w[...], NT, preferred_element_type=F32
+            )
+            part += lax.dot_general(
+                grad_qkv[rows, wide : wide + narrow], key_w[...], NT, preferred_element_type=F32
+            )
+            part += lax.dot_general(
+                grad_qkv[rows, wide + narrow :], value_w[...], NT, preferred_element_type=F32
+            )
+            target[r] = part.astype(target.dtype)
+            x = tokens[rows, :].astype(F32)
+            x = x * lax.rsqrt(jnp.mean(x * x, -1, keepdims=True) + EPS)
+            total += jnp.sum((part * x).reshape(-1, 8, x.shape[1]), 0)
+    gain[...] = total
+
+
+def attention_backward(share, tokens, weights, tables, saved, pieces, *after):
+    rows, width = tokens.shape
+    narrow = saved[1].shape[1]
+    shapes = [
+        jax.ShapeDtypeStruct((rows, width), BF16),
+        jax.ShapeDtypeStruct((rows, saved[0].shape[1] + 2 * narrow), BF16),
+        jax.ShapeDtypeStruct((8, width), F32),
+        jax.ShapeDtypeStruct((2, rows // 4, width), F32),
+        jax.ShapeDtypeStruct((2, rows // 4, width), BF16),
+    ]
+    return scalar_call(
+        attention_backward_body,
+        "attention_backward",
+        share,
+        (tokens, *weights, *tables, *saved, *pieces),
+        shapes,
+        after,
+        [pltpu.VMEM((rows, narrow), F32), pltpu.VMEM((rows, narrow), F32)],
+    )
+
+
+def reduce_body(place_ref, normed, grad_qkv, grad, attended, small, *refs):
+    keep, near, far = refs[-3:]
+    step = pl.program_id(0)
+    first = lax.dot_general(normed[...], grad_qkv[...], TN, preferred_element_type=F32)
+    second = lax.dot_general(grad[...], attended[...], TN, preferred_element_type=F32)
+    part = jnp.concatenate([first, second, small[...]], 1)
+
+    @pl.when(step < 4)
+    def _():
+        keep[...] = part
+
+    @pl.when((step == 4) | (step == 5))
+    def _():
+        near[...] = part.astype(BF16)
+
+    @pl.when(step >= 6)
+    def _():
+        far[...] = part.astype(BF16)
+
+
+def reduce_parts(place, normed, grad_qkv, grad, attended, small, *after):
+    rows, width = normed.shape
+    size = width // 8
+    total = grad_qkv.shape[1] + attended.shape[1] + small.shape[1]
+
+    def shard(e, place):
+        order = jnp.where(e < 4, 2 * e, 2 * e - 7)
+        return jnp.bitwise_xor(place[0], order)
+
+    columns = pl.BlockSpec((rows, size), lambda e, place: (0, shard(e, place)))
+    return pl.pallas_call(
+        reduce_body,
+        grid_spec=pltpu.PrefetchScalarGridSpec(
+            num_scalar_prefetch=1,
+            grid=(8,),
+            in_specs=[
+                columns,
+                whole_block(grad_qkv.shape),
+                columns,
+                whole_block(attended.shape),
+                pl.BlockSpec((size, small.shape[1]), lambda e, place: (shard(e, place), 0)),
+            ]
+            + [any_block()] * len(after),
+            out_specs=[
+                pl.BlockSpec((size, total), lambda e, _: (jnp.minimum(e, 3), 0)),
+                pl.BlockSpec((size, total), lambda e, _: (jnp.clip(e - 4, 0, 1), 0)),
+                pl.BlockSpec((size, total), lambda e, _: (jnp.clip(e - 6, 0, 1), 0)),
+            ],
+        ),
+        out_shape=[
+            jax.ShapeDtypeStruct((4 * size, total), F32),
+            jax.ShapeDtypeStruct((2 * size, total), BF16),
+            jax.ShapeDtypeStruct((2 * size, total), BF16),
+        ],
+        name="reduce_parts",
+    )(place, normed, grad_qkv, grad, attended, small, *after)
+
+
+def unpack_body(place_ref, *refs):
+    pieces = refs[:8]
+    query, key, value, output, small = refs[8:]
+    size = pieces[0].shape[0]
+    wide, narrow = (query.shape[1], key.shape[1])
+    for r, piece in zip(ORDER, pieces):
+        start = pl.multiple_of(jnp.bitwise_xor(place_ref[0], r) * size, size)
+        rows = pl.ds(start, size)
+        part = piece[...].astype(F32)
+        query[rows, :] = part[:, :wide]
+        key[rows, :] = part[:, wide : wide + narrow]
+        value[rows, :] = part[:, wide + narrow : wide + 2 * narrow]
+        begin = wide + 2 * narrow
+        output[:, rows] = part[:, begin : begin + output.shape[0]].T
+        small[rows, :] = part[:, begin + output.shape[0] :]
+
+
+def assemble_body(share_ref, *refs):
     target = refs[-1]
-    start = 0
-    for part in (first, second, third):
-        target[:, start : start + part.shape[1]] = part[...]
-        start += part.shape[1]
-
-
-def join_columns(first, second, third, *after):
-    parts = (first, second, third)
-    shape = (first.shape[0], sum(part.shape[1] for part in parts))
-    return pl.pallas_call(
-        join_body,
-        grid=(1,),
-        in_specs=[whole_block(part.shape) for part in parts] + [any_block()] * len(after),
-        out_specs=whole_block(shape),
-        out_shape=jax.ShapeDtypeStruct(shape, BF16),
-        cost_estimate=cost(1 << 20),
-        name="join_columns",
-    )(*parts, *after)
+    size = refs[0].shape[0]
+    for r in range(4):
+        start = pl.multiple_of(jnp.bitwise_xor(share_ref[0], r) * size, size)
+        target[pl.ds(start, size), :] = refs[r][...].astype(target.dtype)
+
+
+def spread_tensor(value):
+    across = swap_y(value)
+    return [value, swap_core(value), across, swap_core(across)]
+
+
+def assemble(share, pieces, dtype, *after):
+    size, width = pieces[0].shape
+    shapes = [jax.ShapeDtypeStruct((4 * size, width), dtype)]
+    return scalar_call(assemble_body, "assemble", share, pieces, shapes, after)[0]
 
 
 def trade(value, bits):
@@ -925,25 +1183,30 @@
     return column + [trade(shard, 1) for shard in column]
 
 
-def scatter_experts(keep, send_near, send_far):
+def scatter_steps(keep, send_near, send_far, *beside):
     size = keep.shape[0] // 4
-    far = keep[2 * size :].astype(F32) + trade(send_far, 1).astype(F32)
-    far = far.astype(BF16)
-    back = [trade(far[:size], 4), trade(far[size:], 6)]
-    near = trade(send_near, 1).astype(F32)
-    back.append(trade((keep[size : 2 * size].astype(F32) + near[size:]).astype(BF16), 2))
-    total = keep[:size].astype(F32) + near[:size]
+    got_far = trade(send_far, 1)
+    send_near, got_far = lax.optimization_barrier((send_near, got_far))
+    if beside:
+        got_far, *beside = lax.optimization_barrier((got_far, *beside))
+    far = (keep[2 * size :] + got_far.astype(F32)).astype(BF16)
+    got_near = trade(send_near, 1)
+    four, six = (trade(far[:size], 4), trade(far[size:], 6))
+    near = (keep[size : 2 * size] + got_near[size:].astype(F32)).astype(BF16)
+    return (got_near, near, far, (trade(near, 2), four, six), *beside)
+
+
+def scatter_experts(keep, send_near, send_far, *beside):
+    size = keep.shape[0] // 4
+    got_near, _, _, back, *beside = scatter_steps(keep, send_near, send_far, *beside)
+    total = keep[:size] + got_near[:size].astype(F32)
     for part in back:
         total = total + part.astype(F32)
-    return total
-
-
-def scatter_tensor(value, core, row):
-    quarter = value.shape[0] // 4
-    parts = value.reshape(2, 2, quarter, value.shape[1])
-    keep = lax.dynamic_index_in_dim(parts, core, 1, False)
-    send = lax.dynamic_index_in_dim(parts, 1 - core, 1, False)
-    half = keep + swap_core(send.astype(BF16)).astype(F32)
+    return (total, *beside) if beside else total
+
+
+def scatter_tensor(keep, send, row):
+    half = keep + swap_core(send).astype(F32)
     keep = lax.dynamic_index_in_dim(half, row, 0, False)
     send = lax.dynamic_index_in_dim(half, 1 - row, 0, False)
     return keep + swap_y(send.astype(BF16)).astype(F32)
@@ -953,34 +1216,6 @@
     return jnp.where(
         index == 0, jnp.concatenate([first, second], 0), jnp.concatenate([second, first], 0)
     )
-
-
-def gather_tensor(value, core, row):
-    across = swap_y(value)
-    pair = ordered(core, value, swap_core(value))
-    other = ordered(core, across, swap_core(across))
-    return ordered(row, pair, other)
-
-
-def sum_experts(shards, place):
-    size, width = shards.shape[1:]
-
-    def pick(*order):
-        picked = [
-            lax.dynamic_index_in_dim(shards, jnp.bitwise_xor(place, r), 0, False) for r in order
-        ]
-        return jnp.concatenate(picked, 0)
-
-    total = scatter_experts(pick(0, 2, 4, 6), pick(1, 3).astype(BF16), pick(5, 7).astype(BF16))
-    gathered = jnp.stack(gather_experts(total.astype(BF16)))
-    lower = (jnp.bitwise_and(place, 1), jnp.bitwise_and(place, 2), jnp.bitwise_and(place, 4))
-    column, inner, outer = (bit > 0 for bit in lower)
-    halves = jnp.stack([gathered[:4], gathered[4:]])
-    halves = jnp.where(column, halves[::-1], halves)
-    halves = halves.reshape(2, 2, 2, size, width)
-    halves = jnp.where(inner, halves[:, :, ::-1], halves)
-    halves = jnp.where(outer, halves[:, ::-1], halves)
-    return halves.transpose(1, 2, 0, 3, 4).reshape(shards.shape).astype(F32)
 
 
 def per_device(
@@ -1024,9 +1259,6 @@
             expert_in,
             expert_out,
         )
-    local_query = query_weight.shape[1] // HEAD_DIM
-    local_kv = key_matrix.shape[1] // HEAD_DIM
-    group = local_query // local_kv
     quarter = row_count // shares
     place = lax.axis_index("expert")
     share = lax.axis_index("tensor")
@@ -1036,29 +1268,25 @@
     held = expert_in.shape[0] // 2
     base = 8 * (place % 4) + held * half_index
 
-    own_pack, near_pack, far_pack = pack_weights(half_arg, expert_in, expert_out)
+    share_arg, core_arg, place_arg = (share.reshape(1), core.reshape(1), place.reshape(1))
+
+    def quarter_of(values):
+        return lax.dynamic_slice_in_dim(values, share * quarter, quarter, 0)
+
+    local_valid = jnp.sum(valid_mask)
+    routes_mine = quarter_of(routes)
+    note = jnp.concatenate([routes_mine.T, jnp.full((TOP, quarter), local_valid, jnp.int32)], 0)
+    notes = [note] + [trade(note, bits) for bits in (2, 4, 6)]
+
+    own_pack, near_pack, far_pack = pack_weights(half_arg, expert_in, expert_out, *notes[1:])
     near_pack = trade(near_pack, 4)
     far_pack = trade(far_pack, 4)
-
-    def spread_shares(pack):
-        across = swap_y(pack)
-        return [pack, swap_core(pack), across, swap_core(across)]
-
-    own = spread_shares(own_pack)
-
-    def quarter_of(values):
-        return lax.dynamic_slice_in_dim(values, share * quarter, quarter, 0)
-
-    local_valid = jnp.sum(valid_mask)
-    routes_mine = quarter_of(routes)
-    notes = jnp.concatenate(
-        [routes_mine.T, jnp.full((TOP, quarter), local_valid, jnp.int32)], 0
-    )[None]
-    for bits in (1, 2, 4):
-        notes = jnp.concatenate([notes, trade(notes, bits)], 0)
+    own_across = swap_y(own_pack)
+
+    notes = jnp.stack(notes)
+    notes = jnp.concatenate([notes, trade(notes, 1)], 0)
     valid_total = jnp.sum(notes[:, TOP, 0]).astype(F32)
-    notes = jnp.stack([notes[r, :TOP] for r in ORDER])
-    route_rel = jnp.bitwise_and(notes - base, expert_count - 1)
+    route_rel = jnp.bitwise_and(notes[:, :TOP] - base, expert_count - 1)
     route_rel = route_rel.transpose(0, 2, 1).reshape(senders * quarter, TOP)
     router_rel = lax.dynamic_slice_in_dim(
         jnp.concatenate([router_weight, router_weight], 1), base, expert_count, 1
@@ -1067,46 +1295,30 @@
         jnp.concatenate([router_rel, router_rel], 1), ((0, 0), (0, 128 - 2 * expert_count))
     )
 
-    tokens_f32 = tokens.astype(F32)
-    scale_one = lax.rsqrt(jnp.mean(tokens_f32 * tokens_f32, -1, keepdims=True) + EPS)
-    unit_one = tokens_f32 * scale_one
-    first_normed = (unit_one * first_gain).astype(BF16)
-    cosine, sine = rope_tables(row_count, HEAD_DIM)
-    query_linear = jnp.dot(first_normed, query_weight, preferred_element_type=F32)
-    keys_linear = jnp.dot(first_normed, key_matrix, preferred_element_type=F32)
-    value_low = jnp.dot(first_normed, value_matrix, preferred_element_type=F32).astype(BF16)
-    value_low = value_low.reshape(row_count, local_kv, HEAD_DIM)
-    query_rotated = apply_rotary(
-        query_linear.reshape(row_count, local_query, HEAD_DIM), cosine, sine
-    ).astype(BF16)
-    keys_rot = apply_rotary(
-        keys_linear.reshape(row_count, local_kv, HEAD_DIM), cosine, sine
-    ).astype(BF16)
-    query_block = query_rotated.reshape(row_count, local_kv, group, HEAD_DIM)
-    block_of = jnp.arange(row_count, dtype=jnp.int32) // BLOCK
-    allowed = block_of[None, :] <= block_of[:, None]
-
-    def masked_scores():
-        scores = jnp.einsum("qhgd,khd->hgqk", query_block, keys_rot, preferred_element_type=F32)
-        return jnp.where(allowed, scores * ATTN_SCALE, -1e30)
-
-    scores = masked_scores()
-    row_peak = jnp.max(scores, -1, keepdims=True)
-    powers = jnp.exp(scores - row_peak)
-    row_total = jnp.sum(powers, -1, keepdims=True)
-    probs_low = (powers / row_total).astype(BF16)
-    attended = jnp.einsum("hgqk,khd->qhgd", probs_low, value_low, preferred_element_type=F32)
-    attended = attended.reshape(row_count, local_query * HEAD_DIM).astype(BF16)
-    attn_part = jnp.dot(attended, output_weight, preferred_element_type=F32)
-
+    tables = [
+        jnp.concatenate([table[:, 0]] * (2 * SHARE // HEAD_DIM), 1)
+        for table in rope_tables(row_count, HEAD_DIM)
+    ]
+    weights = (query_weight, key_matrix, value_matrix, output_weight)
+    first_normed, query, keys, values, attended, attn_keep, attn_send = attention_forward(
+        core_arg, tokens, first_gain[None], *weights, tables, own_pack
+    )
+    near_pack, own_across, attn_send = lax.optimization_barrier(
+        (near_pack, own_across, attn_send)
+    )
+    own = [own_pack, swap_core(own_pack), own_across, swap_core(own_across)]
     tokens_mine = quarter_of(tokens).astype(F32)
-    hidden = tokens_mine + RESIDUAL * scatter_tensor(attn_part, core, row)
+    hidden = tokens_mine + RESIDUAL * scatter_tensor(attn_keep, attn_send, row)
     scale_two = lax.rsqrt(jnp.mean(hidden * hidden, -1, keepdims=True) + EPS)
     unit_two = hidden * scale_two
     normed_two = (unit_two * second_gain).astype(BF16)
-    row_shards = gather_experts(normed_two)
-    near_pack, far_pack, normed_two = lax.optimization_barrier((near_pack, far_pack, normed_two))
-    near, far = (spread_shares(near_pack), spread_shares(far_pack))
+    column = [normed_two] + [trade(normed_two, bits) for bits in (2, 4, 6)]
+    beside = trade(normed_two, 1)
+    near_pack, far_pack, column[1], beside = lax.optimization_barrier(
+        (near_pack, far_pack, column[1], beside)
+    )
+    row_shards = column + [beside] + [trade(shard, 1) for shard in column[1:]]
+    near, far = (spread_tensor(near_pack), spread_tensor(far_pack))
     keep, send_near, send_far, pre, gated, gates, expert_rows = experts_forward(
         half_arg,
         row_shards,
@@ -1131,50 +1343,50 @@
     mean_part = jnp.concatenate([mean_high, (mean_part - mean_high.astype(F32)).astype(BF16)], 1)
     router_pair = jnp.concatenate([router_weight, router_weight], 1)
     mean_rows = jnp.einsum("te,de->td", mean_part, router_pair, preferred_element_type=F32)
-    layer_output = gather_tensor(output.astype(BF16), core, row)
-
     keep, send_near, send_far, pre_grad, logit_grad, grad_rows = experts_backward(
-        half_arg,
-        gather_experts(grad_moe),
-        gates,
-        router_rel,
-        pre,
-        own,
-        near,
-        far,
-        layer_output,
-        mean_rows,
-    )
-    got_far = trade(send_far, 1)
-    got_near = trade(send_near, 1)
-    in_keep, in_send = grad_expert_ins(1 - half_arg, expert_rows, pre_grad)
-    far_rows = (keep[2 * quarter :] + got_far.astype(F32)).astype(BF16)
-    back_four = trade(far_rows[:quarter], 4)
-    back_six = trade(far_rows[quarter:], 6)
-    in_near, in_far = fold_pairs(in_keep, swap_core(in_send), far_rows)
-    in_across = swap_y(in_far)
+        half_arg, gather_experts(grad_moe), gates, router_rel, pre, own, near, far, mean_rows
+    )
+    got_near, near_rows, far_rows, back = scatter_steps(keep, send_near, send_far)
+    other = 1 - half_arg
+    in_keep, in_send = grad_expert_ins(other, expert_rows, pre_grad, 0, 2)
+    late_keep, late_send = grad_expert_ins(other, expert_rows, pre_grad, 2, 2, in_send)
+    in_near, in_far = fold_pairs(in_keep, swap_core(in_send), late_send, far_rows)
+    in_ready = (in_near + swap_y(in_far).astype(F32)).astype(BF16)
     out_keep, out_send, own_out_keep, own_out_send = grad_expert_outs(
         half_arg, gated, grad_rows, in_far
     )
-    near_rows = (keep[quarter : 2 * quarter] + got_near[quarter:].astype(F32)).astype(BF16)
-    back_two = trade(near_rows, 2)
-    own_in_keep, own_in_send = grad_expert_ins(half_arg, expert_rows, pre_grad, near_rows, out_send)
-    in_back = trade((in_near + in_across.astype(F32)).astype(BF16), 4)
     grad_hidden, grad_attn, grad_second_part = finish_rows(
         keep,
         got_near,
-        back_two,
-        back_four,
-        back_six,
+        *back,
         mean_rows,
         unit_two,
         scale_two,
         second_gain[None],
         grad_out,
-        own_in_send,
-        in_across,
+        out_send,
+        in_ready,
     )
     grad_second_part = jnp.sum(grad_second_part, 0)
+    own_in_keep, own_in_send = grad_expert_ins(
+        half_arg, expert_rows, pre_grad, 0, held, grad_attn
+    )
+    pieces = spread_tensor(grad_attn)
+    late_near, late_far = fold_pairs(late_keep, swap_core(late_send), pieces[2])
+    out_near, out_far = fold_pairs(out_keep, swap_core(out_send), pieces[2])
+    out_ready = (out_near + swap_y(out_far).astype(F32)).astype(BF16)
+    out_back = trade(out_ready, 4)
+    late_ready = (late_near + swap_y(late_far).astype(F32)).astype(BF16)
+    grad_attn, grad_qkv, gain_part, one_keep, one_send = attention_backward(
+        share_arg, tokens, weights, tables, (query, keys, values), pieces, late_far, out_far, own_in_send
+    )
+    in_back = trade(in_ready, 4)
+    late_back = trade(late_ready, 4)
+    grad_one = scatter_tensor(one_keep, one_send, row)
+    own_out_near, own_out_far = fold_pairs(own_out_keep, swap_core(own_out_send), grad_one)
+    own_in_near, own_in_far = fold_pairs(own_in_keep, swap_core(own_in_send), grad_one)
+    own_out_across = swap_y(own_out_far)
+    own_in_across = swap_y(own_in_far)
 
     router_part = jnp.einsum(
         "te,td->ed", logit_grad.astype(BF16), expert_rows, preferred_element_type=F32
@@ -1199,46 +1411,31 @@
     )
     small = small + swap_core(small)
     small = small + swap_y(small)
-    small = jnp.pad(small, ((0, 128 - small.shape[0]), (0, 0))).reshape(8, 16, model_width)
-
-    grad_attn = gather_tensor(grad_attn, core, row)
-    out_near, out_far = fold_pairs(out_keep, swap_core(out_send), grad_attn)
-    out_across = swap_y(out_far)
-    grad_output = jnp.einsum("tc,td->cd", attended, grad_attn, preferred_element_type=F32)
-    grad_attended = jnp.einsum("td,cd->tc", grad_attn, output_weight, preferred_element_type=F32)
-    grad_attended = grad_attended.astype(BF16).reshape(row_count, local_kv, group, HEAD_DIM)
-    attn_probs = jnp.exp(masked_scores() - row_peak) / row_total
-    grad_probs = jnp.einsum("qhgd,khd->hgqk", grad_attended, value_low, preferred_element_type=F32)
-    grad_scores = attn_probs * (grad_probs - jnp.sum(attn_probs * grad_probs, -1, keepdims=True))
-    grad_scores = grad_scores.astype(BF16)
-    grad_query_rot = ATTN_SCALE * jnp.einsum(
-        "hgqk,khd->qhgd", grad_scores, keys_rot, preferred_element_type=F32
-    )
-    grad_keys_rot = ATTN_SCALE * jnp.einsum(
-        "hgqk,qhgd->khd", grad_scores, query_block, preferred_element_type=F32
-    )
-    grad_values = jnp.einsum(
-        "hgqk,qhgd->khd", attn_probs.astype(BF16), grad_attended, preferred_element_type=F32
-    )
-    grad_query_low = unrotate(
-        grad_query_rot.reshape(row_count, local_query, HEAD_DIM), cosine, sine
-    )
-    grad_query_low = grad_query_low.reshape(row_count, local_query * HEAD_DIM).astype(BF16)
-    grad_keys_low = unrotate(grad_keys_rot, cosine, sine)
-    grad_keys_low = grad_keys_low.reshape(row_count, local_kv * HEAD_DIM).astype(BF16)
-    grad_values_low = grad_values.reshape(row_count, local_kv * HEAD_DIM).astype(BF16)
-    out_back = trade((out_near + out_across.astype(F32)).astype(BF16), 4)
-    grad_qkv = join_columns(grad_query_low, grad_keys_low, grad_values_low, out_across)
-    weights_qkv = jnp.concatenate([query_weight, key_matrix, value_matrix], 1)
-    grad_weights = jnp.einsum("td,tc->dc", first_normed, grad_qkv, preferred_element_type=F32)
-    grad_one_part = jnp.einsum("tc,dc->td", grad_qkv, weights_qkv, preferred_element_type=F32)
-    gain_part = jnp.sum(grad_one_part * unit_one, 0).reshape(2, -1)
-    gain_part = jnp.pad(gain_part, ((0, 126), (0, 0))).reshape(8, 16, -1)
-    grad_one = scatter_tensor(grad_one_part, core, row)
-    own_out_near, own_out_far = fold_pairs(own_out_keep, swap_core(own_out_send), grad_qkv)
-    own_in_near, own_in_far = fold_pairs(own_in_keep, swap_core(own_in_send), grad_one)
-    own_out_across = swap_y(own_out_far)
-    own_in_across = swap_y(own_in_far)
+    gain_part = jnp.sum(gain_part, 0).reshape(8, -1)
+    small = jnp.concatenate([small, gain_part.reshape(1, -1)], 0)
+    small = jnp.pad(small, ((0, 128 - small.shape[0]), (0, 0))).T
+    keep, send_near, send_far = reduce_parts(
+        place_arg, first_normed, grad_qkv, grad_attn, attended, small, in_back, late_ready
+    )
+    total, late_back = scatter_experts(keep, send_near, send_far, late_back)
+    total = total.astype(BF16)
+    shapes = [
+        jax.ShapeDtypeStruct(shape, F32)
+        for shape in (
+            query_weight.shape,
+            key_matrix.shape,
+            value_matrix.shape,
+            output_weight.shape,
+            (model_width, 128),
+        )
+    ]
+    grad_query, grad_key, grad_value, grad_output, small = scalar_call(
+        unpack_body, "unpack", place_arg, gather_experts(total), shapes
+    )
+
+    gain_part = small[:, expert_count + 2].reshape(8, -1)
+    gain_part = gain_part + swap_core(gain_part)
+    gain_part = (gain_part + swap_y(gain_part)).reshape(-1)
 
     scale_mine = lax.rsqrt(jnp.mean(tokens_mine * tokens_mine, -1, keepdims=True) + EPS)
     unit_mine = tokens_mine * scale_mine
@@ -1246,38 +1443,27 @@
     grad_tokens = grad_hidden + scale_mine * (
         grad_unit_one - unit_mine * jnp.mean(grad_unit_one * unit_mine, -1, keepdims=True)
     )
-    grad_tokens = gather_tensor(grad_tokens.astype(BF16), core, row).astype(F32)
-    grad_output = jnp.concatenate([grad_output.reshape(8, -1, model_width), small], 1)
-    grad_output = sum_experts(grad_output, place)
-    small = grad_output[:, -16:].reshape(128, model_width)
-    grad_output = grad_output[:, :-16].reshape(-1, model_width)
-    grad_weights = jnp.concatenate(
-        [grad_weights.reshape(8, -1, grad_weights.shape[1]), gain_part], 1
-    )
-    grad_weights = sum_experts(grad_weights, place)
-    gain_part = grad_weights[0, -16:-14]
-    gain_part = gain_part + swap_core(gain_part)
-    grad_first_gain = (gain_part + swap_y(gain_part)).reshape(-1)
-    grad_weights = grad_weights[:, :-16].reshape(model_width, -1)
-    query_columns = query_weight.shape[1]
-    key_columns = query_columns + key_matrix.shape[1]
+    grad_tokens = assemble(share_arg, spread_tensor(grad_tokens.astype(BF16)), F32)
+    layer_output = assemble(share_arg, spread_tensor(output.astype(BF16)), BF16)
     grad_expert_out = ordered(
         half_index, own_out_near + own_out_across.astype(F32), out_back.astype(F32)
     )
     grad_expert_in = ordered(
-        half_index, own_in_near + own_in_across.astype(F32), in_back.astype(F32)
+        half_index,
+        own_in_near + own_in_across.astype(F32),
+        jnp.concatenate([in_back, late_back], 0).astype(F32),
     )
     return (
         layer_output,
-        small[expert_count + 1, 0] / (2.0 * model_width * valid_total),
+        small[0, expert_count + 1] / (2.0 * model_width * valid_total),
         grad_tokens,
-        grad_first_gain,
-        grad_weights[:, :query_columns],
-        grad_weights[:, query_columns:key_columns],
-        grad_weights[:, key_columns:],
+        gain_part,
+        grad_query,
+        grad_key,
+        grad_value,
         grad_output,
-        small[expert_count],
-        small[:expert_count].T,
+        small[:, expert_count],
+        small[:, :expert_count],
         grad_expert_in,
         grad_expert_out,
     )

time: 650 us -> 541 us (0.83)
  the two profiles are of different devices: /device:TPU:0 before, /device:TPU:8 now
where the time goes in v4:
time: 541 us; the launch traced here: 532 us
  waiting for transfers between devices  222 us (41%)
  Pallas kernels  155 us (29%)
  starting transfers between devices  82.3 us (15%)
  other arithmetic  43.3 us (8%)
  local copies, waits for them, and re-layouts  19.9 us (4%)
    ppermute x45, waiting for transfers between devices, trade(): return lax.ppermute(value, 'expert', [(i, i ^ bits) for i in range(8)])  198 us
    ppermute x45, starting transfers between devices, trade(): return lax.ppermute(value, 'expert', [(i, i ^ bits) for i in range(8)])  62.1 us
    pallas_call x1, Pallas kernels, experts_backward(): pl.pallas_call(backward_body, grid_spec=pltpu.PrefetchScalarGridSpec(num_...  31.2 us
    pallas_call x5, Pallas kernels, scalar_call(): pl.pallas_call(body, grid_spec=pltpu.PrefetchScalarGridSpec(num_scalar_pr...  27.7 us
    ppermute x15, waiting for transfers between devices, swap_y(): return lax.ppermute(value, 'tensor', [(i, i ^ 2) for i in range(4)])  22.5 us
    pallas_call x3, Pallas kernels, grad_expert_ins(): pl.pallas_call(grad_in_body, grid_spec=pltpu.PrefetchScalarGridSpec(num_s...  20.9 us
    pallas_call x1, Pallas kernels, experts_forward(): pl.pallas_call(forward_first, grid_spec=pltpu.PrefetchScalarGridSpec(num_...  17.5 us
    ppermute x15, starting transfers between devices, swap_y(): return lax.ppermute(value, 'tensor', [(i, i ^ 2) for i in range(4)])  17.1 us
  transfers between devices with their start and end apart: 81, of which 37 were waited for; matrix products, arithmetic and copies ran while one was open for 9% of the time, Pallas kernels for 18%

profile of v4, /device:TPU:8, one launch (start us, length us, event | category | flops | bytes accessed | tf_op | source)
XLA Modules:
  0.0 531.5 jit_solution(8297608670266010930)
XLA Ops:
  20.3 8.4 %attention_forward.1 = (bf16[512,1024]{1,0:T(8,128)(2,1)}, bf16[512,256]{1,0:T(8,128)(2,1)}, bf16[512,128]{1,0:T(8,128)(2,1)}, bf16[512,128]{1,0:T(8,128)(2,1)},...) custom-call(s32[1]{0:T(128)} %bitcast.1.core_ref, bf16[512,1024]{1,0:T(8,128)(2,1)} %tokens.3, ...), custom_call_target="tpu_custom_call" | custom-call | tf_op jit(solution)/shard_map/attention_forward/pallas_call | solution.py:942
  28.7 21.5 %collective-permute-done.3.refs_14_.refs_15_ = bf16[3072,128]{1,0:T(8,128)(2,1)} collective-permute-done((bf16[3072,128]{1,0:T(8,128)(2,1)}, bf16[3072,128]{1,0:T(8,128)(2,1)}, u32[]{:S(2)}, u32[]{:S(2)}) %collective-permute-start.3) | collective-permute-done | bytes 786464 | tf_op jit(solution)/shard_map/ppermute | solution.py:1170
  71.2 26.9 %collective-permute-done.7.refs_7_.refs_19_ = bf16[3072,128]{1,0:T(8,128)(2,1)} collective-permute-done((bf16[3072,128]{1,0:T(8,128)(2,1)}, bf16[3072,128]{1,0:T(8,128)(2,1)}, u32[]{:S(2)}, u32[]{:S(2)}) %collective-permute-start.7) | collective-permute-done | bytes 786464 | tf_op jit(solution)/shard_map/ppermute | solution.py:1170
  107.3 9.1 %collective-permute-done.11.refs_3_ = bf16[128,1024]{1,0:T(8,128)(2,1)S(1)} collective-permute-done((bf16[128,1024]{1,0:T(8,128)(2,1)S(1)}, bf16[128,1024]{1,0:T(8,128)(2,1)S(1)}, u32[]{:S(2)}, u32[]{:S(2)}) %collective-permute-start.11) | collective-permute-done | bytes 262176 | tf_op jit(solution)/shard_map/ppermute | solution.py:1170
  119.1 6.8 %collective-permute-done.13.refs_6_ = bf16[128,1024]{1,0:T(8,128)(2,1)} collective-permute-done((bf16[128,1024]{1,0:T(8,128)(2,1)}, bf16[128,1024]{1,0:T(8,128)(2,1)}, u32[]{:S(2)}, u32[]{:S(2)}) %collective-permute-start.13) | collective-permute-done | bytes 262176 | tf_op jit(solution)/shard_map/ppermute | solution.py:1170
  138.8 17.5 %experts_forward_a.1 = (f32[1024,1024]{1,0:T(8,128)}, bf16[4,1024,1024]{2,1,0:T(8,128)(2,1)}, bf16[4,1024,512]{2,1,0:T(8,128)(2,1)}, f32[1024,128]{1,0:T(8,128)}, bf16[1024,1024]{1,0:T(8,128)(2,1)}) custom-call(s32[1]{0:T(128)} %bitcast.3.half_ref, bf16[128,1024]{1,0:T(8,128)(2,1)} %copy-done.12, bf16[128,1024]{1,0:T(8,128)(2,1)} %collective-permute-done.8.refs_1_, ...), custom_call_target="tpu_custom_call" | custom-call | tf_op jit(solution)/shard_map/experts_forward_a/pallas_call | solution.py:635
  156.4 17.0 %experts_forward_b.1 = (f32[512,1024]{1,0:T(8,128)}, bf16[256,1024]{1,0:T(8,128)(2,1)}, bf16[256,1024]{1,0:T(8,128)(2,1)}, bf16[4,1024,1024]{2,1,0:T(8,128)(2,1)}, bf16[4,1024,512]{2,1,0:T(8,128)(2,1)}) custom-call(s32[1]{0:T(128)} %bitcast.3.half_ref, ...), custom_call_target="tpu_custom_call", output_to_operand_aliasing={{3}: (12, {}), {4}: (13, {})} | custom-call | tf_op jit(solution)/shard_map/experts_forward_b/pallas_call | solution.py:655
  174.0 14.0 %collective-permute-done.24 = bf16[256,1024]{1,0:T(8,128)(2,1)S(1)} collective-permute-done((bf16[256,1024]{1,0:T(8,128)(2,1)}, bf16[256,1024]{1,0:T(8,128)(2,1)S(1)}, u32[]{:S(2)}, u32[]{:S(2)}) %collective-permute-start.24) | collective-permute-done | bytes 524320 | tf_op jit(solution)/shard_map/ppermute | solution.py:1170
  195.1 6.6 %collective-permute-done.25 = bf16[256,1024]{1,0:T(8,128)(2,1)S(1)} collective-permute-done((bf16[256,1024]{1,0:T(8,128)(2,1)}, bf16[256,1024]{1,0:T(8,128)(2,1)S(1)}, u32[]{:S(2)}, u32[]{:S(2)}) %collective-permute-start.25) | collective-permute-done | bytes 524320 | tf_op jit(solution)/shard_map/ppermute | solution.py:1170
  223.3 5.7 %collective-permute-done.32.refs_1_ = bf16[128,1024]{1,0:T(8,128)(2,1)S(1)} collective-permute-done((bf16[128,1024]{1,0:T(8,128)(2,1)S(1)}, bf16[128,1024]{1,0:T(8,128)(2,1)S(1)}, u32[]{:S(2)}, u32[]{:S(2)}) %collective-permute-start.32) | collective-permute-done | bytes 262176 | tf_op jit(solution)/shard_map/ppermute | solution.py:1170
  231.0 8.3 %collective-permute-done.33.refs_2_ = bf16[128,1024]{1,0:T(8,128)(2,1)S(1)} collective-permute-done((bf16[128,1024]{1,0:T(8,128)(2,1)S(1)}, bf16[128,1024]{1,0:T(8,128)(2,1)S(1)}, u32[]{:S(2)}, u32[]{:S(2)}) %collective-permute-start.33) | collective-permute-done | bytes 262176 | tf_op jit(solution)/shard_map/ppermute | solution.py:1170
  252.0 31.2 %experts_backward.1 = (f32[512,1024]{1,0:T(8,128)}, bf16[256,1024]{1,0:T(8,128)(2,1)}, bf16[256,1024]{1,0:T(8,128)(2,1)}, bf16[4,1024,1024]{2,1,0:T(8,128)(2,1)}...) custom-call(s32[1]{0:T(128)} %bitcast.3.half_ref, bf16[128,1024]{1,0:T(8,128)(2,1)} %copy-done.27, ...), custom_call_target="tpu_custom_call" | custom-call | tf_op jit(solution)/shard_map/experts_backward/pallas_call | solution.py:732
  283.3 5.7 %grad_expert_in.3 = (bf16[2,2,2,512,128]{4,3,2,1,0:T(8,128)(2,1)}, bf16[2,2,2,512,128]{4,3,2,1,0:T(8,128)(2,1)}) custom-call(s32[1]{0:T(128)S(6)} %sub.49.half_ref, bf16[1024,1024]{1,0:T(8,128)(2,1)} %get-tuple-element.100.refs_0_.rows_ref, bf16[4,1024,1024]{2,1,0:T(8,128)(2,1)} %get-tuple-element.123.pre_ref), custom_call_target="tpu_custom_call" | custom-call | tf_op jit(solution)/shard_map/grad_expert_in/pallas_call | solution.py:809
  290.7 5.9 %grad_expert_in.4 = (bf16[2,2,2,512,128]{4,3,2,1,0:T(8,128)(2,1)}, bf16[2,2,2,512,128]{4,3,2,1,0:T(8,128)(2,1)}) custom-call(s32[1]{0:T(128)S(6)} %sub.49.half_ref, bf16[1024,1024]{1,0:T(8,128)(2,1)} %get-tuple-element.100.refs_0_.rows_ref, bf16[4,1024,1024]{2,1,0:T(8,128)(2,1)} %get-tuple-element.123.pre_ref, ...), custom_call_target="tpu_custom_call" | custom-call | tf_op jit(solution)/shard_map/grad_expert_in/pallas_call | solution.py:809
  299.5 5.6 %collective-permute-done.39 = bf16[256,1024]{1,0:T(8,128)(2,1)} collective-permute-done((bf16[256,1024]{1,0:T(8,128)(2,1)}, bf16[256,1024]{1,0:T(8,128)(2,1)}, u32[]{:S(2)}, u32[]{:S(2)}) %collective-permute-start.39) | collective-permute-done | bytes 524320 | tf_op jit(solution)/shard_map/ppermute | solution.py:1170
  313.9 8.7 %grad_expert_out.1 = (bf16[2,4,128,512]{3,2,1,0:T(8,128)(2,1)}, bf16[2,4,128,512]{3,2,1,0:T(8,128)(2,1)}, bf16[2,4,128,512]{3,2,1,0:T(8,128)(2,1)}, bf16[2,4,128,512]{3,2,1,0:T(8,128)(2,1)}) custom-call(s32[1]{0:T(128)} %bitcast.3.half_ref, bf16[4,1024,512]{2,1,0:T(8,128)(2,1)} %get-tuple-element.121.gated_ref, ...), custom_call_target="tpu_custom_call" | custom-call | tf_op jit(solution)/shard_map/grad_expert_out/pallas_call | solution.py:773
  347.4 9.2 %grad_expert_in.5 = (bf16[2,4,2,512,128]{4,3,2,1,0:T(8,128)(2,1)}, bf16[2,4,2,512,128]{4,3,2,1,0:T(8,128)(2,1)}) custom-call(s32[1]{0:T(128)} %bitcast.3.half_ref, bf16[1024,1024]{1,0:T(8,128)(2,1)} %get-tuple-element.100.refs_0_.rows_ref, bf16[4,1024,1024]{2,1,0:T(8,128)(2,1)} %get-tuple-element.123.pre_ref, bf16[128,1024]{1,0:T(8,128)(2,1)} %get-tuple-element.130.refs_0_.first), custom_call_target="tpu_custom_call" | custom-call | tf_op jit(solution)/shard_map/grad_expert_in/pallas_call | solution.py:809
  368.7 10.7 %attention_backward.1 = (bf16[512,1024]{1,0:T(8,128)(2,1)}, bf16[512,512]{1,0:T(8,128)(2,1)}, f32[8,1024]{1,0:T(8,128)}, f32[2,128,1024]{2,1,0:T(8,128)}, bf16[2,128,1024]{2,1,0:T(8,128)(2,1)}) custom-call(s32[1]{0:T(128)} %bitcast.share_ref, bf16[512,1024]{1,0:T(8,128)(2,1)} %tokens.3, bf16[1024,256]{1,0:T(8,128)(2,1)} %query_w.3, bf16[1024,128]{1,0:T(8,128)(2,1)} %key_w.3, ...), custom_call_target="tpu_custom_call" | custom-call | tf_op jit(solution)/shard_map/attention_backward/pallas_call | solution.py:942
  391.7 7.9 %reduce_parts.1 = (f32[512,896]{1,0:T(8,128)}, bf16[256,896]{1,0:T(8,128)(2,1)}, bf16[256,896]{1,0:T(8,128)(2,1)}) custom-call(s32[1]{0:T(128)} %bitcast.13.place_ref, bf16[512,1024]{1,0:T(8,128)(2,1)} %get-tuple-element.111.normed, bf16[512,512]{1,0:T(8,128)(2,1)} %get-tuple-element.136.grad_qkv, bf16[512,1024]{1,0:T(8,128)(2,1)} %get-tuple-element.137.grad, ...), custom_call_target="tpu_custom_call" | custom-call | tf_op jit(solution)/shard_map/reduce_parts/pallas_call | solution.py:1105
  405.7 6.8 %collective-permute-done.55 = bf16[256,896]{1,0:T(8,128)(2,1)S(1)} collective-permute-done((bf16[256,896]{1,0:T(8,128)(2,1)}, bf16[256,896]{1,0:T(8,128)(2,1)S(1)}, u32[]{:S(2)}, u32[]{:S(2)}) %collective-permute-start.55) | collective-permute-done | bytes 458784 | tf_op jit(solution)/shard_map/ppermute | solution.py:1170
  419.9 7.5 %collective-permute-done.56 = bf16[256,896]{1,0:T(8,128)(2,1)S(1)} collective-permute-done((bf16[256,896]{1,0:T(8,128)(2,1)S(1)}, bf16[256,896]{1,0:T(8,128)(2,1)S(1)}, u32[]{:S(2)}, u32[]{:S(2)}) %collective-permute-start.56) | collective-permute-done | bytes 458784 | tf_op jit(solution)/shard_map/ppermute | solution.py:1170
  432.8 25.4 %collective-permute-done.60 = bf16[128,896]{1,0:T(8,128)(2,1)S(1)} collective-permute-done((bf16[128,896]{1,0:T(8,128)(2,1)S(1)}, bf16[128,896]{1,0:T(8,128)(2,1)S(1)}, u32[]{:S(2)}, u32[]{:S(2)}) %collective-permute-start.60) | collective-permute-done | bytes 229408 | tf_op jit(solution)/shard_map/ppermute | solution.py:1170
  482.4 5.8 %collective-permute-done.62.refs_2_ = bf16[128,896]{1,0:T(8,128)(2,1)} collective-permute-done((bf16[128,896]{1,0:T(8,128)(2,1)}, bf16[128,896]{1,0:T(8,128)(2,1)}, u32[]{:S(2)}, u32[]{:S(2)}) %collective-permute-start.62) | collective-permute-done | bytes 229408 | tf_op jit(solution)/shard_map/ppermute | solution.py:1170
  519.0 5.8 %collective-permute-done.74 = f32[8,128]{1,0:T(8,128)S(1)} collective-permute-done((f32[8,128]{1,0:T(8,128)S(1)}, f32[8,128]{1,0:T(8,128)S(1)}, u32[]{:S(2)}, u32[]{:S(2)}) %collective-permute-start.74) | collective-permute-done | bytes 4128 | tf_op jit(solution)/shard_map/ppermute | solution.py:1174
  (371 shorter events, 248.8 us)
Async XLA Ops:
  14.4 35.8 %collective-permute-start.4 = (bf16[6144,128]{1,0:T(8,128)(2,1)}, bf16[6144,128]{1,0:T(8,128)(2,1)S(1)}, u32[]{:S(2)}, u32[]{:S(2)}) collective-permute-start(bf16[6144,128]{1,0:T(8,128)(2,1)} %get-tuple-element.89.refs_0_.refs_10_.refs_3_.refs_11_), channel_id=1, source_target_pairs={{0,2},{1,3},{2,0},{3,1},{4,6},{5,7},{6,4},{7,5},{8,10},{9,11},{10,... | collective-permute-start | bytes 4718600 | tf_op jit(solution)/shard_map/ppermute | solution.py:1174
  15.9 34.3 %collective-permute-start.3 = (bf16[3072,128]{1,0:T(8,128)(2,1)}, bf16[3072,128]{1,0:T(8,128)(2,1)}, u32[]{:S(2)}, u32[]{:S(2)}) collective-permute-start(bf16[3072,128]{1,0:T(8,128)(2,1)} %get-tuple-element.91), channel_id=1, source_target_pairs={{0,16},{4,20},{8,24},{12,28},{16,0},{20,4},{24,8},{28,12},{1,17},{... | collective-permute-start | bytes 2359304 | tf_op jit(solution)/shard_map/ppermute | solution.py:1170
  50.2 51.9 %collective-permute-start.16 = (bf16[6144,128]{1,0:T(8,128)(2,1)S(1)}, bf16[6144,128]{1,0:T(8,128)(2,1)}, u32[]{:S(2)}, u32[]{:S(2)}) collective-permute-start(bf16[6144,128]{1,0:T(8,128)(2,1)S(1)} %copy-done.3), channel_id=1, source_target_pairs={{0,1},{1,0},{2,3},{3,2},{4,5},{5,4},{6,7},{7,6},{8,9},{9,8},{10,11... | collective-permute-start | bytes 4718600 | tf_op jit(solution)/shard_map/ppermute | solution.py:1178
  55.7 42.5 %collective-permute-start.7 = (bf16[3072,128]{1,0:T(8,128)(2,1)}, bf16[3072,128]{1,0:T(8,128)(2,1)}, u32[]{:S(2)}, u32[]{:S(2)}) collective-permute-start(bf16[3072,128]{1,0:T(8,128)(2,1)} %get-tuple-element.95), channel_id=1, source_target_pairs={{0,16},{4,20},{8,24},{12,28},{16,0},{20,4},{24,8},{28,12},{1,17},{... | collective-permute-start | bytes 2359304 | tf_op jit(solution)/shard_map/ppermute | solution.py:1170
  66.4 33.3 %collective-permute-start.8 = (bf16[128,1024]{1,0:T(8,128)(2,1)S(1)}, bf16[128,1024]{1,0:T(8,128)(2,1)}, u32[]{:S(2)}, u32[]{:S(2)}) collective-permute-start(bf16[128,1024]{1,0:T(8,128)(2,1)S(1)} %get-tuple-element.213.refs_0_), channel_id=1, source_target_pairs={{0,8},{4,12},{8,0},{12,4},{16,24},{20,28},{24,16},{28,20},{1,9},{5... | collective-permute-start | bytes 786440 | tf_op jit(solution)/shard_map/ppermute | solution.py:1170
  69.2 30.5 %collective-permute-start.9 = (bf16[128,1024]{1,0:T(8,128)(2,1)S(1)}, bf16[128,1024]{1,0:T(8,128)(2,1)S(1)}, u32[]{:S(2)}, u32[]{:S(2)}) collective-permute-start(bf16[128,1024]{1,0:T(8,128)(2,1)S(1)} %get-tuple-element.213.refs_0_), channel_id=1, source_target_pairs={{0,4},{4,0},{8,12},{12,8},{16,20},{20,16},{24,28},{28,24},{1,5},{5... | collective-permute-start | bytes 786440 | tf_op jit(solution)/shard_map/ppermute | solution.py:1170
  70.7 33.0 %collective-permute-start.10 = (bf16[128,1024]{1,0:T(8,128)(2,1)S(1)}, bf16[128,1024]{1,0:T(8,128)(2,1)S(1)}, u32[]{:S(2)}, u32[]{:S(2)}) collective-permute-start(bf16[128,1024]{1,0:T(8,128)(2,1)S(1)} %get-tuple-element.213.refs_0_), channel_id=1, source_target_pairs={{0,16},{4,20},{8,24},{12,28},{16,0},{20,4},{24,8},{28,12},{1,17},{... | collective-permute-start | bytes 786440 | tf_op jit(solution)/shard_map/ppermute | solution.py:1170
  99.7 30.5 %collective-permute-start.19 = (bf16[3072,128]{1,0:T(8,128)(2,1)}, bf16[3072,128]{1,0:T(8,128)(2,1)}, u32[]{:S(2)}, u32[]{:S(2)}) collective-permute-start(bf16[3072,128]{1,0:T(8,128)(2,1)} %collective-permute-done.3.refs_14_.refs_15_), channel_id=1, source_target_pairs={{0,2},{1,3},{2,0},{3,1},{4,6},{5,7},{6,4},{7,5},{8,10},{9,11},{10,... | collective-permute-start | bytes 2359304 | tf_op jit(solution)/shard_map/ppermute | solution.py:1174
  100.9 35.1 %collective-permute-start.22 = (bf16[3072,128]{1,0:T(8,128)(2,1)}, bf16[3072,128]{1,0:T(8,128)(2,1)}, u32[]{:S(2)}, u32[]{:S(2)}) collective-permute-start(bf16[3072,128]{1,0:T(8,128)(2,1)} %collective-permute-done.7.refs_7_.refs_19_), channel_id=1, source_target_pairs={{0,2},{1,3},{2,0},{3,1},{4,6},{5,7},{6,4},{7,5},{8,10},{9,11},{10,... | collective-permute-start | bytes 2359304 | tf_op jit(solution)/shard_map/ppermute | solution.py:1174
  102.1 35.6 %collective-permute-start.17 = (bf16[6144,128]{1,0:T(8,128)(2,1)S(1)}, bf16[6144,128]{1,0:T(8,128)(2,1)}, u32[]{:S(2)}, u32[]{:S(2)}) collective-permute-start(bf16[6144,128]{1,0:T(8,128)(2,1)S(1)} %collective-permute-done.4.refs_12_.refs_5_.refs_13_), channel_id=1, source_target_pairs={{0,1},{1,0},{2,3},{3,2},{4,5},{5,4},{6,7},{7,6},{8,9},{9,8},{10,11... | collective-permute-start | bytes 4718600 | tf_op jit(solution)/shard_map/ppermute | solution.py:1178
  130.2 26.2 %collective-permute-start.21 = (bf16[3072,128]{1,0:T(8,128)(2,1)}, bf16[3072,128]{1,0:T(8,128)(2,1)}, u32[]{:S(2)}, u32[]{:S(2)}) collective-permute-start(bf16[3072,128]{1,0:T(8,128)(2,1)} %collective-permute-done.7.refs_7_.refs_19_), channel_id=1, source_target_pairs={{0,1},{1,0},{2,3},{3,2},{4,5},{5,4},{6,7},{7,6},{8,9},{9,8},{10,11... | collective-permute-start | bytes 2359304 | tf_op jit(solution)/shard_map/ppermute | solution.py:1178
  296.6 60.1 %collective-permute-start.49 = (bf16[2,2,2,512,128]{4,3,2,1,0:T(8,128)(2,1)}, bf16[2,2,2,512,128]{4,3,2,1,0:T(8,128)(2,1)}, u32[]{:S(2)}, u32[]{:S(2)}) collective-permute-start(bf16[2,2,2,512,128]{4,3,2,1,0:T(8,128)(2,1)} %get-tuple-element.126.refs_0_), channel_id=1, source_target_pairs={{0,1},{1,0},{2,3},{3,2},{4,5},{5,4},{6,7},{7,6},{8,9},{9,8},{10,11... | collective-permute-start | bytes 3145736 | tf_op jit(solution)/shard_map/ppermute | solution.py:1178
  322.6 40.1 %collective-permute-start.50 = (bf16[2,4,128,512]{3,2,1,0:T(8,128)(2,1)}, bf16[2,4,128,512]{3,2,1,0:T(8,128)(2,1)}, u32[]{:S(2)}, u32[]{:S(2)}) collective-permute-start(bf16[2,4,128,512]{3,2,1,0:T(8,128)(2,1)} %get-tuple-element.128.refs_0_), channel_id=1, source_target_pairs={{0,1},{1,0},{2,3},{3,2},{4,5},{5,4},{6,7},{7,6},{8,9},{9,8},{10,11... | collective-permute-start | bytes 3145736 | tf_op jit(solution)/shard_map/ppermute | solution.py:1178
  341.1 26.8 %collective-permute-start.46 = (bf16[128,1024]{1,0:T(8,128)(2,1)}, bf16[128,1024]{1,0:T(8,128)(2,1)S(1)}, u32[]{:S(2)}, u32[]{:S(2)}) collective-permute-start(bf16[128,1024]{1,0:T(8,128)(2,1)} %get-tuple-element.130.refs_0_.first), channel_id=1, source_target_pairs={{0,1},{1,0},{2,3},{3,2},{4,5},{5,4},{6,7},{7,6},{8,9},{9,8},{10,11... | collective-permute-start | bytes 786440 | tf_op jit(solution)/shard_map/ppermute | solution.py:1178
  356.7 34.2 %collective-permute-start.53 = (bf16[2,2,512,128]{3,2,1,0:T(8,128)(2,1)S(1)}, bf16[2,2,512,128]{3,2,1,0:T(8,128)(2,1)S(1)}, u32[]{:S(2)}, u32[]{:S(2)}) collective-permute-start(bf16[2,2,512,128]{3,2,1,0:T(8,128)(2,1)S(1)} %copy-done.23), channel_id=1, source_target_pairs={{0,16},{4,20},{8,24},{12,28},{16,0},{20,4},{24,8},{28,12},{1,17},{... | collective-permute-start | bytes 1572872 | tf_op jit(solution)/shard_map/ppermute | solution.py:1170
  362.1 26.1 %collective-permute-start.54 = (bf16[2,2,512,128]{3,2,1,0:T(8,128)(2,1)}, bf16[2,2,512,128]{3,2,1,0:T(8,128)(2,1)}, u32[]{:S(2)}, u32[]{:S(2)}) collective-permute-start(bf16[2,2,512,128]{3,2,1,0:T(8,128)(2,1)} %get-tuple-element.132.refs_0_), channel_id=1, source_target_pairs={{0,2},{1,3},{2,0},{3,1},{4,6},{5,7},{6,4},{7,5},{8,10},{9,11},{10,... | collective-permute-start | bytes 1572872 | tf_op jit(solution)/shard_map/ppermute | solution.py:1174
  379.6 36.8 %collective-permute-start.29 = (bf16[128,1024]{1,0:T(8,128)(2,1)S(1)}, bf16[128,1024]{1,0:T(8,128)(2,1)}, u32[]{:S(2)}, u32[]{:S(2)}) collective-permute-start(bf16[128,1024]{1,0:T(8,128)(2,1)S(1)} %fusion.43.refs_0_), channel_id=1, source_target_pairs={{0,1},{1,0},{2,3},{3,2},{4,5},{5,4},{6,7},{7,6},{8,9},{9,8},{10,11... | collective-permute-start | bytes 786440 | tf_op jit(solution)/shard_map/ppermute | solution.py:1178
  380.2 99.4 %collective-permute-start.75 = (bf16[2,4,2,512,128]{4,3,2,1,0:T(8,128)(2,1)}, bf16[2,4,2,512,128]{4,3,2,1,0:T(8,128)(2,1)S(1)}, u32[]{:S(2)}, u32[]{:S(2)}) collective-permute-start(bf16[2,4,2,512,128]{4,3,2,1,0:T(8,128)(2,1)} %get-tuple-element.135.refs_2_), channel_id=1, source_target_pairs={{0,1},{1,0},{2,3},{3,2},{4,5},{5,4},{6,7},{7,6},{8,9},{9,8},{10,11... | collective-permute-start | bytes 6291464 | tf_op jit(solution)/shard_map/ppermute | solution.py:1178
  414.5 57.1 %collective-permute-start.77 = (bf16[2,4,128,512]{3,2,1,0:T(8,128)(2,1)S(1)}, bf16[2,4,128,512]{3,2,1,0:T(8,128)(2,1)S(1)}, u32[]{:S(2)}, u32[]{:S(2)}) collective-permute-start(bf16[2,4,128,512]{3,2,1,0:T(8,128)(2,1)S(1)} %copy-done.66), channel_id=1, source_target_pairs={{0,1},{1,0},{2,3},{3,2},{4,5},{5,4},{6,7},{7,6},{8,9},{9,8},{10,11... | collective-permute-start | bytes 3145736 | tf_op jit(solution)/shard_map/ppermute | solution.py:1178
  416.4 55.6 %collective-permute-start.80 = (bf16[4,128,512]{2,1,0:T(8,128)(2,1)S(1)}, bf16[4,128,512]{2,1,0:T(8,128)(2,1)S(1)}, u32[]{:S(2)}, u32[]{:S(2)}) collective-permute-start(bf16[4,128,512]{2,1,0:T(8,128)(2,1)S(1)} %add_convert_fusion), channel_id=1, source_target_pairs={{0,16},{4,20},{8,24},{12,28},{16,0},{20,4},{24,8},{28,12},{1,17},{... | collective-permute-start | bytes 1572872 | tf_op jit(solution)/shard_map/ppermute | solution.py:1170
  427.4 30.8 %collective-permute-start.60 = (bf16[128,896]{1,0:T(8,128)(2,1)S(1)}, bf16[128,896]{1,0:T(8,128)(2,1)S(1)}, u32[]{:S(2)}, u32[]{:S(2)}) collective-permute-start(bf16[128,896]{1,0:T(8,128)(2,1)S(1)} %get-tuple-element.223), channel_id=1, source_target_pairs={{0,24},{4,28},{8,16},{12,20},{16,8},{20,12},{24,0},{28,4},{1,25},{... | collective-permute-start | bytes 688136 | tf_op jit(solution)/shard_map/ppermute | solution.py:1170
  428.4 33.1 %collective-permute-start.59 = (bf16[128,896]{1,0:T(8,128)(2,1)S(1)}, bf16[128,896]{1,0:T(8,128)(2,1)S(1)}, u32[]{:S(2)}, u32[]{:S(2)}) collective-permute-start(bf16[128,896]{1,0:T(8,128)(2,1)S(1)} %get-tuple-element.222), channel_id=1, source_target_pairs={{0,16},{4,20},{8,24},{12,28},{16,0},{20,4},{24,8},{28,12},{1,17},{... | collective-permute-start | bytes 688136 | tf_op jit(solution)/shard_map/ppermute | solution.py:1170
  475.3 25.4 %collective-permute-start.64 = (bf16[128,896]{1,0:T(8,128)(2,1)}, bf16[128,896]{1,0:T(8,128)(2,1)}, u32[]{:S(2)}, u32[]{:S(2)}) collective-permute-start(bf16[128,896]{1,0:T(8,128)(2,1)} %add_convert_fusion.8.refs_0_), channel_id=1, source_target_pairs={{0,4},{4,0},{8,12},{12,8},{16,20},{20,16},{24,28},{28,24},{1,5},{5... | collective-permute-start | bytes 688136 | tf_op jit(solution)/shard_map/ppermute | solution.py:1170
  479.6 30.0 %collective-permute-start.78 = (bf16[4,128,512]{2,1,0:T(8,128)(2,1)}, bf16[4,128,512]{2,1,0:T(8,128)(2,1)}, u32[]{:S(2)}, u32[]{:S(2)}) collective-permute-start(bf16[4,128,512]{2,1,0:T(8,128)(2,1)} %get-tuple-element.164), channel_id=1, source_target_pairs={{0,2},{1,3},{2,0},{3,1},{4,6},{5,7},{6,4},{7,5},{8,10},{9,11},{10,... | collective-permute-start | bytes 1572872 | tf_op jit(solution)/shard_map/ppermute | solution.py:1174
  (125 other events, 1745.6 us)

commit v5 on v4

--- a/solution.py
+++ b/solution.py
@@ -575,7 +575,9 @@
 def forward_second(half_ref, *refs):
     rows_ref, gate_ref, start_ref = refs[:3]
     packs = refs[3:11]
-    keep_ref, near_ref, far_ref, pre_ref, gated_ref, acc, in_buf, out_buf, sems = refs[13:]
+    pre_ref, gated_ref = refs[-6:-4]
+    targets = refs[13:-6]
+    acc, in_buf, out_buf, sems = refs[-4:]
     step, slot, wait = stream_weights(2, packs, half_ref[0], in_buf, out_buf, sems)
     row_count, width = acc.shape
 
@@ -591,31 +593,37 @@
 
     @pl.when(step == 0)
     def _():
-        chunk_loop(row_count, lambda rows: mlp(rows, start_ref))
-
-    @pl.when(step > 0)
-    def _():
-        chunk_loop(row_count, lambda rows: mlp(rows, acc))
+        acc[...] = start_ref[...]
+
+    chunk_loop(row_count, lambda rows: mlp(rows, acc))
 
     @pl.when(step == pl.num_programs(0) - 1)
     def _():
-        spread(acc, keep_ref, near_ref, far_ref)
-
-
-def spread(acc, keep_ref, near_ref, far_ref):
-    part = acc.shape[0] // 4
-    keep_ref[...] = acc[: 2 * part, :]
-    near_ref[...] = acc[2 * part : 3 * part, :].astype(BF16)
-    far_ref[...] = acc[3 * part :, :].astype(BF16)
-
-
-def spread_specs(row_count, width):
-    shapes = [
-        jax.ShapeDtypeStruct((row_count // 2, width), F32),
-        jax.ShapeDtypeStruct((row_count // 4, width), BF16),
-        jax.ShapeDtypeStruct((row_count // 4, width), BF16),
-    ]
+        spread(acc, targets)
+
+
+def spread(acc, targets):
+    size = acc.shape[0] // len(targets)
+    for i, target in enumerate(targets):
+        target[...] = acc[i * size : (i + 1) * size, :].astype(target.dtype)
+
+
+def spread_specs(part, row_count, width):
+    if part == 0:
+        shapes = [jax.ShapeDtypeStruct((row_count // 2, width), F32)]
+    else:
+        shapes = [jax.ShapeDtypeStruct((row_count // 4, width), BF16)] * 2
     return ([whole_block(s.shape) for s in shapes], shapes)
+
+
+def half_rows(shape, part):
+    block = (shape[0] // 2,) + shape[1:]
+    return pl.BlockSpec(block, lambda e, *_: (part, 0))
+
+
+def half_expert(shape, part, first=0):
+    block = (1, shape[1] // 2) + shape[2:]
+    return pl.BlockSpec(block, lambda e, *_: (e + first, part, 0))
 
 
 def expert_block(shape, first=0):
@@ -651,36 +659,46 @@
         out_shape=[sums, pre, gated, gates, rows],
         name="experts_forward_a",
     )(half_index, *shards, route_ids, router, *own, *near)
-    specs, shapes = spread_specs(row_count, width)
-    keep, send_near, send_far, pre, gated = pl.pallas_call(
-        forward_second,
-        grid_spec=pltpu.PrefetchScalarGridSpec(
-            num_scalar_prefetch=1,
-            grid=(2,),
-            in_specs=[whole_block(v.shape) for v in (rows, gates, sums)] + [any_block()] * 10,
-            out_specs=specs + [expert_block(pre.shape, 2), expert_block(gated.shape, 2)],
-            scratch_shapes=[pltpu.VMEM((row_count, width), F32)] + weight_scratch(width, hidden),
-        ),
-        out_shape=shapes + [pre, gated],
-        input_output_aliases={12: 3, 13: 4},
-        name="experts_forward_b",
-    )(half_index, rows, gates, sums_a, *own, *far, pre_a, gated_a)
-    return (keep, send_near, send_far, pre, gated, gates, rows)
+
+    def second(part, pre_a, gated_a):
+        specs, shapes = spread_specs(part, row_count, width)
+        return pl.pallas_call(
+            forward_second,
+            grid_spec=pltpu.PrefetchScalarGridSpec(
+                num_scalar_prefetch=1,
+                grid=(2,),
+                in_specs=[half_rows(v.shape, part) for v in (rows, gates, sums)]
+                + [any_block()] * 10,
+                out_specs=specs
+                + [half_expert(pre.shape, part, 2), half_expert(gated.shape, part, 2)],
+                scratch_shapes=[pltpu.VMEM((row_count // 2, width), F32)]
+                + weight_scratch(width, hidden),
+            ),
+            out_shape=shapes + [pre, gated],
+            input_output_aliases={12: len(shapes), 13: len(shapes) + 1},
+            name="experts_forward_b",
+        )(half_index, rows, gates, sums_a, *own, *far, pre_a, gated_a)
+
+    send_near, send_far, pre_a, gated_a = second(1, pre_a, gated_a)
+    keep, pre_a, gated_a = second(0, pre_a, gated_a)
+    return (keep, send_near, send_far, pre_a, gated_a, gates, rows)
 
 
 def backward_body(half_ref, *refs):
-    shards = refs[:8]
-    gate_ref, router_ref, pre_ref = refs[8:11]
-    packs = refs[11:23]
-    keep_ref, near_ref, far_ref, pre_grad_ref, logit_ref, grad_ref = refs[-10:-4]
+    shards = refs[:4]
+    gate_ref, router_ref, pre_ref = refs[4:7]
+    packs = refs[7:19]
+    pre_grad_ref, logit_ref, grad_ref = refs[-7:-4]
     acc, in_buf, out_buf, sems = refs[-4:]
     step, slot, wait = stream_weights(0, packs, half_ref[0], in_buf, out_buf, sems)
     row_count, width = grad_ref.shape
-    size = row_count // 8
+    size = row_count // 4
+    targets = [ref for ref in refs[19:-7] if ref.shape[0] * 2 == row_count]
+    targets = targets or [refs[-8]]
 
     @pl.when(step == 0)
     def _():
-        for i in range(8):
+        for i in range(4):
             grad_ref[i * size : (i + 1) * size, :] = shards[i][...]
         acc[...] = jnp.zeros_like(acc)
         logit_ref[...] = jnp.zeros_like(logit_ref)
@@ -722,47 +740,52 @@
             )
 
         chunk_loop(row_count, router)
-        spread(acc, keep_ref, near_ref, far_ref)
-
-
-def experts_backward(half_index, shards, gates, router, pre, own, near, far, *after):
+        spread(acc, targets)
+
+
+def experts_backward(part, half_index, shards, gates, router, pre, own, near, far, *before):
     row_count, width = (8 * shards[0].shape[0], shards[0].shape[1])
     local = pre.shape[0]
-    specs, shapes = spread_specs(row_count, width)
+    specs, shapes = spread_specs(part, row_count, width)
+    saved = [
+        jax.ShapeDtypeStruct(pre.shape, BF16),
+        jax.ShapeDtypeStruct((row_count, 128), F32),
+        jax.ShapeDtypeStruct((row_count, width), BF16),
+    ]
     return pl.pallas_call(
         backward_body,
         grid_spec=pltpu.PrefetchScalarGridSpec(
             num_scalar_prefetch=1,
             grid=(local,),
-            in_specs=[whole_block(v.shape) for v in (*shards, gates, router)]
-            + [expert_block(pre.shape)]
-            + [any_block()] * (12 + len(after)),
+            in_specs=[whole_block(v.shape) for v in shards]
+            + [half_rows(gates.shape, part), whole_block(router.shape)]
+            + [half_expert(pre.shape, part)]
+            + [any_block()] * (12 + len(before)),
             out_specs=specs
-            + [
-                expert_block(pre.shape),
-                whole_block((row_count, 128)),
-                whole_block((row_count, width)),
-            ],
-            scratch_shapes=[pltpu.VMEM((row_count, width), F32)]
+            + [half_expert(pre.shape, part)]
+            + [half_rows(v.shape, part) for v in saved[1:]],
+            scratch_shapes=[pltpu.VMEM((row_count // 2, width), F32)]
             + weight_scratch(width, 4 * SHARE),
         ),
-        out_shape=shapes
-        + [
-            jax.ShapeDtypeStruct(pre.shape, BF16),
-            jax.ShapeDtypeStruct((row_count, 128), F32),
-            jax.ShapeDtypeStruct((row_count, width), BF16),
-        ],
+        out_shape=shapes + saved,
+        input_output_aliases={20 + i: len(shapes) + i for i in range(len(before))},
         name="experts_backward",
-    )(half_index, *shards, gates, router, pre, *own, *near, *far, *after)
+    )(half_index, *shards, gates, router, pre, *own, *near, *far, *before)
 
 
 def grad_out_body(half_ref, gated_ref, other_ref, mine_ref, *refs):
-    outs = refs[-4:]
-    turned = gated_ref[0].T
-    for n, source in ((0, other_ref), (2, mine_ref)):
-        product = jnp.dot(turned, source[...], preferred_element_type=F32).astype(BF16)
-        for q in range(4):
-            outs[n + q % 2][q // 2, 0] = product[q * SHARE : (q + 1) * SHARE, :]
+    *outs, turned = refs[-5:]
+    turned[...] = gated_ref[0].T
+
+    def pair(q, carry):
+        for n, source in ((0, other_ref), (2, mine_ref)):
+            for odd in range(2):
+                rows = pl.ds(pl.multiple_of((2 * q + odd) * SHARE, SHARE), SHARE)
+                product = jnp.dot(turned[rows, :], source[...], preferred_element_type=F32)
+                outs[n + odd][q, 0] = product.astype(BF16)
+        return carry
+
+    lax.fori_loop(0, 2, pair, 0)
 
 
 def grad_expert_outs(half_index, gated, grads, *after):
@@ -782,6 +805,7 @@
             ]
             + [any_block()] * len(after),
             out_specs=[pl.BlockSpec((2, 1) + shape[2:], lambda e, *_: (0, e, 0, 0))] * 4,
+            scratch_shapes=[pltpu.VMEM((hidden, row_count), BF16)],
         ),
         out_shape=[jax.ShapeDtypeStruct(shape, BF16)] * 4,
         name="grad_expert_out",
@@ -795,11 +819,16 @@
     def _():
         turned[...] = rows_ref[...].T
 
-    product = jnp.dot(turned[...], pre_ref[0], preferred_element_type=F32).astype(BF16)
-    for q in range(4):
-        for c in range(2):
-            start = (2 * q + c) * SHARE
-            (keep_ref, send_ref)[q % 2][q // 2, 0, c] = product[:, start : start + SHARE]
+    def part(i, carry):
+        rows = pl.ds(pl.multiple_of(i * CHUNK, CHUNK), CHUNK)
+        product = jnp.dot(turned[rows, :], pre_ref[0], preferred_element_type=F32).astype(BF16)
+        for q in range(4):
+            for c in range(2):
+                start = (2 * q + c) * SHARE
+                (keep_ref, send_ref)[q % 2][q // 2, 0, c, rows] = product[:, start : start + SHARE]
+        return carry
+
+    lax.fori_loop(0, turned.shape[0] // CHUNK, part, 0)
 
 
 def grad_expert_ins(half_index, rows, pre_grad, first, count, *after):
@@ -1072,12 +1101,14 @@
     )
 
 
-def reduce_body(place_ref, normed, grad_qkv, grad, attended, small, *refs):
+def reduce_body(place_ref, normed, grad_qkv, grad, attended, small, gain, *refs):
     keep, near, far = refs[-3:]
     step = pl.program_id(0)
     first = lax.dot_general(normed[...], grad_qkv[...], TN, preferred_element_type=F32)
     second = lax.dot_general(grad[...], attended[...], TN, preferred_element_type=F32)
-    part = jnp.concatenate([first, second, small[...]], 1)
+    rest = jnp.zeros((SHARE - small.shape[0] - gain.shape[0], SHARE), F32)
+    third = jnp.concatenate([small[...], gain[...], rest], 0).T
+    part = jnp.concatenate([first, second, third], 1)
 
     @pl.when(step < 4)
     def _():
@@ -1092,10 +1123,10 @@
         far[...] = part.astype(BF16)
 
 
-def reduce_parts(place, normed, grad_qkv, grad, attended, small, *after):
+def reduce_parts(place, normed, grad_qkv, grad, attended, small, gain, *after):
     rows, width = normed.shape
     size = width // 8
-    total = grad_qkv.shape[1] + attended.shape[1] + small.shape[1]
+    total = grad_qkv.shape[1] + attended.shape[1] + SHARE
 
     def shard(e, place):
         order = jnp.where(e < 4, 2 * e, 2 * e - 7)
@@ -1112,7 +1143,8 @@
                 whole_block(grad_qkv.shape),
                 columns,
                 whole_block(attended.shape),
-                pl.BlockSpec((size, small.shape[1]), lambda e, place: (shard(e, place), 0)),
+                pl.BlockSpec((small.shape[0], size), lambda e, place: (0, shard(e, place))),
+                pl.BlockSpec((gain.shape[0], size), lambda e, place: (0, shard(e, place))),
             ]
             + [any_block()] * len(after),
             out_specs=[
@@ -1127,7 +1159,7 @@
             jax.ShapeDtypeStruct((2 * size, total), BF16),
         ],
         name="reduce_parts",
-    )(place, normed, grad_qkv, grad, attended, small, *after)
+    )(place, normed, grad_qkv, grad, attended, small, gain, *after)
 
 
 def unpack_body(place_ref, *refs):
@@ -1186,19 +1218,19 @@
 def scatter_steps(keep, send_near, send_far, *beside):
     size = keep.shape[0] // 4
     got_far = trade(send_far, 1)
-    send_near, got_far = lax.optimization_barrier((send_near, got_far))
+    send_near, got_far, keep = lax.optimization_barrier((send_near, got_far, keep))
     if beside:
         got_far, *beside = lax.optimization_barrier((got_far, *beside))
     far = (keep[2 * size :] + got_far.astype(F32)).astype(BF16)
     got_near = trade(send_near, 1)
     four, six = (trade(far[:size], 4), trade(far[size:], 6))
     near = (keep[size : 2 * size] + got_near[size:].astype(F32)).astype(BF16)
-    return (got_near, near, far, (trade(near, 2), four, six), *beside)
+    return (keep, got_near, near, far, (trade(near, 2), four, six), *beside)
 
 
 def scatter_experts(keep, send_near, send_far, *beside):
     size = keep.shape[0] // 4
-    got_near, _, _, back, *beside = scatter_steps(keep, send_near, send_far, *beside)
+    keep, got_near, _, _, back, *beside = scatter_steps(keep, send_near, send_far, *beside)
     total = keep[:size] + got_near[:size].astype(F32)
     for part in back:
         total = total + part.astype(F32)
@@ -1276,18 +1308,12 @@
     local_valid = jnp.sum(valid_mask)
     routes_mine = quarter_of(routes)
     note = jnp.concatenate([routes_mine.T, jnp.full((TOP, quarter), local_valid, jnp.int32)], 0)
-    notes = [note] + [trade(note, bits) for bits in (2, 4, 6)]
-
-    own_pack, near_pack, far_pack = pack_weights(half_arg, expert_in, expert_out, *notes[1:])
+
+    own_pack, near_pack, far_pack = pack_weights(half_arg, expert_in, expert_out)
     near_pack = trade(near_pack, 4)
     far_pack = trade(far_pack, 4)
     own_across = swap_y(own_pack)
 
-    notes = jnp.stack(notes)
-    notes = jnp.concatenate([notes, trade(notes, 1)], 0)
-    valid_total = jnp.sum(notes[:, TOP, 0]).astype(F32)
-    route_rel = jnp.bitwise_and(notes[:, :TOP] - base, expert_count - 1)
-    route_rel = route_rel.transpose(0, 2, 1).reshape(senders * quarter, TOP)
     router_rel = lax.dynamic_slice_in_dim(
         jnp.concatenate([router_weight, router_weight], 1), base, expert_count, 1
     )
@@ -1308,17 +1334,28 @@
     )
     own = [own_pack, swap_core(own_pack), own_across, swap_core(own_across)]
     tokens_mine = quarter_of(tokens).astype(F32)
-    hidden = tokens_mine + RESIDUAL * scatter_tensor(attn_keep, attn_send, row)
+    near_across = swap_y(near_pack)
+    attn_sum = scatter_tensor(attn_keep, attn_send, row)
+    near_across, attn_sum, note = lax.optimization_barrier((near_across, attn_sum, note))
+    hidden = tokens_mine + RESIDUAL * attn_sum
     scale_two = lax.rsqrt(jnp.mean(hidden * hidden, -1, keepdims=True) + EPS)
     unit_two = hidden * scale_two
     normed_two = (unit_two * second_gain).astype(BF16)
     column = [normed_two] + [trade(normed_two, bits) for bits in (2, 4, 6)]
+    notes = [note] + [trade(note, bits) for bits in (2, 4, 6)]
     beside = trade(normed_two, 1)
-    near_pack, far_pack, column[1], beside = lax.optimization_barrier(
-        (near_pack, far_pack, column[1], beside)
-    )
-    row_shards = column + [beside] + [trade(shard, 1) for shard in column[1:]]
-    near, far = (spread_tensor(near_pack), spread_tensor(far_pack))
+    across = [trade(shard, 1) for shard in column[1:]]
+    far_pack, beside, across[0], across[1], *gathered = lax.optimization_barrier(
+        (far_pack, beside, across[0], across[1], *column[1:])
+    )
+    row_shards = [normed_two, *gathered, beside, *across]
+    near = [near_pack, swap_core(near_pack), near_across, swap_core(near_across)]
+    far = spread_tensor(far_pack)
+    notes = jnp.stack(notes)
+    notes = jnp.concatenate([notes, trade(notes, 1)], 0)
+    valid_total = jnp.sum(notes[:, TOP, 0]).astype(F32)
+    route_rel = jnp.bitwise_and(notes[:, :TOP] - base, expert_count - 1)
+    route_rel = route_rel.transpose(0, 2, 1).reshape(senders * quarter, TOP)
     keep, send_near, send_far, pre, gated, gates, expert_rows = experts_forward(
         half_arg,
         row_shards,
@@ -1343,14 +1380,16 @@
     mean_part = jnp.concatenate([mean_high, (mean_part - mean_high.astype(F32)).astype(BF16)], 1)
     router_pair = jnp.concatenate([router_weight, router_weight], 1)
     mean_rows = jnp.einsum("te,de->td", mean_part, router_pair, preferred_element_type=F32)
-    keep, send_near, send_far, pre_grad, logit_grad, grad_rows = experts_backward(
-        half_arg, gather_experts(grad_moe), gates, router_rel, pre, own, near, far, mean_rows
-    )
-    got_near, near_rows, far_rows, back = scatter_steps(keep, send_near, send_far)
+    shards = gather_experts(grad_moe)
+    packs = (gates, router_rel, pre, own, near, far)
+    send_near, send_far, *saved = experts_backward(1, half_arg, shards[4:], *packs)
+    keep, pre_grad, logit_grad, grad_rows = experts_backward(
+        0, half_arg, shards[:4], *packs, *saved
+    )
+    keep, got_near, near_rows, far_rows, back = scatter_steps(keep, send_near, send_far)
     other = 1 - half_arg
-    in_keep, in_send = grad_expert_ins(other, expert_rows, pre_grad, 0, 2)
-    late_keep, late_send = grad_expert_ins(other, expert_rows, pre_grad, 2, 2, in_send)
-    in_near, in_far = fold_pairs(in_keep, swap_core(in_send), late_send, far_rows)
+    in_keep, in_send = grad_expert_ins(other, expert_rows, pre_grad, 0, 2, far_rows)
+    in_near, in_far = fold_pairs(in_keep, swap_core(in_send), near_rows)
     in_ready = (in_near + swap_y(in_far).astype(F32)).astype(BF16)
     out_keep, out_send, own_out_keep, own_out_send = grad_expert_outs(
         half_arg, gated, grad_rows, in_far
@@ -1368,26 +1407,6 @@
         in_ready,
     )
     grad_second_part = jnp.sum(grad_second_part, 0)
-    own_in_keep, own_in_send = grad_expert_ins(
-        half_arg, expert_rows, pre_grad, 0, held, grad_attn
-    )
-    pieces = spread_tensor(grad_attn)
-    late_near, late_far = fold_pairs(late_keep, swap_core(late_send), pieces[2])
-    out_near, out_far = fold_pairs(out_keep, swap_core(out_send), pieces[2])
-    out_ready = (out_near + swap_y(out_far).astype(F32)).astype(BF16)
-    out_back = trade(out_ready, 4)
-    late_ready = (late_near + swap_y(late_far).astype(F32)).astype(BF16)
-    grad_attn, grad_qkv, gain_part, one_keep, one_send = attention_backward(
-        share_arg, tokens, weights, tables, (query, keys, values), pieces, late_far, out_far, own_in_send
-    )
-    in_back = trade(in_ready, 4)
-    late_back = trade(late_ready, 4)
-    grad_one = scatter_tensor(one_keep, one_send, row)
-    own_out_near, own_out_far = fold_pairs(own_out_keep, swap_core(own_out_send), grad_one)
-    own_in_near, own_in_far = fold_pairs(own_in_keep, swap_core(own_in_send), grad_one)
-    own_out_across = swap_y(own_out_far)
-    own_in_across = swap_y(own_in_far)
-
     router_part = jnp.einsum(
         "te,td->ed", logit_grad.astype(BF16), expert_rows, preferred_element_type=F32
     )
@@ -1406,19 +1425,37 @@
             router_part,
             grad_second_part[None],
             jnp.full((1, model_width), squared_local),
+            jnp.zeros((6, model_width), F32),
         ],
         0,
     )
     small = small + swap_core(small)
     small = small + swap_y(small)
-    gain_part = jnp.sum(gain_part, 0).reshape(8, -1)
-    small = jnp.concatenate([small, gain_part.reshape(1, -1)], 0)
-    small = jnp.pad(small, ((0, 128 - small.shape[0]), (0, 0))).T
+    late_keep, late_send = grad_expert_ins(other, expert_rows, pre_grad, 2, 2, grad_attn)
+    pieces = spread_tensor(grad_attn)
+    late_near, late_far = fold_pairs(late_keep, swap_core(late_send), pieces[2])
+    out_near, out_far = fold_pairs(out_keep, swap_core(out_send), pieces[2])
+    out_ready = (out_near + swap_y(out_far).astype(F32)).astype(BF16)
+    late_ready = (late_near + swap_y(late_far).astype(F32)).astype(BF16)
+    in_back = trade(in_ready, 4)
+    grad_attn, grad_qkv, gain_part, one_keep, one_send = attention_backward(
+        share_arg, tokens, weights, tables, (query, keys, values), pieces, late_ready, in_back, out_far, small
+    )
+    late_back = trade(late_ready, 4)
+    grad_one = scatter_tensor(one_keep, one_send, row)
+    own_out_near, own_out_far = fold_pairs(own_out_keep, swap_core(own_out_send), grad_one)
+    own_out_across = swap_y(own_out_far)
+
     keep, send_near, send_far = reduce_parts(
-        place_arg, first_normed, grad_qkv, grad_attn, attended, small, in_back, late_ready
-    )
+        place_arg, first_normed, grad_qkv, grad_attn, attended, small, gain_part
+    )
+    own_in_keep, own_in_send = grad_expert_ins(
+        half_arg, expert_rows, pre_grad, 0, held, late_back
+    )
+    own_in_near, own_in_far = fold_pairs(own_in_keep, swap_core(own_in_send), grad_one)
+    own_in_across = swap_y(own_in_far)
     total, late_back = scatter_experts(keep, send_near, send_far, late_back)
-    total = total.astype(BF16)
+    total, own_out_across = lax.optimization_barrier((total.astype(BF16), own_out_across))
     shapes = [
         jax.ShapeDtypeStruct(shape, F32)
         for shape in (
@@ -1429,11 +1466,14 @@
             (model_width, 128),
         )
     ]
+    shards = gather_experts(total)
+    out_ready, shards[1] = lax.optimization_barrier((out_ready, shards[1]))
+    out_back = trade(out_ready, 4)
     grad_query, grad_key, grad_value, grad_output, small = scalar_call(
-        unpack_body, "unpack", place_arg, gather_experts(total), shapes
-    )
-
-    gain_part = small[:, expert_count + 2].reshape(8, -1)
+        unpack_body, "unpack", place_arg, shards, shapes
+    )
+
+    gain_part = jnp.sum(small[:, expert_count + 8 : expert_count + 16], 1).reshape(8, -1)
     gain_part = gain_part + swap_core(gain_part)
     gain_part = (gain_part + swap_y(gain_part)).reshape(-1)
 

time: 541 us -> 590 us (1.091)
  the two profiles are of different devices: /device:TPU:8 before, /device:TPU:0 now
where the time goes in v5:
time: 590 us; the launch traced here: 580 us
  waiting for transfers between devices  251 us (43%)
  Pallas kernels  168 us (28%)
  starting transfers between devices  82.6 us (14%)
  other arithmetic  48.9 us (8%)
  local copies, waits for them, and re-layouts  23.2 us (4%)
    ppermute x45, waiting for transfers between devices, trade(): return lax.ppermute(value, 'expert', [(i, i ^ bits) for i in range(8)])  198 us
    ppermute x45, starting transfers between devices, trade(): return lax.ppermute(value, 'expert', [(i, i ^ bits) for i in range(8)])  59.9 us
    ppermute x15, waiting for transfers between devices, swap_y(): return lax.ppermute(value, 'tensor', [(i, i ^ 2) for i in range(4)])  50.9 us
    pallas_call x2, Pallas kernels, experts_backward(): pl.pallas_call(backward_body, grid_spec=pltpu.PrefetchScalarGridSpec(num_...  36 us
    pallas_call x5, Pallas kernels, scalar_call(): pl.pallas_call(body, grid_spec=pltpu.PrefetchScalarGridSpec(num_scalar_pr...  27.6 us
    pallas_call x3, Pallas kernels, grad_expert_ins(): pl.pallas_call(grad_in_body, grid_spec=pltpu.PrefetchScalarGridSpec(num_s...  22.1 us
    pallas_call x2, Pallas kernels, second(): pl.pallas_call(forward_second, grid_spec=pltpu.PrefetchScalarGridSpec(num...  21.7 us
    ppermute x15, starting transfers between devices, swap_y(): return lax.ppermute(value, 'tensor', [(i, i ^ 2) for i in range(4)])  21.3 us
  transfers between devices with their start and end apart: 81, of which 36 were waited for; matrix products, arithmetic and copies ran while one was open for 9% of the time, Pallas kernels for 18%

profile of v5, /device:TPU:0, one launch (start us, length us, event | category | flops | bytes accessed | tf_op | source)
XLA Modules:
  0.0 579.8 jit_solution(17146259346301310795)
XLA Ops:
  12.9 8.2 %attention_forward.1 = (bf16[512,1024]{1,0:T(8,128)(2,1)}, bf16[512,256]{1,0:T(8,128)(2,1)}, bf16[512,128]{1,0:T(8,128)(2,1)}, bf16[512,128]{1,0:T(8,128)(2,1)},...) custom-call(s32[1]{0:T(128)} %bitcast.2.core_ref, bf16[512,1024]{1,0:T(8,128)(2,1)} %tokens.3, ...), custom_call_target="tpu_custom_call" | custom-call | tf_op jit(solution)/shard_map/attention_forward/pallas_call | solution.py:971
  21.2 24.0 %collective-permute-done.refs_14_.refs_11_ = bf16[3072,128]{1,0:T(8,128)(2,1)} collective-permute-done((bf16[3072,128]{1,0:T(8,128)(2,1)}, bf16[3072,128]{1,0:T(8,128)(2,1)}, u32[]{:S(2)}, u32[]{:S(2)}) %collective-permute-start) | collective-permute-done | bytes 786464 | tf_op jit(solution)/shard_map/ppermute | solution.py:1202
  52.9 18.0 %collective-permute-done.4 = bf16[128,1024]{1,0:T(8,128)(2,1)S(1)} collective-permute-done((bf16[128,1024]{1,0:T(8,128)(2,1)}, bf16[128,1024]{1,0:T(8,128)(2,1)S(1)}, u32[]{:S(2)}, u32[]{:S(2)}) %collective-permute-start.4) | collective-permute-done | bytes 262176 | tf_op jit(solution)/shard_map/ppermute | solution.py:1206
  79.7 20.3 %collective-permute-done.5.refs_7_.refs_15_ = bf16[3072,128]{1,0:T(8,128)(2,1)} collective-permute-done((bf16[3072,128]{1,0:T(8,128)(2,1)}, bf16[3072,128]{1,0:T(8,128)(2,1)}, u32[]{:S(2)}, u32[]{:S(2)}) %collective-permute-start.5) | collective-permute-done | bytes 786464 | tf_op jit(solution)/shard_map/ppermute | solution.py:1202
  108.5 6.6 %collective-permute-done.10.refs_6_ = bf16[128,1024]{1,0:T(8,128)(2,1)} collective-permute-done((bf16[128,1024]{1,0:T(8,128)(2,1)}, bf16[128,1024]{1,0:T(8,128)(2,1)}, u32[]{:S(2)}, u32[]{:S(2)}) %collective-permute-start.10) | collective-permute-done | bytes 262176 | tf_op jit(solution)/shard_map/ppermute | solution.py:1202
  148.6 17.6 %experts_forward_a.1 = (f32[1024,1024]{1,0:T(8,128)}, bf16[4,1024,1024]{2,1,0:T(8,128)(2,1)}, bf16[4,1024,512]{2,1,0:T(8,128)(2,1)}, f32[1024,128]{1,0:T(8,128)}, bf16[1024,1024]{1,0:T(8,128)(2,1)}) custom-call(s32[1]{0:T(128)} %bitcast.1.half_ref, bf16[128,1024]{1,0:T(8,128)(2,1)} %copy-done.14, bf16[128,1024]{1,0:T(8,128)(2,1)} %collective-permute-done.7.refs_1_, ...), custom_call_target="tpu_custom_call" | custom-call | tf_op jit(solution)/shard_map/experts_forward_a/pallas_call | solution.py:643
  167.4 10.8 %experts_forward_b.2 = (bf16[256,1024]{1,0:T(8,128)(2,1)}, bf16[256,1024]{1,0:T(8,128)(2,1)}, bf16[4,1024,1024]{2,1,0:T(8,128)(2,1)}, bf16[4,1024,512]{2,1,0:T(8,128)(2,1)}) custom-call(s32[1]{0:T(128)} %bitcast.1.half_ref, bf16[1024,1024]{1,0:T(8,128)(2,1)} %get-tuple-element.124.refs_0_.rows_ref, ...), custom_call_target="tpu_custom_call", output_to_operand_aliasing={{2}: (12, {}), {3}: (13, {})} | custom-call | tf_op jit(solution)/shard_map/experts_forward_b/pallas_call | solution.py:665
  179.8 11.0 %experts_forward_b.3 = (f32[512,1024]{1,0:T(8,128)}, bf16[4,1024,1024]{2,1,0:T(8,128)(2,1)}, bf16[4,1024,512]{2,1,0:T(8,128)(2,1)}) custom-call(s32[1]{0:T(128)} %bitcast.1.half_ref, bf16[1024,1024]{1,0:T(8,128)(2,1)} %get-tuple-element.124.refs_0_.rows_ref, ...), custom_call_target="tpu_custom_call", output_to_operand_aliasing={{1}: (12, {}), {2}: (13, {})} | custom-call | tf_op jit(solution)/shard_map/experts_forward_b/pallas_call | solution.py:665
  207.5 6.9 %collective-permute-done.27 = bf16[128,1024]{1,0:T(8,128)(2,1)S(1)} collective-permute-done((bf16[128,1024]{1,0:T(8,128)(2,1)}, bf16[128,1024]{1,0:T(8,128)(2,1)S(1)}, u32[]{:S(2)}, u32[]{:S(2)}) %collective-permute-start.27) | collective-permute-done | bytes 262176 | tf_op jit(solution)/shard_map/ppermute | solution.py:1202
  235.0 10.4 %collective-permute-done.35.refs_2_ = bf16[128,1024]{1,0:T(8,128)(2,1)S(1)} collective-permute-done((bf16[128,1024]{1,0:T(8,128)(2,1)S(1)}, bf16[128,1024]{1,0:T(8,128)(2,1)S(1)}, u32[]{:S(2)}, u32[]{:S(2)}) %collective-permute-start.35) | collective-permute-done | bytes 262176 | tf_op jit(solution)/shard_map/ppermute | solution.py:1202
  255.3 17.8 %experts_backward.2 = (bf16[256,1024]{1,0:T(8,128)(2,1)}, bf16[256,1024]{1,0:T(8,128)(2,1)}, bf16[4,1024,1024]{2,1,0:T(8,128)(2,1)}, f32[1024,128]{1,0:T(8,128)}, bf16[1024,1024]{1,0:T(8,128)(2,1)}) custom-call(s32[1]{0:T(128)} %bitcast.1.half_ref, bf16[128,1024]{1,0:T(8,128)(2,1)} %copy-done.49, bf16[128,1024]{1,0:T(8,128)(2,1)} %copy-done.50, ...), custom_call_target="tpu_custom_call" | custom-call | tf_op jit(solution)/shard_map/experts_backward/pallas_call | solution.py:755
  274.3 18.2 %experts_backward.3 = (f32[512,1024]{1,0:T(8,128)}, bf16[4,1024,1024]{2,1,0:T(8,128)(2,1)}, f32[1024,128]{1,0:T(8,128)}, bf16[1024,1024]{1,0:T(8,128)(2,1)}) custom-call(s32[1]{0:T(128)} %bitcast.1.half_ref, bf16[128,1024]{1,0:T(8,128)(2,1)} %copy-done.29, ...), custom_call_target="tpu_custom_call", output_to_operand_aliasing={{1}: (20, {}), {2}: (21, {}), {3}: (22, {})} | custom-call | tf_op jit(solution)/shard_map/experts_backward/pallas_call | solution.py:755
  302.9 12.6 %collective-permute-done.40.near = bf16[256,1024]{1,0:T(8,128)(2,1)S(1)} collective-permute-done((bf16[256,1024]{1,0:T(8,128)(2,1)}, bf16[256,1024]{1,0:T(8,128)(2,1)S(1)}, u32[]{:S(2)}, u32[]{:S(2)}) %collective-permute-start.40) | collective-permute-done | bytes 524320 | tf_op jit(solution)/shard_map/ppermute | solution.py:1202
  330.2 10.4 %grad_expert_out.1 = (bf16[2,4,128,512]{3,2,1,0:T(8,128)(2,1)}, bf16[2,4,128,512]{3,2,1,0:T(8,128)(2,1)}, bf16[2,4,128,512]{3,2,1,0:T(8,128)(2,1)}, bf16[2,4,128,512]{3,2,1,0:T(8,128)(2,1)}) custom-call(s32[1]{0:T(128)} %bitcast.1.half_ref, bf16[4,1024,512]{2,1,0:T(8,128)(2,1)} %get-tuple-element.152.gated_ref, ...), custom_call_target="tpu_custom_call" | custom-call | tf_op jit(solution)/shard_map/grad_expert_out/pallas_call | solution.py:796
  360.6 7.8 %collective-permute-done.47.refs_0_.third = bf16[128,1024]{1,0:T(8,128)(2,1)S(1)} collective-permute-done((bf16[128,1024]{1,0:T(8,128)(2,1)S(1)}, bf16[128,1024]{1,0:T(8,128)(2,1)S(1)}, u32[]{:S(2)}, u32[]{:S(2)}) %collective-permute-start.47) | collective-permute-done | bytes 262176 | tf_op jit(solution)/shard_map/ppermute | solution.py:1206
  377.8 10.4 %collective-permute-done.54 = f32[40,1024]{1,0:T(8,128)S(1)} collective-permute-done((f32[40,1024]{1,0:T(8,128)S(1)}, f32[40,1024]{1,0:T(8,128)S(1)}, u32[]{:S(2)}, u32[]{:S(2)}) %collective-permute-start.54) | collective-permute-done | bytes 163872 | tf_op jit(solution)/shard_map/ppermute | solution.py:1206
  399.0 10.7 %attention_backward.1 = (bf16[512,1024]{1,0:T(8,128)(2,1)}, bf16[512,512]{1,0:T(8,128)(2,1)}, f32[8,1024]{1,0:T(8,128)}, f32[2,128,1024]{2,1,0:T(8,128)}, bf16[2,128,1024]{2,1,0:T(8,128)(2,1)}) custom-call(s32[1]{0:T(128)} %bitcast.share_ref, bf16[512,1024]{1,0:T(8,128)(2,1)} %tokens.3, bf16[1024,256]{1,0:T(8,128)(2,1)} %query_w.3, bf16[1024,128]{1,0:T(8,128)(2,1)} %key_w.3, ...), custom_call_target="tpu_custom_call" | custom-call | tf_op jit(solution)/shard_map/attention_backward/pallas_call | solution.py:971
  409.8 7.8 %reduce_parts.1 = (f32[512,896]{1,0:T(8,128)}, bf16[256,896]{1,0:T(8,128)(2,1)}, bf16[256,896]{1,0:T(8,128)(2,1)}) custom-call(s32[1]{0:T(128)} %bitcast.13.place_ref, bf16[512,1024]{1,0:T(8,128)(2,1)} %get-tuple-element.138.normed, bf16[512,512]{1,0:T(8,128)(2,1)} %get-tuple-element.169.grad_qkv, bf16[512,1024]{1,0:T(8,128)(2,1)} %get-tuple-element.170.grad, ...), custom_call_target="tpu_custom_call" | custom-call | tf_op jit(solution)/shard_map/reduce_parts/pallas_call | solution.py:1136
  421.0 9.6 %collective-permute-done.55 = bf16[256,896]{1,0:T(8,128)(2,1)S(1)} collective-permute-done((bf16[256,896]{1,0:T(8,128)(2,1)}, bf16[256,896]{1,0:T(8,128)(2,1)S(1)}, u32[]{:S(2)}, u32[]{:S(2)}) %collective-permute-start.55) | collective-permute-done | bytes 458784 | tf_op jit(solution)/shard_map/ppermute | solution.py:1202
  436.1 8.5 %collective-permute-done.58.refs_0_ = bf16[2,2,512,128]{3,2,1,0:T(8,128)(2,1)S(1)} collective-permute-done((bf16[2,2,512,128]{3,2,1,0:T(8,128)(2,1)S(1)}, bf16[2,2,512,128]{3,2,1,0:T(8,128)(2,1)S(1)}, u32[]{:S(2)}, u32[]{:S(2)}) %collective-permute-start.58) | collective-permute-done | bytes 524320 | tf_op jit(solution)/shard_map/ppermute | solution.py:1202
  445.3 9.8 %grad_expert_in.5 = (bf16[2,4,2,512,128]{4,3,2,1,0:T(8,128)(2,1)}, bf16[2,4,2,512,128]{4,3,2,1,0:T(8,128)(2,1)}) custom-call(s32[1]{0:T(128)} %bitcast.1.half_ref, bf16[1024,1024]{1,0:T(8,128)(2,1)} %get-tuple-element.124.refs_0_.rows_ref, bf16[4,1024,1024]{2,1,0:T(8,128)(2,1)} %get-tuple-element.154.pre_ref, bf16[2,2,512,128]{3,2,1,0:T(8,128)(2,1)} %copy-done.24), custom_call_target="tpu_custom_call" | custom-call | tf_op jit(solution)/shard_map/grad_expert_in/pallas_call | solution.py:838
  474.7 14.0 %collective-permute-done.59 = bf16[128,896]{1,0:T(8,128)(2,1)S(1)} collective-permute-done((bf16[128,896]{1,0:T(8,128)(2,1)S(1)}, bf16[128,896]{1,0:T(8,128)(2,1)S(1)}, u32[]{:S(2)}, u32[]{:S(2)}) %collective-permute-start.59) | collective-permute-done | bytes 229408 | tf_op jit(solution)/shard_map/ppermute | solution.py:1202
  549.4 10.3 %collective-permute-done.77 = f32[8,128]{1,0:T(8,128)S(1)} collective-permute-done((f32[8,128]{1,0:T(8,128)S(1)}, f32[8,128]{1,0:T(8,128)S(1)}, u32[]{:S(2)}, u32[]{:S(2)}) %collective-permute-start.77) | collective-permute-done | bytes 4128 | tf_op jit(solution)/shard_map/ppermute | solution.py:1206
  560.3 10.6 %collective-permute-done.80 = bf16[4,128,512]{2,1,0:T(8,128)(2,1)} collective-permute-done((bf16[4,128,512]{2,1,0:T(8,128)(2,1)}, bf16[4,128,512]{2,1,0:T(8,128)(2,1)}, u32[]{:S(2)}, u32[]{:S(2)}) %collective-permute-start.80) | collective-permute-done | bytes 524320 | tf_op jit(solution)/shard_map/ppermute | solution.py:1202
  (373 shorter events, 283.0 us)
Async XLA Ops:
  5.1 40.1 %collective-permute-start.1 = (bf16[6144,128]{1,0:T(8,128)(2,1)}, bf16[6144,128]{1,0:T(8,128)(2,1)S(1)}, u32[]{:S(2)}, u32[]{:S(2)}) collective-permute-start(bf16[6144,128]{1,0:T(8,128)(2,1)} %get-tuple-element.108.refs_0_.refs_10_.refs_3_.refs_7_), channel_id=1, source_target_pairs={{0,2},{1,3},{2,0},{3,1},{4,6},{5,7},{6,4},{7,5},{8,10},{9,11},{10,... | collective-permute-start | bytes 4718600 | tf_op jit(solution)/shard_map/ppermute | solution.py:1206
  8.1 37.1 %collective-permute-start = (bf16[3072,128]{1,0:T(8,128)(2,1)}, bf16[3072,128]{1,0:T(8,128)(2,1)}, u32[]{:S(2)}, u32[]{:S(2)}) collective-permute-start(bf16[3072,128]{1,0:T(8,128)(2,1)} %get-tuple-element.107), channel_id=1, source_target_pairs={{0,16},{4,20},{8,24},{12,28},{16,0},{20,4},{24,8},{28,12},{1,17},{... | collective-permute-start | bytes 2359304 | tf_op jit(solution)/shard_map/ppermute | solution.py:1202
  45.2 26.9 %collective-permute-start.2 = (bf16[3072,128]{1,0:T(8,128)(2,1)}, bf16[3072,128]{1,0:T(8,128)(2,1)}, u32[]{:S(2)}, u32[]{:S(2)}) collective-permute-start(bf16[3072,128]{1,0:T(8,128)(2,1)} %collective-permute-done.refs_14_.refs_11_), channel_id=1, source_target_pairs={{0,2},{1,3},{2,0},{3,1},{4,6},{5,7},{6,4},{7,5},{8,10},{9,11},{10,... | collective-permute-start | bytes 2359304 | tf_op jit(solution)/shard_map/ppermute | solution.py:1206
  50.2 81.7 %collective-permute-start.17 = (bf16[6144,128]{1,0:T(8,128)(2,1)S(1)}, bf16[6144,128]{1,0:T(8,128)(2,1)}, u32[]{:S(2)}, u32[]{:S(2)}) collective-permute-start(bf16[6144,128]{1,0:T(8,128)(2,1)S(1)} %copy-done.3), channel_id=1, source_target_pairs={{0,1},{1,0},{2,3},{3,2},{4,5},{5,4},{6,7},{7,6},{8,9},{9,8},{10,11... | collective-permute-start | bytes 4718600 | tf_op jit(solution)/shard_map/ppermute | solution.py:1210
  50.2 49.9 %collective-permute-start.5 = (bf16[3072,128]{1,0:T(8,128)(2,1)}, bf16[3072,128]{1,0:T(8,128)(2,1)}, u32[]{:S(2)}, u32[]{:S(2)}) collective-permute-start(bf16[3072,128]{1,0:T(8,128)(2,1)} %get-tuple-element.114), channel_id=1, source_target_pairs={{0,16},{4,20},{8,24},{12,28},{16,0},{20,4},{24,8},{28,12},{1,17},{... | collective-permute-start | bytes 2359304 | tf_op jit(solution)/shard_map/ppermute | solution.py:1202
  75.3 30.3 %collective-permute-start.9 = (bf16[128,1024]{1,0:T(8,128)(2,1)S(1)}, bf16[128,1024]{1,0:T(8,128)(2,1)}, u32[]{:S(2)}, u32[]{:S(2)}) collective-permute-start(bf16[128,1024]{1,0:T(8,128)(2,1)S(1)} %get-tuple-element.237.refs_0_), channel_id=1, source_target_pairs={{0,16},{4,20},{8,24},{12,28},{16,0},{20,4},{24,8},{28,12},{1,17},{... | collective-permute-start | bytes 786440 | tf_op jit(solution)/shard_map/ppermute | solution.py:1202
  75.7 31.5 %collective-permute-start.7 = (bf16[128,1024]{1,0:T(8,128)(2,1)S(1)}, bf16[128,1024]{1,0:T(8,128)(2,1)}, u32[]{:S(2)}, u32[]{:S(2)}) collective-permute-start(bf16[128,1024]{1,0:T(8,128)(2,1)S(1)} %get-tuple-element.237.refs_0_), channel_id=1, source_target_pairs={{0,8},{4,12},{8,0},{12,4},{16,24},{20,28},{24,16},{28,20},{1,9},{5... | collective-permute-start | bytes 786440 | tf_op jit(solution)/shard_map/ppermute | solution.py:1202
  79.4 29.1 %collective-permute-start.11 = (bf16[128,1024]{1,0:T(8,128)(2,1)S(1)}, bf16[128,1024]{1,0:T(8,128)(2,1)}, u32[]{:S(2)}, u32[]{:S(2)}) collective-permute-start(bf16[128,1024]{1,0:T(8,128)(2,1)S(1)} %get-tuple-element.237.refs_0_), channel_id=1, source_target_pairs={{0,24},{4,28},{8,16},{12,20},{16,8},{20,12},{24,0},{28,4},{1,25},{... | collective-permute-start | bytes 786440 | tf_op jit(solution)/shard_map/ppermute | solution.py:1202
  108.5 40.1 %collective-permute-start.18 = (bf16[6144,128]{1,0:T(8,128)(2,1)S(1)}, bf16[6144,128]{1,0:T(8,128)(2,1)}, u32[]{:S(2)}, u32[]{:S(2)}) collective-permute-start(bf16[6144,128]{1,0:T(8,128)(2,1)S(1)} %collective-permute-done.1.refs_12_.refs_5_.refs_9_), channel_id=1, source_target_pairs={{0,1},{1,0},{2,3},{3,2},{4,5},{5,4},{6,7},{7,6},{8,9},{9,8},{10,11... | collective-permute-start | bytes 4718600 | tf_op jit(solution)/shard_map/ppermute | solution.py:1210
  131.8 34.4 %collective-permute-start.21 = (bf16[3072,128]{1,0:T(8,128)(2,1)}, bf16[3072,128]{1,0:T(8,128)(2,1)S(1)}, u32[]{:S(2)}, u32[]{:S(2)}) collective-permute-start(bf16[3072,128]{1,0:T(8,128)(2,1)} %collective-permute-done.5.refs_7_.refs_15_), channel_id=1, source_target_pairs={{0,1},{1,0},{2,3},{3,2},{4,5},{5,4},{6,7},{7,6},{8,9},{9,8},{10,11... | collective-permute-start | bytes 2359304 | tf_op jit(solution)/shard_map/ppermute | solution.py:1210
  136.8 29.5 %collective-permute-start.23 = (bf16[3072,128]{1,0:T(8,128)(2,1)}, bf16[3072,128]{1,0:T(8,128)(2,1)S(1)}, u32[]{:S(2)}, u32[]{:S(2)}) collective-permute-start(bf16[3072,128]{1,0:T(8,128)(2,1)} %collective-permute-done.22.refs_9_.refs_17_), channel_id=1, source_target_pairs={{0,1},{1,0},{2,3},{3,2},{4,5},{5,4},{6,7},{7,6},{8,9},{9,8},{10,11... | collective-permute-start | bytes 2359304 | tf_op jit(solution)/shard_map/ppermute | solution.py:1210
  359.4 29.5 %collective-permute-start.52 = (bf16[2,4,128,512]{3,2,1,0:T(8,128)(2,1)}, bf16[2,4,128,512]{3,2,1,0:T(8,128)(2,1)S(1)}, u32[]{:S(2)}, u32[]{:S(2)}) collective-permute-start(bf16[2,4,128,512]{3,2,1,0:T(8,128)(2,1)} %get-tuple-element.158.refs_0_), channel_id=1, source_target_pairs={{0,1},{1,0},{2,3},{3,2},{4,5},{5,4},{6,7},{7,6},{8,9},{9,8},{10,11... | collective-permute-start | bytes 3145736 | tf_op jit(solution)/shard_map/ppermute | solution.py:1210
  371.5 22.0 %collective-permute-start.50 = (bf16[2,2,512,128]{3,2,1,0:T(8,128)(2,1)}, bf16[2,2,512,128]{3,2,1,0:T(8,128)(2,1)}, u32[]{:S(2)}, u32[]{:S(2)}) collective-permute-start(bf16[2,2,512,128]{3,2,1,0:T(8,128)(2,1)} %get-tuple-element.164), channel_id=1, source_target_pairs={{0,2},{1,3},{2,0},{3,1},{4,6},{5,7},{6,4},{7,5},{8,10},{9,11},{10,... | collective-permute-start | bytes 1572872 | tf_op jit(solution)/shard_map/ppermute | solution.py:1206
  371.8 26.4 %collective-permute-start.51 = (bf16[2,2,512,128]{3,2,1,0:T(8,128)(2,1)S(1)}, bf16[2,2,512,128]{3,2,1,0:T(8,128)(2,1)S(1)}, u32[]{:S(2)}, u32[]{:S(2)}) collective-permute-start(bf16[2,2,512,128]{3,2,1,0:T(8,128)(2,1)S(1)} %copy-done.26), channel_id=1, source_target_pairs={{0,16},{4,20},{8,24},{12,28},{16,0},{20,4},{24,8},{28,12},{1,17},{... | collective-permute-start | bytes 1572872 | tf_op jit(solution)/shard_map/ppermute | solution.py:1202
  409.7 22.6 %collective-permute-start.62 = (bf16[2,128,1024]{2,1,0:T(8,128)(2,1)}, bf16[2,128,1024]{2,1,0:T(8,128)(2,1)S(1)}, u32[]{:S(2)}, u32[]{:S(2)}) collective-permute-start(bf16[2,128,1024]{2,1,0:T(8,128)(2,1)} %get-tuple-element.183), channel_id=1, source_target_pairs={{0,1},{1,0},{2,3},{3,2},{4,5},{5,4},{6,7},{7,6},{8,9},{9,8},{10,11... | collective-permute-start | bytes 1572872 | tf_op jit(solution)/shard_map/ppermute | solution.py:1210
  418.5 26.1 %collective-permute-start.58 = (bf16[2,2,512,128]{3,2,1,0:T(8,128)(2,1)S(1)}, bf16[2,2,512,128]{3,2,1,0:T(8,128)(2,1)S(1)}, u32[]{:S(2)}, u32[]{:S(2)}) collective-permute-start(bf16[2,2,512,128]{3,2,1,0:T(8,128)(2,1)S(1)} %copy-done.27), channel_id=1, source_target_pairs={{0,16},{4,20},{8,24},{12,28},{16,0},{20,4},{24,8},{28,12},{1,17},{... | collective-permute-start | bytes 1572872 | tf_op jit(solution)/shard_map/ppermute | solution.py:1202
  420.7 51.1 %collective-permute-start.30 = (bf16[128,1024]{1,0:T(8,128)(2,1)S(1)}, bf16[128,1024]{1,0:T(8,128)(2,1)}, u32[]{:S(2)}, u32[]{:S(2)}) collective-permute-start(bf16[128,1024]{1,0:T(8,128)(2,1)S(1)} %get-tuple-element.241.refs_0_), channel_id=1, source_target_pairs={{0,2},{1,3},{2,0},{3,1},{4,6},{5,7},{6,4},{7,5},{8,10},{9,11},{10,... | collective-permute-start | bytes 786440 | tf_op jit(solution)/shard_map/ppermute | solution.py:1206
  421.0 39.6 %collective-permute-start.61 = (bf16[2,4,128,512]{3,2,1,0:T(8,128)(2,1)}, bf16[2,4,128,512]{3,2,1,0:T(8,128)(2,1)S(1)}, u32[]{:S(2)}, u32[]{:S(2)}) collective-permute-start(bf16[2,4,128,512]{3,2,1,0:T(8,128)(2,1)} %get-tuple-element.181), channel_id=1, source_target_pairs={{0,1},{1,0},{2,3},{3,2},{4,5},{5,4},{6,7},{7,6},{8,9},{9,8},{10,11... | collective-permute-start | bytes 3145736 | tf_op jit(solution)/shard_map/ppermute | solution.py:1210
  430.6 70.8 %collective-permute-start.65 = (bf16[4,128,512]{2,1,0:T(8,128)(2,1)}, bf16[4,128,512]{2,1,0:T(8,128)(2,1)}, u32[]{:S(2)}, u32[]{:S(2)}) collective-permute-start(bf16[4,128,512]{2,1,0:T(8,128)(2,1)} %get-tuple-element.166.refs_2_), channel_id=1, source_target_pairs={{0,2},{1,3},{2,0},{3,1},{4,6},{5,7},{6,4},{7,5},{8,10},{9,11},{10,... | collective-permute-start | bytes 1572872 | tf_op jit(solution)/shard_map/ppermute | solution.py:1206
  435.3 22.2 %collective-permute-start.63 = (bf16[128,1024]{1,0:T(8,128)(2,1)}, bf16[128,1024]{1,0:T(8,128)(2,1)}, u32[]{:S(2)}, u32[]{:S(2)}) collective-permute-start(bf16[128,1024]{1,0:T(8,128)(2,1)} %fusion.13), channel_id=1, source_target_pairs={{0,2},{1,3},{2,0},{3,1},{4,6},{5,7},{6,4},{7,5},{8,10},{9,11},{10,... | collective-permute-start | bytes 786440 | tf_op jit(solution)/shard_map/ppermute | solution.py:1206
  455.2 76.2 %collective-permute-start.78 = (bf16[2,4,2,512,128]{4,3,2,1,0:T(8,128)(2,1)}, bf16[2,4,2,512,128]{4,3,2,1,0:T(8,128)(2,1)}, u32[]{:S(2)}, u32[]{:S(2)}) collective-permute-start(bf16[2,4,2,512,128]{4,3,2,1,0:T(8,128)(2,1)} %get-tuple-element.195), channel_id=1, source_target_pairs={{0,1},{1,0},{2,3},{3,2},{4,5},{5,4},{6,7},{7,6},{8,9},{9,8},{10,11... | collective-permute-start | bytes 6291464 | tf_op jit(solution)/shard_map/ppermute | solution.py:1210
  465.2 30.7 %collective-permute-start.64 = (bf16[4,128,512]{2,1,0:T(8,128)(2,1)}, bf16[4,128,512]{2,1,0:T(8,128)(2,1)S(1)}, u32[]{:S(2)}, u32[]{:S(2)}) collective-permute-start(bf16[4,128,512]{2,1,0:T(8,128)(2,1)} %get-tuple-element.184), channel_id=1, source_target_pairs={{0,2},{1,3},{2,0},{3,1},{4,6},{5,7},{6,4},{7,5},{8,10},{9,11},{10,... | collective-permute-start | bytes 1572872 | tf_op jit(solution)/shard_map/ppermute | solution.py:1206
  535.8 38.0 %collective-permute-start.79 = (bf16[4,2,512,128]{3,2,1,0:T(8,128)(2,1)}, bf16[4,2,512,128]{3,2,1,0:T(8,128)(2,1)}, u32[]{:S(2)}, u32[]{:S(2)}) collective-permute-start(bf16[4,2,512,128]{3,2,1,0:T(8,128)(2,1)} %get-tuple-element.197), channel_id=1, source_target_pairs={{0,2},{1,3},{2,0},{3,1},{4,6},{5,7},{6,4},{7,5},{8,10},{9,11},{10,... | collective-permute-start | bytes 3145736 | tf_op jit(solution)/shard_map/ppermute | solution.py:1206
  544.2 26.8 %collective-permute-start.80 = (bf16[4,128,512]{2,1,0:T(8,128)(2,1)}, bf16[4,128,512]{2,1,0:T(8,128)(2,1)}, u32[]{:S(2)}, u32[]{:S(2)}) collective-permute-start(bf16[4,128,512]{2,1,0:T(8,128)(2,1)} %add_convert_fusion), channel_id=1, source_target_pairs={{0,16},{4,20},{8,24},{12,28},{16,0},{20,4},{24,8},{28,12},{1,17},{... | collective-permute-start | bytes 1572872 | tf_op jit(solution)/shard_map/ppermute | solution.py:1202
  (125 other events, 1902.7 us)

commit v6 on v5

--- a/solution.py
+++ b/solution.py
@@ -877,10 +877,10 @@
     )(keep, got, *after)
 
 
-def finish_body(keep, near, two, four, six, extra, unit, scale, gain, grad_out, *refs):
+def finish_body(keep, near, four, two, extra, unit, scale, gain, grad_out, *refs):
     hidden_ref, attn_ref, gain_ref = refs[-3:]
     total = keep[...] + near[...].astype(F32) + extra[...]
-    for part in (two, four, six):
+    for part in (four, two):
         total = total + part[...].astype(F32)
     gain_ref[...] = jnp.sum((total * unit[...]).reshape(-1, 8, total.shape[1]), 0)
     weighted = total * gain[...]
@@ -890,13 +890,13 @@
     attn_ref[...] = (RESIDUAL * hidden).astype(BF16)
 
 
-def finish_rows(keep, near, two, four, six, extra, unit, scale, gain, grad_out, *after):
+def finish_rows(keep, near, four, two, extra, unit, scale, gain, grad_out, *after):
     size, width = unit.shape
     block = pl.BlockSpec((size, width), lambda e: (0, 0))
     return pl.pallas_call(
         finish_body,
         grid=(1,),
-        in_specs=[block] * 7
+        in_specs=[block] * 6
         + [whole_block((size, 1)), whole_block((1, width)), block]
         + [any_block()] * len(after),
         out_specs=[block, block, whole_block((8, width))],
@@ -906,7 +906,7 @@
             jax.ShapeDtypeStruct((8, width), F32),
         ],
         name="finish_rows",
-    )(keep, near, two, four, six, extra, unit, scale, gain, grad_out, *after)
+    )(keep, near, four, two, extra, unit, scale, gain, grad_out, *after)
 
 
 def rotated(values, cosine, sine, sign):
@@ -1164,7 +1164,7 @@
 
 def unpack_body(place_ref, *refs):
     pieces = refs[:8]
-    query, key, value, output, small = refs[8:]
+    query, key, value, output, small = refs[-5:]
     size = pieces[0].shape[0]
     wide, narrow = (query.shape[1], key.shape[1])
     for r, piece in zip(ORDER, pieces):
@@ -1225,12 +1225,12 @@
     got_near = trade(send_near, 1)
     four, six = (trade(far[:size], 4), trade(far[size:], 6))
     near = (keep[size : 2 * size] + got_near[size:].astype(F32)).astype(BF16)
-    return (keep, got_near, near, far, (trade(near, 2), four, six), *beside)
+    return (keep, got_near, (trade(near, 2), four, six), *beside)
 
 
 def scatter_experts(keep, send_near, send_far, *beside):
     size = keep.shape[0] // 4
-    keep, got_near, _, _, back, *beside = scatter_steps(keep, send_near, send_far, *beside)
+    keep, got_near, back, *beside = scatter_steps(keep, send_near, send_far, *beside)
     total = keep[:size] + got_near[:size].astype(F32)
     for part in back:
         total = total + part.astype(F32)
@@ -1329,30 +1329,32 @@
     first_normed, query, keys, values, attended, attn_keep, attn_send = attention_forward(
         core_arg, tokens, first_gain[None], *weights, tables, own_pack
     )
-    near_pack, own_across, attn_send = lax.optimization_barrier(
-        (near_pack, own_across, attn_send)
-    )
+    notes = [note] + [trade(note, bits) for bits in (2, 4, 6)]
+    near_pack, own_across, attn_send, *notes = lax.optimization_barrier(
+        (near_pack, own_across, attn_send, *notes)
+    )
+    notes = jnp.stack(notes)
+    others = trade(notes, 1)
     own = [own_pack, swap_core(own_pack), own_across, swap_core(own_across)]
     tokens_mine = quarter_of(tokens).astype(F32)
+    attn_sum = scatter_tensor(attn_keep, attn_send, row)
+    near_pack, attn_sum, others = lax.optimization_barrier((near_pack, attn_sum, others))
     near_across = swap_y(near_pack)
-    attn_sum = scatter_tensor(attn_keep, attn_send, row)
-    near_across, attn_sum, note = lax.optimization_barrier((near_across, attn_sum, note))
     hidden = tokens_mine + RESIDUAL * attn_sum
     scale_two = lax.rsqrt(jnp.mean(hidden * hidden, -1, keepdims=True) + EPS)
     unit_two = hidden * scale_two
     normed_two = (unit_two * second_gain).astype(BF16)
-    column = [normed_two] + [trade(normed_two, bits) for bits in (2, 4, 6)]
-    notes = [note] + [trade(note, bits) for bits in (2, 4, 6)]
     beside = trade(normed_two, 1)
+    last, beside = lax.optimization_barrier((normed_two, beside))
+    column = [normed_two, trade(normed_two, 2), trade(normed_two, 4), trade(last, 6)]
     across = [trade(shard, 1) for shard in column[1:]]
-    far_pack, beside, across[0], across[1], *gathered = lax.optimization_barrier(
-        (far_pack, beside, across[0], across[1], *column[1:])
-    )
-    row_shards = [normed_two, *gathered, beside, *across]
+    far_pack, near_across, *gathered = lax.optimization_barrier(
+        (far_pack, near_across, beside, *across, *column[1:])
+    )
+    row_shards = [normed_two, *gathered[4:], *gathered[:4]]
     near = [near_pack, swap_core(near_pack), near_across, swap_core(near_across)]
     far = spread_tensor(far_pack)
-    notes = jnp.stack(notes)
-    notes = jnp.concatenate([notes, trade(notes, 1)], 0)
+    notes = jnp.concatenate([notes, others], 0)
     valid_total = jnp.sum(notes[:, TOP, 0]).astype(F32)
     route_rel = jnp.bitwise_and(notes[:, :TOP] - base, expert_count - 1)
     route_rel = route_rel.transpose(0, 2, 1).reshape(senders * quarter, TOP)
@@ -1386,10 +1388,17 @@
     keep, pre_grad, logit_grad, grad_rows = experts_backward(
         0, half_arg, shards[:4], *packs, *saved
     )
-    keep, got_near, near_rows, far_rows, back = scatter_steps(keep, send_near, send_far)
+    got_far = trade(send_far, 1)
+    send_near, got_far, keep = lax.optimization_barrier((send_near, got_far, keep))
+    far_rows = (keep[2 * quarter :] + got_far.astype(F32)).astype(BF16)
+    back = trade(far_rows, 4)
+    got_near = trade(send_near, 1)
+    near_rows = keep[quarter : 2 * quarter] + got_near[quarter:].astype(F32)
+    near_rows = (near_rows + back[quarter:].astype(F32)).astype(BF16)
+    near_rows = trade(near_rows, 2)
     other = 1 - half_arg
     in_keep, in_send = grad_expert_ins(other, expert_rows, pre_grad, 0, 2, far_rows)
-    in_near, in_far = fold_pairs(in_keep, swap_core(in_send), near_rows)
+    in_near, in_far = fold_pairs(in_keep, swap_core(in_send))
     in_ready = (in_near + swap_y(in_far).astype(F32)).astype(BF16)
     out_keep, out_send, own_out_keep, own_out_send = grad_expert_outs(
         half_arg, gated, grad_rows, in_far
@@ -1397,7 +1406,8 @@
     grad_hidden, grad_attn, grad_second_part = finish_rows(
         keep,
         got_near,
-        *back,
+        back,
+        near_rows,
         mean_rows,
         unit_two,
         scale_two,
@@ -1446,16 +1456,19 @@
     own_out_near, own_out_far = fold_pairs(own_out_keep, swap_core(own_out_send), grad_one)
     own_out_across = swap_y(own_out_far)
 
+    own_in_keep, own_in_send = grad_expert_ins(
+        half_arg, expert_rows, pre_grad, 0, held, grad_one
+    )
     keep, send_near, send_far = reduce_parts(
-        place_arg, first_normed, grad_qkv, grad_attn, attended, small, gain_part
-    )
-    own_in_keep, own_in_send = grad_expert_ins(
-        half_arg, expert_rows, pre_grad, 0, held, late_back
+        place_arg, first_normed, grad_qkv, grad_attn, attended, small, gain_part, late_back, own_in_send
     )
     own_in_near, own_in_far = fold_pairs(own_in_keep, swap_core(own_in_send), grad_one)
     own_in_across = swap_y(own_in_far)
-    total, late_back = scatter_experts(keep, send_near, send_far, late_back)
-    total, own_out_across = lax.optimization_barrier((total.astype(BF16), own_out_across))
+    out_back = trade(out_ready, 4)
+    total, out_back = scatter_experts(keep, send_near, send_far, out_back)
+    total, own_out_across, own_in_across = lax.optimization_barrier(
+        (total.astype(BF16), own_out_across, own_in_across)
+    )
     shapes = [
         jax.ShapeDtypeStruct(shape, F32)
         for shape in (
@@ -1467,8 +1480,6 @@
         )
     ]
     shards = gather_experts(total)
-    out_ready, shards[1] = lax.optimization_barrier((out_ready, shards[1]))
-    out_back = trade(out_ready, 4)
     grad_query, grad_key, grad_value, grad_output, small = scalar_call(
         unpack_body, "unpack", place_arg, shards, shapes
     )

time: 590 us -> 577 us (0.978)
  waiting for transfers between devices: 251 us -> 236 us
    ppermute x45 -> x44, waiting for transfers between devices: 198 us -> 168 us  [trade(): return lax.ppermute(value, 'expert', [(i, i ^ bits) for i in range(8)])]
    ppermute x15, waiting for transfers between devices: 50.9 us -> 63.7 us  [swap_y(): return lax.ppermute(value, 'tensor', [(i, i ^ 2) for i in range(4)])]
    ppermute x45 -> x44, starting transfers between devices: 59.9 us -> 69.1 us  [trade(): return lax.ppermute(value, 'expert', [(i, i ^ bits) for i in range(8)])]
    unnamed x142 -> x150, local copies, waits for them, and re-layouts: 14.5 us -> 12.1 us
  transfers between devices with their start and end apart: 81 -> 80, of which waited for: 36 -> 35; matrix products, arithmetic and copies ran while one was open for 9% -> 8% of each run, Pallas kernels for 18% -> 17%
where the time goes in v6:
time: 577 us; the launch traced here: 567 us
  waiting for transfers between devices  236 us (41%)
  Pallas kernels  167 us (29%)
  starting transfers between devices  88 us (15%)
  other arithmetic  49.2 us (9%)
  local copies, waits for them, and re-layouts  20.4 us (4%)
    ppermute x44, waiting for transfers between devices, trade(): return lax.ppermute(value, 'expert', [(i, i ^ bits) for i in range(8)])  168 us
    ppermute x44, starting transfers between devices, trade(): return lax.ppermute(value, 'expert', [(i, i ^ bits) for i in range(8)])  69.1 us
    ppermute x15, waiting for transfers between devices, swap_y(): return lax.ppermute(value, 'tensor', [(i, i ^ 2) for i in range(4)])  63.7 us
    pallas_call x2, Pallas kernels, experts_backward(): pl.pallas_call(backward_body, grid_spec=pltpu.PrefetchScalarGridSpec(num_...  36 us
    pallas_call x5, Pallas kernels, scalar_call(): pl.pallas_call(body, grid_spec=pltpu.PrefetchScalarGridSpec(num_scalar_pr...  27.5 us
    pallas_call x3, Pallas kernels, grad_expert_ins(): pl.pallas_call(grad_in_body, grid_spec=pltpu.PrefetchScalarGridSpec(num_s...  22.3 us
    pallas_call x2, Pallas kernels, second(): pl.pallas_call(forward_second, grid_spec=pltpu.PrefetchScalarGridSpec(num...  21.7 us
    pallas_call x1, Pallas kernels, experts_forward(): pl.pallas_call(forward_first, grid_spec=pltpu.PrefetchScalarGridSpec(num_...  17.5 us
  transfers between devices with their start and end apart: 80, of which 35 were waited for; matrix products, arithmetic and copies ran while one was open for 8% of the time, Pallas kernels for 17%

profile of v6, /device:TPU:0, one launch (start us, length us, event | category | flops | bytes accessed | tf_op | source)
XLA Modules:
  0.0 567.4 jit_solution(5438744898157537951)
XLA Ops:
  18.7 8.2 %attention_forward.1 = (bf16[512,1024]{1,0:T(8,128)(2,1)}, bf16[512,256]{1,0:T(8,128)(2,1)}, bf16[512,128]{1,0:T(8,128)(2,1)}, bf16[512,128]{1,0:T(8,128)(2,1)},...) custom-call(s32[1]{0:T(128)} %bitcast.2.core_ref, bf16[512,1024]{1,0:T(8,128)(2,1)} %tokens.3, ...), custom_call_target="tpu_custom_call" | custom-call | tf_op jit(solution)/shard_map/attention_forward/pallas_call | solution.py:971
  27.8 17.9 %collective-permute-done.3 = s32[16,128]{1,0:T(8,128)S(1)} collective-permute-done((s32[16,128]{1,0:T(8,128)S(1)}, s32[16,128]{1,0:T(8,128)S(1)}, u32[]{:S(2)}, u32[]{:S(2)}) %collective-permute-start.3) | collective-permute-done | bytes 8224 | tf_op jit(solution)/shard_map/ppermute | solution.py:1202
  76.5 20.2 %collective-permute-done.8.refs_7_.refs_15_ = bf16[3072,128]{1,0:T(8,128)(2,1)} collective-permute-done((bf16[3072,128]{1,0:T(8,128)(2,1)}, bf16[3072,128]{1,0:T(8,128)(2,1)}, u32[]{:S(2)}, u32[]{:S(2)}) %collective-permute-start.8) | collective-permute-done | bytes 786464 | tf_op jit(solution)/shard_map/ppermute | solution.py:1202
  109.8 7.1 %collective-permute-done.14.refs_6_ = bf16[128,1024]{1,0:T(8,128)(2,1)S(1)} collective-permute-done((bf16[128,1024]{1,0:T(8,128)(2,1)S(1)}, bf16[128,1024]{1,0:T(8,128)(2,1)S(1)}, u32[]{:S(2)}, u32[]{:S(2)}) %collective-permute-start.14) | collective-permute-done | bytes 262176 | tf_op jit(solution)/shard_map/ppermute | solution.py:1202
  125.7 11.4 %collective-permute-done.22.refs_9_.refs_17_ = bf16[3072,128]{1,0:T(8,128)(2,1)} collective-permute-done((bf16[3072,128]{1,0:T(8,128)(2,1)}, bf16[3072,128]{1,0:T(8,128)(2,1)}, u32[]{:S(2)}, u32[]{:S(2)}) %collective-permute-start.22) | collective-permute-done | bytes 786464 | tf_op jit(solution)/shard_map/ppermute | solution.py:1206
  139.7 17.5 %experts_forward_a.1 = (f32[1024,1024]{1,0:T(8,128)}, bf16[4,1024,1024]{2,1,0:T(8,128)(2,1)}, bf16[4,1024,512]{2,1,0:T(8,128)(2,1)}, f32[1024,128]{1,0:T(8,128)}, bf16[1024,1024]{1,0:T(8,128)(2,1)}) custom-call(s32[1]{0:T(128)} %bitcast.1.half_ref, bf16[128,1024]{1,0:T(8,128)(2,1)} %copy-done.13, bf16[128,1024]{1,0:T(8,128)(2,1)} %copy-done.49, ...), custom_call_target="tpu_custom_call" | custom-call | tf_op jit(solution)/shard_map/experts_forward_a/pallas_call | solution.py:643
  158.1 10.8 %experts_forward_b.2 = (bf16[256,1024]{1,0:T(8,128)(2,1)}, bf16[256,1024]{1,0:T(8,128)(2,1)}, bf16[4,1024,1024]{2,1,0:T(8,128)(2,1)}, bf16[4,1024,512]{2,1,0:T(8,128)(2,1)}) custom-call(s32[1]{0:T(128)} %bitcast.1.half_ref, bf16[1024,1024]{1,0:T(8,128)(2,1)} %get-tuple-element.139.refs_0_.rows_ref, ...), custom_call_target="tpu_custom_call", output_to_operand_aliasing={{2}: (12, {}), {3}: (13, {})} | custom-call | tf_op jit(solution)/shard_map/experts_forward_b/pallas_call | solution.py:665
  170.5 11.0 %experts_forward_b.3 = (f32[512,1024]{1,0:T(8,128)}, bf16[4,1024,1024]{2,1,0:T(8,128)(2,1)}, bf16[4,1024,512]{2,1,0:T(8,128)(2,1)}) custom-call(s32[1]{0:T(128)} %bitcast.1.half_ref, bf16[1024,1024]{1,0:T(8,128)(2,1)} %get-tuple-element.139.refs_0_.rows_ref, ...), custom_call_target="tpu_custom_call", output_to_operand_aliasing={{1}: (12, {}), {2}: (13, {})} | custom-call | tf_op jit(solution)/shard_map/experts_forward_b/pallas_call | solution.py:665
  225.5 8.4 %collective-permute-done.33.refs_1_ = bf16[128,1024]{1,0:T(8,128)(2,1)S(1)} collective-permute-done((bf16[128,1024]{1,0:T(8,128)(2,1)S(1)}, bf16[128,1024]{1,0:T(8,128)(2,1)S(1)}, u32[]{:S(2)}, u32[]{:S(2)}) %collective-permute-start.33) | collective-permute-done | bytes 262176 | tf_op jit(solution)/shard_map/ppermute | solution.py:1202
  234.5 8.5 %collective-permute-done.35.refs_2_ = bf16[128,1024]{1,0:T(8,128)(2,1)S(1)} collective-permute-done((bf16[128,1024]{1,0:T(8,128)(2,1)S(1)}, bf16[128,1024]{1,0:T(8,128)(2,1)S(1)}, u32[]{:S(2)}, u32[]{:S(2)}) %collective-permute-start.35) | collective-permute-done | bytes 262176 | tf_op jit(solution)/shard_map/ppermute | solution.py:1202
  253.2 17.8 %experts_backward.2 = (bf16[256,1024]{1,0:T(8,128)(2,1)}, bf16[256,1024]{1,0:T(8,128)(2,1)}, bf16[4,1024,1024]{2,1,0:T(8,128)(2,1)}, f32[1024,128]{1,0:T(8,128)}, bf16[1024,1024]{1,0:T(8,128)(2,1)}) custom-call(s32[1]{0:T(128)} %bitcast.1.half_ref, bf16[128,1024]{1,0:T(8,128)(2,1)} %copy-done.44, bf16[128,1024]{1,0:T(8,128)(2,1)} %copy-done.45, ...), custom_call_target="tpu_custom_call" | custom-call | tf_op jit(solution)/shard_map/experts_backward/pallas_call | solution.py:755
  271.7 18.2 %experts_backward.3 = (f32[512,1024]{1,0:T(8,128)}, bf16[4,1024,1024]{2,1,0:T(8,128)(2,1)}, f32[1024,128]{1,0:T(8,128)}, bf16[1024,1024]{1,0:T(8,128)(2,1)}) custom-call(s32[1]{0:T(128)} %bitcast.1.half_ref, bf16[128,1024]{1,0:T(8,128)(2,1)} %copy-done.29, ...), custom_call_target="tpu_custom_call", output_to_operand_aliasing={{1}: (20, {}), {2}: (21, {}), {3}: (22, {})} | custom-call | tf_op jit(solution)/shard_map/experts_backward/pallas_call | solution.py:755
  310.8 15.1 %collective-permute-done.41.four = bf16[256,1024]{1,0:T(8,128)(2,1)S(1)} collective-permute-done((bf16[256,1024]{1,0:T(8,128)(2,1)S(1)}, bf16[256,1024]{1,0:T(8,128)(2,1)S(1)}, u32[]{:S(2)}, u32[]{:S(2)}) %collective-permute-start.41) | collective-permute-done | bytes 524320 | tf_op jit(solution)/shard_map/ppermute | solution.py:1202
  328.3 10.5 %grad_expert_out.1 = (bf16[2,4,128,512]{3,2,1,0:T(8,128)(2,1)}, bf16[2,4,128,512]{3,2,1,0:T(8,128)(2,1)}, bf16[2,4,128,512]{3,2,1,0:T(8,128)(2,1)}, bf16[2,4,128,512]{3,2,1,0:T(8,128)(2,1)}) custom-call(s32[1]{0:T(128)} %bitcast.1.half_ref, bf16[4,1024,512]{2,1,0:T(8,128)(2,1)} %get-tuple-element.167.gated_ref, ...), custom_call_target="tpu_custom_call" | custom-call | tf_op jit(solution)/shard_map/grad_expert_out/pallas_call | solution.py:796
  369.8 11.2 %collective-permute-done.53 = f32[40,1024]{1,0:T(8,128)S(1)} collective-permute-done((f32[40,1024]{1,0:T(8,128)S(1)}, f32[40,1024]{1,0:T(8,128)S(1)}, u32[]{:S(2)}, u32[]{:S(2)}) %collective-permute-start.53) | collective-permute-done | bytes 163872 | tf_op jit(solution)/shard_map/ppermute | solution.py:1206
  392.1 10.7 %attention_backward.1 = (bf16[512,1024]{1,0:T(8,128)(2,1)}, bf16[512,512]{1,0:T(8,128)(2,1)}, f32[8,1024]{1,0:T(8,128)}, f32[2,128,1024]{2,1,0:T(8,128)}, bf16[2,128,1024]{2,1,0:T(8,128)(2,1)}) custom-call(s32[1]{0:T(128)} %bitcast.share_ref, bf16[512,1024]{1,0:T(8,128)(2,1)} %tokens.3, bf16[1024,256]{1,0:T(8,128)(2,1)} %query_w.3, bf16[1024,128]{1,0:T(8,128)(2,1)} %key_w.3, ...), custom_call_target="tpu_custom_call" | custom-call | tf_op jit(solution)/shard_map/attention_backward/pallas_call | solution.py:971
  407.0 7.9 %collective-permute-done.56 = bf16[128,1024]{1,0:T(8,128)(2,1)S(1)} collective-permute-done((bf16[128,1024]{1,0:T(8,128)(2,1)S(1)}, bf16[128,1024]{1,0:T(8,128)(2,1)S(1)}, u32[]{:S(2)}, u32[]{:S(2)}) %collective-permute-start.56) | collective-permute-done | bytes 262176 | tf_op jit(solution)/shard_map/ppermute | solution.py:1206
  415.9 9.9 %grad_expert_in.5 = (bf16[2,4,2,512,128]{4,3,2,1,0:T(8,128)(2,1)}, bf16[2,4,2,512,128]{4,3,2,1,0:T(8,128)(2,1)}) custom-call(s32[1]{0:T(128)} %bitcast.1.half_ref, bf16[1024,1024]{1,0:T(8,128)(2,1)} %get-tuple-element.139.refs_0_.rows_ref, bf16[4,1024,1024]{2,1,0:T(8,128)(2,1)} %get-tuple-element.169.pre_ref, f32[128,1024]{1,0:T(8,128)} %get-tuple-element.243.refs_0_), custom_call_target="tpu_custom_call" | custom-call | tf_op jit(solution)/shard_map/grad_expert_in/pallas_call | solution.py:838
  429.5 11.8 %collective-permute-done.60 = bf16[4,128,512]{2,1,0:T(8,128)(2,1)S(1)} collective-permute-done((bf16[4,128,512]{2,1,0:T(8,128)(2,1)}, bf16[4,128,512]{2,1,0:T(8,128)(2,1)S(1)}, u32[]{:S(2)}, u32[]{:S(2)}) %collective-permute-start.60) | collective-permute-done | bytes 524320 | tf_op jit(solution)/shard_map/ppermute | solution.py:1206
  446.2 17.3 %collective-permute-done.54.refs_0_ = bf16[2,2,512,128]{3,2,1,0:T(8,128)(2,1)S(1)} collective-permute-done((bf16[2,2,512,128]{3,2,1,0:T(8,128)(2,1)S(1)}, bf16[2,2,512,128]{3,2,1,0:T(8,128)(2,1)S(1)}, u32[]{:S(2)}, u32[]{:S(2)}) %collective-permute-start.54) | collective-permute-done | bytes 524320 | tf_op jit(solution)/shard_map/ppermute | solution.py:1202
  464.3 7.7 %reduce_parts.1 = (f32[512,896]{1,0:T(8,128)}, bf16[256,896]{1,0:T(8,128)(2,1)}, bf16[256,896]{1,0:T(8,128)(2,1)}) custom-call(s32[1]{0:T(128)} %bitcast.13.place_ref, bf16[512,1024]{1,0:T(8,128)(2,1)} %get-tuple-element.153.normed, bf16[512,512]{1,0:T(8,128)(2,1)} %get-tuple-element.184.grad_qkv, bf16[512,1024]{1,0:T(8,128)(2,1)} %get-tuple-element.185.grad, ...), custom_call_target="tpu_custom_call" | custom-call | tf_op jit(solution)/shard_map/reduce_parts/pallas_call | solution.py:1136
  477.5 7.2 %collective-permute-done.57 = bf16[256,896]{1,0:T(8,128)(2,1)S(1)} collective-permute-done((bf16[256,896]{1,0:T(8,128)(2,1)}, bf16[256,896]{1,0:T(8,128)(2,1)S(1)}, u32[]{:S(2)}, u32[]{:S(2)}) %collective-permute-start.57) | collective-permute-done | bytes 458784 | tf_op jit(solution)/shard_map/ppermute | solution.py:1202
  519.1 8.1 %collective-permute-done.65 = bf16[4,128,512]{2,1,0:T(8,128)(2,1)} collective-permute-done((bf16[4,128,512]{2,1,0:T(8,128)(2,1)}, bf16[4,128,512]{2,1,0:T(8,128)(2,1)}, u32[]{:S(2)}, u32[]{:S(2)}) %collective-permute-start.65) | collective-permute-done | bytes 524320 | tf_op jit(solution)/shard_map/ppermute | solution.py:1206
  536.9 8.9 %collective-permute-done.69.refs_2_ = bf16[128,896]{1,0:T(8,128)(2,1)S(1)} collective-permute-done((bf16[128,896]{1,0:T(8,128)(2,1)S(1)}, bf16[128,896]{1,0:T(8,128)(2,1)S(1)}, u32[]{:S(2)}, u32[]{:S(2)}) %collective-permute-start.69) | collective-permute-done | bytes 229408 | tf_op jit(solution)/shard_map/ppermute | solution.py:1202
  (378 shorter events, 279.4 us)
Async XLA Ops:
  5.1 40.6 %collective-permute-start.1 = (bf16[6144,128]{1,0:T(8,128)(2,1)}, bf16[6144,128]{1,0:T(8,128)(2,1)S(1)}, u32[]{:S(2)}, u32[]{:S(2)}) collective-permute-start(bf16[6144,128]{1,0:T(8,128)(2,1)} %get-tuple-element.115.refs_0_.refs_10_.refs_3_.refs_7_), channel_id=1, source_target_pairs={{0,2},{1,3},{2,0},{3,1},{4,6},{5,7},{6,4},{7,5},{8,10},{9,11},{10,... | collective-permute-start | bytes 4718600 | tf_op jit(solution)/shard_map/ppermute | solution.py:1206
  8.1 37.6 %collective-permute-start = (bf16[3072,128]{1,0:T(8,128)(2,1)}, bf16[3072,128]{1,0:T(8,128)(2,1)}, u32[]{:S(2)}, u32[]{:S(2)}) collective-permute-start(bf16[3072,128]{1,0:T(8,128)(2,1)} %get-tuple-element.114), channel_id=1, source_target_pairs={{0,16},{4,20},{8,24},{12,28},{16,0},{20,4},{24,8},{28,12},{1,17},{... | collective-permute-start | bytes 2359304 | tf_op jit(solution)/shard_map/ppermute | solution.py:1202
  13.6 32.1 %collective-permute-start.3 = (s32[16,128]{1,0:T(8,128)S(1)}, s32[16,128]{1,0:T(8,128)S(1)}, u32[]{:S(2)}, u32[]{:S(2)}) collective-permute-start(s32[16,128]{1,0:T(8,128)S(1)} %concatenate.46), channel_id=1, source_target_pairs={{0,16},{4,20},{8,24},{12,28},{16,0},{20,4},{24,8},{28,12},{1,17},{... | collective-permute-start | bytes 24584 | tf_op jit(solution)/shard_map/ppermute | solution.py:1202
  13.9 31.7 %collective-permute-start.4 = (s32[16,128]{1,0:T(8,128)S(1)}, s32[16,128]{1,0:T(8,128)S(1)}, u32[]{:S(2)}, u32[]{:S(2)}) collective-permute-start(s32[16,128]{1,0:T(8,128)S(1)} %concatenate.46), channel_id=1, source_target_pairs={{0,24},{4,28},{8,16},{12,20},{16,8},{20,12},{24,0},{28,4},{1,25},{... | collective-permute-start | bytes 24584 | tf_op jit(solution)/shard_map/ppermute | solution.py:1202
  52.6 44.0 %collective-permute-start.8 = (bf16[3072,128]{1,0:T(8,128)(2,1)}, bf16[3072,128]{1,0:T(8,128)(2,1)}, u32[]{:S(2)}, u32[]{:S(2)}) collective-permute-start(bf16[3072,128]{1,0:T(8,128)(2,1)} %get-tuple-element.125), channel_id=1, source_target_pairs={{0,16},{4,20},{8,24},{12,28},{16,0},{20,4},{24,8},{28,12},{1,17},{... | collective-permute-start | bytes 2359304 | tf_op jit(solution)/shard_map/ppermute | solution.py:1202
  67.7 52.2 %collective-permute-start.9 = (bf16[3072,128]{1,0:T(8,128)(2,1)}, bf16[3072,128]{1,0:T(8,128)(2,1)}, u32[]{:S(2)}, u32[]{:S(2)}) collective-permute-start(bf16[3072,128]{1,0:T(8,128)(2,1)} %collective-permute-done.refs_14_.refs_11_), channel_id=1, source_target_pairs={{0,2},{1,3},{2,0},{3,1},{4,6},{5,7},{6,4},{7,5},{8,10},{9,11},{10,... | collective-permute-start | bytes 2359304 | tf_op jit(solution)/shard_map/ppermute | solution.py:1206
  68.2 57.0 %collective-permute-start.17 = (bf16[6144,128]{1,0:T(8,128)(2,1)S(1)}, bf16[6144,128]{1,0:T(8,128)(2,1)}, u32[]{:S(2)}, u32[]{:S(2)}) collective-permute-start(bf16[6144,128]{1,0:T(8,128)(2,1)S(1)} %copy-done.3), channel_id=1, source_target_pairs={{0,1},{1,0},{2,3},{3,2},{4,5},{5,4},{6,7},{7,6},{8,9},{9,8},{10,11... | collective-permute-start | bytes 4718600 | tf_op jit(solution)/shard_map/ppermute | solution.py:1210
  68.2 31.1 %collective-permute-start.11 = (bf16[128,1024]{1,0:T(8,128)(2,1)S(1)}, bf16[128,1024]{1,0:T(8,128)(2,1)S(1)}, u32[]{:S(2)}, u32[]{:S(2)}) collective-permute-start(bf16[128,1024]{1,0:T(8,128)(2,1)S(1)} %get-tuple-element.128.refs_0_), channel_id=1, source_target_pairs={{0,8},{4,12},{8,0},{12,4},{16,24},{20,28},{24,16},{28,20},{1,9},{5... | collective-permute-start | bytes 786440 | tf_op jit(solution)/shard_map/ppermute | solution.py:1202
  73.7 34.0 %collective-permute-start.13 = (bf16[128,1024]{1,0:T(8,128)(2,1)S(1)}, bf16[128,1024]{1,0:T(8,128)(2,1)S(1)}, u32[]{:S(2)}, u32[]{:S(2)}) collective-permute-start(bf16[128,1024]{1,0:T(8,128)(2,1)S(1)} %get-tuple-element.128.refs_0_), channel_id=1, source_target_pairs={{0,16},{4,20},{8,24},{12,28},{16,0},{20,4},{24,8},{28,12},{1,17},{... | collective-permute-start | bytes 786440 | tf_op jit(solution)/shard_map/ppermute | solution.py:1202
  125.2 32.0 %collective-permute-start.21 = (bf16[3072,128]{1,0:T(8,128)(2,1)}, bf16[3072,128]{1,0:T(8,128)(2,1)}, u32[]{:S(2)}, u32[]{:S(2)}) collective-permute-start(bf16[3072,128]{1,0:T(8,128)(2,1)} %collective-permute-done.8.refs_7_.refs_15_), channel_id=1, source_target_pairs={{0,1},{1,0},{2,3},{3,2},{4,5},{5,4},{6,7},{7,6},{8,9},{9,8},{10,11... | collective-permute-start | bytes 2359304 | tf_op jit(solution)/shard_map/ppermute | solution.py:1210
  188.2 23.1 %collective-permute-start.27 = (bf16[128,1024]{1,0:T(8,128)(2,1)}, bf16[128,1024]{1,0:T(8,128)(2,1)S(1)}, u32[]{:S(2)}, u32[]{:S(2)}) collective-permute-start(bf16[128,1024]{1,0:T(8,128)(2,1)} %get-tuple-element.254), channel_id=1, source_target_pairs={{0,16},{4,20},{8,24},{12,28},{16,0},{20,4},{24,8},{28,12},{1,17},{... | collective-permute-start | bytes 786440 | tf_op jit(solution)/shard_map/ppermute | solution.py:1202
  298.4 27.5 %collective-permute-start.41 = (bf16[256,1024]{1,0:T(8,128)(2,1)S(1)}, bf16[256,1024]{1,0:T(8,128)(2,1)S(1)}, u32[]{:S(2)}, u32[]{:S(2)}) collective-permute-start(bf16[256,1024]{1,0:T(8,128)(2,1)S(1)} %copy-done.25), channel_id=1, source_target_pairs={{0,16},{4,20},{8,24},{12,28},{16,0},{20,4},{24,8},{28,12},{1,17},{... | collective-permute-start | bytes 1572872 | tf_op jit(solution)/shard_map/ppermute | solution.py:1202
  302.1 23.8 %collective-permute-start.40 = (bf16[256,1024]{1,0:T(8,128)(2,1)}, bf16[256,1024]{1,0:T(8,128)(2,1)S(1)}, u32[]{:S(2)}, u32[]{:S(2)}) collective-permute-start(bf16[256,1024]{1,0:T(8,128)(2,1)} %get-tuple-element.165), channel_id=1, source_target_pairs={{0,4},{4,0},{8,12},{12,8},{16,20},{20,16},{24,28},{28,24},{1,5},{5... | collective-permute-start | bytes 1572872 | tf_op jit(solution)/shard_map/ppermute | solution.py:1202
  308.0 30.7 %collective-permute-start.44 = (bf16[2,2,512,128]{3,2,1,0:T(8,128)(2,1)}, bf16[2,2,512,128]{3,2,1,0:T(8,128)(2,1)}, u32[]{:S(2)}, u32[]{:S(2)}) collective-permute-start(bf16[2,2,512,128]{3,2,1,0:T(8,128)(2,1)} %get-tuple-element.172.refs_0_), channel_id=1, source_target_pairs={{0,2},{1,3},{2,0},{3,1},{4,6},{5,7},{6,4},{7,5},{8,10},{9,11},{10,... | collective-permute-start | bytes 1572872 | tf_op jit(solution)/shard_map/ppermute | solution.py:1206
  352.1 29.5 %collective-permute-start.51 = (bf16[2,4,128,512]{3,2,1,0:T(8,128)(2,1)}, bf16[2,4,128,512]{3,2,1,0:T(8,128)(2,1)S(1)}, u32[]{:S(2)}, u32[]{:S(2)}) collective-permute-start(bf16[2,4,128,512]{3,2,1,0:T(8,128)(2,1)} %get-tuple-element.173.refs_0_), channel_id=1, source_target_pairs={{0,1},{1,0},{2,3},{3,2},{4,5},{5,4},{6,7},{7,6},{8,9},{9,8},{10,11... | collective-permute-start | bytes 3145736 | tf_op jit(solution)/shard_map/ppermute | solution.py:1210
  365.8 25.6 %collective-permute-start.50 = (bf16[2,2,512,128]{3,2,1,0:T(8,128)(2,1)S(1)}, bf16[2,2,512,128]{3,2,1,0:T(8,128)(2,1)S(1)}, u32[]{:S(2)}, u32[]{:S(2)}) collective-permute-start(bf16[2,2,512,128]{3,2,1,0:T(8,128)(2,1)S(1)} %copy-done.23), channel_id=1, source_target_pairs={{0,16},{4,20},{8,24},{12,28},{16,0},{20,4},{24,8},{28,12},{1,17},{... | collective-permute-start | bytes 1572872 | tf_op jit(solution)/shard_map/ppermute | solution.py:1202
  425.8 61.8 %collective-permute-start.66 = (bf16[2,4,2,512,128]{4,3,2,1,0:T(8,128)(2,1)}, bf16[2,4,2,512,128]{4,3,2,1,0:T(8,128)(2,1)}, u32[]{:S(2)}, u32[]{:S(2)}) collective-permute-start(bf16[2,4,2,512,128]{4,3,2,1,0:T(8,128)(2,1)} %get-tuple-element.190.refs_1_), channel_id=1, source_target_pairs={{0,1},{1,0},{2,3},{3,2},{4,5},{5,4},{6,7},{7,6},{8,9},{9,8},{10,11... | collective-permute-start | bytes 6291464 | tf_op jit(solution)/shard_map/ppermute | solution.py:1210
  425.9 46.2 %collective-permute-start.64 = (bf16[2,4,128,512]{3,2,1,0:T(8,128)(2,1)}, bf16[2,4,128,512]{3,2,1,0:T(8,128)(2,1)}, u32[]{:S(2)}, u32[]{:S(2)}) collective-permute-start(bf16[2,4,128,512]{3,2,1,0:T(8,128)(2,1)} %get-tuple-element.200), channel_id=1, source_target_pairs={{0,1},{1,0},{2,3},{3,2},{4,5},{5,4},{6,7},{7,6},{8,9},{9,8},{10,11... | collective-permute-start | bytes 3145736 | tf_op jit(solution)/shard_map/ppermute | solution.py:1210
  426.8 36.7 %collective-permute-start.54 = (bf16[2,2,512,128]{3,2,1,0:T(8,128)(2,1)S(1)}, bf16[2,2,512,128]{3,2,1,0:T(8,128)(2,1)S(1)}, u32[]{:S(2)}, u32[]{:S(2)}) collective-permute-start(bf16[2,2,512,128]{3,2,1,0:T(8,128)(2,1)S(1)} %copy-done.24), channel_id=1, source_target_pairs={{0,16},{4,20},{8,24},{12,28},{16,0},{20,4},{24,8},{28,12},{1,17},{... | collective-permute-start | bytes 1572872 | tf_op jit(solution)/shard_map/ppermute | solution.py:1202
  442.4 43.7 %collective-permute-start.61 = (bf16[4,128,512]{2,1,0:T(8,128)(2,1)}, bf16[4,128,512]{2,1,0:T(8,128)(2,1)}, u32[]{:S(2)}, u32[]{:S(2)}) collective-permute-start(bf16[4,128,512]{2,1,0:T(8,128)(2,1)} %add_convert_fusion), channel_id=1, source_target_pairs={{0,16},{4,20},{8,24},{12,28},{16,0},{20,4},{24,8},{28,12},{1,17},{... | collective-permute-start | bytes 1572872 | tf_op jit(solution)/shard_map/ppermute | solution.py:1202
  446.2 46.6 %collective-permute-start.29 = (bf16[128,1024]{1,0:T(8,128)(2,1)S(1)}, bf16[128,1024]{1,0:T(8,128)(2,1)}, u32[]{:S(2)}, u32[]{:S(2)}) collective-permute-start(bf16[128,1024]{1,0:T(8,128)(2,1)S(1)} %copy-done.36), channel_id=1, source_target_pairs={{0,1},{1,0},{2,3},{3,2},{4,5},{5,4},{6,7},{7,6},{8,9},{9,8},{10,11... | collective-permute-start | bytes 786440 | tf_op jit(solution)/shard_map/ppermute | solution.py:1210
  463.6 36.4 %collective-permute-start.31 = (bf16[128,1024]{1,0:T(8,128)(2,1)}, bf16[128,1024]{1,0:T(8,128)(2,1)}, u32[]{:S(2)}, u32[]{:S(2)}) collective-permute-start(bf16[128,1024]{1,0:T(8,128)(2,1)} %collective-permute-done.30.refs_2_), channel_id=1, source_target_pairs={{0,1},{1,0},{2,3},{3,2},{4,5},{5,4},{6,7},{7,6},{8,9},{9,8},{10,11... | collective-permute-start | bytes 786440 | tf_op jit(solution)/shard_map/ppermute | solution.py:1210
  492.1 35.1 %collective-permute-start.67 = (bf16[4,2,512,128]{3,2,1,0:T(8,128)(2,1)}, bf16[4,2,512,128]{3,2,1,0:T(8,128)(2,1)}, u32[]{:S(2)}, u32[]{:S(2)}) collective-permute-start(bf16[4,2,512,128]{3,2,1,0:T(8,128)(2,1)} %get-tuple-element.203), channel_id=1, source_target_pairs={{0,2},{1,3},{2,0},{3,1},{4,6},{5,7},{6,4},{7,5},{8,10},{9,11},{10,... | collective-permute-start | bytes 3145736 | tf_op jit(solution)/shard_map/ppermute | solution.py:1206
  497.6 29.6 %collective-permute-start.65 = (bf16[4,128,512]{2,1,0:T(8,128)(2,1)}, bf16[4,128,512]{2,1,0:T(8,128)(2,1)}, u32[]{:S(2)}, u32[]{:S(2)}) collective-permute-start(bf16[4,128,512]{2,1,0:T(8,128)(2,1)} %get-tuple-element.201), channel_id=1, source_target_pairs={{0,2},{1,3},{2,0},{3,1},{4,6},{5,7},{6,4},{7,5},{8,10},{9,11},{10,... | collective-permute-start | bytes 1572872 | tf_op jit(solution)/shard_map/ppermute | solution.py:1206
  (128 other events, 1687.4 us)

commit v7 on v6

--- a/solution.py
+++ b/solution.py
@@ -659,6 +659,8 @@
         out_shape=[sums, pre, gated, gates, rows],
         name="experts_forward_a",
     )(half_index, *shards, route_ids, router, *own, *near)
+    far_pack, far_across, sums_a = lax.optimization_barrier((*far, sums_a))
+    far = [far_pack, swap_core(far_pack), far_across, swap_core(far_across)]
 
     def second(part, pre_a, gated_a):
         specs, shapes = spread_specs(part, row_count, width)
@@ -681,7 +683,7 @@
 
     send_near, send_far, pre_a, gated_a = second(1, pre_a, gated_a)
     keep, pre_a, gated_a = second(0, pre_a, gated_a)
-    return (keep, send_near, send_far, pre_a, gated_a, gates, rows)
+    return (keep, send_near, send_far, pre_a, gated_a, gates, rows, far)
 
 
 def backward_body(half_ref, *refs):
@@ -1339,26 +1341,26 @@
     tokens_mine = quarter_of(tokens).astype(F32)
     attn_sum = scatter_tensor(attn_keep, attn_send, row)
     near_pack, attn_sum, others = lax.optimization_barrier((near_pack, attn_sum, others))
-    near_across = swap_y(near_pack)
     hidden = tokens_mine + RESIDUAL * attn_sum
     scale_two = lax.rsqrt(jnp.mean(hidden * hidden, -1, keepdims=True) + EPS)
     unit_two = hidden * scale_two
     normed_two = (unit_two * second_gain).astype(BF16)
     beside = trade(normed_two, 1)
-    last, beside = lax.optimization_barrier((normed_two, beside))
-    column = [normed_two, trade(normed_two, 2), trade(normed_two, 4), trade(last, 6)]
+    near_pack, beside = lax.optimization_barrier((near_pack, beside))
+    near_across = swap_y(near_pack)
+    column = [normed_two] + [trade(normed_two, bits) for bits in (2, 4, 6)]
     across = [trade(shard, 1) for shard in column[1:]]
     far_pack, near_across, *gathered = lax.optimization_barrier(
         (far_pack, near_across, beside, *across, *column[1:])
     )
     row_shards = [normed_two, *gathered[4:], *gathered[:4]]
     near = [near_pack, swap_core(near_pack), near_across, swap_core(near_across)]
-    far = spread_tensor(far_pack)
+    far = (far_pack, swap_y(far_pack))
     notes = jnp.concatenate([notes, others], 0)
     valid_total = jnp.sum(notes[:, TOP, 0]).astype(F32)
     route_rel = jnp.bitwise_and(notes[:, :TOP] - base, expert_count - 1)
     route_rel = route_rel.transpose(0, 2, 1).reshape(senders * quarter, TOP)
-    keep, send_near, send_far, pre, gated, gates, expert_rows = experts_forward(
+    keep, send_near, send_far, pre, gated, gates, expert_rows, far = experts_forward(
         half_arg,
         row_shards,
         route_rel,
@@ -1393,9 +1395,6 @@
     far_rows = (keep[2 * quarter :] + got_far.astype(F32)).astype(BF16)
     back = trade(far_rows, 4)
     got_near = trade(send_near, 1)
-    near_rows = keep[quarter : 2 * quarter] + got_near[quarter:].astype(F32)
-    near_rows = (near_rows + back[quarter:].astype(F32)).astype(BF16)
-    near_rows = trade(near_rows, 2)
     other = 1 - half_arg
     in_keep, in_send = grad_expert_ins(other, expert_rows, pre_grad, 0, 2, far_rows)
     in_near, in_far = fold_pairs(in_keep, swap_core(in_send))
@@ -1403,6 +1402,11 @@
     out_keep, out_send, own_out_keep, own_out_send = grad_expert_outs(
         half_arg, gated, grad_rows, in_far
     )
+    late_keep, late_send = grad_expert_ins(other, expert_rows, pre_grad, 2, 2, in_far)
+    back, out_send, late_send = lax.optimization_barrier((back, out_send, late_send))
+    near_rows = keep[quarter : 2 * quarter] + got_near[quarter:].astype(F32)
+    near_rows = (near_rows + back[quarter:].astype(F32)).astype(BF16)
+    near_rows = trade(near_rows, 2)
     grad_hidden, grad_attn, grad_second_part = finish_rows(
         keep,
         got_near,
@@ -1413,7 +1417,6 @@
         scale_two,
         second_gain[None],
         grad_out,
-        out_send,
         in_ready,
     )
     grad_second_part = jnp.sum(grad_second_part, 0)
@@ -1441,31 +1444,30 @@
     )
     small = small + swap_core(small)
     small = small + swap_y(small)
-    late_keep, late_send = grad_expert_ins(other, expert_rows, pre_grad, 2, 2, grad_attn)
+    own_in_keep, own_in_send = grad_expert_ins(
+        half_arg, expert_rows, pre_grad, 0, held, grad_attn
+    )
     pieces = spread_tensor(grad_attn)
     late_near, late_far = fold_pairs(late_keep, swap_core(late_send), pieces[2])
     out_near, out_far = fold_pairs(out_keep, swap_core(out_send), pieces[2])
     out_ready = (out_near + swap_y(out_far).astype(F32)).astype(BF16)
     late_ready = (late_near + swap_y(late_far).astype(F32)).astype(BF16)
     in_back = trade(in_ready, 4)
+    before = (late_far, out_far, own_in_send, in_back)
     grad_attn, grad_qkv, gain_part, one_keep, one_send = attention_backward(
-        share_arg, tokens, weights, tables, (query, keys, values), pieces, late_ready, in_back, out_far, small
+        share_arg, tokens, weights, tables, (query, keys, values), pieces, *before
     )
     late_back = trade(late_ready, 4)
     grad_one = scatter_tensor(one_keep, one_send, row)
     own_out_near, own_out_far = fold_pairs(own_out_keep, swap_core(own_out_send), grad_one)
     own_out_across = swap_y(own_out_far)
-
-    own_in_keep, own_in_send = grad_expert_ins(
-        half_arg, expert_rows, pre_grad, 0, held, grad_one
-    )
-    keep, send_near, send_far = reduce_parts(
-        place_arg, first_normed, grad_qkv, grad_attn, attended, small, gain_part, late_back, own_in_send
-    )
     own_in_near, own_in_far = fold_pairs(own_in_keep, swap_core(own_in_send), grad_one)
     own_in_across = swap_y(own_in_far)
-    out_back = trade(out_ready, 4)
-    total, out_back = scatter_experts(keep, send_near, send_far, out_back)
+    before = (late_ready,)
+    keep, send_near, send_far = reduce_parts(
+        place_arg, first_normed, grad_qkv, grad_attn, attended, small, gain_part, *before
+    )
+    total, late_back = scatter_experts(keep, send_near, send_far, late_back)
     total, own_out_across, own_in_across = lax.optimization_barrier(
         (total.astype(BF16), own_out_across, own_in_across)
     )
@@ -1480,8 +1482,10 @@
         )
     ]
     shards = gather_experts(total)
+    out_ready, shards[1] = lax.optimization_barrier((out_ready, shards[1]))
+    out_back = trade(out_ready, 4)
     grad_query, grad_key, grad_value, grad_output, small = scalar_call(
-        unpack_body, "unpack", place_arg, shards, shapes
+        unpack_body, "unpack", place_arg, shards, shapes, (out_back,)
     )
 
     gain_part = jnp.sum(small[:, expert_count + 8 : expert_count + 16], 1).reshape(8, -1)

time: 577 us -> 561 us (0.972)
  waiting for transfers between devices: 236 us -> 217 us
    ppermute x15, waiting for transfers between devices: 63.7 us -> 39.5 us  [swap_y(): return lax.ppermute(value, 'tensor', [(i, i ^ 2) for i in range(4)])]
    unnamed x150 -> x124, local copies, waits for them, and re-layouts: 12.1 us -> 7.79 us
  transfers between devices with their start and end apart: 80 -> 80, of which waited for: 35 -> 37; matrix products, arithmetic and copies ran while one was open for 8% -> 10% of each run, Pallas kernels for 17% -> 23%
where the time goes in v7:
time: 561 us; the launch traced here: 551 us
  waiting for transfers between devices  217 us (39%)
  Pallas kernels  167 us (30%)
  starting transfers between devices  89.9 us (16%)
  other arithmetic  53.7 us (10%)
  local copies, waits for them, and re-layouts  15.9 us (3%)
    ppermute x44, waiting for transfers between devices, trade(): return lax.ppermute(value, 'expert', [(i, i ^ bits) for i in range(8)])  173 us
    ppermute x44, starting transfers between devices, trade(): return lax.ppermute(value, 'expert', [(i, i ^ bits) for i in range(8)])  70.3 us
    ppermute x15, waiting for transfers between devices, swap_y(): return lax.ppermute(value, 'tensor', [(i, i ^ 2) for i in range(4)])  39.5 us
    pallas_call x2, Pallas kernels, experts_backward(): pl.pallas_call(backward_body, grid_spec=pltpu.PrefetchScalarGridSpec(num_...  36 us
    pallas_call x5, Pallas kernels, scalar_call(): pl.pallas_call(body, grid_spec=pltpu.PrefetchScalarGridSpec(num_scalar_pr...  27.6 us
    pallas_call x3, Pallas kernels, grad_expert_ins(): pl.pallas_call(grad_in_body, grid_spec=pltpu.PrefetchScalarGridSpec(num_s...  21.8 us
    pallas_call x2, Pallas kernels, second(): pl.pallas_call(forward_second, grid_spec=pltpu.PrefetchScalarGridSpec(num...  21.7 us
    pallas_call x1, Pallas kernels, experts_forward(): pl.pallas_call(forward_first, grid_spec=pltpu.PrefetchScalarGridSpec(num_...  17.6 us
  transfers between devices with their start and end apart: 80, of which 37 were waited for; matrix products, arithmetic and copies ran while one was open for 10% of the time, Pallas kernels for 23%

profile of v7, /device:TPU:0, one launch (start us, length us, event | category | flops | bytes accessed | tf_op | source)
XLA Modules:
  0.0 550.7 jit_solution(16513422827576389116)
XLA Ops:
  18.7 8.2 %attention_forward.1 = (bf16[512,1024]{1,0:T(8,128)(2,1)}, bf16[512,256]{1,0:T(8,128)(2,1)}, bf16[512,128]{1,0:T(8,128)(2,1)}, bf16[512,128]{1,0:T(8,128)(2,1)},...) custom-call(s32[1]{0:T(128)} %bitcast.2.core_ref, bf16[512,1024]{1,0:T(8,128)(2,1)} %tokens.3, ...), custom_call_target="tpu_custom_call" | custom-call | tf_op jit(solution)/shard_map/attention_forward/pallas_call | solution.py:973
  27.8 17.9 %collective-permute-done.3 = s32[16,128]{1,0:T(8,128)S(1)} collective-permute-done((s32[16,128]{1,0:T(8,128)S(1)}, s32[16,128]{1,0:T(8,128)S(1)}, u32[]{:S(2)}, u32[]{:S(2)}) %collective-permute-start.3) | collective-permute-done | bytes 8224 | tf_op jit(solution)/shard_map/ppermute | solution.py:1204
  74.2 22.5 %collective-permute-done.8.refs_7_.refs_15_ = bf16[3072,128]{1,0:T(8,128)(2,1)} collective-permute-done((bf16[3072,128]{1,0:T(8,128)(2,1)}, bf16[3072,128]{1,0:T(8,128)(2,1)}, u32[]{:S(2)}, u32[]{:S(2)}) %collective-permute-start.8) | collective-permute-done | bytes 786464 | tf_op jit(solution)/shard_map/ppermute | solution.py:1204
  99.5 8.3 %collective-permute-done.13.refs_2_ = bf16[128,1024]{1,0:T(8,128)(2,1)S(1)} collective-permute-done((bf16[128,1024]{1,0:T(8,128)(2,1)S(1)}, bf16[128,1024]{1,0:T(8,128)(2,1)S(1)}, u32[]{:S(2)}, u32[]{:S(2)}) %collective-permute-start.13) | collective-permute-done | bytes 262176 | tf_op jit(solution)/shard_map/ppermute | solution.py:1204
  127.8 17.6 %experts_forward_a.1 = (f32[1024,1024]{1,0:T(8,128)}, bf16[4,1024,1024]{2,1,0:T(8,128)(2,1)}, bf16[4,1024,512]{2,1,0:T(8,128)(2,1)}, f32[1024,128]{1,0:T(8,128)}, bf16[1024,1024]{1,0:T(8,128)(2,1)}) custom-call(s32[1]{0:T(128)} %bitcast.1.half_ref, bf16[128,1024]{1,0:T(8,128)(2,1)} %copy-done.12, bf16[128,1024]{1,0:T(8,128)(2,1)} %collective-permute-done.11.refs_1_, ...), custom_call_target="tpu_custom_call" | custom-call | tf_op jit(solution)/shard_map/experts_forward_a/pallas_call | solution.py:643
  150.0 10.8 %experts_forward_b.2 = (bf16[256,1024]{1,0:T(8,128)(2,1)}, bf16[256,1024]{1,0:T(8,128)(2,1)}, bf16[4,1024,1024]{2,1,0:T(8,128)(2,1)}, bf16[4,1024,512]{2,1,0:T(8,128)(2,1)}) custom-call(s32[1]{0:T(128)} %bitcast.1.half_ref, bf16[1024,1024]{1,0:T(8,128)(2,1)} %get-tuple-element.147.refs_0_.rows_ref, ...), custom_call_target="tpu_custom_call", output_to_operand_aliasing={{2}: (12, {}), {3}: (13, {})} | custom-call | tf_op jit(solution)/shard_map/experts_forward_b/pallas_call | solution.py:667
  162.3 11.0 %experts_forward_b.3 = (f32[512,1024]{1,0:T(8,128)}, bf16[4,1024,1024]{2,1,0:T(8,128)(2,1)}, bf16[4,1024,512]{2,1,0:T(8,128)(2,1)}) custom-call(s32[1]{0:T(128)} %bitcast.1.half_ref, bf16[1024,1024]{1,0:T(8,128)(2,1)} %get-tuple-element.147.refs_0_.rows_ref, ...), custom_call_target="tpu_custom_call", output_to_operand_aliasing={{1}: (12, {}), {2}: (13, {})} | custom-call | tf_op jit(solution)/shard_map/experts_forward_b/pallas_call | solution.py:667
  195.5 7.4 %collective-permute-done.27 = bf16[128,1024]{1,0:T(8,128)(2,1)S(1)} collective-permute-done((bf16[128,1024]{1,0:T(8,128)(2,1)}, bf16[128,1024]{1,0:T(8,128)(2,1)S(1)}, u32[]{:S(2)}, u32[]{:S(2)}) %collective-permute-start.27) | collective-permute-done | bytes 262176 | tf_op jit(solution)/shard_map/ppermute | solution.py:1204
  216.3 7.6 %collective-permute-done.33.refs_1_ = bf16[128,1024]{1,0:T(8,128)(2,1)S(1)} collective-permute-done((bf16[128,1024]{1,0:T(8,128)(2,1)S(1)}, bf16[128,1024]{1,0:T(8,128)(2,1)S(1)}, u32[]{:S(2)}, u32[]{:S(2)}) %collective-permute-start.33) | collective-permute-done | bytes 262176 | tf_op jit(solution)/shard_map/ppermute | solution.py:1204
  225.3 8.7 %collective-permute-done.35.refs_2_ = bf16[128,1024]{1,0:T(8,128)(2,1)S(1)} collective-permute-done((bf16[128,1024]{1,0:T(8,128)(2,1)S(1)}, bf16[128,1024]{1,0:T(8,128)(2,1)S(1)}, u32[]{:S(2)}, u32[]{:S(2)}) %collective-permute-start.35) | collective-permute-done | bytes 262176 | tf_op jit(solution)/shard_map/ppermute | solution.py:1204
  244.0 17.8 %experts_backward.2 = (bf16[256,1024]{1,0:T(8,128)(2,1)}, bf16[256,1024]{1,0:T(8,128)(2,1)}, bf16[4,1024,1024]{2,1,0:T(8,128)(2,1)}, f32[1024,128]{1,0:T(8,128)}, bf16[1024,1024]{1,0:T(8,128)(2,1)}) custom-call(s32[1]{0:T(128)} %bitcast.1.half_ref, bf16[128,1024]{1,0:T(8,128)(2,1)} %copy-done.37, bf16[128,1024]{1,0:T(8,128)(2,1)} %copy-done.38, ...), custom_call_target="tpu_custom_call" | custom-call | tf_op jit(solution)/shard_map/experts_backward/pallas_call | solution.py:757
  262.6 18.2 %experts_backward.3 = (f32[512,1024]{1,0:T(8,128)}, bf16[4,1024,1024]{2,1,0:T(8,128)(2,1)}, f32[1024,128]{1,0:T(8,128)}, bf16[1024,1024]{1,0:T(8,128)(2,1)}) custom-call(s32[1]{0:T(128)} %bitcast.1.half_ref, bf16[128,1024]{1,0:T(8,128)(2,1)} %copy-done.23, ...), custom_call_target="tpu_custom_call", output_to_operand_aliasing={{1}: (20, {}), {2}: (21, {}), {3}: (22, {})} | custom-call | tf_op jit(solution)/shard_map/experts_backward/pallas_call | solution.py:757
  283.0 6.1 %grad_expert_in.3 = (bf16[2,2,2,512,128]{4,3,2,1,0:T(8,128)(2,1)}, bf16[2,2,2,512,128]{4,3,2,1,0:T(8,128)(2,1)}) custom-call(s32[1]{0:T(128)S(6)} %sub.46.half_ref, bf16[1024,1024]{1,0:T(8,128)(2,1)} %get-tuple-element.147.refs_0_.rows_ref, bf16[4,1024,1024]{2,1,0:T(8,128)(2,1)} %get-tuple-element.180.pre_ref, bf16[256,1024]{1,0:T(8,128)(2,1)} %add_convert_fusion.3.refs_0_), custom_call_target="tpu_custom_call" | custom-call | tf_op jit(solution)/shard_map/grad_expert_in/pallas_call | solution.py:840
  301.9 6.1 %grad_expert_in.4 = (bf16[2,2,2,512,128]{4,3,2,1,0:T(8,128)(2,1)}, bf16[2,2,2,512,128]{4,3,2,1,0:T(8,128)(2,1)}) custom-call(s32[1]{0:T(128)S(6)} %sub.46.half_ref, bf16[1024,1024]{1,0:T(8,128)(2,1)} %get-tuple-element.147.refs_0_.rows_ref, bf16[4,1024,1024]{2,1,0:T(8,128)(2,1)} %get-tuple-element.180.pre_ref, ...), custom_call_target="tpu_custom_call" | custom-call | tf_op jit(solution)/shard_map/grad_expert_in/pallas_call | solution.py:840
  308.0 10.2 %grad_expert_out.1 = (bf16[2,4,128,512]{3,2,1,0:T(8,128)(2,1)}, bf16[2,4,128,512]{3,2,1,0:T(8,128)(2,1)}, bf16[2,4,128,512]{3,2,1,0:T(8,128)(2,1)}, bf16[2,4,128,512]{3,2,1,0:T(8,128)(2,1)}) custom-call(s32[1]{0:T(128)} %bitcast.1.half_ref, bf16[4,1024,512]{2,1,0:T(8,128)(2,1)} %get-tuple-element.178.gated_ref, ...), custom_call_target="tpu_custom_call" | custom-call | tf_op jit(solution)/shard_map/grad_expert_out/pallas_call | solution.py:798
  325.0 5.5 collective-permute-done.43.two
  343.7 9.6 %grad_expert_in.5 = (bf16[2,4,2,512,128]{4,3,2,1,0:T(8,128)(2,1)}, bf16[2,4,2,512,128]{4,3,2,1,0:T(8,128)(2,1)}) custom-call(s32[1]{0:T(128)} %bitcast.1.half_ref, bf16[1024,1024]{1,0:T(8,128)(2,1)} %get-tuple-element.147.refs_0_.rows_ref, bf16[4,1024,1024]{2,1,0:T(8,128)(2,1)} %get-tuple-element.180.pre_ref, bf16[128,1024]{1,0:T(8,128)(2,1)} %get-tuple-element.188.refs_0_.first), custom_call_target="tpu_custom_call" | custom-call | tf_op jit(solution)/shard_map/grad_expert_in/pallas_call | solution.py:840
  361.4 10.8 %attention_backward.1 = (bf16[512,1024]{1,0:T(8,128)(2,1)}, bf16[512,512]{1,0:T(8,128)(2,1)}, f32[8,1024]{1,0:T(8,128)}, f32[2,128,1024]{2,1,0:T(8,128)}, bf16[2,128,1024]{2,1,0:T(8,128)(2,1)}) custom-call(s32[1]{0:T(128)} %bitcast.share_ref, bf16[512,1024]{1,0:T(8,128)(2,1)} %tokens.3, bf16[1024,256]{1,0:T(8,128)(2,1)} %query_w.3, bf16[1024,128]{1,0:T(8,128)(2,1)} %key_w.3, ...), custom_call_target="tpu_custom_call" | custom-call | tf_op jit(solution)/shard_map/attention_backward/pallas_call | solution.py:973
  388.8 8.0 %collective-permute-done.53 = bf16[2,2,512,128]{3,2,1,0:T(8,128)(2,1)S(1)} collective-permute-done((bf16[2,2,512,128]{3,2,1,0:T(8,128)(2,1)S(1)}, bf16[2,2,512,128]{3,2,1,0:T(8,128)(2,1)S(1)}, u32[]{:S(2)}, u32[]{:S(2)}) %collective-permute-start.53) | collective-permute-done | bytes 524320 | tf_op jit(solution)/shard_map/ppermute | solution.py:1208
  399.0 8.1 %reduce_parts.1 = (f32[512,896]{1,0:T(8,128)}, bf16[256,896]{1,0:T(8,128)(2,1)}, bf16[256,896]{1,0:T(8,128)(2,1)}) custom-call(s32[1]{0:T(128)} %bitcast.13.place_ref, bf16[512,1024]{1,0:T(8,128)(2,1)} %get-tuple-element.164.normed, bf16[512,512]{1,0:T(8,128)(2,1)} %get-tuple-element.196.grad_qkv, bf16[512,1024]{1,0:T(8,128)(2,1)} %get-tuple-element.197.grad, ...), custom_call_target="tpu_custom_call" | custom-call | tf_op jit(solution)/shard_map/reduce_parts/pallas_call | solution.py:1138
  423.4 9.1 %collective-permute-done.57 = bf16[2,2,512,128]{3,2,1,0:T(8,128)(2,1)} collective-permute-done((bf16[2,2,512,128]{3,2,1,0:T(8,128)(2,1)S(1)}, bf16[2,2,512,128]{3,2,1,0:T(8,128)(2,1)}, u32[]{:S(2)}, u32[]{:S(2)}) %collective-permute-start.57) | collective-permute-done | bytes 524320 | tf_op jit(solution)/shard_map/ppermute | solution.py:1204
  449.3 13.3 %collective-permute-done.58 = bf16[128,896]{1,0:T(8,128)(2,1)} collective-permute-done((bf16[128,896]{1,0:T(8,128)(2,1)S(1)}, bf16[128,896]{1,0:T(8,128)(2,1)}, u32[]{:S(2)}, u32[]{:S(2)}) %collective-permute-start.58) | collective-permute-done | bytes 229408 | tf_op jit(solution)/shard_map/ppermute | solution.py:1204
  470.3 14.8 %collective-permute-done.63 = bf16[4,128,512]{2,1,0:T(8,128)(2,1)} collective-permute-done((bf16[4,128,512]{2,1,0:T(8,128)(2,1)}, bf16[4,128,512]{2,1,0:T(8,128)(2,1)}, u32[]{:S(2)}, u32[]{:S(2)}) %collective-permute-start.63) | collective-permute-done | bytes 524320 | tf_op jit(solution)/shard_map/ppermute | solution.py:1208
  500.2 19.8 %collective-permute-done.68.refs_2_ = bf16[128,896]{1,0:T(8,128)(2,1)S(1)} collective-permute-done((bf16[128,896]{1,0:T(8,128)(2,1)S(1)}, bf16[128,896]{1,0:T(8,128)(2,1)S(1)}, u32[]{:S(2)}, u32[]{:S(2)}) %collective-permute-start.68) | collective-permute-done | bytes 229408 | tf_op jit(solution)/shard_map/ppermute | solution.py:1204
  (352 shorter events, 269.0 us)
Async XLA Ops:
  5.1 40.6 %collective-permute-start.1 = (bf16[6144,128]{1,0:T(8,128)(2,1)}, bf16[6144,128]{1,0:T(8,128)(2,1)S(1)}, u32[]{:S(2)}, u32[]{:S(2)}) collective-permute-start(bf16[6144,128]{1,0:T(8,128)(2,1)} %get-tuple-element.123.refs_0_.refs_10_.refs_3_.refs_7_), channel_id=1, source_target_pairs={{0,2},{1,3},{2,0},{3,1},{4,6},{5,7},{6,4},{7,5},{8,10},{9,11},{10,... | collective-permute-start | bytes 4718600 | tf_op jit(solution)/shard_map/ppermute | solution.py:1208
  8.1 37.6 %collective-permute-start = (bf16[3072,128]{1,0:T(8,128)(2,1)}, bf16[3072,128]{1,0:T(8,128)(2,1)}, u32[]{:S(2)}, u32[]{:S(2)}) collective-permute-start(bf16[3072,128]{1,0:T(8,128)(2,1)} %get-tuple-element.122), channel_id=1, source_target_pairs={{0,16},{4,20},{8,24},{12,28},{16,0},{20,4},{24,8},{28,12},{1,17},{... | collective-permute-start | bytes 2359304 | tf_op jit(solution)/shard_map/ppermute | solution.py:1204
  13.6 32.1 %collective-permute-start.3 = (s32[16,128]{1,0:T(8,128)S(1)}, s32[16,128]{1,0:T(8,128)S(1)}, u32[]{:S(2)}, u32[]{:S(2)}) collective-permute-start(s32[16,128]{1,0:T(8,128)S(1)} %concatenate.46), channel_id=1, source_target_pairs={{0,16},{4,20},{8,24},{12,28},{16,0},{20,4},{24,8},{28,12},{1,17},{... | collective-permute-start | bytes 24584 | tf_op jit(solution)/shard_map/ppermute | solution.py:1204
  13.9 31.7 %collective-permute-start.4 = (s32[16,128]{1,0:T(8,128)S(1)}, s32[16,128]{1,0:T(8,128)S(1)}, u32[]{:S(2)}, u32[]{:S(2)}) collective-permute-start(s32[16,128]{1,0:T(8,128)S(1)} %concatenate.46), channel_id=1, source_target_pairs={{0,24},{4,28},{8,16},{12,20},{16,8},{20,12},{24,0},{28,4},{1,25},{... | collective-permute-start | bytes 24584 | tf_op jit(solution)/shard_map/ppermute | solution.py:1204
  52.6 44.0 %collective-permute-start.8 = (bf16[3072,128]{1,0:T(8,128)(2,1)}, bf16[3072,128]{1,0:T(8,128)(2,1)}, u32[]{:S(2)}, u32[]{:S(2)}) collective-permute-start(bf16[3072,128]{1,0:T(8,128)(2,1)} %get-tuple-element.133), channel_id=1, source_target_pairs={{0,16},{4,20},{8,24},{12,28},{16,0},{20,4},{24,8},{28,12},{1,17},{... | collective-permute-start | bytes 2359304 | tf_op jit(solution)/shard_map/ppermute | solution.py:1204
  67.7 29.0 %collective-permute-start.11 = (bf16[128,1024]{1,0:T(8,128)(2,1)S(1)}, bf16[128,1024]{1,0:T(8,128)(2,1)}, u32[]{:S(2)}, u32[]{:S(2)}) collective-permute-start(bf16[128,1024]{1,0:T(8,128)(2,1)S(1)} %get-tuple-element.267.refs_0_), channel_id=1, source_target_pairs={{0,8},{4,12},{8,0},{12,4},{16,24},{20,28},{24,16},{28,20},{1,9},{5... | collective-permute-start | bytes 786440 | tf_op jit(solution)/shard_map/ppermute | solution.py:1204
  68.4 39.4 %collective-permute-start.13 = (bf16[128,1024]{1,0:T(8,128)(2,1)S(1)}, bf16[128,1024]{1,0:T(8,128)(2,1)S(1)}, u32[]{:S(2)}, u32[]{:S(2)}) collective-permute-start(bf16[128,1024]{1,0:T(8,128)(2,1)S(1)} %get-tuple-element.267.refs_0_), channel_id=1, source_target_pairs={{0,16},{4,20},{8,24},{12,28},{16,0},{20,4},{24,8},{28,12},{1,17},{... | collective-permute-start | bytes 786440 | tf_op jit(solution)/shard_map/ppermute | solution.py:1204
  73.7 51.0 %collective-permute-start.10 = (bf16[3072,128]{1,0:T(8,128)(2,1)}, bf16[3072,128]{1,0:T(8,128)(2,1)}, u32[]{:S(2)}, u32[]{:S(2)}) collective-permute-start(bf16[3072,128]{1,0:T(8,128)(2,1)} %collective-permute-done.refs_14_.refs_11_), channel_id=1, source_target_pairs={{0,2},{1,3},{2,0},{3,1},{4,6},{5,7},{6,4},{7,5},{8,10},{9,11},{10,... | collective-permute-start | bytes 2359304 | tf_op jit(solution)/shard_map/ppermute | solution.py:1208
  74.2 53.6 %collective-permute-start.17 = (bf16[6144,128]{1,0:T(8,128)(2,1)S(1)}, bf16[6144,128]{1,0:T(8,128)(2,1)}, u32[]{:S(2)}, u32[]{:S(2)}) collective-permute-start(bf16[6144,128]{1,0:T(8,128)(2,1)S(1)} %copy-done.3), channel_id=1, source_target_pairs={{0,1},{1,0},{2,3},{3,2},{4,5},{5,4},{6,7},{7,6},{8,9},{9,8},{10,11... | collective-permute-start | bytes 4718600 | tf_op jit(solution)/shard_map/ppermute | solution.py:1212
  96.7 31.1 %collective-permute-start.18 = (bf16[6144,128]{1,0:T(8,128)(2,1)S(1)}, bf16[6144,128]{1,0:T(8,128)(2,1)}, u32[]{:S(2)}, u32[]{:S(2)}) collective-permute-start(bf16[6144,128]{1,0:T(8,128)(2,1)S(1)} %collective-permute-done.1.refs_12_.refs_5_.refs_9_), channel_id=1, source_target_pairs={{0,1},{1,0},{2,3},{3,2},{4,5},{5,4},{6,7},{7,6},{8,9},{9,8},{10,11... | collective-permute-start | bytes 4718600 | tf_op jit(solution)/shard_map/ppermute | solution.py:1212
  292.0 28.4 %collective-permute-start.41 = (bf16[256,1024]{1,0:T(8,128)(2,1)}, bf16[256,1024]{1,0:T(8,128)(2,1)}, u32[]{:S(2)}, u32[]{:S(2)}) collective-permute-start(bf16[256,1024]{1,0:T(8,128)(2,1)} %add_convert_fusion.3.refs_0_), channel_id=1, source_target_pairs={{0,16},{4,20},{8,24},{12,28},{16,0},{20,4},{24,8},{28,12},{1,17},{... | collective-permute-start | bytes 1572872 | tf_op jit(solution)/shard_map/ppermute | solution.py:1204
  322.6 30.7 %collective-permute-start.48 = (bf16[2,2,2,512,128]{4,3,2,1,0:T(8,128)(2,1)}, bf16[2,2,2,512,128]{4,3,2,1,0:T(8,128)(2,1)}, u32[]{:S(2)}, u32[]{:S(2)}) collective-permute-start(bf16[2,2,2,512,128]{4,3,2,1,0:T(8,128)(2,1)} %get-tuple-element.190), channel_id=1, source_target_pairs={{0,1},{1,0},{2,3},{3,2},{4,5},{5,4},{6,7},{7,6},{8,9},{9,8},{10,11... | collective-permute-start | bytes 3145736 | tf_op jit(solution)/shard_map/ppermute | solution.py:1212
  343.2 29.1 %collective-permute-start.51 = (f32[40,1024]{1,0:T(8,128)}, f32[40,1024]{1,0:T(8,128)}, u32[]{:S(2)}, u32[]{:S(2)}) collective-permute-start(f32[40,1024]{1,0:T(8,128)} %maximum_maximum_fusion), channel_id=1, source_target_pairs={{0,1},{1,0},{2,3},{3,2},{4,5},{5,4},{6,7},{7,6},{8,9},{9,8},{10,11... | collective-permute-start | bytes 491528 | tf_op jit(solution)/shard_map/ppermute | solution.py:1212
  353.3 80.7 %collective-permute-start.64 = (bf16[2,4,2,512,128]{4,3,2,1,0:T(8,128)(2,1)}, bf16[2,4,2,512,128]{4,3,2,1,0:T(8,128)(2,1)}, u32[]{:S(2)}, u32[]{:S(2)}) collective-permute-start(bf16[2,4,2,512,128]{4,3,2,1,0:T(8,128)(2,1)} %get-tuple-element.195.refs_2_), channel_id=1, source_target_pairs={{0,1},{1,0},{2,3},{3,2},{4,5},{5,4},{6,7},{7,6},{8,9},{9,8},{10,11... | collective-permute-start | bytes 6291464 | tf_op jit(solution)/shard_map/ppermute | solution.py:1212
  375.4 35.2 %collective-permute-start.60 = (bf16[2,4,128,512]{3,2,1,0:T(8,128)(2,1)}, bf16[2,4,128,512]{3,2,1,0:T(8,128)(2,1)}, u32[]{:S(2)}, u32[]{:S(2)}) collective-permute-start(bf16[2,4,128,512]{3,2,1,0:T(8,128)(2,1)} %get-tuple-element.211), channel_id=1, source_target_pairs={{0,1},{1,0},{2,3},{3,2},{4,5},{5,4},{6,7},{7,6},{8,9},{9,8},{10,11... | collective-permute-start | bytes 3145736 | tf_op jit(solution)/shard_map/ppermute | solution.py:1212
  386.2 54.1 %collective-permute-start.29 = (bf16[128,1024]{1,0:T(8,128)(2,1)S(1)}, bf16[128,1024]{1,0:T(8,128)(2,1)}, u32[]{:S(2)}, u32[]{:S(2)}) collective-permute-start(bf16[128,1024]{1,0:T(8,128)(2,1)S(1)} %copy-done.28), channel_id=1, source_target_pairs={{0,1},{1,0},{2,3},{3,2},{4,5},{5,4},{6,7},{7,6},{8,9},{9,8},{10,11... | collective-permute-start | bytes 786440 | tf_op jit(solution)/shard_map/ppermute | solution.py:1212
  386.2 55.5 %collective-permute-start.31 = (bf16[128,1024]{1,0:T(8,128)(2,1)}, bf16[128,1024]{1,0:T(8,128)(2,1)}, u32[]{:S(2)}, u32[]{:S(2)}) collective-permute-start(bf16[128,1024]{1,0:T(8,128)(2,1)} %collective-permute-done.30.refs_2_), channel_id=1, source_target_pairs={{0,1},{1,0},{2,3},{3,2},{4,5},{5,4},{6,7},{7,6},{8,9},{9,8},{10,11... | collective-permute-start | bytes 786440 | tf_op jit(solution)/shard_map/ppermute | solution.py:1212
  438.4 46.7 %collective-permute-start.65 = (bf16[4,2,512,128]{3,2,1,0:T(8,128)(2,1)}, bf16[4,2,512,128]{3,2,1,0:T(8,128)(2,1)S(1)}, u32[]{:S(2)}, u32[]{:S(2)}) collective-permute-start(bf16[4,2,512,128]{3,2,1,0:T(8,128)(2,1)} %get-tuple-element.216), channel_id=1, source_target_pairs={{0,2},{1,3},{2,0},{3,1},{4,6},{5,7},{6,4},{7,5},{8,10},{9,11},{10,... | collective-permute-start | bytes 3145736 | tf_op jit(solution)/shard_map/ppermute | solution.py:1208
  440.3 45.1 %collective-permute-start.66 = (bf16[4,128,512]{2,1,0:T(8,128)(2,1)}, bf16[4,128,512]{2,1,0:T(8,128)(2,1)}, u32[]{:S(2)}, u32[]{:S(2)}) collective-permute-start(bf16[4,128,512]{2,1,0:T(8,128)(2,1)} %get-tuple-element.194.refs_1_), channel_id=1, source_target_pairs={{0,2},{1,3},{2,0},{3,1},{4,6},{5,7},{6,4},{7,5},{8,10},{9,11},{10,... | collective-permute-start | bytes 1572872 | tf_op jit(solution)/shard_map/ppermute | solution.py:1208
  441.7 43.5 %collective-permute-start.63 = (bf16[4,128,512]{2,1,0:T(8,128)(2,1)}, bf16[4,128,512]{2,1,0:T(8,128)(2,1)}, u32[]{:S(2)}, u32[]{:S(2)}) collective-permute-start(bf16[4,128,512]{2,1,0:T(8,128)(2,1)} %get-tuple-element.214), channel_id=1, source_target_pairs={{0,2},{1,3},{2,0},{3,1},{4,6},{5,7},{6,4},{7,5},{8,10},{9,11},{10,... | collective-permute-start | bytes 1572872 | tf_op jit(solution)/shard_map/ppermute | solution.py:1208
  491.3 28.7 %collective-permute-start.68 = (bf16[128,896]{1,0:T(8,128)(2,1)S(1)}, bf16[128,896]{1,0:T(8,128)(2,1)S(1)}, u32[]{:S(2)}, u32[]{:S(2)}) collective-permute-start(bf16[128,896]{1,0:T(8,128)(2,1)S(1)} %add_convert_fusion.8.refs_0_), channel_id=1, source_target_pairs={{0,16},{4,20},{8,24},{12,28},{16,0},{20,4},{24,8},{28,12},{1,17},{... | collective-permute-start | bytes 688136 | tf_op jit(solution)/shard_map/ppermute | solution.py:1204
  495.4 30.4 %collective-permute-start.70 = (bf16[128,896]{1,0:T(8,128)(2,1)S(1)}, bf16[128,896]{1,0:T(8,128)(2,1)S(1)}, u32[]{:S(2)}, u32[]{:S(2)}) collective-permute-start(bf16[128,896]{1,0:T(8,128)(2,1)S(1)} %add_convert_fusion.8.refs_0_), channel_id=1, source_target_pairs={{0,4},{4,0},{8,12},{12,8},{16,20},{20,16},{24,28},{28,24},{1,5},{5... | collective-permute-start | bytes 688136 | tf_op jit(solution)/shard_map/ppermute | solution.py:1204
  496.0 40.2 %collective-permute-start.74 = (bf16[4,128,512]{2,1,0:T(8,128)(2,1)}, bf16[4,128,512]{2,1,0:T(8,128)(2,1)}, u32[]{:S(2)}, u32[]{:S(2)}) collective-permute-start(bf16[4,128,512]{2,1,0:T(8,128)(2,1)} %add_convert_fusion), channel_id=1, source_target_pairs={{0,16},{4,20},{8,24},{12,28},{16,0},{20,4},{24,8},{28,12},{1,17},{... | collective-permute-start | bytes 1572872 | tf_op jit(solution)/shard_map/ppermute | solution.py:1204
  498.7 27.1 %collective-permute-start.71 = (bf16[128,896]{1,0:T(8,128)(2,1)}, bf16[128,896]{1,0:T(8,128)(2,1)S(1)}, u32[]{:S(2)}, u32[]{:S(2)}) collective-permute-start(bf16[128,896]{1,0:T(8,128)(2,1)} %collective-permute-done.67.refs_1_), channel_id=1, source_target_pairs={{0,4},{4,0},{8,12},{12,8},{16,20},{20,16},{24,28},{28,24},{1,5},{5... | collective-permute-start | bytes 688136 | tf_op jit(solution)/shard_map/ppermute | solution.py:1204
  (115 other events, 1613.0 us)

commit v8 on v7

--- a/solution.py
+++ b/solution.py
@@ -1384,6 +1384,7 @@
     mean_part = jnp.concatenate([mean_high, (mean_part - mean_high.astype(F32)).astype(BF16)], 1)
     router_pair = jnp.concatenate([router_weight, router_weight], 1)
     mean_rows = jnp.einsum("te,de->td", mean_part, router_pair, preferred_element_type=F32)
+    out_pieces = spread_tensor(output.astype(BF16))
     shards = gather_experts(grad_moe)
     packs = (gates, router_rel, pre, own, near, far)
     send_near, send_far, *saved = experts_backward(1, half_arg, shards[4:], *packs)
@@ -1396,14 +1397,41 @@
     back = trade(far_rows, 4)
     got_near = trade(send_near, 1)
     other = 1 - half_arg
-    in_keep, in_send = grad_expert_ins(other, expert_rows, pre_grad, 0, 2, far_rows)
+    in_keep, in_send = grad_expert_ins(
+        other, expert_rows, pre_grad, 0, 2, far_rows, *out_pieces[1:]
+    )
     in_near, in_far = fold_pairs(in_keep, swap_core(in_send))
     in_ready = (in_near + swap_y(in_far).astype(F32)).astype(BF16)
     out_keep, out_send, own_out_keep, own_out_send = grad_expert_outs(
         half_arg, gated, grad_rows, in_far
     )
     late_keep, late_send = grad_expert_ins(other, expert_rows, pre_grad, 2, 2, in_far)
-    back, out_send, late_send = lax.optimization_barrier((back, out_send, late_send))
+    router_part = jnp.einsum(
+        "te,td->ed", logit_grad.astype(BF16), expert_rows, preferred_element_type=F32
+    )
+    router_part = router_part[:expert_count] + router_part[expert_count : 2 * expert_count]
+    router_part = lax.dynamic_slice_in_dim(
+        jnp.concatenate([router_part, router_part], 0),
+        jnp.bitwise_and(expert_count - base, expert_count - 1),
+        expert_count,
+        0,
+    )
+    mean_router = jnp.einsum("te,td->ed", mean_part, normed_two, preferred_element_type=F32)
+    router_part = router_part + mean_router[:expert_count] + mean_router[expert_count:]
+
+    small = jnp.concatenate(
+        [
+            router_part,
+            jnp.full((1, model_width), squared_local),
+            jnp.zeros((7, model_width), F32),
+        ],
+        0,
+    )
+    small = small + swap_core(small)
+    small = small + swap_y(small)
+    back, out_send, late_send, small = lax.optimization_barrier(
+        (back, out_send, late_send, small)
+    )
     near_rows = keep[quarter : 2 * quarter] + got_near[quarter:].astype(F32)
     near_rows = (near_rows + back[quarter:].astype(F32)).astype(BF16)
     near_rows = trade(near_rows, 2)
@@ -1419,31 +1447,6 @@
         grad_out,
         in_ready,
     )
-    grad_second_part = jnp.sum(grad_second_part, 0)
-    router_part = jnp.einsum(
-        "te,td->ed", logit_grad.astype(BF16), expert_rows, preferred_element_type=F32
-    )
-    router_part = router_part[:expert_count] + router_part[expert_count : 2 * expert_count]
-    router_part = lax.dynamic_slice_in_dim(
-        jnp.concatenate([router_part, router_part], 0),
-        jnp.bitwise_and(expert_count - base, expert_count - 1),
-        expert_count,
-        0,
-    )
-    mean_router = jnp.einsum("te,td->ed", mean_part, normed_two, preferred_element_type=F32)
-    router_part = router_part + mean_router[:expert_count] + mean_router[expert_count:]
-
-    small = jnp.concatenate(
-        [
-            router_part,
-            grad_second_part[None],
-            jnp.full((1, model_width), squared_local),
-            jnp.zeros((6, model_width), F32),
-        ],
-        0,
-    )
-    small = small + swap_core(small)
-    small = small + swap_y(small)
     own_in_keep, own_in_send = grad_expert_ins(
         half_arg, expert_rows, pre_grad, 0, held, grad_attn
     )
@@ -1464,13 +1467,13 @@
     own_in_near, own_in_far = fold_pairs(own_in_keep, swap_core(own_in_send), grad_one)
     own_in_across = swap_y(own_in_far)
     before = (late_ready,)
+    gains = jnp.concatenate([grad_second_part, gain_part], 0)
     keep, send_near, send_far = reduce_parts(
-        place_arg, first_normed, grad_qkv, grad_attn, attended, small, gain_part, *before
-    )
-    total, late_back = scatter_experts(keep, send_near, send_far, late_back)
-    total, own_out_across, own_in_across = lax.optimization_barrier(
-        (total.astype(BF16), own_out_across, own_in_across)
-    )
+        place_arg, first_normed, grad_qkv, grad_attn, attended, small, gains, *before
+    )
+    out_back = trade(out_ready, 4)
+    total, late_back, out_back = scatter_experts(keep, send_near, send_far, late_back, out_back)
+    total = total.astype(BF16)
     shapes = [
         jax.ShapeDtypeStruct(shape, F32)
         for shape in (
@@ -1482,15 +1485,14 @@
         )
     ]
     shards = gather_experts(total)
-    out_ready, shards[1] = lax.optimization_barrier((out_ready, shards[1]))
-    out_back = trade(out_ready, 4)
     grad_query, grad_key, grad_value, grad_output, small = scalar_call(
-        unpack_body, "unpack", place_arg, shards, shapes, (out_back,)
-    )
-
-    gain_part = jnp.sum(small[:, expert_count + 8 : expert_count + 16], 1).reshape(8, -1)
-    gain_part = gain_part + swap_core(gain_part)
-    gain_part = (gain_part + swap_y(gain_part)).reshape(-1)
+        unpack_body, "unpack", place_arg, shards, shapes, (own_out_across, own_in_across)
+    )
+
+    gains = small[:, expert_count + 8 : expert_count + 24].reshape(model_width, 2, 8)
+    gains = jnp.sum(gains, 2).T.reshape(16, -1)
+    gains = gains + swap_core(gains)
+    gains = (gains + swap_y(gains)).reshape(2, -1)
 
     scale_mine = lax.rsqrt(jnp.mean(tokens_mine * tokens_mine, -1, keepdims=True) + EPS)
     unit_mine = tokens_mine * scale_mine
@@ -1499,7 +1501,7 @@
         grad_unit_one - unit_mine * jnp.mean(grad_unit_one * unit_mine, -1, keepdims=True)
     )
     grad_tokens = assemble(share_arg, spread_tensor(grad_tokens.astype(BF16)), F32)
-    layer_output = assemble(share_arg, spread_tensor(output.astype(BF16)), BF16)
+    layer_output = assemble(share_arg, out_pieces, BF16)
     grad_expert_out = ordered(
         half_index, own_out_near + own_out_across.astype(F32), out_back.astype(F32)
     )
@@ -1510,14 +1512,14 @@
     )
     return (
         layer_output,
-        small[0, expert_count + 1] / (2.0 * model_width * valid_total),
+        small[0, expert_count] / (2.0 * model_width * valid_total),
         grad_tokens,
-        gain_part,
+        gains[1],
         grad_query,
         grad_key,
         grad_value,
         grad_output,
-        small[:, expert_count],
+        gains[0],
         small[:, :expert_count],
         grad_expert_in,
         grad_expert_out,

time: 561 us -> 520 us (0.927); the launches traced: 551 us -> 515 us
  waiting for transfers between devices: 217 us -> 168 us
  Pallas kernels: 167 us -> 177 us
  local copies, waits for them, and re-layouts: 15.9 us -> 21.9 us
    ppermute x44, waiting for transfers between devices: 173 us -> 144 us  [trade(): return lax.ppermute(value, 'expert', [(i, i ^ bits) for i in range(8)])]
    ppermute x15, waiting for transfers between devices: 39.5 us -> 19.1 us  [swap_y(): return lax.ppermute(value, 'tensor', [(i, i ^ 2) for i in range(4)])]
    pallas_call x3, Pallas kernels: 21.8 us -> 31.7 us  [grad_expert_ins(): pl.pallas_call(grad_in_body, grid_spec=pltpu.PrefetchScalarGridSpec(num_s...]
  transfers between devices with their start and end apart: 80 -> 80, of which waited for: 37 -> 32; matrix products, arithmetic and copies ran while one was open for 10% -> 11% of each run, Pallas kernels for 23% -> 28%
where the time goes in v8:
time: 520 us; the launch traced here: 515 us
  Pallas kernels  177 us (34%)
  waiting for transfers between devices  168 us (32%)
  starting transfers between devices  87.8 us (17%)
  other arithmetic  52.2 us (10%)
  local copies, waits for them, and re-layouts  21.9 us (4%)
    ppermute x44, waiting for transfers between devices, trade(): return lax.ppermute(value, 'expert', [(i, i ^ bits) for i in range(8)])  144 us
    ppermute x44, starting transfers between devices, trade(): return lax.ppermute(value, 'expert', [(i, i ^ bits) for i in range(8)])  69.4 us
    pallas_call x2, Pallas kernels, experts_backward(): pl.pallas_call(backward_body, grid_spec=pltpu.PrefetchScalarGridSpec(num_...  36.2 us
    pallas_call x3, Pallas kernels, grad_expert_ins(): pl.pallas_call(grad_in_body, grid_spec=pltpu.PrefetchScalarGridSpec(num_s...  31.7 us
    pallas_call x5, Pallas kernels, scalar_call(): pl.pallas_call(body, grid_spec=pltpu.PrefetchScalarGridSpec(num_scalar_pr...  27.6 us
    pallas_call x2, Pallas kernels, second(): pl.pallas_call(forward_second, grid_spec=pltpu.PrefetchScalarGridSpec(num...  21.8 us
    ppermute x15, waiting for transfers between devices, swap_y(): return lax.ppermute(value, 'tensor', [(i, i ^ 2) for i in range(4)])  19.1 us
    pallas_call x1, Pallas kernels, experts_forward(): pl.pallas_call(forward_first, grid_spec=pltpu.PrefetchScalarGridSpec(num_...  17.6 us
  transfers between devices with their start and end apart: 80, of which 32 were waited for; matrix products, arithmetic and copies ran while one was open for 11% of the time, Pallas kernels for 28%

profile of v8, /device:TPU:0, one launch (start us, length us, event | category | flops | bytes accessed | tf_op | source)
XLA Modules:
  0.0 515.4 jit_solution(3929952634088265623)
XLA Ops:
  18.7 8.2 %attention_forward.1 = (bf16[512,1024]{1,0:T(8,128)(2,1)}, bf16[512,256]{1,0:T(8,128)(2,1)}, bf16[512,128]{1,0:T(8,128)(2,1)}, bf16[512,128]{1,0:T(8,128)(2,1)},...) custom-call(s32[1]{0:T(128)} %bitcast.2.core_ref, bf16[512,1024]{1,0:T(8,128)(2,1)} %tokens.3, ...), custom_call_target="tpu_custom_call" | custom-call | tf_op jit(solution)/shard_map/attention_forward/pallas_call | solution.py:973
  27.8 17.9 %collective-permute-done.3 = s32[16,128]{1,0:T(8,128)S(1)} collective-permute-done((s32[16,128]{1,0:T(8,128)S(1)}, s32[16,128]{1,0:T(8,128)S(1)}, u32[]{:S(2)}, u32[]{:S(2)}) %collective-permute-start.3) | collective-permute-done | bytes 8224 | tf_op jit(solution)/shard_map/ppermute | solution.py:1204
  74.2 22.5 %collective-permute-done.8.refs_7_.refs_15_ = bf16[3072,128]{1,0:T(8,128)(2,1)} collective-permute-done((bf16[3072,128]{1,0:T(8,128)(2,1)}, bf16[3072,128]{1,0:T(8,128)(2,1)}, u32[]{:S(2)}, u32[]{:S(2)}) %collective-permute-start.8) | collective-permute-done | bytes 786464 | tf_op jit(solution)/shard_map/ppermute | solution.py:1204
  99.5 8.3 %collective-permute-done.13.refs_2_ = bf16[128,1024]{1,0:T(8,128)(2,1)S(1)} collective-permute-done((bf16[128,1024]{1,0:T(8,128)(2,1)S(1)}, bf16[128,1024]{1,0:T(8,128)(2,1)S(1)}, u32[]{:S(2)}, u32[]{:S(2)}) %collective-permute-start.13) | collective-permute-done | bytes 262176 | tf_op jit(solution)/shard_map/ppermute | solution.py:1204
  127.8 17.6 %experts_forward_a.1 = (f32[1024,1024]{1,0:T(8,128)}, bf16[4,1024,1024]{2,1,0:T(8,128)(2,1)}, bf16[4,1024,512]{2,1,0:T(8,128)(2,1)}, f32[1024,128]{1,0:T(8,128)}, bf16[1024,1024]{1,0:T(8,128)(2,1)}) custom-call(s32[1]{0:T(128)} %bitcast.1.half_ref, bf16[128,1024]{1,0:T(8,128)(2,1)} %copy-done.14, bf16[128,1024]{1,0:T(8,128)(2,1)} %collective-permute-done.11.refs_1_, ...), custom_call_target="tpu_custom_call" | custom-call | tf_op jit(solution)/shard_map/experts_forward_a/pallas_call | solution.py:643
  150.0 10.9 %experts_forward_b.2 = (bf16[256,1024]{1,0:T(8,128)(2,1)}, bf16[256,1024]{1,0:T(8,128)(2,1)}, bf16[4,1024,1024]{2,1,0:T(8,128)(2,1)}, bf16[4,1024,512]{2,1,0:T(8,128)(2,1)}) custom-call(s32[1]{0:T(128)} %bitcast.1.half_ref, bf16[1024,1024]{1,0:T(8,128)(2,1)} %get-tuple-element.144.refs_0_.rows_ref, ...), custom_call_target="tpu_custom_call", output_to_operand_aliasing={{2}: (12, {}), {3}: (13, {})} | custom-call | tf_op jit(solution)/shard_map/experts_forward_b/pallas_call | solution.py:667
  162.5 10.9 %experts_forward_b.3 = (f32[512,1024]{1,0:T(8,128)}, bf16[4,1024,1024]{2,1,0:T(8,128)(2,1)}, bf16[4,1024,512]{2,1,0:T(8,128)(2,1)}) custom-call(s32[1]{0:T(128)} %bitcast.1.half_ref, bf16[1024,1024]{1,0:T(8,128)(2,1)} %get-tuple-element.144.refs_0_.rows_ref, ...), custom_call_target="tpu_custom_call", output_to_operand_aliasing={{1}: (12, {}), {2}: (13, {})} | custom-call | tf_op jit(solution)/shard_map/experts_forward_b/pallas_call | solution.py:667
  195.7 7.4 %collective-permute-done.27 = bf16[128,1024]{1,0:T(8,128)(2,1)S(1)} collective-permute-done((bf16[128,1024]{1,0:T(8,128)(2,1)}, bf16[128,1024]{1,0:T(8,128)(2,1)S(1)}, u32[]{:S(2)}, u32[]{:S(2)}) %collective-permute-start.27) | collective-permute-done | bytes 262176 | tf_op jit(solution)/shard_map/ppermute | solution.py:1204
  216.9 7.2 %collective-permute-done.33.refs_1_ = bf16[128,1024]{1,0:T(8,128)(2,1)S(1)} collective-permute-done((bf16[128,1024]{1,0:T(8,128)(2,1)S(1)}, bf16[128,1024]{1,0:T(8,128)(2,1)S(1)}, u32[]{:S(2)}, u32[]{:S(2)}) %collective-permute-start.33) | collective-permute-done | bytes 262176 | tf_op jit(solution)/shard_map/ppermute | solution.py:1204
  225.5 8.7 %collective-permute-done.35.refs_2_ = bf16[128,1024]{1,0:T(8,128)(2,1)S(1)} collective-permute-done((bf16[128,1024]{1,0:T(8,128)(2,1)S(1)}, bf16[128,1024]{1,0:T(8,128)(2,1)S(1)}, u32[]{:S(2)}, u32[]{:S(2)}) %collective-permute-start.35) | collective-permute-done | bytes 262176 | tf_op jit(solution)/shard_map/ppermute | solution.py:1204
  244.2 17.8 %experts_backward.2 = (bf16[256,1024]{1,0:T(8,128)(2,1)}, bf16[256,1024]{1,0:T(8,128)(2,1)}, bf16[4,1024,1024]{2,1,0:T(8,128)(2,1)}, f32[1024,128]{1,0:T(8,128)}, bf16[1024,1024]{1,0:T(8,128)(2,1)}) custom-call(s32[1]{0:T(128)} %bitcast.1.half_ref, bf16[128,1024]{1,0:T(8,128)(2,1)} %copy-done.48, bf16[128,1024]{1,0:T(8,128)(2,1)} %copy-done.49, ...), custom_call_target="tpu_custom_call" | custom-call | tf_op jit(solution)/shard_map/experts_backward/pallas_call | solution.py:757
  263.7 18.4 %experts_backward.3 = (f32[512,1024]{1,0:T(8,128)}, bf16[4,1024,1024]{2,1,0:T(8,128)(2,1)}, f32[1024,128]{1,0:T(8,128)}, bf16[1024,1024]{1,0:T(8,128)(2,1)}) custom-call(s32[1]{0:T(128)} %bitcast.1.half_ref, bf16[128,1024]{1,0:T(8,128)(2,1)} %copy-done.28, ...), custom_call_target="tpu_custom_call", output_to_operand_aliasing={{1}: (20, {}), {2}: (21, {}), {3}: (22, {})} | custom-call | tf_op jit(solution)/shard_map/experts_backward/pallas_call | solution.py:757
  286.6 16.1 %grad_expert_in.3 = (bf16[2,2,2,512,128]{4,3,2,1,0:T(8,128)(2,1)}, bf16[2,2,2,512,128]{4,3,2,1,0:T(8,128)(2,1)}) custom-call(s32[1]{0:T(128)S(6)} %sub.46.half_ref, bf16[1024,1024]{1,0:T(8,128)(2,1)} %get-tuple-element.144.refs_0_.rows_ref, bf16[4,1024,1024]{2,1,0:T(8,128)(2,1)} %get-tuple-element.177.pre_ref, bf16[256,1024]{1,0:T(8,128)(2,1)} %add_convert_fusion.3.refs_0_, ...), custom_call_target="tpu_custom_call" | custom-call | tf_op jit(solution)/shard_map/grad_expert_in/pallas_call | solution.py:840
  316.5 6.1 %grad_expert_in.4 = (bf16[2,2,2,512,128]{4,3,2,1,0:T(8,128)(2,1)}, bf16[2,2,2,512,128]{4,3,2,1,0:T(8,128)(2,1)}) custom-call(s32[1]{0:T(128)S(6)} %sub.46.half_ref, bf16[1024,1024]{1,0:T(8,128)(2,1)} %get-tuple-element.144.refs_0_.rows_ref, bf16[4,1024,1024]{2,1,0:T(8,128)(2,1)} %get-tuple-element.177.pre_ref, ...), custom_call_target="tpu_custom_call" | custom-call | tf_op jit(solution)/shard_map/grad_expert_in/pallas_call | solution.py:840
  322.6 10.2 %grad_expert_out.1 = (bf16[2,4,128,512]{3,2,1,0:T(8,128)(2,1)}, bf16[2,4,128,512]{3,2,1,0:T(8,128)(2,1)}, bf16[2,4,128,512]{3,2,1,0:T(8,128)(2,1)}, bf16[2,4,128,512]{3,2,1,0:T(8,128)(2,1)}) custom-call(s32[1]{0:T(128)} %bitcast.1.half_ref, bf16[4,1024,512]{2,1,0:T(8,128)(2,1)} %get-tuple-element.175.gated_ref, ...), custom_call_target="tpu_custom_call" | custom-call | tf_op jit(solution)/shard_map/grad_expert_out/pallas_call | solution.py:798
  350.5 5.8 %collective-permute-done.48.refs_0_.third = bf16[128,1024]{1,0:T(8,128)(2,1)S(1)} collective-permute-done((bf16[128,1024]{1,0:T(8,128)(2,1)}, bf16[128,1024]{1,0:T(8,128)(2,1)S(1)}, u32[]{:S(2)}, u32[]{:S(2)}) %collective-permute-start.48) | collective-permute-done | bytes 262176 | tf_op jit(solution)/shard_map/ppermute | solution.py:1208
  361.0 9.6 %grad_expert_in.5 = (bf16[2,4,2,512,128]{4,3,2,1,0:T(8,128)(2,1)}, bf16[2,4,2,512,128]{4,3,2,1,0:T(8,128)(2,1)}) custom-call(s32[1]{0:T(128)} %bitcast.1.half_ref, bf16[1024,1024]{1,0:T(8,128)(2,1)} %get-tuple-element.144.refs_0_.rows_ref, bf16[4,1024,1024]{2,1,0:T(8,128)(2,1)} %get-tuple-element.177.pre_ref, bf16[128,1024]{1,0:T(8,128)(2,1)} %get-tuple-element.186.refs_0_.first), custom_call_target="tpu_custom_call" | custom-call | tf_op jit(solution)/shard_map/grad_expert_in/pallas_call | solution.py:840
  375.0 10.9 %attention_backward.1 = (bf16[512,1024]{1,0:T(8,128)(2,1)}, bf16[512,512]{1,0:T(8,128)(2,1)}, f32[8,1024]{1,0:T(8,128)}, f32[2,128,1024]{2,1,0:T(8,128)}, bf16[2,128,1024]{2,1,0:T(8,128)(2,1)}) custom-call(s32[1]{0:T(128)} %bitcast.share_ref, bf16[512,1024]{1,0:T(8,128)(2,1)} %tokens.3, bf16[1024,256]{1,0:T(8,128)(2,1)} %query_w.3, bf16[1024,128]{1,0:T(8,128)(2,1)} %key_w.3, ...), custom_call_target="tpu_custom_call" | custom-call | tf_op jit(solution)/shard_map/attention_backward/pallas_call | solution.py:973
  393.8 7.6 %collective-permute-done.53 = bf16[2,2,512,128]{3,2,1,0:T(8,128)(2,1)S(1)} collective-permute-done((bf16[2,2,512,128]{3,2,1,0:T(8,128)(2,1)S(1)}, bf16[2,2,512,128]{3,2,1,0:T(8,128)(2,1)S(1)}, u32[]{:S(2)}, u32[]{:S(2)}) %collective-permute-start.53) | collective-permute-done | bytes 524320 | tf_op jit(solution)/shard_map/ppermute | solution.py:1208
  403.0 7.7 %reduce_parts.1 = (f32[512,896]{1,0:T(8,128)}, bf16[256,896]{1,0:T(8,128)(2,1)}, bf16[256,896]{1,0:T(8,128)(2,1)}) custom-call(s32[1]{0:T(128)} %bitcast.13.place_ref, bf16[512,1024]{1,0:T(8,128)(2,1)} %get-tuple-element.161.normed, bf16[512,512]{1,0:T(8,128)(2,1)} %get-tuple-element.194.grad_qkv, bf16[512,1024]{1,0:T(8,128)(2,1)} %get-tuple-element.195.grad, ...), custom_call_target="tpu_custom_call" | custom-call | tf_op jit(solution)/shard_map/reduce_parts/pallas_call | solution.py:1138
  423.9 6.1 %collective-permute-done.59 = bf16[4,128,512]{2,1,0:T(8,128)(2,1)S(1)} collective-permute-done((bf16[4,128,512]{2,1,0:T(8,128)(2,1)}, bf16[4,128,512]{2,1,0:T(8,128)(2,1)S(1)}, u32[]{:S(2)}, u32[]{:S(2)}) %collective-permute-start.59) | collective-permute-done | bytes 524320 | tf_op jit(solution)/shard_map/ppermute | solution.py:1204
  430.6 9.9 %collective-permute-done.57 = bf16[2,2,512,128]{3,2,1,0:T(8,128)(2,1)} collective-permute-done((bf16[2,2,512,128]{3,2,1,0:T(8,128)(2,1)S(1)}, bf16[2,2,512,128]{3,2,1,0:T(8,128)(2,1)}, u32[]{:S(2)}, u32[]{:S(2)}) %collective-permute-start.57) | collective-permute-done | bytes 524320 | tf_op jit(solution)/shard_map/ppermute | solution.py:1204
  452.9 7.8 %collective-permute-done.60 = bf16[128,896]{1,0:T(8,128)(2,1)S(1)} collective-permute-done((bf16[128,896]{1,0:T(8,128)(2,1)S(1)}, bf16[128,896]{1,0:T(8,128)(2,1)S(1)}, u32[]{:S(2)}, u32[]{:S(2)}) %collective-permute-start.60) | collective-permute-done | bytes 229408 | tf_op jit(solution)/shard_map/ppermute | solution.py:1204
  478.5 8.8 %collective-permute-done.63.refs_2_ = bf16[128,896]{1,0:T(8,128)(2,1)S(1)} collective-permute-done((bf16[128,896]{1,0:T(8,128)(2,1)}, bf16[128,896]{1,0:T(8,128)(2,1)S(1)}, u32[]{:S(2)}, u32[]{:S(2)}) %collective-permute-start.63) | collective-permute-done | bytes 229408 | tf_op jit(solution)/shard_map/ppermute | solution.py:1204
  (369 shorter events, 248.8 us)
Async XLA Ops:
  5.1 40.6 %collective-permute-start.1 = (bf16[6144,128]{1,0:T(8,128)(2,1)}, bf16[6144,128]{1,0:T(8,128)(2,1)S(1)}, u32[]{:S(2)}, u32[]{:S(2)}) collective-permute-start(bf16[6144,128]{1,0:T(8,128)(2,1)} %get-tuple-element.120.refs_0_.refs_10_.refs_3_.refs_7_), channel_id=1, source_target_pairs={{0,2},{1,3},{2,0},{3,1},{4,6},{5,7},{6,4},{7,5},{8,10},{9,11},{10,... | collective-permute-start | bytes 4718600 | tf_op jit(solution)/shard_map/ppermute | solution.py:1208
  8.1 37.6 %collective-permute-start = (bf16[3072,128]{1,0:T(8,128)(2,1)}, bf16[3072,128]{1,0:T(8,128)(2,1)}, u32[]{:S(2)}, u32[]{:S(2)}) collective-permute-start(bf16[3072,128]{1,0:T(8,128)(2,1)} %get-tuple-element.119), channel_id=1, source_target_pairs={{0,16},{4,20},{8,24},{12,28},{16,0},{20,4},{24,8},{28,12},{1,17},{... | collective-permute-start | bytes 2359304 | tf_op jit(solution)/shard_map/ppermute | solution.py:1204
  13.6 32.1 %collective-permute-start.3 = (s32[16,128]{1,0:T(8,128)S(1)}, s32[16,128]{1,0:T(8,128)S(1)}, u32[]{:S(2)}, u32[]{:S(2)}) collective-permute-start(s32[16,128]{1,0:T(8,128)S(1)} %concatenate.49), channel_id=1, source_target_pairs={{0,16},{4,20},{8,24},{12,28},{16,0},{20,4},{24,8},{28,12},{1,17},{... | collective-permute-start | bytes 24584 | tf_op jit(solution)/shard_map/ppermute | solution.py:1204
  13.9 31.7 %collective-permute-start.4 = (s32[16,128]{1,0:T(8,128)S(1)}, s32[16,128]{1,0:T(8,128)S(1)}, u32[]{:S(2)}, u32[]{:S(2)}) collective-permute-start(s32[16,128]{1,0:T(8,128)S(1)} %concatenate.49), channel_id=1, source_target_pairs={{0,24},{4,28},{8,16},{12,20},{16,8},{20,12},{24,0},{28,4},{1,25},{... | collective-permute-start | bytes 24584 | tf_op jit(solution)/shard_map/ppermute | solution.py:1204
  52.6 44.0 %collective-permute-start.8 = (bf16[3072,128]{1,0:T(8,128)(2,1)}, bf16[3072,128]{1,0:T(8,128)(2,1)}, u32[]{:S(2)}, u32[]{:S(2)}) collective-permute-start(bf16[3072,128]{1,0:T(8,128)(2,1)} %get-tuple-element.130), channel_id=1, source_target_pairs={{0,16},{4,20},{8,24},{12,28},{16,0},{20,4},{24,8},{28,12},{1,17},{... | collective-permute-start | bytes 2359304 | tf_op jit(solution)/shard_map/ppermute | solution.py:1204
  67.7 29.0 %collective-permute-start.11 = (bf16[128,1024]{1,0:T(8,128)(2,1)S(1)}, bf16[128,1024]{1,0:T(8,128)(2,1)}, u32[]{:S(2)}, u32[]{:S(2)}) collective-permute-start(bf16[128,1024]{1,0:T(8,128)(2,1)S(1)} %get-tuple-element.261.refs_0_), channel_id=1, source_target_pairs={{0,8},{4,12},{8,0},{12,4},{16,24},{20,28},{24,16},{28,20},{1,9},{5... | collective-permute-start | bytes 786440 | tf_op jit(solution)/shard_map/ppermute | solution.py:1204
  68.4 39.4 %collective-permute-start.13 = (bf16[128,1024]{1,0:T(8,128)(2,1)S(1)}, bf16[128,1024]{1,0:T(8,128)(2,1)S(1)}, u32[]{:S(2)}, u32[]{:S(2)}) collective-permute-start(bf16[128,1024]{1,0:T(8,128)(2,1)S(1)} %get-tuple-element.261.refs_0_), channel_id=1, source_target_pairs={{0,16},{4,20},{8,24},{12,28},{16,0},{20,4},{24,8},{28,12},{1,17},{... | collective-permute-start | bytes 786440 | tf_op jit(solution)/shard_map/ppermute | solution.py:1204
  73.7 51.0 %collective-permute-start.10 = (bf16[3072,128]{1,0:T(8,128)(2,1)}, bf16[3072,128]{1,0:T(8,128)(2,1)}, u32[]{:S(2)}, u32[]{:S(2)}) collective-permute-start(bf16[3072,128]{1,0:T(8,128)(2,1)} %collective-permute-done.refs_14_.refs_11_), channel_id=1, source_target_pairs={{0,2},{1,3},{2,0},{3,1},{4,6},{5,7},{6,4},{7,5},{8,10},{9,11},{10,... | collective-permute-start | bytes 2359304 | tf_op jit(solution)/shard_map/ppermute | solution.py:1208
  74.2 53.6 %collective-permute-start.17 = (bf16[6144,128]{1,0:T(8,128)(2,1)S(1)}, bf16[6144,128]{1,0:T(8,128)(2,1)}, u32[]{:S(2)}, u32[]{:S(2)}) collective-permute-start(bf16[6144,128]{1,0:T(8,128)(2,1)S(1)} %copy-done.3), channel_id=1, source_target_pairs={{0,1},{1,0},{2,3},{3,2},{4,5},{5,4},{6,7},{7,6},{8,9},{9,8},{10,11... | collective-permute-start | bytes 4718600 | tf_op jit(solution)/shard_map/ppermute | solution.py:1212
  96.7 31.1 %collective-permute-start.18 = (bf16[6144,128]{1,0:T(8,128)(2,1)S(1)}, bf16[6144,128]{1,0:T(8,128)(2,1)}, u32[]{:S(2)}, u32[]{:S(2)}) collective-permute-start(bf16[6144,128]{1,0:T(8,128)(2,1)S(1)} %collective-permute-done.1.refs_12_.refs_5_.refs_9_), channel_id=1, source_target_pairs={{0,1},{1,0},{2,3},{3,2},{4,5},{5,4},{6,7},{7,6},{8,9},{9,8},{10,11... | collective-permute-start | bytes 4718600 | tf_op jit(solution)/shard_map/ppermute | solution.py:1212
  236.3 27.4 %collective-permute-start.30 = (bf16[128,1024]{1,0:T(8,128)(2,1)}, bf16[128,1024]{1,0:T(8,128)(2,1)S(1)}, u32[]{:S(2)}, u32[]{:S(2)}) collective-permute-start(bf16[128,1024]{1,0:T(8,128)(2,1)} %get-tuple-element.263.refs_0_), channel_id=1, source_target_pairs={{0,2},{1,3},{2,0},{3,1},{4,6},{5,7},{6,4},{7,5},{8,10},{9,11},{10,... | collective-permute-start | bytes 786440 | tf_op jit(solution)/shard_map/ppermute | solution.py:1208
  237.9 48.0 %collective-permute-start.29 = (bf16[128,1024]{1,0:T(8,128)(2,1)}, bf16[128,1024]{1,0:T(8,128)(2,1)S(1)}, u32[]{:S(2)}, u32[]{:S(2)}) collective-permute-start(bf16[128,1024]{1,0:T(8,128)(2,1)} %get-tuple-element.263.refs_0_), channel_id=1, source_target_pairs={{0,1},{1,0},{2,3},{3,2},{4,5},{5,4},{6,7},{7,6},{8,9},{9,8},{10,11... | collective-permute-start | bytes 786440 | tf_op jit(solution)/shard_map/ppermute | solution.py:1212
  303.5 29.3 %collective-permute-start.41 = (bf16[256,1024]{1,0:T(8,128)(2,1)S(1)}, bf16[256,1024]{1,0:T(8,128)(2,1)S(1)}, u32[]{:S(2)}, u32[]{:S(2)}) collective-permute-start(bf16[256,1024]{1,0:T(8,128)(2,1)S(1)} %copy-done.23), channel_id=1, source_target_pairs={{0,16},{4,20},{8,24},{12,28},{16,0},{20,4},{24,8},{28,12},{1,17},{... | collective-permute-start | bytes 1572872 | tf_op jit(solution)/shard_map/ppermute | solution.py:1204
  307.9 27.4 %collective-permute-start.40 = (bf16[256,1024]{1,0:T(8,128)(2,1)}, bf16[256,1024]{1,0:T(8,128)(2,1)S(1)}, u32[]{:S(2)}, u32[]{:S(2)}) collective-permute-start(bf16[256,1024]{1,0:T(8,128)(2,1)} %get-tuple-element.173), channel_id=1, source_target_pairs={{0,4},{4,0},{8,12},{12,8},{16,20},{20,16},{24,28},{28,24},{1,5},{5... | collective-permute-start | bytes 1572872 | tf_op jit(solution)/shard_map/ppermute | solution.py:1204
  312.7 25.4 %collective-permute-start.46 = (bf16[2,2,512,128]{3,2,1,0:T(8,128)(2,1)}, bf16[2,2,512,128]{3,2,1,0:T(8,128)(2,1)}, u32[]{:S(2)}, u32[]{:S(2)}) collective-permute-start(bf16[2,2,512,128]{3,2,1,0:T(8,128)(2,1)} %get-tuple-element.180.refs_0_), channel_id=1, source_target_pairs={{0,2},{1,3},{2,0},{3,1},{4,6},{5,7},{6,4},{7,5},{8,10},{9,11},{10,... | collective-permute-start | bytes 1572872 | tf_op jit(solution)/shard_map/ppermute | solution.py:1208
  334.8 35.8 %collective-permute-start.50 = (bf16[2,2,2,512,128]{4,3,2,1,0:T(8,128)(2,1)}, bf16[2,2,2,512,128]{4,3,2,1,0:T(8,128)(2,1)S(1)}, u32[]{:S(2)}, u32[]{:S(2)}) collective-permute-start(bf16[2,2,2,512,128]{4,3,2,1,0:T(8,128)(2,1)} %get-tuple-element.188), channel_id=1, source_target_pairs={{0,1},{1,0},{2,3},{3,2},{4,5},{5,4},{6,7},{7,6},{8,9},{9,8},{10,11... | collective-permute-start | bytes 3145736 | tf_op jit(solution)/shard_map/ppermute | solution.py:1212
  360.6 29.0 %collective-permute-start.58 = (bf16[4,128,512]{2,1,0:T(8,128)(2,1)}, bf16[4,128,512]{2,1,0:T(8,128)(2,1)}, u32[]{:S(2)}, u32[]{:S(2)}) collective-permute-start(bf16[4,128,512]{2,1,0:T(8,128)(2,1)} %get-tuple-element.192.refs_1_), channel_id=1, source_target_pairs={{0,2},{1,3},{2,0},{3,1},{4,6},{5,7},{6,4},{7,5},{8,10},{9,11},{10,... | collective-permute-start | bytes 1572872 | tf_op jit(solution)/shard_map/ppermute | solution.py:1208
  386.0 28.2 %collective-permute-start.69 = (bf16[2,4,128,512]{3,2,1,0:T(8,128)(2,1)}, bf16[2,4,128,512]{3,2,1,0:T(8,128)(2,1)}, u32[]{:S(2)}, u32[]{:S(2)}) collective-permute-start(bf16[2,4,128,512]{3,2,1,0:T(8,128)(2,1)} %get-tuple-element.210), channel_id=1, source_target_pairs={{0,1},{1,0},{2,3},{3,2},{4,5},{5,4},{6,7},{7,6},{8,9},{9,8},{10,11... | collective-permute-start | bytes 3145736 | tf_op jit(solution)/shard_map/ppermute | solution.py:1212
  386.5 60.3 %collective-permute-start.73 = (bf16[2,4,2,512,128]{4,3,2,1,0:T(8,128)(2,1)}, bf16[2,4,2,512,128]{4,3,2,1,0:T(8,128)(2,1)}, u32[]{:S(2)}, u32[]{:S(2)}) collective-permute-start(bf16[2,4,2,512,128]{4,3,2,1,0:T(8,128)(2,1)} %get-tuple-element.193.refs_2_), channel_id=1, source_target_pairs={{0,1},{1,0},{2,3},{3,2},{4,5},{5,4},{6,7},{7,6},{8,9},{9,8},{10,11... | collective-permute-start | bytes 6291464 | tf_op jit(solution)/shard_map/ppermute | solution.py:1212
  391.6 38.4 %collective-permute-start.59 = (bf16[4,128,512]{2,1,0:T(8,128)(2,1)}, bf16[4,128,512]{2,1,0:T(8,128)(2,1)S(1)}, u32[]{:S(2)}, u32[]{:S(2)}) collective-permute-start(bf16[4,128,512]{2,1,0:T(8,128)(2,1)} %add_convert_fusion), channel_id=1, source_target_pairs={{0,16},{4,20},{8,24},{12,28},{16,0},{20,4},{24,8},{28,12},{1,17},{... | collective-permute-start | bytes 1572872 | tf_op jit(solution)/shard_map/ppermute | solution.py:1204
  401.5 39.0 %collective-permute-start.57 = (bf16[2,2,512,128]{3,2,1,0:T(8,128)(2,1)S(1)}, bf16[2,2,512,128]{3,2,1,0:T(8,128)(2,1)}, u32[]{:S(2)}, u32[]{:S(2)}) collective-permute-start(bf16[2,2,512,128]{3,2,1,0:T(8,128)(2,1)S(1)} %add_convert_fusion.1.refs_0_), channel_id=1, source_target_pairs={{0,16},{4,20},{8,24},{12,28},{16,0},{20,4},{24,8},{28,12},{1,17},{... | collective-permute-start | bytes 1572872 | tf_op jit(solution)/shard_map/ppermute | solution.py:1204
  417.8 50.0 %collective-permute-start.72 = (bf16[4,128,512]{2,1,0:T(8,128)(2,1)}, bf16[4,128,512]{2,1,0:T(8,128)(2,1)S(1)}, u32[]{:S(2)}, u32[]{:S(2)}) collective-permute-start(bf16[4,128,512]{2,1,0:T(8,128)(2,1)} %get-tuple-element.213), channel_id=1, source_target_pairs={{0,2},{1,3},{2,0},{3,1},{4,6},{5,7},{6,4},{7,5},{8,10},{9,11},{10,... | collective-permute-start | bytes 1572872 | tf_op jit(solution)/shard_map/ppermute | solution.py:1208
  422.3 30.2 %collective-permute-start.76 = (bf16[128,1024]{1,0:T(8,128)(2,1)S(1)}, bf16[128,1024]{1,0:T(8,128)(2,1)}, u32[]{:S(2)}, u32[]{:S(2)}) collective-permute-start(bf16[128,1024]{1,0:T(8,128)(2,1)S(1)} %fusion.6.refs_0_), channel_id=1, source_target_pairs={{0,2},{1,3},{2,0},{3,1},{4,6},{5,7},{6,4},{7,5},{8,10},{9,11},{10,... | collective-permute-start | bytes 786440 | tf_op jit(solution)/shard_map/ppermute | solution.py:1208
  452.5 46.0 %collective-permute-start.74 = (bf16[4,2,512,128]{3,2,1,0:T(8,128)(2,1)}, bf16[4,2,512,128]{3,2,1,0:T(8,128)(2,1)S(1)}, u32[]{:S(2)}, u32[]{:S(2)}) collective-permute-start(bf16[4,2,512,128]{3,2,1,0:T(8,128)(2,1)} %get-tuple-element.215), channel_id=1, source_target_pairs={{0,2},{1,3},{2,0},{3,1},{4,6},{5,7},{6,4},{7,5},{8,10},{9,11},{10,... | collective-permute-start | bytes 3145736 | tf_op jit(solution)/shard_map/ppermute | solution.py:1208
  (122 other events, 1607.7 us)

commit v9 on v8

--- a/solution.py
+++ b/solution.py
@@ -350,7 +350,7 @@
 
 BF16 = jnp.bfloat16
 F32 = jnp.float32
-CHUNK = 256
+CHUNK = 512
 SHARE = 128
 PACK = 12 * SHARE
 NT = (((1,), (1,)), ((), ()))

time: 520 us -> 511 us (0.983)
  Pallas kernels: 177 us -> 161 us
    pallas_call x3, Pallas kernels: 31.7 us -> 20.7 us  [grad_expert_ins(): pl.pallas_call(grad_in_body, grid_spec=pltpu.PrefetchScalarGridSpec(num_s...]
  transfers between devices with their start and end apart: 80 -> 80, of which waited for: 32 -> 34; matrix products, arithmetic and copies ran while one was open for 11% -> 11% of each run, Pallas kernels for 28% -> 27%
where the time goes in v9:
time: 511 us; the launch traced here: 501 us
  waiting for transfers between devices  166 us (32%)
  Pallas kernels  161 us (32%)
  starting transfers between devices  91.9 us (18%)
  other arithmetic  52.2 us (10%)
  local copies, waits for them, and re-layouts  21.8 us (4%)
    ppermute x44, waiting for transfers between devices, trade(): return lax.ppermute(value, 'expert', [(i, i ^ bits) for i in range(8)])  143 us
    ppermute x44, starting transfers between devices, trade(): return lax.ppermute(value, 'expert', [(i, i ^ bits) for i in range(8)])  69.6 us
    pallas_call x2, Pallas kernels, experts_backward(): pl.pallas_call(backward_body, grid_spec=pltpu.PrefetchScalarGridSpec(num_...  33 us
    pallas_call x5, Pallas kernels, scalar_call(): pl.pallas_call(body, grid_spec=pltpu.PrefetchScalarGridSpec(num_scalar_pr...  27.6 us
    pallas_call x2, Pallas kernels, second(): pl.pallas_call(forward_second, grid_spec=pltpu.PrefetchScalarGridSpec(num...  20.8 us
    pallas_call x3, Pallas kernels, grad_expert_ins(): pl.pallas_call(grad_in_body, grid_spec=pltpu.PrefetchScalarGridSpec(num_s...  20.7 us
    ppermute x15, starting transfers between devices, swap_y(): return lax.ppermute(value, 'tensor', [(i, i ^ 2) for i in range(4)])  19.3 us
    ppermute x15, waiting for transfers between devices, swap_y(): return lax.ppermute(value, 'tensor', [(i, i ^ 2) for i in range(4)])  17.7 us
  transfers between devices with their start and end apart: 80, of which 34 were waited for; matrix products, arithmetic and copies ran while one was open for 11% of the time, Pallas kernels for 27%

profile of v9, /device:TPU:0, one launch (start us, length us, event | category | flops | bytes accessed | tf_op | source)
XLA Modules:
  0.0 501.2 jit_solution(8512983917948830735)
XLA Ops:
  18.7 8.2 %attention_forward.1 = (bf16[512,1024]{1,0:T(8,128)(2,1)}, bf16[512,256]{1,0:T(8,128)(2,1)}, bf16[512,128]{1,0:T(8,128)(2,1)}, bf16[512,128]{1,0:T(8,128)(2,1)},...) custom-call(s32[1]{0:T(128)} %bitcast.2.core_ref, bf16[512,1024]{1,0:T(8,128)(2,1)} %tokens.3, ...), custom_call_target="tpu_custom_call" | custom-call | tf_op jit(solution)/shard_map/attention_forward/pallas_call | solution.py:973
  27.8 17.9 %collective-permute-done.3 = s32[16,128]{1,0:T(8,128)S(1)} collective-permute-done((s32[16,128]{1,0:T(8,128)S(1)}, s32[16,128]{1,0:T(8,128)S(1)}, u32[]{:S(2)}, u32[]{:S(2)}) %collective-permute-start.3) | collective-permute-done | bytes 8224 | tf_op jit(solution)/shard_map/ppermute | solution.py:1204
  74.2 22.5 %collective-permute-done.8.refs_7_.refs_15_ = bf16[3072,128]{1,0:T(8,128)(2,1)} collective-permute-done((bf16[3072,128]{1,0:T(8,128)(2,1)}, bf16[3072,128]{1,0:T(8,128)(2,1)}, u32[]{:S(2)}, u32[]{:S(2)}) %collective-permute-start.8) | collective-permute-done | bytes 786464 | tf_op jit(solution)/shard_map/ppermute | solution.py:1204
  99.5 8.3 %collective-permute-done.13.refs_2_ = bf16[128,1024]{1,0:T(8,128)(2,1)S(1)} collective-permute-done((bf16[128,1024]{1,0:T(8,128)(2,1)S(1)}, bf16[128,1024]{1,0:T(8,128)(2,1)S(1)}, u32[]{:S(2)}, u32[]{:S(2)}) %collective-permute-start.13) | collective-permute-done | bytes 262176 | tf_op jit(solution)/shard_map/ppermute | solution.py:1204
  127.8 16.6 %experts_forward_a.1 = (f32[1024,1024]{1,0:T(8,128)}, bf16[4,1024,1024]{2,1,0:T(8,128)(2,1)}, bf16[4,1024,512]{2,1,0:T(8,128)(2,1)}, f32[1024,128]{1,0:T(8,128)}, bf16[1024,1024]{1,0:T(8,128)(2,1)}) custom-call(s32[1]{0:T(128)} %bitcast.1.half_ref, bf16[128,1024]{1,0:T(8,128)(2,1)} %copy-done.14, bf16[128,1024]{1,0:T(8,128)(2,1)} %collective-permute-done.11.refs_1_, ...), custom_call_target="tpu_custom_call" | custom-call | tf_op jit(solution)/shard_map/experts_forward_a/pallas_call | solution.py:643
  149.4 10.2 %experts_forward_b.2 = (bf16[256,1024]{1,0:T(8,128)(2,1)}, bf16[256,1024]{1,0:T(8,128)(2,1)}, bf16[4,1024,1024]{2,1,0:T(8,128)(2,1)}, bf16[4,1024,512]{2,1,0:T(8,128)(2,1)}) custom-call(s32[1]{0:T(128)} %bitcast.1.half_ref, bf16[1024,1024]{1,0:T(8,128)(2,1)} %get-tuple-element.144.refs_0_.rows_ref, ...), custom_call_target="tpu_custom_call", output_to_operand_aliasing={{2}: (12, {}), {3}: (13, {})} | custom-call | tf_op jit(solution)/shard_map/experts_forward_b/pallas_call | solution.py:667
  161.2 10.6 %experts_forward_b.3 = (f32[512,1024]{1,0:T(8,128)}, bf16[4,1024,1024]{2,1,0:T(8,128)(2,1)}, bf16[4,1024,512]{2,1,0:T(8,128)(2,1)}) custom-call(s32[1]{0:T(128)} %bitcast.1.half_ref, bf16[1024,1024]{1,0:T(8,128)(2,1)} %get-tuple-element.144.refs_0_.rows_ref, ...), custom_call_target="tpu_custom_call", output_to_operand_aliasing={{1}: (12, {}), {2}: (13, {})} | custom-call | tf_op jit(solution)/shard_map/experts_forward_b/pallas_call | solution.py:667
  194.2 7.5 %collective-permute-done.27 = bf16[128,1024]{1,0:T(8,128)(2,1)S(1)} collective-permute-done((bf16[128,1024]{1,0:T(8,128)(2,1)}, bf16[128,1024]{1,0:T(8,128)(2,1)S(1)}, u32[]{:S(2)}, u32[]{:S(2)}) %collective-permute-start.27) | collective-permute-done | bytes 262176 | tf_op jit(solution)/shard_map/ppermute | solution.py:1204
  215.4 7.3 %collective-permute-done.33.refs_1_ = bf16[128,1024]{1,0:T(8,128)(2,1)S(1)} collective-permute-done((bf16[128,1024]{1,0:T(8,128)(2,1)S(1)}, bf16[128,1024]{1,0:T(8,128)(2,1)S(1)}, u32[]{:S(2)}, u32[]{:S(2)}) %collective-permute-start.33) | collective-permute-done | bytes 262176 | tf_op jit(solution)/shard_map/ppermute | solution.py:1204
  224.0 8.9 %collective-permute-done.35.refs_2_ = bf16[128,1024]{1,0:T(8,128)(2,1)S(1)} collective-permute-done((bf16[128,1024]{1,0:T(8,128)(2,1)S(1)}, bf16[128,1024]{1,0:T(8,128)(2,1)S(1)}, u32[]{:S(2)}, u32[]{:S(2)}) %collective-permute-start.35) | collective-permute-done | bytes 262176 | tf_op jit(solution)/shard_map/ppermute | solution.py:1204
  242.8 16.1 %experts_backward.2 = (bf16[256,1024]{1,0:T(8,128)(2,1)}, bf16[256,1024]{1,0:T(8,128)(2,1)}, bf16[4,1024,1024]{2,1,0:T(8,128)(2,1)}, f32[1024,128]{1,0:T(8,128)}, bf16[1024,1024]{1,0:T(8,128)(2,1)}) custom-call(s32[1]{0:T(128)} %bitcast.1.half_ref, bf16[128,1024]{1,0:T(8,128)(2,1)} %copy-done.48, bf16[128,1024]{1,0:T(8,128)(2,1)} %copy-done.49, ...), custom_call_target="tpu_custom_call" | custom-call | tf_op jit(solution)/shard_map/experts_backward/pallas_call | solution.py:757
  260.5 16.9 %experts_backward.3 = (f32[512,1024]{1,0:T(8,128)}, bf16[4,1024,1024]{2,1,0:T(8,128)(2,1)}, f32[1024,128]{1,0:T(8,128)}, bf16[1024,1024]{1,0:T(8,128)(2,1)}) custom-call(s32[1]{0:T(128)} %bitcast.1.half_ref, bf16[128,1024]{1,0:T(8,128)(2,1)} %copy-done.28, ...), custom_call_target="tpu_custom_call", output_to_operand_aliasing={{1}: (20, {}), {2}: (21, {}), {3}: (22, {})} | custom-call | tf_op jit(solution)/shard_map/experts_backward/pallas_call | solution.py:757
  282.0 5.8 %grad_expert_in.3 = (bf16[2,2,2,512,128]{4,3,2,1,0:T(8,128)(2,1)}, bf16[2,2,2,512,128]{4,3,2,1,0:T(8,128)(2,1)}) custom-call(s32[1]{0:T(128)S(6)} %sub.46.half_ref, bf16[1024,1024]{1,0:T(8,128)(2,1)} %get-tuple-element.144.refs_0_.rows_ref, bf16[4,1024,1024]{2,1,0:T(8,128)(2,1)} %get-tuple-element.177.pre_ref, bf16[256,1024]{1,0:T(8,128)(2,1)} %add_convert_fusion.3.refs_0_, ...), custom_call_target="tpu_custom_call" | custom-call | tf_op jit(solution)/shard_map/grad_expert_in/pallas_call | solution.py:840
  301.1 5.7 %grad_expert_in.4 = (bf16[2,2,2,512,128]{4,3,2,1,0:T(8,128)(2,1)}, bf16[2,2,2,512,128]{4,3,2,1,0:T(8,128)(2,1)}) custom-call(s32[1]{0:T(128)S(6)} %sub.46.half_ref, bf16[1024,1024]{1,0:T(8,128)(2,1)} %get-tuple-element.144.refs_0_.rows_ref, bf16[4,1024,1024]{2,1,0:T(8,128)(2,1)} %get-tuple-element.177.pre_ref, ...), custom_call_target="tpu_custom_call" | custom-call | tf_op jit(solution)/shard_map/grad_expert_in/pallas_call | solution.py:840
  306.8 10.2 %grad_expert_out.1 = (bf16[2,4,128,512]{3,2,1,0:T(8,128)(2,1)}, bf16[2,4,128,512]{3,2,1,0:T(8,128)(2,1)}, bf16[2,4,128,512]{3,2,1,0:T(8,128)(2,1)}, bf16[2,4,128,512]{3,2,1,0:T(8,128)(2,1)}) custom-call(s32[1]{0:T(128)} %bitcast.1.half_ref, bf16[4,1024,512]{2,1,0:T(8,128)(2,1)} %get-tuple-element.175.gated_ref, ...), custom_call_target="tpu_custom_call" | custom-call | tf_op jit(solution)/shard_map/grad_expert_out/pallas_call | solution.py:798
  324.3 4.9 collective-permute-done.45.two
  346.8 9.1 %grad_expert_in.5 = (bf16[2,4,2,512,128]{4,3,2,1,0:T(8,128)(2,1)}, bf16[2,4,2,512,128]{4,3,2,1,0:T(8,128)(2,1)}) custom-call(s32[1]{0:T(128)} %bitcast.1.half_ref, bf16[1024,1024]{1,0:T(8,128)(2,1)} %get-tuple-element.144.refs_0_.rows_ref, bf16[4,1024,1024]{2,1,0:T(8,128)(2,1)} %get-tuple-element.177.pre_ref, bf16[128,1024]{1,0:T(8,128)(2,1)} %get-tuple-element.186.refs_0_.first), custom_call_target="tpu_custom_call" | custom-call | tf_op jit(solution)/shard_map/grad_expert_in/pallas_call | solution.py:840
  360.6 10.9 %attention_backward.1 = (bf16[512,1024]{1,0:T(8,128)(2,1)}, bf16[512,512]{1,0:T(8,128)(2,1)}, f32[8,1024]{1,0:T(8,128)}, f32[2,128,1024]{2,1,0:T(8,128)}, bf16[2,128,1024]{2,1,0:T(8,128)(2,1)}) custom-call(s32[1]{0:T(128)} %bitcast.share_ref, bf16[512,1024]{1,0:T(8,128)(2,1)} %tokens.3, bf16[1024,256]{1,0:T(8,128)(2,1)} %query_w.3, bf16[1024,128]{1,0:T(8,128)(2,1)} %key_w.3, ...), custom_call_target="tpu_custom_call" | custom-call | tf_op jit(solution)/shard_map/attention_backward/pallas_call | solution.py:973
  379.4 7.5 %collective-permute-done.53 = bf16[2,2,512,128]{3,2,1,0:T(8,128)(2,1)S(1)} collective-permute-done((bf16[2,2,512,128]{3,2,1,0:T(8,128)(2,1)S(1)}, bf16[2,2,512,128]{3,2,1,0:T(8,128)(2,1)S(1)}, u32[]{:S(2)}, u32[]{:S(2)}) %collective-permute-start.53) | collective-permute-done | bytes 524320 | tf_op jit(solution)/shard_map/ppermute | solution.py:1208
  388.7 7.7 %reduce_parts.1 = (f32[512,896]{1,0:T(8,128)}, bf16[256,896]{1,0:T(8,128)(2,1)}, bf16[256,896]{1,0:T(8,128)(2,1)}) custom-call(s32[1]{0:T(128)} %bitcast.13.place_ref, bf16[512,1024]{1,0:T(8,128)(2,1)} %get-tuple-element.161.normed, bf16[512,512]{1,0:T(8,128)(2,1)} %get-tuple-element.194.grad_qkv, bf16[512,1024]{1,0:T(8,128)(2,1)} %get-tuple-element.195.grad, ...), custom_call_target="tpu_custom_call" | custom-call | tf_op jit(solution)/shard_map/reduce_parts/pallas_call | solution.py:1138
  408.4 5.9 %collective-permute-done.59 = bf16[4,128,512]{2,1,0:T(8,128)(2,1)S(1)} collective-permute-done((bf16[4,128,512]{2,1,0:T(8,128)(2,1)}, bf16[4,128,512]{2,1,0:T(8,128)(2,1)S(1)}, u32[]{:S(2)}, u32[]{:S(2)}) %collective-permute-start.59) | collective-permute-done | bytes 524320 | tf_op jit(solution)/shard_map/ppermute | solution.py:1204
  414.9 9.9 %collective-permute-done.57 = bf16[2,2,512,128]{3,2,1,0:T(8,128)(2,1)} collective-permute-done((bf16[2,2,512,128]{3,2,1,0:T(8,128)(2,1)S(1)}, bf16[2,2,512,128]{3,2,1,0:T(8,128)(2,1)}, u32[]{:S(2)}, u32[]{:S(2)}) %collective-permute-start.57) | collective-permute-done | bytes 524320 | tf_op jit(solution)/shard_map/ppermute | solution.py:1204
  438.6 6.7 %collective-permute-done.60 = bf16[128,896]{1,0:T(8,128)(2,1)S(1)} collective-permute-done((bf16[128,896]{1,0:T(8,128)(2,1)S(1)}, bf16[128,896]{1,0:T(8,128)(2,1)S(1)}, u32[]{:S(2)}, u32[]{:S(2)}) %collective-permute-start.60) | collective-permute-done | bytes 229408 | tf_op jit(solution)/shard_map/ppermute | solution.py:1204
  462.9 8.7 %collective-permute-done.63.refs_2_ = bf16[128,896]{1,0:T(8,128)(2,1)S(1)} collective-permute-done((bf16[128,896]{1,0:T(8,128)(2,1)}, bf16[128,896]{1,0:T(8,128)(2,1)S(1)}, u32[]{:S(2)}, u32[]{:S(2)}) %collective-permute-start.63) | collective-permute-done | bytes 229408 | tf_op jit(solution)/shard_map/ppermute | solution.py:1204
  (369 shorter events, 252.9 us)
Async XLA Ops:
  5.1 40.6 %collective-permute-start.1 = (bf16[6144,128]{1,0:T(8,128)(2,1)}, bf16[6144,128]{1,0:T(8,128)(2,1)S(1)}, u32[]{:S(2)}, u32[]{:S(2)}) collective-permute-start(bf16[6144,128]{1,0:T(8,128)(2,1)} %get-tuple-element.120.refs_0_.refs_10_.refs_3_.refs_7_), channel_id=1, source_target_pairs={{0,2},{1,3},{2,0},{3,1},{4,6},{5,7},{6,4},{7,5},{8,10},{9,11},{10,... | collective-permute-start | bytes 4718600 | tf_op jit(solution)/shard_map/ppermute | solution.py:1208
  8.1 37.6 %collective-permute-start = (bf16[3072,128]{1,0:T(8,128)(2,1)}, bf16[3072,128]{1,0:T(8,128)(2,1)}, u32[]{:S(2)}, u32[]{:S(2)}) collective-permute-start(bf16[3072,128]{1,0:T(8,128)(2,1)} %get-tuple-element.119), channel_id=1, source_target_pairs={{0,16},{4,20},{8,24},{12,28},{16,0},{20,4},{24,8},{28,12},{1,17},{... | collective-permute-start | bytes 2359304 | tf_op jit(solution)/shard_map/ppermute | solution.py:1204
  13.6 32.1 %collective-permute-start.3 = (s32[16,128]{1,0:T(8,128)S(1)}, s32[16,128]{1,0:T(8,128)S(1)}, u32[]{:S(2)}, u32[]{:S(2)}) collective-permute-start(s32[16,128]{1,0:T(8,128)S(1)} %concatenate.49), channel_id=1, source_target_pairs={{0,16},{4,20},{8,24},{12,28},{16,0},{20,4},{24,8},{28,12},{1,17},{... | collective-permute-start | bytes 24584 | tf_op jit(solution)/shard_map/ppermute | solution.py:1204
  13.9 31.7 %collective-permute-start.4 = (s32[16,128]{1,0:T(8,128)S(1)}, s32[16,128]{1,0:T(8,128)S(1)}, u32[]{:S(2)}, u32[]{:S(2)}) collective-permute-start(s32[16,128]{1,0:T(8,128)S(1)} %concatenate.49), channel_id=1, source_target_pairs={{0,24},{4,28},{8,16},{12,20},{16,8},{20,12},{24,0},{28,4},{1,25},{... | collective-permute-start | bytes 24584 | tf_op jit(solution)/shard_map/ppermute | solution.py:1204
  52.6 44.0 %collective-permute-start.8 = (bf16[3072,128]{1,0:T(8,128)(2,1)}, bf16[3072,128]{1,0:T(8,128)(2,1)}, u32[]{:S(2)}, u32[]{:S(2)}) collective-permute-start(bf16[3072,128]{1,0:T(8,128)(2,1)} %get-tuple-element.130), channel_id=1, source_target_pairs={{0,16},{4,20},{8,24},{12,28},{16,0},{20,4},{24,8},{28,12},{1,17},{... | collective-permute-start | bytes 2359304 | tf_op jit(solution)/shard_map/ppermute | solution.py:1204
  67.7 29.0 %collective-permute-start.11 = (bf16[128,1024]{1,0:T(8,128)(2,1)S(1)}, bf16[128,1024]{1,0:T(8,128)(2,1)}, u32[]{:S(2)}, u32[]{:S(2)}) collective-permute-start(bf16[128,1024]{1,0:T(8,128)(2,1)S(1)} %get-tuple-element.261.refs_0_), channel_id=1, source_target_pairs={{0,8},{4,12},{8,0},{12,4},{16,24},{20,28},{24,16},{28,20},{1,9},{5... | collective-permute-start | bytes 786440 | tf_op jit(solution)/shard_map/ppermute | solution.py:1204
  68.4 39.4 %collective-permute-start.13 = (bf16[128,1024]{1,0:T(8,128)(2,1)S(1)}, bf16[128,1024]{1,0:T(8,128)(2,1)S(1)}, u32[]{:S(2)}, u32[]{:S(2)}) collective-permute-start(bf16[128,1024]{1,0:T(8,128)(2,1)S(1)} %get-tuple-element.261.refs_0_), channel_id=1, source_target_pairs={{0,16},{4,20},{8,24},{12,28},{16,0},{20,4},{24,8},{28,12},{1,17},{... | collective-permute-start | bytes 786440 | tf_op jit(solution)/shard_map/ppermute | solution.py:1204
  73.7 51.0 %collective-permute-start.10 = (bf16[3072,128]{1,0:T(8,128)(2,1)}, bf16[3072,128]{1,0:T(8,128)(2,1)}, u32[]{:S(2)}, u32[]{:S(2)}) collective-permute-start(bf16[3072,128]{1,0:T(8,128)(2,1)} %collective-permute-done.refs_14_.refs_11_), channel_id=1, source_target_pairs={{0,2},{1,3},{2,0},{3,1},{4,6},{5,7},{6,4},{7,5},{8,10},{9,11},{10,... | collective-permute-start | bytes 2359304 | tf_op jit(solution)/shard_map/ppermute | solution.py:1208
  74.2 53.6 %collective-permute-start.17 = (bf16[6144,128]{1,0:T(8,128)(2,1)S(1)}, bf16[6144,128]{1,0:T(8,128)(2,1)}, u32[]{:S(2)}, u32[]{:S(2)}) collective-permute-start(bf16[6144,128]{1,0:T(8,128)(2,1)S(1)} %copy-done.3), channel_id=1, source_target_pairs={{0,1},{1,0},{2,3},{3,2},{4,5},{5,4},{6,7},{7,6},{8,9},{9,8},{10,11... | collective-permute-start | bytes 4718600 | tf_op jit(solution)/shard_map/ppermute | solution.py:1212
  96.7 31.1 %collective-permute-start.18 = (bf16[6144,128]{1,0:T(8,128)(2,1)S(1)}, bf16[6144,128]{1,0:T(8,128)(2,1)}, u32[]{:S(2)}, u32[]{:S(2)}) collective-permute-start(bf16[6144,128]{1,0:T(8,128)(2,1)S(1)} %collective-permute-done.1.refs_12_.refs_5_.refs_9_), channel_id=1, source_target_pairs={{0,1},{1,0},{2,3},{3,2},{4,5},{5,4},{6,7},{7,6},{8,9},{9,8},{10,11... | collective-permute-start | bytes 4718600 | tf_op jit(solution)/shard_map/ppermute | solution.py:1212
  234.9 25.6 %collective-permute-start.30 = (bf16[128,1024]{1,0:T(8,128)(2,1)}, bf16[128,1024]{1,0:T(8,128)(2,1)S(1)}, u32[]{:S(2)}, u32[]{:S(2)}) collective-permute-start(bf16[128,1024]{1,0:T(8,128)(2,1)} %get-tuple-element.263.refs_0_), channel_id=1, source_target_pairs={{0,2},{1,3},{2,0},{3,1},{4,6},{5,7},{6,4},{7,5},{8,10},{9,11},{10,... | collective-permute-start | bytes 786440 | tf_op jit(solution)/shard_map/ppermute | solution.py:1208
  237.2 44.0 %collective-permute-start.29 = (bf16[128,1024]{1,0:T(8,128)(2,1)}, bf16[128,1024]{1,0:T(8,128)(2,1)S(1)}, u32[]{:S(2)}, u32[]{:S(2)}) collective-permute-start(bf16[128,1024]{1,0:T(8,128)(2,1)} %get-tuple-element.263.refs_0_), channel_id=1, source_target_pairs={{0,1},{1,0},{2,3},{3,2},{4,5},{5,4},{6,7},{7,6},{8,9},{9,8},{10,11... | collective-permute-start | bytes 786440 | tf_op jit(solution)/shard_map/ppermute | solution.py:1212
  288.5 28.5 %collective-permute-start.41 = (bf16[256,1024]{1,0:T(8,128)(2,1)S(1)}, bf16[256,1024]{1,0:T(8,128)(2,1)S(1)}, u32[]{:S(2)}, u32[]{:S(2)}) collective-permute-start(bf16[256,1024]{1,0:T(8,128)(2,1)S(1)} %copy-done.23), channel_id=1, source_target_pairs={{0,16},{4,20},{8,24},{12,28},{16,0},{20,4},{24,8},{28,12},{1,17},{... | collective-permute-start | bytes 1572872 | tf_op jit(solution)/shard_map/ppermute | solution.py:1204
  292.8 26.6 %collective-permute-start.40 = (bf16[256,1024]{1,0:T(8,128)(2,1)}, bf16[256,1024]{1,0:T(8,128)(2,1)S(1)}, u32[]{:S(2)}, u32[]{:S(2)}) collective-permute-start(bf16[256,1024]{1,0:T(8,128)(2,1)} %get-tuple-element.173), channel_id=1, source_target_pairs={{0,4},{4,0},{8,12},{12,8},{16,20},{20,16},{24,28},{28,24},{1,5},{5... | collective-permute-start | bytes 1572872 | tf_op jit(solution)/shard_map/ppermute | solution.py:1204
  319.0 37.0 %collective-permute-start.50 = (bf16[2,2,2,512,128]{4,3,2,1,0:T(8,128)(2,1)}, bf16[2,2,2,512,128]{4,3,2,1,0:T(8,128)(2,1)S(1)}, u32[]{:S(2)}, u32[]{:S(2)}) collective-permute-start(bf16[2,2,2,512,128]{4,3,2,1,0:T(8,128)(2,1)} %get-tuple-element.188), channel_id=1, source_target_pairs={{0,1},{1,0},{2,3},{3,2},{4,5},{5,4},{6,7},{7,6},{8,9},{9,8},{10,11... | collective-permute-start | bytes 3145736 | tf_op jit(solution)/shard_map/ppermute | solution.py:1212
  334.9 24.9 %collective-permute-start.52 = (bf16[2,2,512,128]{3,2,1,0:T(8,128)(2,1)S(1)}, bf16[2,2,512,128]{3,2,1,0:T(8,128)(2,1)S(1)}, u32[]{:S(2)}, u32[]{:S(2)}) collective-permute-start(bf16[2,2,512,128]{3,2,1,0:T(8,128)(2,1)S(1)} %copy-done.24), channel_id=1, source_target_pairs={{0,16},{4,20},{8,24},{12,28},{16,0},{20,4},{24,8},{28,12},{1,17},{... | collective-permute-start | bytes 1572872 | tf_op jit(solution)/shard_map/ppermute | solution.py:1204
  345.1 28.8 %collective-permute-start.58 = (bf16[4,128,512]{2,1,0:T(8,128)(2,1)}, bf16[4,128,512]{2,1,0:T(8,128)(2,1)}, u32[]{:S(2)}, u32[]{:S(2)}) collective-permute-start(bf16[4,128,512]{2,1,0:T(8,128)(2,1)} %get-tuple-element.192.refs_1_), channel_id=1, source_target_pairs={{0,2},{1,3},{2,0},{3,1},{4,6},{5,7},{6,4},{7,5},{8,10},{9,11},{10,... | collective-permute-start | bytes 1572872 | tf_op jit(solution)/shard_map/ppermute | solution.py:1208
  371.6 28.2 %collective-permute-start.69 = (bf16[2,4,128,512]{3,2,1,0:T(8,128)(2,1)}, bf16[2,4,128,512]{3,2,1,0:T(8,128)(2,1)}, u32[]{:S(2)}, u32[]{:S(2)}) collective-permute-start(bf16[2,4,128,512]{3,2,1,0:T(8,128)(2,1)} %get-tuple-element.210), channel_id=1, source_target_pairs={{0,1},{1,0},{2,3},{3,2},{4,5},{5,4},{6,7},{7,6},{8,9},{9,8},{10,11... | collective-permute-start | bytes 3145736 | tf_op jit(solution)/shard_map/ppermute | solution.py:1212
  372.1 59.2 %collective-permute-start.73 = (bf16[2,4,2,512,128]{4,3,2,1,0:T(8,128)(2,1)}, bf16[2,4,2,512,128]{4,3,2,1,0:T(8,128)(2,1)}, u32[]{:S(2)}, u32[]{:S(2)}) collective-permute-start(bf16[2,4,2,512,128]{4,3,2,1,0:T(8,128)(2,1)} %get-tuple-element.193.refs_2_), channel_id=1, source_target_pairs={{0,1},{1,0},{2,3},{3,2},{4,5},{5,4},{6,7},{7,6},{8,9},{9,8},{10,11... | collective-permute-start | bytes 6291464 | tf_op jit(solution)/shard_map/ppermute | solution.py:1212
  375.9 38.4 %collective-permute-start.59 = (bf16[4,128,512]{2,1,0:T(8,128)(2,1)}, bf16[4,128,512]{2,1,0:T(8,128)(2,1)S(1)}, u32[]{:S(2)}, u32[]{:S(2)}) collective-permute-start(bf16[4,128,512]{2,1,0:T(8,128)(2,1)} %add_convert_fusion), channel_id=1, source_target_pairs={{0,16},{4,20},{8,24},{12,28},{16,0},{20,4},{24,8},{28,12},{1,17},{... | collective-permute-start | bytes 1572872 | tf_op jit(solution)/shard_map/ppermute | solution.py:1204
  387.1 37.7 %collective-permute-start.57 = (bf16[2,2,512,128]{3,2,1,0:T(8,128)(2,1)S(1)}, bf16[2,2,512,128]{3,2,1,0:T(8,128)(2,1)}, u32[]{:S(2)}, u32[]{:S(2)}) collective-permute-start(bf16[2,2,512,128]{3,2,1,0:T(8,128)(2,1)S(1)} %add_convert_fusion.1.refs_0_), channel_id=1, source_target_pairs={{0,16},{4,20},{8,24},{12,28},{16,0},{20,4},{24,8},{28,12},{1,17},{... | collective-permute-start | bytes 1572872 | tf_op jit(solution)/shard_map/ppermute | solution.py:1204
  403.4 48.8 %collective-permute-start.72 = (bf16[4,128,512]{2,1,0:T(8,128)(2,1)}, bf16[4,128,512]{2,1,0:T(8,128)(2,1)S(1)}, u32[]{:S(2)}, u32[]{:S(2)}) collective-permute-start(bf16[4,128,512]{2,1,0:T(8,128)(2,1)} %get-tuple-element.213), channel_id=1, source_target_pairs={{0,2},{1,3},{2,0},{3,1},{4,6},{5,7},{6,4},{7,5},{8,10},{9,11},{10,... | collective-permute-start | bytes 1572872 | tf_op jit(solution)/shard_map/ppermute | solution.py:1208
  407.9 28.9 %collective-permute-start.76 = (bf16[128,1024]{1,0:T(8,128)(2,1)S(1)}, bf16[128,1024]{1,0:T(8,128)(2,1)}, u32[]{:S(2)}, u32[]{:S(2)}) collective-permute-start(bf16[128,1024]{1,0:T(8,128)(2,1)S(1)} %fusion.6.refs_0_), channel_id=1, source_target_pairs={{0,2},{1,3},{2,0},{3,1},{4,6},{5,7},{6,4},{7,5},{8,10},{9,11},{10,... | collective-permute-start | bytes 786440 | tf_op jit(solution)/shard_map/ppermute | solution.py:1208
  436.8 46.0 %collective-permute-start.74 = (bf16[4,2,512,128]{3,2,1,0:T(8,128)(2,1)}, bf16[4,2,512,128]{3,2,1,0:T(8,128)(2,1)S(1)}, u32[]{:S(2)}, u32[]{:S(2)}) collective-permute-start(bf16[4,2,512,128]{3,2,1,0:T(8,128)(2,1)} %get-tuple-element.215), channel_id=1, source_target_pairs={{0,2},{1,3},{2,0},{3,1},{4,6},{5,7},{6,4},{7,5},{8,10},{9,11},{10,... | collective-permute-start | bytes 3145736 | tf_op jit(solution)/shard_map/ppermute | solution.py:1208
  (122 other events, 1574.7 us)

commit v10 on v9

--- a/solution.py
+++ b/solution.py
@@ -1398,14 +1398,14 @@
     got_near = trade(send_near, 1)
     other = 1 - half_arg
     in_keep, in_send = grad_expert_ins(
-        other, expert_rows, pre_grad, 0, 2, far_rows, *out_pieces[1:]
+        other, expert_rows, pre_grad, 0, 3, far_rows, *out_pieces[1:]
     )
     in_near, in_far = fold_pairs(in_keep, swap_core(in_send))
     in_ready = (in_near + swap_y(in_far).astype(F32)).astype(BF16)
     out_keep, out_send, own_out_keep, own_out_send = grad_expert_outs(
         half_arg, gated, grad_rows, in_far
     )
-    late_keep, late_send = grad_expert_ins(other, expert_rows, pre_grad, 2, 2, in_far)
+    late_keep, late_send = grad_expert_ins(other, expert_rows, pre_grad, 3, 1, in_far)
     router_part = jnp.einsum(
         "te,td->ed", logit_grad.astype(BF16), expert_rows, preferred_element_type=F32
     )

time: 511 us -> 544 us (1.065)
  waiting for transfers between devices: 166 us -> 204 us
    ppermute x15, waiting for transfers between devices: 17.7 us -> 46.2 us  [swap_y(): return lax.ppermute(value, 'tensor', [(i, i ^ 2) for i in range(4)])]
    ppermute x44, waiting for transfers between devices: 143 us -> 151 us  [trade(): return lax.ppermute(value, 'expert', [(i, i ^ bits) for i in range(8)])]
    unnamed x138 -> x144, local copies, waits for them, and re-layouts: 10.6 us -> 11.6 us
  transfers between devices with their start and end apart: 80 -> 80, of which waited for: 34 -> 33; matrix products, arithmetic and copies ran while one was open for 11% -> 10% of each run, Pallas kernels for 27% -> 23%
where the time goes in v10:
time: 544 us; the launch traced here: 534 us
  waiting for transfers between devices  204 us (38%)
  Pallas kernels  163 us (30%)
  starting transfers between devices  90.4 us (17%)
  other arithmetic  48.7 us (9%)
  local copies, waits for them, and re-layouts  21.8 us (4%)
    ppermute x44, waiting for transfers between devices, trade(): return lax.ppermute(value, 'expert', [(i, i ^ bits) for i in range(8)])  151 us
    ppermute x44, starting transfers between devices, trade(): return lax.ppermute(value, 'expert', [(i, i ^ bits) for i in range(8)])  68.7 us
    ppermute x15, waiting for transfers between devices, swap_y(): return lax.ppermute(value, 'tensor', [(i, i ^ 2) for i in range(4)])  46.2 us
    pallas_call x2, Pallas kernels, experts_backward(): pl.pallas_call(backward_body, grid_spec=pltpu.PrefetchScalarGridSpec(num_...  32.8 us
    pallas_call x5, Pallas kernels, scalar_call(): pl.pallas_call(body, grid_spec=pltpu.PrefetchScalarGridSpec(num_scalar_pr...  27.5 us
    pallas_call x3, Pallas kernels, grad_expert_ins(): pl.pallas_call(grad_in_body, grid_spec=pltpu.PrefetchScalarGridSpec(num_s...  21.4 us
    pallas_call x2, Pallas kernels, second(): pl.pallas_call(forward_second, grid_spec=pltpu.PrefetchScalarGridSpec(num...  20.8 us
    ppermute x15, starting transfers between devices, swap_y(): return lax.ppermute(value, 'tensor', [(i, i ^ 2) for i in range(4)])  19.1 us
  transfers between devices with their start and end apart: 80, of which 33 were waited for; matrix products, arithmetic and copies ran while one was open for 10% of the time, Pallas kernels for 23%

profile of v10, /device:TPU:0, one launch (start us, length us, event | category | flops | bytes accessed | tf_op | source)
XLA Modules:
  0.0 534.2 jit_solution(5965038560680260482)
XLA Ops:
  18.7 8.2 %attention_forward.1 = (bf16[512,1024]{1,0:T(8,128)(2,1)}, bf16[512,256]{1,0:T(8,128)(2,1)}, bf16[512,128]{1,0:T(8,128)(2,1)}, bf16[512,128]{1,0:T(8,128)(2,1)},...) custom-call(s32[1]{0:T(128)} %bitcast.2.core_ref, bf16[512,1024]{1,0:T(8,128)(2,1)} %tokens.3, ...), custom_call_target="tpu_custom_call" | custom-call | tf_op jit(solution)/shard_map/attention_forward/pallas_call | solution.py:973
  27.8 17.9 %collective-permute-done.3 = s32[16,128]{1,0:T(8,128)S(1)} collective-permute-done((s32[16,128]{1,0:T(8,128)S(1)}, s32[16,128]{1,0:T(8,128)S(1)}, u32[]{:S(2)}, u32[]{:S(2)}) %collective-permute-start.3) | collective-permute-done | bytes 8224 | tf_op jit(solution)/shard_map/ppermute | solution.py:1204
  72.9 22.5 %collective-permute-done.8.refs_7_.refs_15_ = bf16[3072,128]{1,0:T(8,128)(2,1)} collective-permute-done((bf16[3072,128]{1,0:T(8,128)(2,1)}, bf16[3072,128]{1,0:T(8,128)(2,1)}, u32[]{:S(2)}, u32[]{:S(2)}) %collective-permute-start.8) | collective-permute-done | bytes 786464 | tf_op jit(solution)/shard_map/ppermute | solution.py:1204
  98.2 8.3 %collective-permute-done.13.refs_2_ = bf16[128,1024]{1,0:T(8,128)(2,1)S(1)} collective-permute-done((bf16[128,1024]{1,0:T(8,128)(2,1)S(1)}, bf16[128,1024]{1,0:T(8,128)(2,1)S(1)}, u32[]{:S(2)}, u32[]{:S(2)}) %collective-permute-start.13) | collective-permute-done | bytes 262176 | tf_op jit(solution)/shard_map/ppermute | solution.py:1204
  126.6 16.6 %experts_forward_a.1 = (f32[1024,1024]{1,0:T(8,128)}, bf16[4,1024,1024]{2,1,0:T(8,128)(2,1)}, bf16[4,1024,512]{2,1,0:T(8,128)(2,1)}, f32[1024,128]{1,0:T(8,128)}, bf16[1024,1024]{1,0:T(8,128)(2,1)}) custom-call(s32[1]{0:T(128)} %bitcast.1.half_ref, bf16[128,1024]{1,0:T(8,128)(2,1)} %copy-done.13, bf16[128,1024]{1,0:T(8,128)(2,1)} %collective-permute-done.11.refs_1_, ...), custom_call_target="tpu_custom_call" | custom-call | tf_op jit(solution)/shard_map/experts_forward_a/pallas_call | solution.py:643
  148.2 10.2 %experts_forward_b.2 = (bf16[256,1024]{1,0:T(8,128)(2,1)}, bf16[256,1024]{1,0:T(8,128)(2,1)}, bf16[4,1024,1024]{2,1,0:T(8,128)(2,1)}, bf16[4,1024,512]{2,1,0:T(8,128)(2,1)}) custom-call(s32[1]{0:T(128)} %bitcast.1.half_ref, bf16[1024,1024]{1,0:T(8,128)(2,1)} %get-tuple-element.144.refs_0_.rows_ref, ...), custom_call_target="tpu_custom_call", output_to_operand_aliasing={{2}: (12, {}), {3}: (13, {})} | custom-call | tf_op jit(solution)/shard_map/experts_forward_b/pallas_call | solution.py:667
  160.0 10.6 %experts_forward_b.3 = (f32[512,1024]{1,0:T(8,128)}, bf16[4,1024,1024]{2,1,0:T(8,128)(2,1)}, bf16[4,1024,512]{2,1,0:T(8,128)(2,1)}) custom-call(s32[1]{0:T(128)} %bitcast.1.half_ref, bf16[1024,1024]{1,0:T(8,128)(2,1)} %get-tuple-element.144.refs_0_.rows_ref, ...), custom_call_target="tpu_custom_call", output_to_operand_aliasing={{1}: (12, {}), {2}: (13, {})} | custom-call | tf_op jit(solution)/shard_map/experts_forward_b/pallas_call | solution.py:667
  193.0 7.5 %collective-permute-done.27 = bf16[128,1024]{1,0:T(8,128)(2,1)S(1)} collective-permute-done((bf16[128,1024]{1,0:T(8,128)(2,1)}, bf16[128,1024]{1,0:T(8,128)(2,1)S(1)}, u32[]{:S(2)}, u32[]{:S(2)}) %collective-permute-start.27) | collective-permute-done | bytes 262176 | tf_op jit(solution)/shard_map/ppermute | solution.py:1204
  213.7 7.7 %collective-permute-done.33.refs_1_ = bf16[128,1024]{1,0:T(8,128)(2,1)S(1)} collective-permute-done((bf16[128,1024]{1,0:T(8,128)(2,1)S(1)}, bf16[128,1024]{1,0:T(8,128)(2,1)S(1)}, u32[]{:S(2)}, u32[]{:S(2)}) %collective-permute-start.33) | collective-permute-done | bytes 262176 | tf_op jit(solution)/shard_map/ppermute | solution.py:1204
  222.6 8.8 %collective-permute-done.35.refs_2_ = bf16[128,1024]{1,0:T(8,128)(2,1)S(1)} collective-permute-done((bf16[128,1024]{1,0:T(8,128)(2,1)S(1)}, bf16[128,1024]{1,0:T(8,128)(2,1)S(1)}, u32[]{:S(2)}, u32[]{:S(2)}) %collective-permute-start.35) | collective-permute-done | bytes 262176 | tf_op jit(solution)/shard_map/ppermute | solution.py:1204
  241.4 16.2 %experts_backward.2 = (bf16[256,1024]{1,0:T(8,128)(2,1)}, bf16[256,1024]{1,0:T(8,128)(2,1)}, bf16[4,1024,1024]{2,1,0:T(8,128)(2,1)}, f32[1024,128]{1,0:T(8,128)}, bf16[1024,1024]{1,0:T(8,128)(2,1)}) custom-call(s32[1]{0:T(128)} %bitcast.1.half_ref, bf16[128,1024]{1,0:T(8,128)(2,1)} %copy-done.50, bf16[128,1024]{1,0:T(8,128)(2,1)} %copy-done.51, ...), custom_call_target="tpu_custom_call" | custom-call | tf_op jit(solution)/shard_map/experts_backward/pallas_call | solution.py:757
  264.6 16.7 %experts_backward.3 = (f32[512,1024]{1,0:T(8,128)}, bf16[4,1024,1024]{2,1,0:T(8,128)(2,1)}, f32[1024,128]{1,0:T(8,128)}, bf16[1024,1024]{1,0:T(8,128)(2,1)}) custom-call(s32[1]{0:T(128)} %bitcast.1.half_ref, bf16[128,1024]{1,0:T(8,128)(2,1)} %copy-done.31, ...), custom_call_target="tpu_custom_call", output_to_operand_aliasing={{1}: (20, {}), {2}: (21, {}), {3}: (22, {})} | custom-call | tf_op jit(solution)/shard_map/experts_backward/pallas_call | solution.py:757
  284.3 7.8 %grad_expert_in.3 = (bf16[2,3,2,512,128]{4,3,2,1,0:T(8,128)(2,1)}, bf16[2,3,2,512,128]{4,3,2,1,0:T(8,128)(2,1)}) custom-call(s32[1]{0:T(128)S(6)} %sub.46.half_ref, bf16[1024,1024]{1,0:T(8,128)(2,1)} %get-tuple-element.144.refs_0_.rows_ref, bf16[4,1024,1024]{2,1,0:T(8,128)(2,1)} %get-tuple-element.177.pre_ref, bf16[256,1024]{1,0:T(8,128)(2,1)} %add_convert_fusion.2.refs_0_, ...), custom_call_target="tpu_custom_call" | custom-call | tf_op jit(solution)/shard_map/grad_expert_in/pallas_call | solution.py:840
  308.7 14.8 %collective-permute-done.44 = f32[40,1024]{1,0:T(8,128)S(1)} collective-permute-done((f32[40,1024]{1,0:T(8,128)S(1)}, f32[40,1024]{1,0:T(8,128)S(1)}, u32[]{:S(2)}, u32[]{:S(2)}) %collective-permute-start.44) | collective-permute-done | bytes 163872 | tf_op jit(solution)/shard_map/ppermute | solution.py:1208
  328.4 10.3 %grad_expert_out.1 = (bf16[2,4,128,512]{3,2,1,0:T(8,128)(2,1)}, bf16[2,4,128,512]{3,2,1,0:T(8,128)(2,1)}, bf16[2,4,128,512]{3,2,1,0:T(8,128)(2,1)}, bf16[2,4,128,512]{3,2,1,0:T(8,128)(2,1)}) custom-call(s32[1]{0:T(128)} %bitcast.1.half_ref, bf16[4,1024,512]{2,1,0:T(8,128)(2,1)} %get-tuple-element.175.gated_ref, ...), custom_call_target="tpu_custom_call" | custom-call | tf_op jit(solution)/shard_map/grad_expert_out/pallas_call | solution.py:798
  359.4 6.6 %collective-permute-done.48.refs_0_.third = bf16[128,1024]{1,0:T(8,128)(2,1)S(1)} collective-permute-done((bf16[128,1024]{1,0:T(8,128)(2,1)}, bf16[128,1024]{1,0:T(8,128)(2,1)S(1)}, u32[]{:S(2)}, u32[]{:S(2)}) %collective-permute-start.48) | collective-permute-done | bytes 262176 | tf_op jit(solution)/shard_map/ppermute | solution.py:1208
  375.1 9.3 %grad_expert_in.5 = (bf16[2,4,2,512,128]{4,3,2,1,0:T(8,128)(2,1)}, bf16[2,4,2,512,128]{4,3,2,1,0:T(8,128)(2,1)}) custom-call(s32[1]{0:T(128)} %bitcast.1.half_ref, bf16[1024,1024]{1,0:T(8,128)(2,1)} %get-tuple-element.144.refs_0_.rows_ref, bf16[4,1024,1024]{2,1,0:T(8,128)(2,1)} %get-tuple-element.177.pre_ref, bf16[128,1024]{1,0:T(8,128)(2,1)} %get-tuple-element.186.refs_0_.first), custom_call_target="tpu_custom_call" | custom-call | tf_op jit(solution)/shard_map/grad_expert_in/pallas_call | solution.py:840
  387.3 10.7 %attention_backward.1 = (bf16[512,1024]{1,0:T(8,128)(2,1)}, bf16[512,512]{1,0:T(8,128)(2,1)}, f32[8,1024]{1,0:T(8,128)}, f32[2,128,1024]{2,1,0:T(8,128)}, bf16[2,128,1024]{2,1,0:T(8,128)(2,1)}) custom-call(s32[1]{0:T(128)} %bitcast.share_ref, bf16[512,1024]{1,0:T(8,128)(2,1)} %tokens.3, bf16[1024,256]{1,0:T(8,128)(2,1)} %query_w.3, bf16[1024,128]{1,0:T(8,128)(2,1)} %key_w.3, ...), custom_call_target="tpu_custom_call" | custom-call | tf_op jit(solution)/shard_map/attention_backward/pallas_call | solution.py:973
  399.9 7.8 %reduce_parts.1 = (f32[512,896]{1,0:T(8,128)}, bf16[256,896]{1,0:T(8,128)(2,1)}, bf16[256,896]{1,0:T(8,128)(2,1)}) custom-call(s32[1]{0:T(128)} %bitcast.13.place_ref, bf16[512,1024]{1,0:T(8,128)(2,1)} %get-tuple-element.161.normed, bf16[512,512]{1,0:T(8,128)(2,1)} %get-tuple-element.194.grad_qkv, bf16[512,1024]{1,0:T(8,128)(2,1)} %get-tuple-element.195.grad, ...), custom_call_target="tpu_custom_call" | custom-call | tf_op jit(solution)/shard_map/reduce_parts/pallas_call | solution.py:1138
  410.0 10.6 %collective-permute-done.54 = bf16[256,896]{1,0:T(8,128)(2,1)S(1)} collective-permute-done((bf16[256,896]{1,0:T(8,128)(2,1)}, bf16[256,896]{1,0:T(8,128)(2,1)S(1)}, u32[]{:S(2)}, u32[]{:S(2)}) %collective-permute-start.54) | collective-permute-done | bytes 458784 | tf_op jit(solution)/shard_map/ppermute | solution.py:1204
  423.7 22.5 %collective-permute-done.57 = bf16[1,2,512,128]{3,2,1,0:T(8,128)(2,1)S(1)} collective-permute-done((bf16[1,2,512,128]{3,2,1,0:T(8,128)(2,1)S(1)}, bf16[1,2,512,128]{3,2,1,0:T(8,128)(2,1)S(1)}, u32[]{:S(2)}, u32[]{:S(2)}) %collective-permute-start.57) | collective-permute-done | bytes 262176 | tf_op jit(solution)/shard_map/ppermute | solution.py:1204
  448.6 5.9 %collective-permute-done.71 = bf16[128,1024]{1,0:T(8,128)(2,1)S(1)} collective-permute-done((bf16[128,1024]{1,0:T(8,128)(2,1)S(1)}, bf16[128,1024]{1,0:T(8,128)(2,1)S(1)}, u32[]{:S(2)}, u32[]{:S(2)}) %collective-permute-start.71) | collective-permute-done | bytes 262176 | tf_op jit(solution)/shard_map/ppermute | solution.py:1208
  472.4 10.0 %collective-permute-done.76.refs_2_ = bf16[128,1024]{1,0:T(8,128)(2,1)} collective-permute-done((bf16[128,1024]{1,0:T(8,128)(2,1)S(1)}, bf16[128,1024]{1,0:T(8,128)(2,1)}, u32[]{:S(2)}, u32[]{:S(2)}) %collective-permute-start.76) | collective-permute-done | bytes 262176 | tf_op jit(solution)/shard_map/ppermute | solution.py:1208
  497.9 6.2 %collective-permute-done.63.refs_2_ = bf16[128,896]{1,0:T(8,128)(2,1)S(1)} collective-permute-done((bf16[128,896]{1,0:T(8,128)(2,1)}, bf16[128,896]{1,0:T(8,128)(2,1)S(1)}, u32[]{:S(2)}, u32[]{:S(2)}) %collective-permute-start.63) | collective-permute-done | bytes 229408 | tf_op jit(solution)/shard_map/ppermute | solution.py:1204
  (375 shorter events, 256.0 us)
Async XLA Ops:
  5.1 40.6 %collective-permute-start.1 = (bf16[6144,128]{1,0:T(8,128)(2,1)}, bf16[6144,128]{1,0:T(8,128)(2,1)S(1)}, u32[]{:S(2)}, u32[]{:S(2)}) collective-permute-start(bf16[6144,128]{1,0:T(8,128)(2,1)} %get-tuple-element.120.refs_0_.refs_10_.refs_3_.refs_7_), channel_id=1, source_target_pairs={{0,2},{1,3},{2,0},{3,1},{4,6},{5,7},{6,4},{7,5},{8,10},{9,11},{10,... | collective-permute-start | bytes 4718600 | tf_op jit(solution)/shard_map/ppermute | solution.py:1208
  8.1 37.6 %collective-permute-start = (bf16[3072,128]{1,0:T(8,128)(2,1)}, bf16[3072,128]{1,0:T(8,128)(2,1)}, u32[]{:S(2)}, u32[]{:S(2)}) collective-permute-start(bf16[3072,128]{1,0:T(8,128)(2,1)} %get-tuple-element.119), channel_id=1, source_target_pairs={{0,16},{4,20},{8,24},{12,28},{16,0},{20,4},{24,8},{28,12},{1,17},{... | collective-permute-start | bytes 2359304 | tf_op jit(solution)/shard_map/ppermute | solution.py:1204
  13.6 32.1 %collective-permute-start.3 = (s32[16,128]{1,0:T(8,128)S(1)}, s32[16,128]{1,0:T(8,128)S(1)}, u32[]{:S(2)}, u32[]{:S(2)}) collective-permute-start(s32[16,128]{1,0:T(8,128)S(1)} %concatenate.49), channel_id=1, source_target_pairs={{0,16},{4,20},{8,24},{12,28},{16,0},{20,4},{24,8},{28,12},{1,17},{... | collective-permute-start | bytes 24584 | tf_op jit(solution)/shard_map/ppermute | solution.py:1204
  13.9 31.7 %collective-permute-start.4 = (s32[16,128]{1,0:T(8,128)S(1)}, s32[16,128]{1,0:T(8,128)S(1)}, u32[]{:S(2)}, u32[]{:S(2)}) collective-permute-start(s32[16,128]{1,0:T(8,128)S(1)} %concatenate.49), channel_id=1, source_target_pairs={{0,24},{4,28},{8,16},{12,20},{16,8},{20,12},{24,0},{28,4},{1,25},{... | collective-permute-start | bytes 24584 | tf_op jit(solution)/shard_map/ppermute | solution.py:1204
  51.4 44.0 %collective-permute-start.8 = (bf16[3072,128]{1,0:T(8,128)(2,1)}, bf16[3072,128]{1,0:T(8,128)(2,1)}, u32[]{:S(2)}, u32[]{:S(2)}) collective-permute-start(bf16[3072,128]{1,0:T(8,128)(2,1)} %get-tuple-element.130), channel_id=1, source_target_pairs={{0,16},{4,20},{8,24},{12,28},{16,0},{20,4},{24,8},{28,12},{1,17},{... | collective-permute-start | bytes 2359304 | tf_op jit(solution)/shard_map/ppermute | solution.py:1204
  66.5 29.0 %collective-permute-start.11 = (bf16[128,1024]{1,0:T(8,128)(2,1)S(1)}, bf16[128,1024]{1,0:T(8,128)(2,1)}, u32[]{:S(2)}, u32[]{:S(2)}) collective-permute-start(bf16[128,1024]{1,0:T(8,128)(2,1)S(1)} %get-tuple-element.261.refs_0_), channel_id=1, source_target_pairs={{0,8},{4,12},{8,0},{12,4},{16,24},{20,28},{24,16},{28,20},{1,9},{5... | collective-permute-start | bytes 786440 | tf_op jit(solution)/shard_map/ppermute | solution.py:1204
  67.2 39.4 %collective-permute-start.13 = (bf16[128,1024]{1,0:T(8,128)(2,1)S(1)}, bf16[128,1024]{1,0:T(8,128)(2,1)S(1)}, u32[]{:S(2)}, u32[]{:S(2)}) collective-permute-start(bf16[128,1024]{1,0:T(8,128)(2,1)S(1)} %get-tuple-element.261.refs_0_), channel_id=1, source_target_pairs={{0,16},{4,20},{8,24},{12,28},{16,0},{20,4},{24,8},{28,12},{1,17},{... | collective-permute-start | bytes 786440 | tf_op jit(solution)/shard_map/ppermute | solution.py:1204
  72.5 51.0 %collective-permute-start.10 = (bf16[3072,128]{1,0:T(8,128)(2,1)}, bf16[3072,128]{1,0:T(8,128)(2,1)}, u32[]{:S(2)}, u32[]{:S(2)}) collective-permute-start(bf16[3072,128]{1,0:T(8,128)(2,1)} %collective-permute-done.refs_14_.refs_11_), channel_id=1, source_target_pairs={{0,2},{1,3},{2,0},{3,1},{4,6},{5,7},{6,4},{7,5},{8,10},{9,11},{10,... | collective-permute-start | bytes 2359304 | tf_op jit(solution)/shard_map/ppermute | solution.py:1208
  72.9 53.7 %collective-permute-start.17 = (bf16[6144,128]{1,0:T(8,128)(2,1)S(1)}, bf16[6144,128]{1,0:T(8,128)(2,1)}, u32[]{:S(2)}, u32[]{:S(2)}) collective-permute-start(bf16[6144,128]{1,0:T(8,128)(2,1)S(1)} %copy-done.3), channel_id=1, source_target_pairs={{0,1},{1,0},{2,3},{3,2},{4,5},{5,4},{6,7},{7,6},{8,9},{9,8},{10,11... | collective-permute-start | bytes 4718600 | tf_op jit(solution)/shard_map/ppermute | solution.py:1212
  95.4 31.1 %collective-permute-start.18 = (bf16[6144,128]{1,0:T(8,128)(2,1)S(1)}, bf16[6144,128]{1,0:T(8,128)(2,1)}, u32[]{:S(2)}, u32[]{:S(2)}) collective-permute-start(bf16[6144,128]{1,0:T(8,128)(2,1)S(1)} %collective-permute-done.1.refs_12_.refs_5_.refs_9_), channel_id=1, source_target_pairs={{0,1},{1,0},{2,3},{3,2},{4,5},{5,4},{6,7},{7,6},{8,9},{9,8},{10,11... | collective-permute-start | bytes 4718600 | tf_op jit(solution)/shard_map/ppermute | solution.py:1212
  257.6 23.7 %collective-permute-start.39 = (bf16[256,1024]{1,0:T(8,128)(2,1)}, bf16[256,1024]{1,0:T(8,128)(2,1)S(1)}, u32[]{:S(2)}, u32[]{:S(2)}) collective-permute-start(bf16[256,1024]{1,0:T(8,128)(2,1)} %get-tuple-element.167), channel_id=1, source_target_pairs={{0,4},{4,0},{8,12},{12,8},{16,20},{20,16},{24,28},{28,24},{1,5},{5... | collective-permute-start | bytes 1572872 | tf_op jit(solution)/shard_map/ppermute | solution.py:1204
  300.0 43.8 %collective-permute-start.46 = (bf16[3,2,512,128]{3,2,1,0:T(8,128)(2,1)}, bf16[3,2,512,128]{3,2,1,0:T(8,128)(2,1)}, u32[]{:S(2)}, u32[]{:S(2)}) collective-permute-start(bf16[3,2,512,128]{3,2,1,0:T(8,128)(2,1)} %get-tuple-element.180.refs_0_), channel_id=1, source_target_pairs={{0,2},{1,3},{2,0},{3,1},{4,6},{5,7},{6,4},{7,5},{8,10},{9,11},{10,... | collective-permute-start | bytes 2359304 | tf_op jit(solution)/shard_map/ppermute | solution.py:1208
  301.5 37.2 %collective-permute-start.41 = (bf16[256,1024]{1,0:T(8,128)(2,1)S(1)}, bf16[256,1024]{1,0:T(8,128)(2,1)S(1)}, u32[]{:S(2)}, u32[]{:S(2)}) collective-permute-start(bf16[256,1024]{1,0:T(8,128)(2,1)S(1)} %copy-done.26), channel_id=1, source_target_pairs={{0,16},{4,20},{8,24},{12,28},{16,0},{20,4},{24,8},{28,12},{1,17},{... | collective-permute-start | bytes 1572872 | tf_op jit(solution)/shard_map/ppermute | solution.py:1204
  305.8 33.0 %collective-permute-start.40 = (bf16[256,1024]{1,0:T(8,128)(2,1)}, bf16[256,1024]{1,0:T(8,128)(2,1)S(1)}, u32[]{:S(2)}, u32[]{:S(2)}) collective-permute-start(bf16[256,1024]{1,0:T(8,128)(2,1)} %get-tuple-element.173), channel_id=1, source_target_pairs={{0,4},{4,0},{8,12},{12,8},{16,20},{20,16},{24,28},{28,24},{1,5},{5... | collective-permute-start | bytes 1572872 | tf_op jit(solution)/shard_map/ppermute | solution.py:1204
  338.8 31.7 %collective-permute-start.51 = (bf16[2,4,128,512]{3,2,1,0:T(8,128)(2,1)}, bf16[2,4,128,512]{3,2,1,0:T(8,128)(2,1)}, u32[]{:S(2)}, u32[]{:S(2)}) collective-permute-start(bf16[2,4,128,512]{3,2,1,0:T(8,128)(2,1)} %get-tuple-element.191), channel_id=1, source_target_pairs={{0,1},{1,0},{2,3},{3,2},{4,5},{5,4},{6,7},{7,6},{8,9},{9,8},{10,11... | collective-permute-start | bytes 3145736 | tf_op jit(solution)/shard_map/ppermute | solution.py:1212
  345.1 41.2 %collective-permute-start.52 = (bf16[3,2,512,128]{3,2,1,0:T(8,128)(2,1)S(1)}, bf16[3,2,512,128]{3,2,1,0:T(8,128)(2,1)S(1)}, u32[]{:S(2)}, u32[]{:S(2)}) collective-permute-start(bf16[3,2,512,128]{3,2,1,0:T(8,128)(2,1)S(1)} %add_convert_fusion.refs_0_), channel_id=1, source_target_pairs={{0,16},{4,20},{8,24},{12,28},{16,0},{20,4},{24,8},{28,12},{1,17},{... | collective-permute-start | bytes 2359304 | tf_op jit(solution)/shard_map/ppermute | solution.py:1204
  374.1 35.2 %collective-permute-start.58 = (bf16[4,128,512]{2,1,0:T(8,128)(2,1)}, bf16[4,128,512]{2,1,0:T(8,128)(2,1)S(1)}, u32[]{:S(2)}, u32[]{:S(2)}) collective-permute-start(bf16[4,128,512]{2,1,0:T(8,128)(2,1)} %get-tuple-element.192.refs_1_), channel_id=1, source_target_pairs={{0,2},{1,3},{2,0},{3,1},{4,6},{5,7},{6,4},{7,5},{8,10},{9,11},{10,... | collective-permute-start | bytes 1572872 | tf_op jit(solution)/shard_map/ppermute | solution.py:1208
  384.4 81.7 %collective-permute-start.73 = (bf16[2,4,2,512,128]{4,3,2,1,0:T(8,128)(2,1)}, bf16[2,4,2,512,128]{4,3,2,1,0:T(8,128)(2,1)}, u32[]{:S(2)}, u32[]{:S(2)}) collective-permute-start(bf16[2,4,2,512,128]{4,3,2,1,0:T(8,128)(2,1)} %get-tuple-element.193.refs_2_), channel_id=1, source_target_pairs={{0,1},{1,0},{2,3},{3,2},{4,5},{5,4},{6,7},{7,6},{8,9},{9,8},{10,11... | collective-permute-start | bytes 6291464 | tf_op jit(solution)/shard_map/ppermute | solution.py:1212
  409.5 38.2 %collective-permute-start.59 = (bf16[4,128,512]{2,1,0:T(8,128)(2,1)S(1)}, bf16[4,128,512]{2,1,0:T(8,128)(2,1)S(1)}, u32[]{:S(2)}, u32[]{:S(2)}) collective-permute-start(bf16[4,128,512]{2,1,0:T(8,128)(2,1)S(1)} %add_convert_fusion.1), channel_id=1, source_target_pairs={{0,16},{4,20},{8,24},{12,28},{16,0},{20,4},{24,8},{28,12},{1,17},{... | collective-permute-start | bytes 1572872 | tf_op jit(solution)/shard_map/ppermute | solution.py:1204
  409.9 47.1 %collective-permute-start.69 = (bf16[2,4,128,512]{3,2,1,0:T(8,128)(2,1)S(1)}, bf16[2,4,128,512]{3,2,1,0:T(8,128)(2,1)S(1)}, u32[]{:S(2)}, u32[]{:S(2)}) collective-permute-start(bf16[2,4,128,512]{3,2,1,0:T(8,128)(2,1)S(1)} %copy-done.68), channel_id=1, source_target_pairs={{0,1},{1,0},{2,3},{3,2},{4,5},{5,4},{6,7},{7,6},{8,9},{9,8},{10,11... | collective-permute-start | bytes 3145736 | tf_op jit(solution)/shard_map/ppermute | solution.py:1212
  420.6 25.7 %collective-permute-start.57 = (bf16[1,2,512,128]{3,2,1,0:T(8,128)(2,1)S(1)}, bf16[1,2,512,128]{3,2,1,0:T(8,128)(2,1)S(1)}, u32[]{:S(2)}, u32[]{:S(2)}) collective-permute-start(bf16[1,2,512,128]{3,2,1,0:T(8,128)(2,1)S(1)} %copy-done.42), channel_id=1, source_target_pairs={{0,16},{4,20},{8,24},{12,28},{16,0},{20,4},{24,8},{28,12},{1,17},{... | collective-permute-start | bytes 786440 | tf_op jit(solution)/shard_map/ppermute | solution.py:1204
  420.9 43.5 %collective-permute-start.55 = (bf16[256,896]{1,0:T(8,128)(2,1)}, bf16[256,896]{1,0:T(8,128)(2,1)}, u32[]{:S(2)}, u32[]{:S(2)}) collective-permute-start(bf16[256,896]{1,0:T(8,128)(2,1)} %get-tuple-element.205), channel_id=1, source_target_pairs={{0,4},{4,0},{8,12},{12,8},{16,20},{20,16},{24,28},{28,24},{1,5},{5... | collective-permute-start | bytes 1376264 | tf_op jit(solution)/shard_map/ppermute | solution.py:1204
  461.7 25.6 %collective-permute-start.72 = (bf16[4,128,512]{2,1,0:T(8,128)(2,1)}, bf16[4,128,512]{2,1,0:T(8,128)(2,1)S(1)}, u32[]{:S(2)}, u32[]{:S(2)}) collective-permute-start(bf16[4,128,512]{2,1,0:T(8,128)(2,1)} %get-tuple-element.213), channel_id=1, source_target_pairs={{0,2},{1,3},{2,0},{3,1},{4,6},{5,7},{6,4},{7,5},{8,10},{9,11},{10,... | collective-permute-start | bytes 1572872 | tf_op jit(solution)/shard_map/ppermute | solution.py:1208
  470.9 45.1 %collective-permute-start.74 = (bf16[4,2,512,128]{3,2,1,0:T(8,128)(2,1)}, bf16[4,2,512,128]{3,2,1,0:T(8,128)(2,1)S(1)}, u32[]{:S(2)}, u32[]{:S(2)}) collective-permute-start(bf16[4,2,512,128]{3,2,1,0:T(8,128)(2,1)} %get-tuple-element.215), channel_id=1, source_target_pairs={{0,2},{1,3},{2,0},{3,1},{4,6},{5,7},{6,4},{7,5},{8,10},{9,11},{10,... | collective-permute-start | bytes 3145736 | tf_op jit(solution)/shard_map/ppermute | solution.py:1208
  (125 other events, 1712.6 us)
